TPU v7x, 128 devices: a whole 4x4x4 slice. The times are simulated.
128 devices in a mesh: tok: 16 (over z, x_hi, core), ch: 8 (over y, x_lo).
Axes of the slice: x: 4 (x_hi: 2, x_lo: 2; x = x_hi * 2 + x_lo), y: 4, z: 4, core: 2. Of those that a mesh axis runs over, the one named last changes fastest.
Arguments:
- activations: bfloat16 [2048, 8192], P('ch', 'tok'), may hold values from -6 to 6
- proj_weight: bfloat16 [8192, 24576], P('tok', 'ch'), may hold values from -0.0625 to 0.0625
- short_taps: float32 [3, 3, 8192], replicated, may hold values from -3.5 to 3.5
- residues: float32 [16, 8192], replicated, may hold values from -0.25 to 0.25
- decay_rates: float32 [16, 8192], replicated, may hold values from 0.00012207031 to 0.1
- skip_gain: float32 [8192], replicated, may hold values from 0.5 to 1.5
- out_weight: bfloat16 [8192, 8192], P('ch', 'tok'), may hold values from -0.0625 to 0.0625
Outputs:
- layer_out: bfloat16 [2048, 8192], P('ch', 'tok')
All inputs are finite; a program needn't handle non-finite values.
Results may differ from a plain program's by a relative error of at most 0.035.
Values may be sent and summed in bfloat16 or wider, within the bound.
No kernel may reach another device: no remote copies, remote signals or barrier semaphores. Data moves between devices by JAX's collectives and lax.ppermute only.
A program may use at most 192 MiB of HBM per device.

v0:
```python
import math

import jax
import jax.numpy as jnp
from jax import lax
from jax.sharding import PartitionSpec as P

GROUP = 64


EXACT_PRODUCT = lax.Precision.HIGHEST


def phase_table(row_count, col_count, period):
    row_ids = lax.broadcasted_iota(jnp.int32, (row_count, col_count), 0)
    col_ids = lax.broadcasted_iota(jnp.int32, (row_count, col_count), 1)
    angles = (row_ids * col_ids % period).astype(jnp.float32) * (-2.0 * math.pi / period)
    return (jnp.cos(angles), jnp.sin(angles))


def forward_transform(signal, tables):
    cos_rows, sin_rows, cos_twist, sin_twist, cos_cols, sin_cols = tables
    chan_count = signal.shape[0]
    shaped = signal.reshape(chan_count, cos_rows.shape[0], cos_cols.shape[0])
    step_real = jnp.einsum("ka,cab->ckb", cos_rows, shaped, precision=EXACT_PRODUCT)
    step_imag = jnp.einsum("ka,cab->ckb", sin_rows, shaped, precision=EXACT_PRODUCT)
    turn_real = step_real * cos_twist - step_imag * sin_twist
    turn_imag = step_real * sin_twist + step_imag * cos_twist
    spec_real = jnp.einsum(
        "ckb,bm->ckm", turn_real, cos_cols, precision=EXACT_PRODUCT
    ) - jnp.einsum("ckb,bm->ckm", turn_imag, sin_cols, precision=EXACT_PRODUCT)
    spec_imag = jnp.einsum(
        "ckb,bm->ckm", turn_real, sin_cols, precision=EXACT_PRODUCT
    ) + jnp.einsum("ckb,bm->ckm", turn_imag, cos_cols, precision=EXACT_PRODUCT)
    return (spec_real, spec_imag)


def inverse_transform(spec_real, spec_imag, tables):
    cos_rows, sin_rows, cos_twist, sin_twist, cos_cols, sin_cols = tables
    step_real = jnp.einsum(
        "ckm,mb->ckb", spec_real, cos_cols, precision=EXACT_PRODUCT
    ) + jnp.einsum("ckm,mb->ckb", spec_imag, sin_cols, precision=EXACT_PRODUCT)
    step_imag = jnp.einsum(
        "ckm,mb->ckb", spec_imag, cos_cols, precision=EXACT_PRODUCT
    ) - jnp.einsum("ckm,mb->ckb", spec_real, sin_cols, precision=EXACT_PRODUCT)
    turn_real = step_real * cos_twist + step_imag * sin_twist
    turn_imag = step_imag * cos_twist - step_real * sin_twist
    restored = jnp.einsum("nk,ckb->cnb", cos_rows, turn_real, precision=EXACT_PRODUCT) + jnp.einsum(
        "nk,ckb->cnb", sin_rows, turn_imag, precision=EXACT_PRODUCT
    )
    length_total = cos_rows.shape[0] * cos_cols.shape[0]
    return restored.reshape(restored.shape[0], length_total) / float(length_total)


def body(activations, proj_weight, short_taps, residues, decay_rates, skip_gain, out_weight):
    tok_devices = lax.axis_size("tok")
    block_index = lax.axis_index("ch") * tok_devices + lax.axis_index("tok")
    seq_len = activations.shape[0] * lax.axis_size("ch")
    rows_all = lax.all_gather(activations, "ch", axis=0, tiled=True)
    summed = lax.psum_scatter(
        jnp.dot(rows_all, proj_weight, preferred_element_type=jnp.float32).astype(jnp.bfloat16),
        "tok",
        scatter_dimension=0,
        tiled=True,
    )
    moved = lax.all_to_all(summed, "tok", split_axis=1, concat_axis=0, tiled=True)
    projected = moved.T
    chan_dev = projected.shape[0] // 3
    grouped = projected.reshape(chan_dev // GROUP, 3, GROUP, seq_len)
    start_chan = block_index * chan_dev
    tap_slice = lax.dynamic_slice_in_dim(short_taps, start_chan, chan_dev, 2)
    tap_count = tap_slice.shape[1]

    def featurize(component):
        values = grouped[:, component].reshape(chan_dev, seq_len).astype(jnp.float32)
        padded = jnp.pad(values, ((0, 0), (tap_count - 1, 0)))
        result = jnp.zeros_like(values)
        for offset in range(tap_count):
            begin = tap_count - 1 - offset
            result = (
                result + tap_slice[component, offset][:, None] * padded[:, begin : begin + seq_len]
            )
        return result

    queries = featurize(0)
    key_feat = featurize(1)
    value_feat = featurize(2)
    gate_input = key_feat * value_feat
    chan_res = lax.dynamic_slice_in_dim(residues, start_chan, chan_dev, 1)
    chan_rates = lax.dynamic_slice_in_dim(decay_rates, start_chan, chan_dev, 1)
    chan_skip = lax.dynamic_slice_in_dim(skip_gain, start_chan, chan_dev, 0)
    positions = lax.iota(jnp.float32, seq_len)[None, :]
    kernel = jnp.zeros((chan_dev, seq_len), jnp.float32)
    for term_index in range(chan_res.shape[0]):
        kernel = kernel + chan_res[term_index][:, None] * jnp.exp(
            -chan_rates[term_index][:, None] * positions
        )
    length_total = 2 * seq_len
    col_count = min(128, length_total)
    row_count = length_total // col_count
    cos_rows, sin_rows = phase_table(row_count, row_count, row_count)
    cos_twist, sin_twist = phase_table(row_count, col_count, length_total)
    cos_cols, sin_cols = phase_table(col_count, col_count, col_count)
    tables = (cos_rows, sin_rows, cos_twist, sin_twist, cos_cols, sin_cols)
    padding = ((0, 0), (0, seq_len))
    gate_real, gate_imag = forward_transform(jnp.pad(gate_input, padding), tables)
    kern_real, kern_imag = forward_transform(jnp.pad(kernel, padding), tables)
    prod_real = gate_real * kern_real - gate_imag * kern_imag
    prod_imag = gate_real * kern_imag + gate_imag * kern_real
    convolved = (
        inverse_transform(prod_real, prod_imag, tables)[:, :seq_len]
        + chan_skip[:, None] * gate_input
    )
    gated = (queries * convolved).astype(jnp.bfloat16)
    gathered = lax.all_gather(gated, "tok", axis=0, tiled=True)
    return lax.psum_scatter(
        lax.dot_general(
            gathered, out_weight, (((0,), (0,)), ((), ())), preferred_element_type=jnp.float32
        ).astype(jnp.bfloat16),
        "ch",
        scatter_dimension=0,
        tiled=True,
    )


def solution(mesh):
    return jax.shard_map(
        body,
        mesh=mesh,
        in_specs=(P("ch", "tok"), P("tok", "ch"), P(), P(), P(), P(), P("ch", "tok")),
        out_specs=P("ch", "tok"),
        check_vma=False,
    )
```

profile of v0, /device:TPU:1, one launch (start us, length us, event | category | flops | bytes accessed | tf_op | source)
XLA Modules:
  0.0 353.5 jit_solution(7788107723489792872)
XLA Ops:
  6.5 0.7 all-gather.3.cloned.1.call-update
  7.3 0.0 reduce-scatter.3.cloned.1.call-start
  7.3 56.8 %all-gather.3.cloned.1.call-done = bf16[2048,512]{1,0:T(8,128)(2,1)} async-done(((bf16[256,512]{1,0:T(8,128)(2,1)}), bf16[2048,512]{1,0:T(8,128)(2,1)}) %all-gather.3.cloned.1.call-update) | async-done | bytes 2097168 | tf_op jit(solution)/shard_map/all_gather | solution.py:59
  64.1 11.2 %convolution_convert_fusion = bf16[2048,3072]{1,0:T(8,128)(2,1)} fusion(bf16[2048,512]{1,0:T(8,128)(2,1)} %all-gather.3.cloned.1.call-done, bf16[512,3072]{1,0:T(8,128)(2,1)S(1)} %copy-done), kind=kOutput, calls=%fused_computation | convolution fusion | flops 6448742400 | bytes 17825792 | tf_op jit(solution)/shard_map/dot_general | solution.py:61
  75.4 0.0 reduce-scatter.3.cloned.1.call-update
  75.4 1.2 fusion.119
  76.7 1.6 multiply_add_fusion.3
  78.3 0.1 pad_bitcast_fusion
  78.4 0.2 copy.12
  78.6 0.8 dynamic_slice.15
  79.3 0.1 fusion.86
  79.4 1.1 convolution_bitcast_fusion
  80.5 1.1 convolution_bitcast_fusion.1
  81.7 2.2 fusion.29
  83.9 2.2 fusion.30
  86.1 110.6 %reduce-scatter.3.cloned.1.call-done = bf16[128,3072]{1,0:T(8,128)(2,1)} async-done(((bf16[2048,3072]{1,0:T(8,128)(2,1)}), bf16[128,3072]{1,0:T(8,128)(2,1)}) %reduce-scatter.3.cloned.1.call-update) | async-done | bytes 786448 | tf_op jit(solution)/shard_map/reduce_scatter | solution.py:60
  196.7 2.3 copy.8
  199.0 5.3 %all-to-all-start = ((bf16[128,16,192]{0,2,1:T(8,128)(2,1)}), bf16[128,16,192]{0,2,1:T(8,128)(2,1)}, u32[]{:S(2)}, u32[]{:S(2)}) async-start(bf16[128,16,192]{0,2,1:T(8,128)(2,1)} %bitcast.185), calls=%async_computation.1 | async-start | bytes 1572864 | tf_op jit(solution)/shard_map/all_to_all | solution.py:66
  204.3 0.2 all-gather.5.cloned.1.call-start
  204.6 1.0 fusion.114
  205.6 4.1 %convolution_add_fusion.2 = f32[64,32,128]{2,1,0:T(8,128)} fusion(f32[64,32,128]{2,1,0:T(8,128)} %fusion.29, f32[64,32,128]{2,1,0:T(8,128)} %copy-done.1, f32[64,32,128]{2,1,0:T(8,128)} %copy-done.3, f32[32,128]{1,0:T(8,128)S(1)} %get-tuple-element.67, f32[32,128]{1,0:T(8,128)S(1)} %get-tuple-element.68), kind=kOutput, calls=%fused_computation.6 | convolution fusion | flops 403931136 | bytes 4227072 | tf_op jit(solution)/shard_map/ckb,bm->ckm/dot_general | solution.py:34
  209.7 2.2 convolution_subtract_fusion.1
  211.9 7.0 %all-to-all-done = bf16[128,16,192]{0,2,1:T(8,128)(2,1)} async-done(((bf16[128,16,192]{0,2,1:T(8,128)(2,1)}), bf16[128,16,192]{0,2,1:T(8,128)(2,1)}, u32[]{:S(2)}, u32[]{:S(2)}) %all-to-all-start) | async-done | bytes 786464 | tf_op jit(solution)/shard_map/all_to_all | solution.py:66
  218.9 1.2 copy_bitcast_fusion.1
  220.2 0.1 fusion.31
  220.3 0.7 fusion.17
  221.0 0.1 pad_bitcast_fusion.1
  221.1 0.2 copy.11
  221.3 1.1 convolution_bitcast_fusion.2
  222.4 1.1 convolution_bitcast_fusion.3
  223.5 1.2 fusion.28
  224.7 1.2 fusion.27
  226.0 1.2 convolution_subtract_fusion.2
  227.3 1.4 multiply_subtract_fusion
  228.7 1.5 fusion.43
  230.2 1.2 fusion.45
  231.4 1.2 convolution_subtract_fusion
  232.7 1.2 convolution_add_fusion.1
  233.9 1.2 fusion.4
  235.1 1.2 fusion
  236.3 0.6 copy.16
  236.9 1.1 fusion.12
  238.0 0.0 all-gather.5.cloned.1.call-update
  238.1 0.0 reduce-scatter.5.cloned.1.call-start
  238.1 52.9 %all-gather.5.cloned.1.call-done = bf16[1024,2048]{1,0:T(8,128)(2,1)} async-done(((bf16[64,2048]{1,0:T(8,128)(2,1)}), bf16[1024,2048]{1,0:T(8,128)(2,1)}) %all-gather.5.cloned.1.call-update) | async-done | bytes 4194320 | tf_op jit(solution)/shard_map/all_gather | solution.py:115
  291.0 6.2 %convolution_convert_fusion.1 = bf16[2048,512]{1,0:T(8,128)(2,1)} fusion(bf16[1024,2048]{1,0:T(8,128)(2,1)} %all-gather.5.cloned.1.call-done, bf16[1024,512]{1,0:T(8,128)(2,1)} %param.13), kind=kOutput, calls=%fused_computation.1 | convolution fusion | flops 2148532224 | bytes 7340032 | tf_op jit(solution)/shard_map/dot_general | solution.py:117
  297.2 0.0 reduce-scatter.5.cloned.1.call-update
  297.2 49.8 %reduce-scatter.5.cloned.1.call-done = bf16[256,512]{1,0:T(8,128)(2,1)} async-done(((bf16[2048,512]{1,0:T(8,128)(2,1)}), bf16[256,512]{1,0:T(8,128)(2,1)}) %reduce-scatter.5.cloned.1.call-update) | async-done | bytes 262160 | tf_op jit(solution)/shard_map/reduce_scatter | solution.py:116
  (17 shorter events, 0.0 us)
Async XLA Ops:
  6.5 57.6 %copy-start = (bf16[512,3072]{1,0:T(8,128)(2,1)S(1)}, bf16[512,3072]{1,0:T(8,128)(2,1)}, u32[]{:S(2)}) copy-start(bf16[512,3072]{1,0:T(8,128)(2,1)} %param.8) | copy-start | bytes 9437188
  6.5 57.6 %all-gather.3.cloned.1.call-start = ((), (), s32[]{:S(2)}) async-start(), calls=%async_computation.3 | async-start | bytes 2359296 | tf_op jit(solution)/shard_map/all_gather | solution.py:59
  7.3 189.4 %reduce-scatter.3.cloned.1.call-start = ((), (), s32[]{:S(2)}) async-start(), calls=%async_computation.4 | async-start | bytes 13369344 | tf_op jit(solution)/shard_map/reduce_scatter | solution.py:60
  80.5 3.3 copy-start.1
  81.6 2.2 copy-start.3
  199.0 19.9 %all-to-all-start = ((bf16[128,16,192]{0,2,1:T(8,128)(2,1)}), bf16[128,16,192]{0,2,1:T(8,128)(2,1)}, u32[]{:S(2)}, u32[]{:S(2)}) async-start(bf16[128,16,192]{0,2,1:T(8,128)(2,1)} %bitcast.185), calls=%async_computation.1 | async-start | bytes 1572864 | tf_op jit(solution)/shard_map/all_to_all | solution.py:66
  204.3 86.7 %all-gather.5.cloned.1.call-start = ((), (), s32[]{:S(2)}) async-start(), calls=%async_computation.5 | async-start | bytes 4456448 | tf_op jit(solution)/shard_map/all_gather | solution.py:115
  204.5 5.1 %copy-start.2 = (f32[64,32,128]{2,1,0:T(8,128)S(1)}, f32[64,32,128]{2,1,0:T(8,128)}, u32[]{:S(2)}) copy-start(f32[64,32,128]{2,1,0:T(8,128)} %copy-done.1) | copy-start | bytes 3145732
  204.6 5.1 %copy-start.4 = (f32[64,32,128]{2,1,0:T(8,128)S(1)}, f32[64,32,128]{2,1,0:T(8,128)}, u32[]{:S(2)}) copy-start(f32[64,32,128]{2,1,0:T(8,128)} %copy-done.3) | copy-start | bytes 3145732
  204.6 5.1 %copy-start.5 = (f32[64,32,128]{2,1,0:T(8,128)S(1)}, f32[64,32,128]{2,1,0:T(8,128)}, u32[]{:S(2)}) copy-start(f32[64,32,128]{2,1,0:T(8,128)} %fusion.30) | copy-start | bytes 3145732
  224.7 2.5 copy-start.6
  224.7 2.5 copy-start.7
  238.1 108.9 %reduce-scatter.5.cloned.1.call-start = ((), (), s32[]{:S(2)}) async-start(), calls=%async_computation.6 | async-start | bytes 2359296 | tf_op jit(solution)/shard_map/reduce_scatter | solution.py:116
Sparse Core Ops, SparseCore 0:
  9.0 55.0 all-gather.2
  75.5 121.0 reduce-scatter.2
  238.2 52.7 all-gather.4
  297.3 49.5 reduce-scatter.4
where the time goes:
time: 354 us
  waiting for transfers between devices  278 us (79%)
  matrix products  45.3 us (13%)
  between operations  13.4 us (4%)
  local copies, waits for them, and re-layouts  6.5 us (2%)
  starting transfers between devices  5.63 us (2%)
  other arithmetic  4.87 us (1%)
    reduce_scatter x1, waiting for transfers between devices, body(): lax.psum_scatter(jnp.dot(rows_all, proj_weight, preferred_element_type=jn...  111 us
    all_gather x1, waiting for transfers between devices, body(): rows_all = lax.all_gather(activations, 'ch', axis=0, tiled=True)  56.8 us
    all_gather x1, waiting for transfers between devices, body(): gathered = lax.all_gather(gated, 'tok', axis=0, tiled=True)  52.9 us
    reduce_scatter x1, waiting for transfers between devices, body(): lax.psum_scatter(lax.dot_general(gathered, out_weight, (((0,), (0,)), (()...  49.8 us
    dot_general x1, matrix products, body(): jnp.dot(rows_all, proj_weight, preferred_element_type=jnp.float32)  11.2 us
  transfers between devices with their start and end apart: 5, of which 5 were waited for; matrix products, arithmetic and copies ran while one was open for 5% of the time, Pallas kernels for 0%

commit v1 on v0

v1 whole, which is shorter than its diff:
```python
import jax
import jax.numpy as jnp
from jax import lax
from jax.experimental import pallas as pl
from jax.experimental.pallas import tpu as pltpu
from jax.sharding import PartitionSpec as P

Z, XH, CORES = 4, 2, 2
Y, XL = 4, 2
BLOCKS = Y * XL
LANES = 128
BF = jnp.bfloat16
F32 = jnp.float32


def tok_perm(move):
    pairs = []
    for z in range(Z):
        for xh in range(XH):
            for c in range(CORES):
                nz, nx, nc = move(z, xh, c)
                pairs.append(((z * XH + xh) * CORES + c, ((nz % Z) * XH + nx) * CORES + nc))
    return pairs


def ch_perm(move):
    pairs = []
    for y in range(Y):
        for xl in range(XL):
            ny, nx = move(y, xl)
            pairs.append((y * XL + xl, (ny % Y) * XL + nx))
    return pairs


CORE_SWAP = tok_perm(lambda z, xh, c: (z, xh, 1 - c))
Z_UP = tok_perm(lambda z, xh, c: (z + 1, xh, c))
Z_DOWN = tok_perm(lambda z, xh, c: (z - 1, xh, c))
X_SWAP = tok_perm(lambda z, xh, c: (z, 1 - xh, c))


def tok_send(value, perm):
    return lax.ppermute(value, "tok", perm)


def ch_send(value, perm):
    return lax.ppermute(value, "ch", perm)


def swap(value):
    return tok_send(value, CORE_SWAP)


def add(*terms):
    total = terms[0].astype(F32)
    for term in terms[1:]:
        total = total + term.astype(F32)
    return total.astype(BF)


def whole(shape):
    return pl.BlockSpec(shape, lambda *_: (0,) * len(shape))


def project_kernel(pieces, targets, where_ref, *refs):
    rows_refs, (own_ref, other_ref), out_refs = (
        refs[:pieces],
        refs[pieces : pieces + 2],
        refs[pieces + 2 :],
    )
    rows = jnp.concatenate([ref[...] for ref in rows_refs], axis=0)
    depth = own_ref.shape[0]
    product = jnp.dot(rows[:, :depth], own_ref[...], preferred_element_type=F32) + jnp.dot(
        rows[:, depth:], other_ref[...], preferred_element_type=F32
    )
    product = product.astype(BF)
    for target in range(targets):

        @pl.when(pl.program_id(0) == target)
        def _(target=target):
            out_refs[target][...] = product


def project(pieces, own_weight, other_weight, where, steps):
    depth, cols = own_weight.shape
    width = cols // (Z * XH)
    tokens = sum(piece.shape[0] for piece in pieces)
    targets = len(steps) * XH

    def source(g, where_ref):
        step = steps[0]
        for k in range(1, len(steps)):
            step = jnp.where(g // XH == k, steps[k], step)
        return (0, ((where_ref[0] + step) % Z) * XH + (where_ref[1] + g) % XH)

    outs = pl.pallas_call(
        lambda *refs: project_kernel(len(pieces), targets, *refs),
        out_shape=[jax.ShapeDtypeStruct((tokens, width), BF)] * targets,
        grid_spec=pltpu.PrefetchScalarGridSpec(
            num_scalar_prefetch=1,
            grid=(targets,),
            in_specs=[whole(piece.shape) for piece in pieces]
            + [pl.BlockSpec((depth, width), source)] * 2,
            out_specs=[whole((tokens, width))] * targets,
        ),
        cost_estimate=pl.CostEstimate(
            flops=2 * tokens * 2 * depth * width * targets,
            bytes_accessed=2 * (tokens * 2 * depth + 2 * depth * width * targets + tokens * width * targets),
            transcendentals=0,
        ),
        name="project",
    )(where, *pieces, own_weight, other_weight)
    return {(steps[k // XH], k % XH): outs[k] for k in range(targets)}


def reduce_chips(pieces, own_weight, other_weight, where):
    part = project(pieces, own_weight, other_weight, where, (2,))
    from_below = tok_send(part[2, 0], Z_UP)
    from_above = tok_send(part[2, 1], Z_DOWN)
    part.update(project(pieces, own_weight, other_weight, where, (1, 3)))
    far_below = tok_send(part[1, 1], Z_UP)
    near_above = tok_send(part[3, 0], Z_DOWN)
    part.update(project(pieces, own_weight, other_weight, where, (0,)))
    far_above = tok_send(add(part[3, 1], from_above), Z_DOWN)
    near_below = tok_send(add(part[1, 0], from_below), Z_UP)
    across = tok_send(add(part[0, 1], far_below, far_above), X_SWAP)
    return [part[0, 0], near_above, near_below, across]


def features(block):
    half = LANES // 2
    low = lax.broadcasted_iota(jnp.int32, (1, LANES), 1) < half
    first, second, third = (block[:, k * LANES : (k + 1) * LANES] for k in range(3))
    return (
        jnp.where(low, first, second),
        jnp.where(low, pltpu.roll(first, half, 1), pltpu.roll(third, half, 1)),
        jnp.where(low, second, third),
    )


def every(ref, row, length):
    return ref[pl.ds(row, BLOCKS, stride=length), :]


def local_kernel(groups, where_ref, taps_ref, rates_ref, *refs):
    count = 4
    term_refs = [refs[g * count : (g + 1) * count] for g in range(groups)]
    query_ref, gate_ref, edge_ref = refs[groups * count : groups * count + 3]
    raw_refs = refs[groups * count + 3 : groups * count + 6]
    key_ref, value_ref = refs[groups * count + 6 :]
    length = gate_ref.shape[0] // BLOCKS
    order = rates_ref.shape[0]
    rows = lax.broadcasted_iota(jnp.int32, (length, LANES), 0)
    for g in range(groups):
        for dy in range(Y):
            here = slice(dy * length, (dy + 1) * length)
            block = term_refs[g][0][here, :].astype(F32)
            for ref in term_refs[g][1:]:
                block = block + ref[here, :].astype(F32)
            spot = (lax.rem(where_ref[3] + dy, Y)) * XL + lax.rem(where_ref[4] + g, XL)
            there = pl.ds(pl.multiple_of(spot * length, length), length)
            mixed = []
            for f, raw in enumerate(features(block)):
                raw_refs[f][there, :] = raw
                total = taps_ref[3 * f : 3 * f + 1, :] * raw
                for back in (1, 2):
                    moved = jnp.where(rows >= back, pltpu.roll(raw, back, 0), 0.0)
                    total = total + taps_ref[3 * f + back : 3 * f + back + 1, :] * moved
                mixed.append(total)
            query_ref[there, :] = mixed[0]
            key_ref[there, :] = mixed[1]
            value_ref[there, :] = mixed[2]
            gate_ref[there, :] = mixed[1] * mixed[2]
    decay = [
        jnp.broadcast_to(jnp.exp(-rates_ref[n : n + 1, :]), (BLOCKS, LANES)) for n in range(order)
    ]

    def step(r, states):
        gate = every(gate_ref, r, length)
        return tuple(decay[n] * states[n] + gate for n in range(order))

    states = lax.fori_loop(
        2, length, step, tuple(jnp.zeros((BLOCKS, LANES), F32) for _ in range(order)), unroll=6
    )
    for n in range(order):
        edge_ref[n] = states[n]
    at = order
    for r in (0, 1):
        edge_ref[at] = every(key_ref, r, length)
        edge_ref[at + 1] = every(value_ref, r, length)
        at += 2
    for f in range(3):
        for r in (length - 1, length - 2):
            edge_ref[at] = every(raw_refs[f], r, length)
            at += 1


def filter_kernel(where_ref, taps_ref, rates_ref, weights_ref, skip_ref, mine_ref, theirs_ref, query_ref, gate_ref, out_ref, work):
    length = gate_ref.shape[0] // BLOCKS
    order = rates_ref.shape[0]
    core = where_ref[2]
    first = core == 0
    spots = lax.broadcasted_iota(jnp.int32, (BLOCKS, LANES), 0)

    def later(value, count):
        return jnp.where(spots >= count, pltpu.roll(value, count, 0), 0.0)

    def tap(f, back):
        return taps_ref[3 * f + back : 3 * f + back + 1, :]

    def head(ref, before_ref, is_first):
        def before(f, back):
            value = before_ref[order + 4 + 2 * f + back - 1]
            return jnp.where(is_first, later(value, 1), value)

        key0 = ref[order] + tap(1, 1) * before(1, 1) + tap(1, 2) * before(1, 2)
        value0 = ref[order + 1] + tap(2, 1) * before(2, 1) + tap(2, 2) * before(2, 2)
        key1 = ref[order + 2] + tap(1, 2) * before(1, 1)
        value1 = ref[order + 3] + tap(2, 2) * before(2, 1)
        query0 = tap(0, 1) * before(0, 1) + tap(0, 2) * before(0, 2)
        query1 = tap(0, 2) * before(0, 1)
        return key0 * value0, key1 * value1, query0, query1

    gate0, gate1, query0, query1 = head(mine_ref, theirs_ref, first)
    their0, their1, _, _ = head(theirs_ref, mine_ref, jnp.logical_not(first))
    decay, states = [], []
    for n in range(order):
        rate = rates_ref[n : n + 1, :]
        factor0, factor1 = jnp.exp(-(length - 1) * rate), jnp.exp(-(length - 2) * rate)
        ours = mine_ref[n] + factor0 * gate0 + factor1 * gate1
        theirs = theirs_ref[n] + factor0 * their0 + factor1 * their1
        early, late = jnp.where(first, ours, theirs), jnp.where(first, theirs, ours)
        half = jnp.exp(-length * rate)
        total = half * early + late
        for count in (1, 2, 4):
            total = total + jnp.exp(-(2 * length * count) * rate) * later(total, count)
        before = later(total, 1)
        states.append(jnp.where(first, before, half * before + early))
        decay.append(jnp.broadcast_to(jnp.exp(-rate), (BLOCKS, LANES)))
    weights = [jnp.broadcast_to(weights_ref[n : n + 1, :], (BLOCKS, LANES)) for n in range(order)]
    skip = jnp.broadcast_to(skip_ref[...], (BLOCKS, LANES))

    def advance(r, states, gate, query):
        states = tuple(decay[n] * states[n] + gate for n in range(order))
        terms = [weights[n] * states[n] for n in range(order)] + [skip * gate]
        while len(terms) > 1:
            terms = [a + b for a, b in zip(terms[::2], terms[1::2])] + terms[len(terms) // 2 * 2 :]
        work[pl.ds(r, BLOCKS, stride=length), :] = query * terms[0]
        return states

    states = advance(0, tuple(states), gate0, every(query_ref, 0, length) + query0)
    states = advance(1, states, gate1, every(query_ref, 1, length) + query1)
    lax.fori_loop(
        2,
        length,
        lambda r, states: advance(r, states, every(gate_ref, r, length), every(query_ref, r, length)),
        states,
        unroll=6,
    )
    for g in range(XL):
        for dy in range(Y):
            spot = (lax.rem(where_ref[3] + dy, Y)) * XL + lax.rem(where_ref[4] + g, XL)
            there = pl.ds(pl.multiple_of(spot * length, length), length)
            place = (g * Y + dy) * length
            out_ref[place : place + length, :] = work[there, :].astype(BF)


def local_part(where, taps, rates, groups):
    tokens = sum(terms[0].shape[0] for terms in groups)
    flat = [term for terms in groups for term in terms]
    edges = rates.shape[0] + 10
    tall = jax.ShapeDtypeStruct((tokens, LANES), F32)
    return pl.pallas_call(
        lambda *refs: local_kernel(len(groups), *refs),
        out_shape=(tall, tall, jax.ShapeDtypeStruct((edges, BLOCKS, LANES), F32)),
        in_specs=[pl.BlockSpec(memory_space=pltpu.SMEM)]
        + [pl.BlockSpec(memory_space=pltpu.VMEM)] * (2 + len(flat)),
        out_specs=[pl.BlockSpec(memory_space=pltpu.VMEM)] * 3,
        scratch_shapes=[pltpu.VMEM((tokens, LANES), F32)] * 5,
        name="local_part",
    )(where, taps, rates, *flat)


def filtered(where, taps, rates, weights, skip, mine, theirs, query, gate):
    vmem = pl.BlockSpec(memory_space=pltpu.VMEM)
    return pl.pallas_call(
        filter_kernel,
        out_shape=jax.ShapeDtypeStruct(gate.shape, BF),
        in_specs=[pl.BlockSpec(memory_space=pltpu.SMEM)] + [vmem] * 8,
        out_specs=vmem,
        scratch_shapes=[pltpu.VMEM(gate.shape, F32)],
        name="filtered",
    )(where, taps, rates, weights, skip, mine, theirs, query, gate)


def output_kernel(count, where_ref, *refs):
    piece_refs, (own_ref, other_ref), out_refs = refs[:count], refs[count : count + 2], refs[count + 2 :]
    cols = own_ref.shape[1]
    swapped = where_ref[2] == 1
    rows = out_refs[0].shape[0]

    def weight(k):
        chip = lax.rem(where_ref[0] + k // XH, Z) * XH + lax.rem(where_ref[1] + k, XH)
        return pl.ds(pl.multiple_of(chip * LANES, LANES), LANES)

    for k in range(0, count, 2):
        left = jnp.concatenate([piece_refs[k][...], piece_refs[k + 1][...]], axis=1)
        for side, ref in enumerate((own_ref, other_ref)):
            right = jnp.concatenate([ref[weight(k), :], ref[weight(k + 1), :]], axis=0)
            product = jnp.dot(left, right, preferred_element_type=F32)
            acc = refs[-1]
            if k == 0:
                acc[side] = product
            else:
                acc[side] += product
    for d, out_ref in enumerate(out_refs[:-1]):
        for side in range(2):
            out_ref[:, side * cols : (side + 1) * cols] = acc[side, d * rows : (d + 1) * rows, :].astype(BF)


def output_parts(where, pieces, own_weight, other_weight):
    tokens = pieces[0].shape[0]
    cols = own_weight.shape[1]
    vmem = pl.BlockSpec(memory_space=pltpu.VMEM)
    return pl.pallas_call(
        lambda *refs: output_kernel(len(pieces), *refs),
        out_shape=[jax.ShapeDtypeStruct((tokens // BLOCKS, 2 * cols), BF)] * BLOCKS,
        in_specs=[pl.BlockSpec(memory_space=pltpu.SMEM)] + [vmem] * (len(pieces) + 2),
        out_specs=[vmem] * BLOCKS,
        scratch_shapes=[pltpu.VMEM((2, tokens, cols), F32)],
        name="output_parts",
    )(where, *pieces, own_weight, other_weight)


def body(activations, proj_weight, short_taps, residues, decay_rates, skip_gain, out_weight):
    tok_index = lax.axis_index("tok")
    ch_index = lax.axis_index("ch")
    z, xh, core = tok_index // (XH * CORES), tok_index // CORES % XH, tok_index % CORES
    y, xl = ch_index // XL, ch_index % XL
    where = jnp.stack([z, xh, core, y, xl]).astype(jnp.int32)
    length = activations.shape[0] // CORES

    kept = lax.dynamic_slice_in_dim(activations, core * length, length, 0)
    other = swap(lax.dynamic_slice_in_dim(activations, (1 - core) * length, length, 0))
    mine = jnp.concatenate([kept, other], axis=1)
    other_weight = swap(proj_weight)
    other_out = swap(out_weight)

    start = (ch_index * (Z * XH) + z * XH + xh) * LANES
    taps = lax.dynamic_slice_in_dim(short_taps, start, LANES, 2).reshape(-1, LANES)
    weights = lax.dynamic_slice_in_dim(residues, start, LANES, 1)
    rates = lax.dynamic_slice_in_dim(decay_rates, start, LANES, 1)
    skip = lax.dynamic_slice_in_dim(skip_gain, start, LANES, 0)[None]

    groups = []
    for dx in range(XL):
        pieces = []
        for dy in range(Y):
            if dx or dy:
                pieces.append(ch_send(mine, ch_perm(lambda y, xl, dx=dx, dy=dy: (y - dy, xl ^ dx))))
            else:
                pieces.append(mine)
        groups.append(reduce_chips(pieces, proj_weight, other_weight, where))
    query, gate, edges = local_part(where, taps, rates, groups)
    gated = filtered(where, taps, rates, weights, skip, edges, swap(edges), query, gate)

    pieces = [gated]
    for k in range(1, Z * XH):
        dz, dx = k // XH, k % XH
        pieces.append(tok_send(gated, tok_perm(lambda z, xh, c, dz=dz, dx=dx: (z - dz, xh ^ dx, c))))
    parts = output_parts(where, pieces, out_weight, other_out)
    terms = [parts[0]]
    for k in range(1, BLOCKS):
        dx, dy = k // Y, k % Y
        terms.append(ch_send(parts[k], ch_perm(lambda y, xl, dx=dx, dy=dy: (y + dy, xl ^ dx))))
    total = add(*terms)
    cols = out_weight.shape[1]
    kept, other = total[:, :cols], swap(total[:, cols:])
    return jnp.where(core == 0, jnp.concatenate([kept, other]), jnp.concatenate([other, kept]))


def solution(mesh):
    return jax.shard_map(
        body,
        mesh=mesh,
        in_specs=(P("ch", "tok"), P("tok", "ch"), P(), P(), P(), P(), P("ch", "tok")),
        out_specs=P("ch", "tok"),
        check_vma=False,
    )
```

time: 354 us -> 220 us (0.62)
  waiting for transfers between devices: 278 us -> 102 us
  starting transfers between devices: 5.63 us -> 56 us
  Pallas kernels: 0 us -> 46.7 us
  matrix products: 45.3 us -> 0 us
  between operations: 13.4 us -> 0.43 us
    reduce_scatter x2 -> x0, waiting for transfers between devices: 160 us -> none  [the longest x1 111 us: body(): lax.psum_scatter(jnp.dot(rows_all, proj_weight, preferred_element_type=jn...]
    all_gather x2 -> x0, waiting for transfers between devices: 110 us -> none  [the longest x1 56.8 us: body(): rows_all = lax.all_gather(activations, 'ch', axis=0, tiled=True)]
    ppermute x0 -> x40, waiting for transfers between devices: none -> 102 us  [the longest x26 66.7 us: tok_send(): return lax.ppermute(value, 'tok', perm)]
    ppermute x0 -> x40, starting transfers between devices: none -> 56 us  [the longest x26 39.7 us: tok_send(): return lax.ppermute(value, 'tok', perm)]
    pallas_call x0 -> x9, Pallas kernels: none -> 46.7 us  [the longest x6 32.2 us: project(): pl.pallas_call(lambda *refs: project_kernel(len(pieces), targets, *refs),...]
    dot_general x20 -> x0, matrix products: 45.3 us -> none  [the longest x1 11.2 us: body(): jnp.dot(rows_all, proj_weight, preferred_element_type=jnp.float32)]
    all_to_all x1 -> x0, waiting for transfers between devices: 7.03 us -> none  [body(): lax.all_to_all(summed, 'tok', split_axis=1, concat_axis=0, tiled=True)]
    all_to_all x1 -> x0, starting transfers between devices: 5.33 us -> none  [body(): lax.all_to_all(summed, 'tok', split_axis=1, concat_axis=0, tiled=True)]
  transfers between devices with their start and end apart: 5 -> 40, of which waited for: 5 -> 18; matrix products, arithmetic and copies ran while one was open for 5% -> 4% of each run, Pallas kernels for 0% -> 19%
where the time goes in v1:
time: 220 us; the launch traced here: 218 us
  waiting for transfers between devices  102 us (46%)
  starting transfers between devices  56 us (25%)
  Pallas kernels  46.7 us (21%)
  local copies, waits for them, and re-layouts  8.87 us (4%)
  other arithmetic  3.75 us (2%)
    ppermute x26, waiting for transfers between devices, tok_send(): return lax.ppermute(value, 'tok', perm)  66.7 us
    ppermute x26, starting transfers between devices, tok_send(): return lax.ppermute(value, 'tok', perm)  39.7 us
    ppermute x14, waiting for transfers between devices, ch_send(): return lax.ppermute(value, 'ch', perm)  35.3 us
    pallas_call x6, Pallas kernels, project(): pl.pallas_call(lambda *refs: project_kernel(len(pieces), targets, *refs),...  32.2 us
    ppermute x14, starting transfers between devices, ch_send(): return lax.ppermute(value, 'ch', perm)  16.3 us
    pallas_call x1, Pallas kernels, output_parts(): pl.pallas_call(lambda *refs: output_kernel(len(pieces), *refs), out_shape...  5.66 us
    pallas_call x1, Pallas kernels, local_part(): pl.pallas_call(lambda *refs: local_kernel(len(groups), *refs), out_shape=...  4.61 us
  transfers between devices with their start and end apart: 40, of which 18 were waited for; matrix products, arithmetic and copies ran while one was open for 4% of the time, Pallas kernels for 19%

profile of v1, /device:TPU:1, one launch (start us, length us, event | category | flops | bytes accessed | tf_op | source)
XLA Modules:
  0.0 217.7 jit_solution(8882565958619860818)
XLA Ops:
  0.0 1.4 collective-permute-start.4
  2.6 4.3 %collective-permute-done = bf16[128,512]{1,0:T(8,128)(2,1)S(1)} collective-permute-done((bf16[128,512]{1,0:T(8,128)(2,1)S(1)}, bf16[128,512]{1,0:T(8,128)(2,1)S(1)}, u32[]{:S(2)}, u32[]{:S(2)}) %collective-permute-start) | collective-permute-done | bytes 131104 | tf_op jit(solution)/shard_map/ppermute | solution.py:42
  6.9 1.4 collective-permute-start.12
  8.3 2.7 %collective-permute-start.13 = (bf16[128,1024]{1,0:T(8,128)(2,1)S(1)}, bf16[128,1024]{1,0:T(8,128)(2,1)S(1)}, u32[]{:S(2)}, u32[]{:S(2)}) collective-permute-start(bf16[128,1024]{1,0:T(8,128)(2,1)S(1)} %pad_maximum_fusion.refs_1_), channel_id=1, source_target_pairs={{0,7},{1,6},{2,1},{3,0},{4,3},{5,2},{6,5},{7,4},{8,15},{9,14},{10,... | collective-permute-start | bytes 786440 | tf_op jit(solution)/shard_map/ppermute | solution.py:46
  11.0 1.3 collective-permute-start.14
  13.0 1.6 collective-permute-done.12.refs_1_
  14.5 2.8 %collective-permute-start.1 = (bf16[128,1024]{1,0:T(8,128)(2,1)S(1)}, bf16[128,1024]{1,0:T(8,128)(2,1)S(1)}, u32[]{:S(2)}, u32[]{:S(2)}) collective-permute-start(bf16[128,1024]{1,0:T(8,128)(2,1)S(1)} %pad_maximum_fusion.refs_1_), channel_id=1, source_target_pairs={{0,6},{1,7},{2,0},{3,1},{4,2},{5,3},{6,4},{7,5},{8,14},{9,15},{10,... | collective-permute-start | bytes 786440 | tf_op jit(solution)/shard_map/ppermute | solution.py:46
  17.4 3.9 %collective-permute-done.13.refs_2_ = bf16[128,1024]{1,0:T(8,128)(2,1)S(1)} collective-permute-done((bf16[128,1024]{1,0:T(8,128)(2,1)S(1)}, bf16[128,1024]{1,0:T(8,128)(2,1)S(1)}, u32[]{:S(2)}, u32[]{:S(2)}) %collective-permute-start.13) | collective-permute-done | bytes 262176 | tf_op jit(solution)/shard_map/ppermute | solution.py:46
  21.3 2.6 %collective-permute-start.2 = (bf16[128,1024]{1,0:T(8,128)(2,1)S(1)}, bf16[128,1024]{1,0:T(8,128)(2,1)S(1)}, u32[]{:S(2)}, u32[]{:S(2)}) collective-permute-start(bf16[128,1024]{1,0:T(8,128)(2,1)S(1)} %pad_maximum_fusion.refs_1_), channel_id=1, source_target_pairs={{0,4},{1,5},{2,6},{3,7},{4,0},{5,1},{6,2},{7,3},{8,12},{9,13},{10,... | collective-permute-start | bytes 786440 | tf_op jit(solution)/shard_map/ppermute | solution.py:46
  23.9 4.7 %collective-permute-done.14.refs_3_ = bf16[128,1024]{1,0:T(8,128)(2,1)S(1)} collective-permute-done((bf16[128,1024]{1,0:T(8,128)(2,1)S(1)}, bf16[128,1024]{1,0:T(8,128)(2,1)S(1)}, u32[]{:S(2)}, u32[]{:S(2)}) %collective-permute-start.14) | collective-permute-done | bytes 262176 | tf_op jit(solution)/shard_map/ppermute | solution.py:46
  29.6 4.7 %collective-permute-done.15.refs_4_ = bf16[128,1024]{1,0:T(8,128)(2,1)S(1)} collective-permute-done((bf16[128,1024]{1,0:T(8,128)(2,1)S(1)}, bf16[128,1024]{1,0:T(8,128)(2,1)S(1)}, u32[]{:S(2)}, u32[]{:S(2)}) %collective-permute-start.15) | collective-permute-done | bytes 262176 | tf_op jit(solution)/shard_map/ppermute | solution.py:46
  34.3 1.3 collective-permute-start.31
  35.6 4.6 %project.11 = (bf16[512,384]{1,0:T(8,128)(2,1)}, bf16[512,384]{1,0:T(8,128)(2,1)}) custom-call(s32[5]{0:T(128)} %stack.23.refs_0_.where_ref, bf16[128,1024]{1,0:T(8,128)(2,1)} %copy-done.2, bf16[128,1024]{1,0:T(8,128)(2,1)} %copy-done.3, bf16[128,1024]{1,0:T(8,128)(2,1)} %copy-done.5, bf16[128,1024]{1,0:T(8,128)(2,1)} %copy-done.6, ...), custom_call_target="tpu_custom_call" | custom-call | flops 805306368 | bytes 3407872 | tf_op jit(solution)/shard_map/project/pallas_call | solution.py:95
  40.2 3.8 %collective-permute-start.20 = (bf16[512,384]{1,0:T(8,128)(2,1)}, bf16[512,384]{1,0:T(8,128)(2,1)S(1)}, u32[]{:S(2)}, u32[]{:S(2)}) collective-permute-start(bf16[512,384]{1,0:T(8,128)(2,1)} %get-tuple-element.47), channel_id=1, source_target_pairs={{0,96},{8,104},{16,112},{24,120},{32,0},{40,8},{48,16},{56,24},{64... | collective-permute-start | bytes 1179656 | tf_op jit(solution)/shard_map/ppermute | solution.py:42
  44.0 6.8 %project.10 = (bf16[512,384]{1,0:T(8,128)(2,1)}, bf16[512,384]{1,0:T(8,128)(2,1)}, bf16[512,384]{1,0:T(8,128)(2,1)}, bf16[512,384]{1,0:T(8,128)(2,1)}) custom-call(s32[5]{0:T(128)} %stack.23.refs_0_.where_ref, bf16[128,1024]{1,0:T(8,128)(2,1)} %copy-done.2, bf16[128,1024]{1,0:T(8,128)(2,1)} %copy-done.3, bf16[128,1024]{1,0:T(8,128)(2,1)} %copy-done.5, ...), custom_call_target="tpu_custom_call" | custom-call | flops 1610612736 | bytes 5767168 | tf_op jit(solution)/shard_map/project/pallas_call | solution.py:95
  52.4 4.6 %project.8 = (bf16[512,384]{1,0:T(8,128)(2,1)}, bf16[512,384]{1,0:T(8,128)(2,1)}) custom-call(s32[5]{0:T(128)} %stack.23.refs_0_.where_ref, bf16[128,1024]{1,0:T(8,128)(2,1)} %copy-done.1, bf16[128,1024]{1,0:T(8,128)(2,1)} %copy-done.4, bf16[128,1024]{1,0:T(8,128)(2,1)} %copy-done.7, bf16[128,1024]{1,0:T(8,128)(2,1)} %copy-done.8, ...), custom_call_target="tpu_custom_call" | custom-call | flops 805306368 | bytes 3407872 | tf_op jit(solution)/shard_map/project/pallas_call | solution.py:95
  57.0 2.7 %collective-permute-start.9 = (bf16[512,384]{1,0:T(8,128)(2,1)}, bf16[512,384]{1,0:T(8,128)(2,1)S(1)}, u32[]{:S(2)}, u32[]{:S(2)}) collective-permute-start(bf16[512,384]{1,0:T(8,128)(2,1)} %get-tuple-element.39), channel_id=1, source_target_pairs={{0,96},{8,104},{16,112},{24,120},{32,0},{40,8},{48,16},{56,24},{64... | collective-permute-start | bytes 1179656 | tf_op jit(solution)/shard_map/ppermute | solution.py:42
  59.6 4.6 %project.9 = (bf16[512,384]{1,0:T(8,128)(2,1)}, bf16[512,384]{1,0:T(8,128)(2,1)}) custom-call(s32[5]{0:T(128)} %stack.23.refs_0_.where_ref, bf16[128,1024]{1,0:T(8,128)(2,1)} %copy-done.2, bf16[128,1024]{1,0:T(8,128)(2,1)} %copy-done.3, bf16[128,1024]{1,0:T(8,128)(2,1)} %copy-done.5, bf16[128,1024]{1,0:T(8,128)(2,1)} %copy-done.6, ...), custom_call_target="tpu_custom_call" | custom-call | flops 805306368 | bytes 3407872 | tf_op jit(solution)/shard_map/project/pallas_call | solution.py:95
  64.3 4.6 %project.6 = (bf16[512,384]{1,0:T(8,128)(2,1)}, bf16[512,384]{1,0:T(8,128)(2,1)}) custom-call(s32[5]{0:T(128)} %stack.23.refs_0_.where_ref, bf16[128,1024]{1,0:T(8,128)(2,1)} %copy-done.1, bf16[128,1024]{1,0:T(8,128)(2,1)} %copy-done.4, bf16[128,1024]{1,0:T(8,128)(2,1)} %copy-done.7, bf16[128,1024]{1,0:T(8,128)(2,1)} %copy-done.8, ...), custom_call_target="tpu_custom_call" | custom-call | flops 805306368 | bytes 3407872 | tf_op jit(solution)/shard_map/project/pallas_call | solution.py:95
  68.8 7.0 %project.7 = (bf16[512,384]{1,0:T(8,128)(2,1)}, bf16[512,384]{1,0:T(8,128)(2,1)}, bf16[512,384]{1,0:T(8,128)(2,1)}, bf16[512,384]{1,0:T(8,128)(2,1)}) custom-call(s32[5]{0:T(128)} %stack.23.refs_0_.where_ref, bf16[128,1024]{1,0:T(8,128)(2,1)} %copy-done.1, bf16[128,1024]{1,0:T(8,128)(2,1)} %copy-done.4, bf16[128,1024]{1,0:T(8,128)(2,1)} %copy-done.7, ...), custom_call_target="tpu_custom_call" | custom-call | flops 1610612736 | bytes 5767168 | tf_op jit(solution)/shard_map/project/pallas_call | solution.py:95
  76.5 2.5 %collective-permute-start.21 = (bf16[512,384]{1,0:T(8,128)(2,1)S(1)}, bf16[512,384]{1,0:T(8,128)(2,1)S(1)}, u32[]{:S(2)}, u32[]{:S(2)}) collective-permute-start(bf16[512,384]{1,0:T(8,128)(2,1)S(1)} %add_convert_fusion.1), channel_id=1, source_target_pairs={{0,96},{8,104},{16,112},{24,120},{32,0},{40,8},{48,16},{56,24},{64... | collective-permute-start | bytes 1179656 | tf_op jit(solution)/shard_map/ppermute | solution.py:42
  80.1 14.8 %collective-permute-done.6 = bf16[512,384]{1,0:T(8,128)(2,1)S(1)} collective-permute-done((bf16[512,384]{1,0:T(8,128)(2,1)}, bf16[512,384]{1,0:T(8,128)(2,1)S(1)}, u32[]{:S(2)}, u32[]{:S(2)}) %collective-permute-start.6) | collective-permute-done | bytes 393248 | tf_op jit(solution)/shard_map/ppermute | solution.py:42
  96.9 6.2 %collective-permute-done.10 = bf16[512,384]{1,0:T(8,128)(2,1)S(1)} collective-permute-done((bf16[512,384]{1,0:T(8,128)(2,1)S(1)}, bf16[512,384]{1,0:T(8,128)(2,1)S(1)}, u32[]{:S(2)}, u32[]{:S(2)}) %collective-permute-start.10) | collective-permute-done | bytes 393248 | tf_op jit(solution)/shard_map/ppermute | solution.py:42
  103.2 8.3 %collective-permute-done.16.refs_8_ = bf16[512,384]{1,0:T(8,128)(2,1)S(1)} collective-permute-done((bf16[512,384]{1,0:T(8,128)(2,1)S(1)}, bf16[512,384]{1,0:T(8,128)(2,1)S(1)}, u32[]{:S(2)}, u32[]{:S(2)}) %collective-permute-start.16) | collective-permute-done | bytes 393248 | tf_op jit(solution)/shard_map/ppermute | solution.py:42
  111.5 2.7 %collective-permute-start.22 = (bf16[512,384]{1,0:T(8,128)(2,1)S(1)}, bf16[512,384]{1,0:T(8,128)(2,1)}, u32[]{:S(2)}, u32[]{:S(2)}) collective-permute-start(bf16[512,384]{1,0:T(8,128)(2,1)S(1)} %add_convert_fusion), channel_id=1, source_target_pairs={{0,16},{8,24},{16,0},{24,8},{32,48},{40,56},{48,32},{56,40},{64,80... | collective-permute-start | bytes 1179656 | tf_op jit(solution)/shard_map/ppermute | solution.py:42
  114.2 5.7 %collective-permute-done.5.refs_4_ = bf16[512,384]{1,0:T(8,128)(2,1)S(1)} collective-permute-done((bf16[512,384]{1,0:T(8,128)(2,1)S(1)}, bf16[512,384]{1,0:T(8,128)(2,1)S(1)}, u32[]{:S(2)}, u32[]{:S(2)}) %collective-permute-start.5) | collective-permute-done | bytes 393248 | tf_op jit(solution)/shard_map/ppermute | solution.py:42
  119.9 2.7 %collective-permute-start.11 = (bf16[512,384]{1,0:T(8,128)(2,1)S(1)}, bf16[512,384]{1,0:T(8,128)(2,1)}, u32[]{:S(2)}, u32[]{:S(2)}) collective-permute-start(bf16[512,384]{1,0:T(8,128)(2,1)S(1)} %add_convert_fusion.3), channel_id=1, source_target_pairs={{0,16},{8,24},{16,0},{24,8},{32,48},{40,56},{48,32},{56,40},{64,80... | collective-permute-start | bytes 1179656 | tf_op jit(solution)/shard_map/ppermute | solution.py:42
  124.6 1.3 constant_dynamic-slice_fusion.2.weights_ref
  125.9 6.8 %collective-permute-done.11.refs_6_ = bf16[512,384]{1,0:T(8,128)(2,1)} collective-permute-done((bf16[512,384]{1,0:T(8,128)(2,1)S(1)}, bf16[512,384]{1,0:T(8,128)(2,1)}, u32[]{:S(2)}, u32[]{:S(2)}) %collective-permute-start.11) | collective-permute-done | bytes 393248 | tf_op jit(solution)/shard_map/ppermute | solution.py:42
  132.8 4.6 %local_part.1 = (f32[1024,128]{1,0:T(8,128)}, f32[1024,128]{1,0:T(8,128)}, f32[26,8,128]{2,1,0:T(8,128)}) custom-call(s32[5]{0:T(128)} %stack.23.refs_0_.where_ref, f32[9,128]{1,0:T(8,128)} %reshape.3.refs_1_.taps_ref, f32[16,128]{1,0:T(8,128)} %constant_dynamic-slice_fusion.3.refs_2_.rates_ref, bf16[512,384]{1,0:T(8,128)(2,1)} %get-tuple-element.32.refs_3_, ...), custom_call_target="tpu_custom_call" | custom-call | tf_op jit(solution)/shard_map/local_part/pallas_call | solution.py:272
  137.4 2.8 %collective-permute-start.23 = (f32[26,8,128]{2,1,0:T(8,128)}, f32[26,8,128]{2,1,0:T(8,128)S(1)}, u32[]{:S(2)}, u32[]{:S(2)}) collective-permute-start(f32[26,8,128]{2,1,0:T(8,128)} %get-tuple-element.48.mine_ref), channel_id=1, source_target_pairs={{0,8},{8,0},{16,24},{24,16},{32,40},{40,32},{48,56},{56,48},{64,72... | collective-permute-start | bytes 319496 | tf_op jit(solution)/shard_map/ppermute | solution.py:42
  140.2 1.3 dynamic-slice_bitcast_fusion.skip_ref
  142.1 4.2 %filtered.1.refs_1_ = bf16[1024,128]{1,0:T(8,128)(2,1)} custom-call(s32[5]{0:T(128)} %stack.23.refs_0_.where_ref, f32[9,128]{1,0:T(8,128)} %reshape.3.refs_1_.taps_ref, f32[16,128]{1,0:T(8,128)} %constant_dynamic-slice_fusion.3.refs_2_.rates_ref, f32[16,128]{1,0:T(8,128)} %constant_dynamic-slice_fusion.2.weights_ref, ...), custom_call_target="tpu_custom_call" | custom-call | tf_op jit(solution)/shard_map/filtered/pallas_call | solution.py:285
  146.4 2.7 %collective-permute-start.24 = (bf16[1024,128]{1,0:T(8,128)(2,1)}, bf16[1024,128]{1,0:T(8,128)(2,1)S(1)}, u32[]{:S(2)}, u32[]{:S(2)}) collective-permute-start(bf16[1024,128]{1,0:T(8,128)(2,1)} %filtered.1.refs_1_), channel_id=1, source_target_pairs={{0,16},{8,24},{16,0},{24,8},{32,48},{40,56},{48,32},{56,40},{64,80... | collective-permute-start | bytes 786440 | tf_op jit(solution)/shard_map/ppermute | solution.py:42
  150.0 2.3 %collective-permute-start.27 = (bf16[1024,128]{1,0:T(8,128)(2,1)}, bf16[1024,128]{1,0:T(8,128)(2,1)S(1)}, u32[]{:S(2)}, u32[]{:S(2)}) collective-permute-start(bf16[1024,128]{1,0:T(8,128)(2,1)} %filtered.1.refs_1_), channel_id=1, source_target_pairs={{0,64},{8,72},{16,80},{24,88},{32,96},{40,104},{48,112},{56,120},{... | collective-permute-start | bytes 786440 | tf_op jit(solution)/shard_map/ppermute | solution.py:42
  152.3 3.1 %collective-permute-start.28 = (bf16[1024,128]{1,0:T(8,128)(2,1)}, bf16[1024,128]{1,0:T(8,128)(2,1)S(1)}, u32[]{:S(2)}, u32[]{:S(2)}) collective-permute-start(bf16[1024,128]{1,0:T(8,128)(2,1)} %filtered.1.refs_1_), channel_id=1, source_target_pairs={{0,80},{8,88},{16,64},{24,72},{32,112},{40,120},{48,96},{56,104},{... | collective-permute-start | bytes 786440 | tf_op jit(solution)/shard_map/ppermute | solution.py:42
  156.9 10.2 %collective-permute-done.25.refs_3_ = bf16[1024,128]{1,0:T(8,128)(2,1)S(1)} collective-permute-done((bf16[1024,128]{1,0:T(8,128)(2,1)}, bf16[1024,128]{1,0:T(8,128)(2,1)S(1)}, u32[]{:S(2)}, u32[]{:S(2)}) %collective-permute-start.25) | collective-permute-done | bytes 262176 | tf_op jit(solution)/shard_map/ppermute | solution.py:42
  167.2 4.5 %collective-permute-done.29.refs_7_ = bf16[1024,128]{1,0:T(8,128)(2,1)S(1)} collective-permute-done((bf16[1024,128]{1,0:T(8,128)(2,1)}, bf16[1024,128]{1,0:T(8,128)(2,1)S(1)}, u32[]{:S(2)}, u32[]{:S(2)}) %collective-permute-start.29) | collective-permute-done | bytes 262176 | tf_op jit(solution)/shard_map/ppermute | solution.py:42
  171.7 4.5 %collective-permute-done.30.refs_8_ = bf16[1024,128]{1,0:T(8,128)(2,1)S(1)} collective-permute-done((bf16[1024,128]{1,0:T(8,128)(2,1)}, bf16[1024,128]{1,0:T(8,128)(2,1)S(1)}, u32[]{:S(2)}, u32[]{:S(2)}) %collective-permute-start.30) | collective-permute-done | bytes 262176 | tf_op jit(solution)/shard_map/ppermute | solution.py:42
  176.9 5.7 %output_parts.1 = (bf16[128,1024]{1,0:T(8,128)(2,1)}, bf16[128,1024]{1,0:T(8,128)(2,1)}, bf16[128,1024]{1,0:T(8,128)(2,1)}, bf16[128,1024]{1,0:T(8,128)(2,1)}, b...) custom-call(s32[5]{0:T(128)} %stack.23.refs_0_.where_ref, ...), custom_call_target="tpu_custom_call" | custom-call | tf_op jit(solution)/shard_map/output_parts/pallas_call | solution.py:324
  182.6 1.3 collective-permute-start.33
  183.9 1.4 collective-permute-start.34
  185.3 1.8 collective-permute-start.36
  187.0 8.7 %collective-permute-done.32 = bf16[128,1024]{1,0:T(8,128)(2,1)S(1)} collective-permute-done((bf16[128,1024]{1,0:T(8,128)(2,1)}, bf16[128,1024]{1,0:T(8,128)(2,1)S(1)}, u32[]{:S(2)}, u32[]{:S(2)}) %collective-permute-start.32) | collective-permute-done | bytes 262176 | tf_op jit(solution)/shard_map/ppermute | solution.py:46
  195.8 9.7 %collective-permute-done.37 = bf16[128,1024]{1,0:T(8,128)(2,1)S(1)} collective-permute-done((bf16[128,1024]{1,0:T(8,128)(2,1)}, bf16[128,1024]{1,0:T(8,128)(2,1)S(1)}, u32[]{:S(2)}, u32[]{:S(2)}) %collective-permute-start.37) | collective-permute-done | bytes 262176 | tf_op jit(solution)/shard_map/ppermute | solution.py:46
  205.5 1.9 collective-permute-done.38
  207.5 1.3 add_convert_fusion.6
  208.8 7.1 %collective-permute-start.39 = (bf16[128,512]{1,0:T(8,128)(2,1)S(1)}, bf16[128,512]{1,0:T(8,128)(2,1)S(1)}, u32[]{:S(2)}, u32[]{:S(2)}) collective-permute-start(bf16[128,512]{1,0:T(8,128)(2,1)S(1)} %get-tuple-element.60), channel_id=1, source_target_pairs={{0,8},{8,0},{16,24},{24,16},{32,40},{40,32},{48,56},{56,48},{64,72... | collective-permute-start | bytes 393224 | tf_op jit(solution)/shard_map/ppermute | solution.py:42
  (114 shorter events, 15.6 us)
Async XLA Ops:
  0.0 124.0 %copy-start = (f32[16,8192]{1,0:T(8,128)S(1)}, f32[16,8192]{1,0:T(8,128)}, u32[]{:S(2)}) copy-start(f32[16,8192]{1,0:T(8,128)} %param.11) | copy-start | bytes 1572868
  0.0 35.6 %collective-permute-start.4 = (bf16[512,3072]{1,0:T(8,128)(2,1)}, bf16[512,3072]{1,0:T(8,128)(2,1)}, u32[]{:S(2)}, u32[]{:S(2)}) collective-permute-start(bf16[512,3072]{1,0:T(8,128)(2,1)} %refs_5_.11), channel_id=1, source_target_pairs={{0,8},{8,0},{16,24},{24,16},{32,40},{40,32},{48,56},{56,48},{64,72... | collective-permute-start | bytes 9437192 | tf_op jit(solution)/shard_map/ppermute | solution.py:42
  2.4 4.5 %collective-permute-start = (bf16[128,512]{1,0:T(8,128)(2,1)S(1)}, bf16[128,512]{1,0:T(8,128)(2,1)S(1)}, u32[]{:S(2)}, u32[]{:S(2)}) collective-permute-start(bf16[128,512]{1,0:T(8,128)(2,1)S(1)} %get-tuple-element.62), channel_id=1, source_target_pairs={{0,8},{8,0},{16,24},{24,16},{32,40},{40,32},{48,56},{56,48},{64,72... | collective-permute-start | bytes 393224 | tf_op jit(solution)/shard_map/ppermute | solution.py:42
  6.9 33.3 %copy-start.1 = (bf16[128,1024]{1,0:T(8,128)(2,1)}, bf16[128,1024]{1,0:T(8,128)(2,1)S(1)}, u32[]{:S(2)}) copy-start(bf16[128,1024]{1,0:T(8,128)(2,1)S(1)} %pad_maximum_fusion.refs_1_) | copy-start | bytes 786436
  6.9 7.6 %collective-permute-start.12 = (bf16[128,1024]{1,0:T(8,128)(2,1)S(1)}, bf16[128,1024]{1,0:T(8,128)(2,1)S(1)}, u32[]{:S(2)}, u32[]{:S(2)}) collective-permute-start(bf16[128,1024]{1,0:T(8,128)(2,1)S(1)} %pad_maximum_fusion.refs_1_), channel_id=1, source_target_pairs={{0,1},{1,0},{2,3},{3,2},{4,5},{5,4},{6,7},{7,6},{8,9},{9,8},{10,11... | collective-permute-start | bytes 786440 | tf_op jit(solution)/shard_map/ppermute | solution.py:46
  8.3 13.0 %collective-permute-start.13 = (bf16[128,1024]{1,0:T(8,128)(2,1)S(1)}, bf16[128,1024]{1,0:T(8,128)(2,1)S(1)}, u32[]{:S(2)}, u32[]{:S(2)}) collective-permute-start(bf16[128,1024]{1,0:T(8,128)(2,1)S(1)} %pad_maximum_fusion.refs_1_), channel_id=1, source_target_pairs={{0,7},{1,6},{2,1},{3,0},{4,3},{5,2},{6,5},{7,4},{8,15},{9,14},{10,... | collective-permute-start | bytes 786440 | tf_op jit(solution)/shard_map/ppermute | solution.py:46
  11.0 17.6 %collective-permute-start.14 = (bf16[128,1024]{1,0:T(8,128)(2,1)S(1)}, bf16[128,1024]{1,0:T(8,128)(2,1)S(1)}, u32[]{:S(2)}, u32[]{:S(2)}) collective-permute-start(bf16[128,1024]{1,0:T(8,128)(2,1)S(1)} %pad_maximum_fusion.refs_1_), channel_id=1, source_target_pairs={{0,5},{1,4},{2,7},{3,6},{4,1},{5,0},{6,3},{7,2},{8,13},{9,12},{10,... | collective-permute-start | bytes 786440 | tf_op jit(solution)/shard_map/ppermute | solution.py:46
  12.3 22.0 %collective-permute-start.15 = (bf16[128,1024]{1,0:T(8,128)(2,1)S(1)}, bf16[128,1024]{1,0:T(8,128)(2,1)S(1)}, u32[]{:S(2)}, u32[]{:S(2)}) collective-permute-start(bf16[128,1024]{1,0:T(8,128)(2,1)S(1)} %pad_maximum_fusion.refs_1_), channel_id=1, source_target_pairs={{0,3},{1,2},{2,5},{3,4},{4,7},{5,6},{6,1},{7,0},{8,11},{9,10},{10,... | collective-permute-start | bytes 786440 | tf_op jit(solution)/shard_map/ppermute | solution.py:46
  14.5 21.1 %copy-start.2 = (bf16[128,1024]{1,0:T(8,128)(2,1)}, bf16[128,1024]{1,0:T(8,128)(2,1)S(1)}, u32[]{:S(2)}) copy-start(bf16[128,1024]{1,0:T(8,128)(2,1)S(1)} %collective-permute-done.12.refs_1_) | copy-start | bytes 786436
  14.5 36.3 %collective-permute-start.1 = (bf16[128,1024]{1,0:T(8,128)(2,1)S(1)}, bf16[128,1024]{1,0:T(8,128)(2,1)S(1)}, u32[]{:S(2)}, u32[]{:S(2)}) collective-permute-start(bf16[128,1024]{1,0:T(8,128)(2,1)S(1)} %pad_maximum_fusion.refs_1_), channel_id=1, source_target_pairs={{0,6},{1,7},{2,0},{3,1},{4,2},{5,3},{6,4},{7,5},{8,14},{9,15},{10,... | collective-permute-start | bytes 786440 | tf_op jit(solution)/shard_map/ppermute | solution.py:46
  21.3 29.7 %collective-permute-start.2 = (bf16[128,1024]{1,0:T(8,128)(2,1)S(1)}, bf16[128,1024]{1,0:T(8,128)(2,1)S(1)}, u32[]{:S(2)}, u32[]{:S(2)}) collective-permute-start(bf16[128,1024]{1,0:T(8,128)(2,1)S(1)} %pad_maximum_fusion.refs_1_), channel_id=1, source_target_pairs={{0,4},{1,5},{2,6},{3,7},{4,0},{5,1},{6,2},{7,3},{8,12},{9,13},{10,... | collective-permute-start | bytes 786440 | tf_op jit(solution)/shard_map/ppermute | solution.py:46
  28.6 22.5 %collective-permute-start.3 = (bf16[128,1024]{1,0:T(8,128)(2,1)S(1)}, bf16[128,1024]{1,0:T(8,128)(2,1)S(1)}, u32[]{:S(2)}, u32[]{:S(2)}) collective-permute-start(bf16[128,1024]{1,0:T(8,128)(2,1)S(1)} %pad_maximum_fusion.refs_1_), channel_id=1, source_target_pairs={{0,2},{1,3},{2,4},{3,5},{4,6},{5,7},{6,0},{7,1},{8,10},{9,11},{10,... | collective-permute-start | bytes 786440 | tf_op jit(solution)/shard_map/ppermute | solution.py:46
  34.3 118.0 %collective-permute-start.31 = (bf16[1024,512]{1,0:T(8,128)(2,1)}, bf16[1024,512]{1,0:T(8,128)(2,1)}, u32[]{:S(2)}, u32[]{:S(2)}) collective-permute-start(bf16[1024,512]{1,0:T(8,128)(2,1)} %refs_9_.1), channel_id=1, source_target_pairs={{0,8},{8,0},{16,24},{24,16},{32,40},{40,32},{48,56},{56,48},{64,72... | collective-permute-start | bytes 3145736 | tf_op jit(solution)/shard_map/ppermute | solution.py:42
  40.2 35.6 %collective-permute-start.20 = (bf16[512,384]{1,0:T(8,128)(2,1)}, bf16[512,384]{1,0:T(8,128)(2,1)S(1)}, u32[]{:S(2)}, u32[]{:S(2)}) collective-permute-start(bf16[512,384]{1,0:T(8,128)(2,1)} %get-tuple-element.47), channel_id=1, source_target_pairs={{0,96},{8,104},{16,112},{24,120},{32,0},{40,8},{48,16},{56,24},{64... | collective-permute-start | bytes 1179656 | tf_op jit(solution)/shard_map/ppermute | solution.py:42
  50.9 44.1 %collective-permute-start.19 = (bf16[512,384]{1,0:T(8,128)(2,1)}, bf16[512,384]{1,0:T(8,128)(2,1)S(1)}, u32[]{:S(2)}, u32[]{:S(2)}) collective-permute-start(bf16[512,384]{1,0:T(8,128)(2,1)} %get-tuple-element.45), channel_id=1, source_target_pairs={{0,32},{8,40},{16,48},{24,56},{32,64},{40,72},{48,80},{56,88},{64,... | collective-permute-start | bytes 1179656 | tf_op jit(solution)/shard_map/ppermute | solution.py:42
  51.0 25.1 %collective-permute-start.17 = (bf16[512,384]{1,0:T(8,128)(2,1)S(1)}, bf16[512,384]{1,0:T(8,128)(2,1)S(1)}, u32[]{:S(2)}, u32[]{:S(2)}) collective-permute-start(bf16[512,384]{1,0:T(8,128)(2,1)S(1)} %copy-done.27), channel_id=1, source_target_pairs={{0,32},{8,40},{16,48},{24,56},{32,64},{40,72},{48,80},{56,88},{64,... | collective-permute-start | bytes 1179656 | tf_op jit(solution)/shard_map/ppermute | solution.py:42
  57.0 19.5 %collective-permute-start.9 = (bf16[512,384]{1,0:T(8,128)(2,1)}, bf16[512,384]{1,0:T(8,128)(2,1)S(1)}, u32[]{:S(2)}, u32[]{:S(2)}) collective-permute-start(bf16[512,384]{1,0:T(8,128)(2,1)} %get-tuple-element.39), channel_id=1, source_target_pairs={{0,96},{8,104},{16,112},{24,120},{32,0},{40,8},{48,16},{56,24},{64... | collective-permute-start | bytes 1179656 | tf_op jit(solution)/shard_map/ppermute | solution.py:42
  75.8 19.3 %copy-start.26 = (bf16[512,384]{1,0:T(8,128)(2,1)S(1)}, bf16[512,384]{1,0:T(8,128)(2,1)}, u32[]{:S(2)}) copy-start(bf16[512,384]{1,0:T(8,128)(2,1)} %get-tuple-element.33) | copy-start | bytes 1179652
  75.8 20.4 %copy-start.10 = (bf16[512,384]{1,0:T(8,128)(2,1)S(1)}, bf16[512,384]{1,0:T(8,128)(2,1)}, u32[]{:S(2)}) copy-start(bf16[512,384]{1,0:T(8,128)(2,1)} %get-tuple-element.44) | copy-start | bytes 1179652
  75.8 20.5 %collective-permute-start.8 = (bf16[512,384]{1,0:T(8,128)(2,1)}, bf16[512,384]{1,0:T(8,128)(2,1)S(1)}, u32[]{:S(2)}, u32[]{:S(2)}) collective-permute-start(bf16[512,384]{1,0:T(8,128)(2,1)} %get-tuple-element.37), channel_id=1, source_target_pairs={{0,32},{8,40},{16,48},{24,56},{32,64},{40,72},{48,80},{56,88},{64,... | collective-permute-start | bytes 1179656 | tf_op jit(solution)/shard_map/ppermute | solution.py:42
  75.9 27.1 %copy-start.9 = (bf16[512,384]{1,0:T(8,128)(2,1)S(1)}, bf16[512,384]{1,0:T(8,128)(2,1)}, u32[]{:S(2)}) copy-start(bf16[512,384]{1,0:T(8,128)(2,1)} %get-tuple-element.36) | copy-start | bytes 1179652
  76.1 18.8 %collective-permute-start.6 = (bf16[512,384]{1,0:T(8,128)(2,1)}, bf16[512,384]{1,0:T(8,128)(2,1)S(1)}, u32[]{:S(2)}, u32[]{:S(2)}) collective-permute-start(bf16[512,384]{1,0:T(8,128)(2,1)} %get-tuple-element.35), channel_id=1, source_target_pairs={{0,32},{8,40},{16,48},{24,56},{32,64},{40,72},{48,80},{56,88},{64,... | collective-permute-start | bytes 1179656 | tf_op jit(solution)/shard_map/ppermute | solution.py:42
  76.5 18.6 %collective-permute-start.21 = (bf16[512,384]{1,0:T(8,128)(2,1)S(1)}, bf16[512,384]{1,0:T(8,128)(2,1)S(1)}, u32[]{:S(2)}, u32[]{:S(2)}) collective-permute-start(bf16[512,384]{1,0:T(8,128)(2,1)S(1)} %add_convert_fusion.1), channel_id=1, source_target_pairs={{0,96},{8,104},{16,112},{24,120},{32,0},{40,8},{48,16},{56,24},{64... | collective-permute-start | bytes 1179656 | tf_op jit(solution)/shard_map/ppermute | solution.py:42
  94.9 8.2 %collective-permute-start.10 = (bf16[512,384]{1,0:T(8,128)(2,1)S(1)}, bf16[512,384]{1,0:T(8,128)(2,1)S(1)}, u32[]{:S(2)}, u32[]{:S(2)}) collective-permute-start(bf16[512,384]{1,0:T(8,128)(2,1)S(1)} %add_convert_fusion.4), channel_id=1, source_target_pairs={{0,96},{8,104},{16,112},{24,120},{32,0},{40,8},{48,16},{56,24},{64... | collective-permute-start | bytes 1179656 | tf_op jit(solution)/shard_map/ppermute | solution.py:42
  95.0 16.5 %collective-permute-start.16 = (bf16[512,384]{1,0:T(8,128)(2,1)S(1)}, bf16[512,384]{1,0:T(8,128)(2,1)S(1)}, u32[]{:S(2)}, u32[]{:S(2)}) collective-permute-start(bf16[512,384]{1,0:T(8,128)(2,1)S(1)} %copy-done.25), channel_id=1, source_target_pairs={{0,96},{8,104},{16,112},{24,120},{32,0},{40,8},{48,16},{56,24},{64... | collective-permute-start | bytes 1179656 | tf_op jit(solution)/shard_map/ppermute | solution.py:42
  95.1 24.8 %collective-permute-start.5 = (bf16[512,384]{1,0:T(8,128)(2,1)S(1)}, bf16[512,384]{1,0:T(8,128)(2,1)S(1)}, u32[]{:S(2)}, u32[]{:S(2)}) collective-permute-start(bf16[512,384]{1,0:T(8,128)(2,1)S(1)} %copy-done.26), channel_id=1, source_target_pairs={{0,96},{8,104},{16,112},{24,120},{32,0},{40,8},{48,16},{56,24},{64... | collective-permute-start | bytes 1179656 | tf_op jit(solution)/shard_map/ppermute | solution.py:42
  96.4 29.5 %collective-permute-start.18 = (bf16[512,384]{1,0:T(8,128)(2,1)S(1)}, bf16[512,384]{1,0:T(8,128)(2,1)S(1)}, u32[]{:S(2)}, u32[]{:S(2)}) collective-permute-start(bf16[512,384]{1,0:T(8,128)(2,1)S(1)} %add_convert_fusion.2), channel_id=1, source_target_pairs={{0,32},{8,40},{16,48},{24,56},{32,64},{40,72},{48,80},{56,88},{64,... | collective-permute-start | bytes 1179656 | tf_op jit(solution)/shard_map/ppermute | solution.py:42
  103.1 22.8 %collective-permute-start.7 = (bf16[512,384]{1,0:T(8,128)(2,1)S(1)}, bf16[512,384]{1,0:T(8,128)(2,1)}, u32[]{:S(2)}, u32[]{:S(2)}) collective-permute-start(bf16[512,384]{1,0:T(8,128)(2,1)S(1)} %add_convert_fusion.5), channel_id=1, source_target_pairs={{0,32},{8,40},{16,48},{24,56},{32,64},{40,72},{48,80},{56,88},{64,... | collective-permute-start | bytes 1179656 | tf_op jit(solution)/shard_map/ppermute | solution.py:42
  111.5 21.2 %copy-start.14 = (bf16[512,384]{1,0:T(8,128)(2,1)}, bf16[512,384]{1,0:T(8,128)(2,1)S(1)}, u32[]{:S(2)}) copy-start(bf16[512,384]{1,0:T(8,128)(2,1)S(1)} %collective-permute-done.16.refs_8_) | copy-start | bytes 1179652
  111.5 14.4 %collective-permute-start.22 = (bf16[512,384]{1,0:T(8,128)(2,1)S(1)}, bf16[512,384]{1,0:T(8,128)(2,1)}, u32[]{:S(2)}, u32[]{:S(2)}) collective-permute-start(bf16[512,384]{1,0:T(8,128)(2,1)S(1)} %add_convert_fusion), channel_id=1, source_target_pairs={{0,16},{8,24},{16,0},{24,8},{32,48},{40,56},{48,32},{56,40},{64,80... | collective-permute-start | bytes 1179656 | tf_op jit(solution)/shard_map/ppermute | solution.py:42
  119.9 12.8 %collective-permute-start.11 = (bf16[512,384]{1,0:T(8,128)(2,1)S(1)}, bf16[512,384]{1,0:T(8,128)(2,1)}, u32[]{:S(2)}, u32[]{:S(2)}) collective-permute-start(bf16[512,384]{1,0:T(8,128)(2,1)S(1)} %add_convert_fusion.3), channel_id=1, source_target_pairs={{0,16},{8,24},{16,0},{24,8},{32,48},{40,56},{48,32},{56,40},{64,80... | collective-permute-start | bytes 1179656 | tf_op jit(solution)/shard_map/ppermute | solution.py:42
  137.4 4.1 %collective-permute-start.23 = (f32[26,8,128]{2,1,0:T(8,128)}, f32[26,8,128]{2,1,0:T(8,128)S(1)}, u32[]{:S(2)}, u32[]{:S(2)}) collective-permute-start(f32[26,8,128]{2,1,0:T(8,128)} %get-tuple-element.48.mine_ref), channel_id=1, source_target_pairs={{0,8},{8,0},{16,24},{24,16},{32,40},{40,32},{48,56},{56,48},{64,72... | collective-permute-start | bytes 319496 | tf_op jit(solution)/shard_map/ppermute | solution.py:42
  146.4 9.4 %collective-permute-start.24 = (bf16[1024,128]{1,0:T(8,128)(2,1)}, bf16[1024,128]{1,0:T(8,128)(2,1)S(1)}, u32[]{:S(2)}, u32[]{:S(2)}) collective-permute-start(bf16[1024,128]{1,0:T(8,128)(2,1)} %filtered.1.refs_1_), channel_id=1, source_target_pairs={{0,16},{8,24},{16,0},{24,8},{32,48},{40,56},{48,32},{56,40},{64,80... | collective-permute-start | bytes 786440 | tf_op jit(solution)/shard_map/ppermute | solution.py:42
  149.1 18.0 %collective-permute-start.25 = (bf16[1024,128]{1,0:T(8,128)(2,1)}, bf16[1024,128]{1,0:T(8,128)(2,1)S(1)}, u32[]{:S(2)}, u32[]{:S(2)}) collective-permute-start(bf16[1024,128]{1,0:T(8,128)(2,1)} %filtered.1.refs_1_), channel_id=1, source_target_pairs={{0,96},{8,104},{16,112},{24,120},{32,0},{40,8},{48,16},{56,24},{64... | collective-permute-start | bytes 786440 | tf_op jit(solution)/shard_map/ppermute | solution.py:42
  150.0 17.1 %collective-permute-start.26 = (bf16[1024,128]{1,0:T(8,128)(2,1)}, bf16[1024,128]{1,0:T(8,128)(2,1)S(1)}, u32[]{:S(2)}, u32[]{:S(2)}) collective-permute-start(bf16[1024,128]{1,0:T(8,128)(2,1)} %filtered.1.refs_1_), channel_id=1, source_target_pairs={{0,112},{8,120},{16,96},{24,104},{32,16},{40,24},{48,0},{56,8},{64... | collective-permute-start | bytes 786440 | tf_op jit(solution)/shard_map/ppermute | solution.py:42
  150.0 17.1 %collective-permute-start.27 = (bf16[1024,128]{1,0:T(8,128)(2,1)}, bf16[1024,128]{1,0:T(8,128)(2,1)S(1)}, u32[]{:S(2)}, u32[]{:S(2)}) collective-permute-start(bf16[1024,128]{1,0:T(8,128)(2,1)} %filtered.1.refs_1_), channel_id=1, source_target_pairs={{0,64},{8,72},{16,80},{24,88},{32,96},{40,104},{48,112},{56,120},{... | collective-permute-start | bytes 786440 | tf_op jit(solution)/shard_map/ppermute | solution.py:42
  152.3 14.9 %collective-permute-start.28 = (bf16[1024,128]{1,0:T(8,128)(2,1)}, bf16[1024,128]{1,0:T(8,128)(2,1)S(1)}, u32[]{:S(2)}, u32[]{:S(2)}) collective-permute-start(bf16[1024,128]{1,0:T(8,128)(2,1)} %filtered.1.refs_1_), channel_id=1, source_target_pairs={{0,80},{8,88},{16,64},{24,72},{32,112},{40,120},{48,96},{56,104},{... | collective-permute-start | bytes 786440 | tf_op jit(solution)/shard_map/ppermute | solution.py:42
  155.7 20.4 %copy-start.17 = (bf16[1024,128]{1,0:T(8,128)(2,1)}, bf16[1024,128]{1,0:T(8,128)(2,1)S(1)}, u32[]{:S(2)}) copy-start(bf16[1024,128]{1,0:T(8,128)(2,1)S(1)} %collective-permute-done.24.refs_2_) | copy-start | bytes 786436
  155.7 15.9 %collective-permute-start.29 = (bf16[1024,128]{1,0:T(8,128)(2,1)}, bf16[1024,128]{1,0:T(8,128)(2,1)S(1)}, u32[]{:S(2)}, u32[]{:S(2)}) collective-permute-start(bf16[1024,128]{1,0:T(8,128)(2,1)} %filtered.1.refs_1_), channel_id=1, source_target_pairs={{0,32},{8,40},{16,48},{24,56},{32,64},{40,72},{48,80},{56,88},{64,... | collective-permute-start | bytes 786440 | tf_op jit(solution)/shard_map/ppermute | solution.py:42
  167.1 9.0 %collective-permute-start.30 = (bf16[1024,128]{1,0:T(8,128)(2,1)}, bf16[1024,128]{1,0:T(8,128)(2,1)S(1)}, u32[]{:S(2)}, u32[]{:S(2)}) collective-permute-start(bf16[1024,128]{1,0:T(8,128)(2,1)} %filtered.1.refs_1_), channel_id=1, source_target_pairs={{0,48},{8,56},{16,32},{24,40},{32,80},{40,88},{48,64},{56,72},{64,... | collective-permute-start | bytes 786440 | tf_op jit(solution)/shard_map/ppermute | solution.py:42
  182.6 13.2 %collective-permute-start.32 = (bf16[128,1024]{1,0:T(8,128)(2,1)}, bf16[128,1024]{1,0:T(8,128)(2,1)S(1)}, u32[]{:S(2)}, u32[]{:S(2)}) collective-permute-start(bf16[128,1024]{1,0:T(8,128)(2,1)} %get-tuple-element.52), channel_id=1, source_target_pairs={{0,2},{1,3},{2,4},{3,5},{4,6},{5,7},{6,0},{7,1},{8,10},{9,11},{10,... | collective-permute-start | bytes 786440 | tf_op jit(solution)/shard_map/ppermute | solution.py:46
  182.6 13.2 %collective-permute-start.33 = (bf16[128,1024]{1,0:T(8,128)(2,1)}, bf16[128,1024]{1,0:T(8,128)(2,1)S(1)}, u32[]{:S(2)}, u32[]{:S(2)}) collective-permute-start(bf16[128,1024]{1,0:T(8,128)(2,1)} %get-tuple-element.53), channel_id=1, source_target_pairs={{0,4},{1,5},{2,6},{3,7},{4,0},{5,1},{6,2},{7,3},{8,12},{9,13},{10,... | collective-permute-start | bytes 786440 | tf_op jit(solution)/shard_map/ppermute | solution.py:46
  183.9 11.9 %collective-permute-start.34 = (bf16[128,1024]{1,0:T(8,128)(2,1)}, bf16[128,1024]{1,0:T(8,128)(2,1)S(1)}, u32[]{:S(2)}, u32[]{:S(2)}) collective-permute-start(bf16[128,1024]{1,0:T(8,128)(2,1)} %get-tuple-element.54), channel_id=1, source_target_pairs={{0,6},{1,7},{2,0},{3,1},{4,2},{5,3},{6,4},{7,5},{8,14},{9,15},{10,... | collective-permute-start | bytes 786440 | tf_op jit(solution)/shard_map/ppermute | solution.py:46
  185.3 10.5 %collective-permute-start.35 = (bf16[128,1024]{1,0:T(8,128)(2,1)}, bf16[128,1024]{1,0:T(8,128)(2,1)S(1)}, u32[]{:S(2)}, u32[]{:S(2)}) collective-permute-start(bf16[128,1024]{1,0:T(8,128)(2,1)} %get-tuple-element.55), channel_id=1, source_target_pairs={{0,1},{1,0},{2,3},{3,2},{4,5},{5,4},{6,7},{7,6},{8,9},{9,8},{10,11... | collective-permute-start | bytes 786440 | tf_op jit(solution)/shard_map/ppermute | solution.py:46
  185.3 10.5 %collective-permute-start.36 = (bf16[128,1024]{1,0:T(8,128)(2,1)}, bf16[128,1024]{1,0:T(8,128)(2,1)S(1)}, u32[]{:S(2)}, u32[]{:S(2)}) collective-permute-start(bf16[128,1024]{1,0:T(8,128)(2,1)} %get-tuple-element.56), channel_id=1, source_target_pairs={{0,3},{1,2},{2,5},{3,4},{4,7},{5,6},{6,1},{7,0},{8,11},{9,10},{10,... | collective-permute-start | bytes 786440 | tf_op jit(solution)/shard_map/ppermute | solution.py:46
  195.8 9.8 %collective-permute-start.37 = (bf16[128,1024]{1,0:T(8,128)(2,1)}, bf16[128,1024]{1,0:T(8,128)(2,1)S(1)}, u32[]{:S(2)}, u32[]{:S(2)}) collective-permute-start(bf16[128,1024]{1,0:T(8,128)(2,1)} %get-tuple-element.57), channel_id=1, source_target_pairs={{0,5},{1,4},{2,7},{3,6},{4,1},{5,0},{6,3},{7,2},{8,13},{9,12},{10,... | collective-permute-start | bytes 786440 | tf_op jit(solution)/shard_map/ppermute | solution.py:46
  195.8 11.7 %collective-permute-start.38 = (bf16[128,1024]{1,0:T(8,128)(2,1)}, bf16[128,1024]{1,0:T(8,128)(2,1)S(1)}, u32[]{:S(2)}, u32[]{:S(2)}) collective-permute-start(bf16[128,1024]{1,0:T(8,128)(2,1)} %get-tuple-element.58), channel_id=1, source_target_pairs={{0,7},{1,6},{2,1},{3,0},{4,3},{5,2},{6,5},{7,4},{8,15},{9,14},{10,... | collective-permute-start | bytes 786440 | tf_op jit(solution)/shard_map/ppermute | solution.py:46
  208.8 8.1 %collective-permute-start.39 = (bf16[128,512]{1,0:T(8,128)(2,1)S(1)}, bf16[128,512]{1,0:T(8,128)(2,1)S(1)}, u32[]{:S(2)}, u32[]{:S(2)}) collective-permute-start(bf16[128,512]{1,0:T(8,128)(2,1)S(1)} %get-tuple-element.60), channel_id=1, source_target_pairs={{0,8},{8,0},{16,24},{24,16},{32,40},{40,32},{48,56},{56,48},{64,72... | collective-permute-start | bytes 393224 | tf_op jit(solution)/shard_map/ppermute | solution.py:42
  (20 other events, 150.2 us)

commit v2 on v1

v2 whole, which is shorter than its diff:
```python
import jax
import jax.numpy as jnp
from jax import lax
from jax.experimental import pallas as pl
from jax.experimental.pallas import tpu as pltpu
from jax.sharding import PartitionSpec as P

Z, XH, CORES = 4, 2, 2
Y, XL = 4, 2
BLOCKS = Y * XL
LANES = 128
BF = jnp.bfloat16
F32 = jnp.float32


def tok_perm(move):
    pairs = []
    for z in range(Z):
        for xh in range(XH):
            for c in range(CORES):
                nz, nx, nc = move(z, xh, c)
                pairs.append(((z * XH + xh) * CORES + c, ((nz % Z) * XH + nx) * CORES + nc))
    return pairs


def ch_perm(move):
    pairs = []
    for y in range(Y):
        for xl in range(XL):
            ny, nx = move(y, xl)
            pairs.append((y * XL + xl, (ny % Y) * XL + nx))
    return pairs


CORE_SWAP = tok_perm(lambda z, xh, c: (z, xh, 1 - c))
Z_UP = tok_perm(lambda z, xh, c: (z + 1, xh, c))
Z_DOWN = tok_perm(lambda z, xh, c: (z - 1, xh, c))
X_SWAP = tok_perm(lambda z, xh, c: (z, 1 - xh, c))


def tok_send(value, perm):
    return lax.ppermute(value, "tok", perm)


def ch_send(value, perm):
    return lax.ppermute(value, "ch", perm)


def swap(value):
    return tok_send(value, CORE_SWAP)


def add(*terms):
    total = terms[0].astype(F32)
    for term in terms[1:]:
        total = total + term.astype(F32)
    return total.astype(BF)


def whole(shape):
    return pl.BlockSpec(shape, lambda *_: (0,) * len(shape))


TARGETS = [(2, 0), (1, 1), (2, 1), (3, 0), (1, 0), (0, 0), (0, 1), (3, 1)]


def chip_of(where_ref, dz, dx):
    return ((where_ref[0] + dz) & (Z - 1)) * XH + ((where_ref[1] + dx) & (XH - 1))


def reorder_kernel(targets, axis, where_ref, in_ref, out_ref, sems):
    size = in_ref.shape[axis] // len(targets)
    copies = []
    for k, (dz, dx) in enumerate(targets):
        source = pl.ds(pl.multiple_of(chip_of(where_ref, dz, dx) * size, size), size)
        place = pl.ds(k * size, size)
        if axis == 0:
            pair = in_ref.at[source, :], out_ref.at[place, :]
        else:
            pair = in_ref.at[:, source], out_ref.at[:, place]
        copies.append(pltpu.make_async_copy(*pair, sems.at[k]))
        copies[-1].start()
    for copy in copies:
        copy.wait()


def by_target(weight, where, targets, axis):
    return pl.pallas_call(
        lambda *refs: reorder_kernel(targets, axis, *refs),
        out_shape=jax.ShapeDtypeStruct(weight.shape, weight.dtype),
        in_specs=[pl.BlockSpec(memory_space=pltpu.SMEM), pl.BlockSpec(memory_space=pl.ANY)],
        out_specs=pl.BlockSpec(memory_space=pltpu.VMEM),
        scratch_shapes=[pltpu.SemaphoreType.DMA((len(targets),))],
        name="by_target",
    )(where, weight)


def product(rows, weights, first, last):
    depth, cols = weights[0].shape
    width = cols // len(TARGETS)
    columns = slice(first * width, last * width)
    return (
        jnp.dot(rows[:, :depth], weights[0][:, columns], preferred_element_type=F32)
        + jnp.dot(rows[:, depth:], weights[1][:, columns], preferred_element_type=F32)
    ).astype(BF)


def split(value, count):
    width = value.shape[1] // count
    return [value[:, k * width : (k + 1) * width] for k in range(count)]


def reduce_ring_first(rows, weights):
    up = tok_send(product(rows, weights, 0, 2), Z_UP)
    down = tok_send(product(rows, weights, 2, 4), Z_DOWN)
    near_up, near, far, far_down = split(product(rows, weights, 4, 8), 4)
    near_in, far_in = split(up, 2)
    far_more, near_more = split(down, 2)
    near_up = tok_send(add(near_up, near_in), Z_UP)
    far_down = tok_send(add(far_down, far_more), Z_DOWN)
    across = tok_send(add(far, far_in, far_down), X_SWAP)
    return [add(near, near_more), near_up, across]


def reduce_pair_first(rows, weights):
    far1, far2 = split(tok_send(product(rows, weights, 1, 3), X_SWAP), 2)
    far0, far3 = split(tok_send(product(rows, weights, 6, 8), X_SWAP), 2)
    near2 = product(rows, weights, 0, 1)
    near3, near1, near0 = split(product(rows, weights, 3, 6), 3)
    half = rows.shape[0] // 2
    first, second = slice(0, half), slice(half, None)

    def both(near, far, side):
        return near[side].astype(F32) + far[side].astype(F32)

    up = tok_send(jnp.stack([both(near2, far2, first), both(near1, far1, second)]).astype(BF), Z_UP)
    down = tok_send(jnp.stack([both(near2, far2, second), both(near3, far3, first)]).astype(BF), Z_DOWN)
    from_below = tok_send((both(near1, far1, first) + up[0].astype(F32)).astype(BF), Z_UP)
    from_above = tok_send((both(near3, far3, second) + down[0].astype(F32)).astype(BF), Z_DOWN)
    return [
        jnp.concatenate(
            [
                both(near0, far0, first) + down[1].astype(F32) + from_below.astype(F32),
                both(near0, far0, second) + up[1].astype(F32) + from_above.astype(F32),
            ]
        ).astype(BF)
    ]


def features(block):
    half = LANES // 2
    low = lax.broadcasted_iota(jnp.int32, (1, LANES), 1) < half
    first, second, third = (block[:, k * LANES : (k + 1) * LANES] for k in range(3))
    return (
        jnp.where(low, first, second),
        jnp.where(low, pltpu.roll(first, half, 1), pltpu.roll(third, half, 1)),
        jnp.where(low, second, third),
    )


def every(ref, row, length):
    return ref[pl.ds(row, BLOCKS, stride=length), :]


def local_kernel(groups, counts, where_ref, taps_ref, rates_ref, *refs):
    flat = sum(counts)
    starts = [sum(counts[:g]) for g in range(len(counts))]
    term_refs = [refs[start : start + count] for start, count in zip(starts, counts)]
    query_ref, gate_ref, edge_ref = refs[flat : flat + 3]
    raw_refs = refs[flat + 3 : flat + 6]
    key_ref, value_ref = refs[flat + 6 :]
    length = gate_ref.shape[0] // BLOCKS
    order = rates_ref.shape[0]
    rows = lax.broadcasted_iota(jnp.int32, (length, LANES), 0)
    for refs_here, group in zip(term_refs, groups):
        for place, (dy, dx) in enumerate(group):
            here = slice(place * length, (place + 1) * length)
            block = refs_here[0][here, :].astype(F32)
            for ref in refs_here[1:]:
                block = block + ref[here, :].astype(F32)
            spot = ((where_ref[3] + dy) & (Y - 1)) * XL + ((where_ref[4] + dx) & (XL - 1))
            there = pl.ds(pl.multiple_of(spot * length, length), length)
            mixed = []
            for f, raw in enumerate(features(block)):
                raw_refs[f][there, :] = raw
                total = taps_ref[f, 0:1, :] * raw
                for back in (1, 2):
                    moved = jnp.where(rows >= back, pltpu.roll(raw, back, 0), 0.0)
                    total = total + taps_ref[f, back : back + 1, :] * moved
                mixed.append(total)
            query_ref[there, :] = mixed[0]
            key_ref[there, :] = mixed[1]
            value_ref[there, :] = mixed[2]
            gate_ref[there, :] = mixed[1] * mixed[2]
    decay = [
        jnp.broadcast_to(jnp.exp(-rates_ref[n : n + 1, :]), (BLOCKS, LANES)) for n in range(order)
    ]

    def step(r, states):
        gate = every(gate_ref, r, length)
        return tuple(decay[n] * states[n] + gate for n in range(order))

    states = lax.fori_loop(
        2, length, step, tuple(jnp.zeros((BLOCKS, LANES), F32) for _ in range(order)), unroll=6
    )
    for n in range(order):
        edge_ref[n] = states[n]
    at = order
    for r in (0, 1):
        edge_ref[at] = every(key_ref, r, length)
        edge_ref[at + 1] = every(value_ref, r, length)
        at += 2
    for f in range(3):
        for r in (length - 1, length - 2):
            edge_ref[at] = every(raw_refs[f], r, length)
            at += 1


def filter_kernel(where_ref, taps_ref, rates_ref, weights_ref, skip_ref, mine_ref, theirs_ref, query_ref, gate_ref, out_ref, work):
    length = gate_ref.shape[0] // BLOCKS
    order = rates_ref.shape[0]
    core = where_ref[2]
    first = core == 0
    spots = lax.broadcasted_iota(jnp.int32, (BLOCKS, LANES), 0)

    def later(value, count):
        return jnp.where(spots >= count, pltpu.roll(value, count, 0), 0.0)

    def tap(f, back):
        return taps_ref[f, back : back + 1, :]

    def head(ref, before_ref, is_first):
        def before(f, back):
            value = before_ref[order + 4 + 2 * f + back - 1]
            return jnp.where(is_first, later(value, 1), value)

        key0 = ref[order] + tap(1, 1) * before(1, 1) + tap(1, 2) * before(1, 2)
        value0 = ref[order + 1] + tap(2, 1) * before(2, 1) + tap(2, 2) * before(2, 2)
        key1 = ref[order + 2] + tap(1, 2) * before(1, 1)
        value1 = ref[order + 3] + tap(2, 2) * before(2, 1)
        query0 = tap(0, 1) * before(0, 1) + tap(0, 2) * before(0, 2)
        query1 = tap(0, 2) * before(0, 1)
        return key0 * value0, key1 * value1, query0, query1

    gate0, gate1, query0, query1 = head(mine_ref, theirs_ref, first)
    their0, their1, _, _ = head(theirs_ref, mine_ref, jnp.logical_not(first))
    decay, states = [], []
    for n in range(order):
        rate = rates_ref[n : n + 1, :]
        factor0, factor1 = jnp.exp(-(length - 1) * rate), jnp.exp(-(length - 2) * rate)
        ours = mine_ref[n] + factor0 * gate0 + factor1 * gate1
        theirs = theirs_ref[n] + factor0 * their0 + factor1 * their1
        early, late = jnp.where(first, ours, theirs), jnp.where(first, theirs, ours)
        half = jnp.exp(-length * rate)
        total = half * early + late
        for count in (1, 2, 4):
            total = total + jnp.exp(-(2 * length * count) * rate) * later(total, count)
        before = later(total, 1)
        states.append(jnp.where(first, before, half * before + early))
        decay.append(jnp.broadcast_to(jnp.exp(-rate), (BLOCKS, LANES)))
    weights = [jnp.broadcast_to(weights_ref[n : n + 1, :], (BLOCKS, LANES)) for n in range(order)]
    skip = jnp.broadcast_to(skip_ref[...], (BLOCKS, LANES))

    def advance(r, states, gate, query):
        states = tuple(decay[n] * states[n] + gate for n in range(order))
        terms = [weights[n] * states[n] for n in range(order)] + [skip * gate]
        while len(terms) > 1:
            terms = [a + b for a, b in zip(terms[::2], terms[1::2])] + terms[len(terms) // 2 * 2 :]
        work[pl.ds(r, BLOCKS, stride=length), :] = query * terms[0]
        return states

    states = advance(0, tuple(states), gate0, every(query_ref, 0, length) + query0)
    states = advance(1, states, gate1, every(query_ref, 1, length) + query1)
    lax.fori_loop(
        2,
        length,
        lambda r, states: advance(r, states, every(gate_ref, r, length), every(query_ref, r, length)),
        states,
        unroll=6,
    )
    for g in range(XL):
        for dy in range(Y):
            spot = ((where_ref[3] + dy) & (Y - 1)) * XL + ((where_ref[4] + g) & (XL - 1))
            there = pl.ds(pl.multiple_of(spot * length, length), length)
            place = (g * Y + dy) * length
            out_ref[place : place + length, :] = work[there, :].astype(BF)


def own_lanes(shape):
    return pl.BlockSpec(shape, lambda _, where_ref: (0,) * (len(shape) - 1) + (where_ref[5],))


def local_part(where, taps, rates, groups, blocks):
    tokens = sum(len(group) for group in blocks) * blocks_length(groups[0][0], blocks[0])
    flat = [term for terms in groups for term in terms]
    edges = (rates.shape[0] + 10, BLOCKS, LANES)
    tall = jax.ShapeDtypeStruct((tokens, LANES), F32)
    return pl.pallas_call(
        lambda *refs: local_kernel(blocks, [len(terms) for terms in groups], *refs),
        out_shape=(tall, tall, jax.ShapeDtypeStruct(edges, F32)),
        grid_spec=pltpu.PrefetchScalarGridSpec(
            num_scalar_prefetch=1,
            grid=(1,),
            in_specs=[own_lanes(taps.shape[:-1] + (LANES,)), own_lanes(rates.shape[:-1] + (LANES,))]
            + [whole(term.shape) for term in flat],
            out_specs=[whole(tall.shape), whole(tall.shape), whole(edges)],
            scratch_shapes=[pltpu.VMEM((tokens, LANES), F32)] * 5,
        ),
        name="local_part",
    )(where, taps, rates, *flat)


def blocks_length(term, group):
    return term.shape[0] // len(group)


def filtered(where, taps, rates, weights, skip, mine, theirs, query, gate):
    return pl.pallas_call(
        filter_kernel,
        out_shape=jax.ShapeDtypeStruct(gate.shape, BF),
        grid_spec=pltpu.PrefetchScalarGridSpec(
            num_scalar_prefetch=1,
            grid=(1,),
            in_specs=[own_lanes(array.shape[:-1] + (LANES,)) for array in (taps, rates, weights, skip)]
            + [whole(array.shape) for array in (mine, theirs, query, gate)],
            out_specs=whole(gate.shape),
            scratch_shapes=[pltpu.VMEM(gate.shape, F32)],
        ),
        name="filtered",
    )(where, taps, rates, weights, skip, mine, theirs, query, gate)


def body(activations, proj_weight, short_taps, residues, decay_rates, skip_gain, out_weight):
    tok_index = lax.axis_index("tok")
    ch_index = lax.axis_index("ch")
    z, xh, core = tok_index >> 2, (tok_index >> 1) & 1, tok_index & 1
    y, xl = ch_index >> 1, ch_index & 1
    where = jnp.stack([z, xh, core, y, xl, ch_index * (Z * XH) + (tok_index >> 1)]).astype(jnp.int32)
    length = activations.shape[0] // CORES

    kept = lax.dynamic_slice_in_dim(activations, core * length, length, 0)
    other = swap(lax.dynamic_slice_in_dim(activations, (1 - core) * length, length, 0))
    mine = jnp.concatenate([kept, other], axis=1)
    mine, proj_weight = lax.optimization_barrier((mine, proj_weight))
    ordered = by_target(proj_weight, where, TARGETS, 1)
    weights = (ordered, swap(ordered))

    def along(value, dy):
        return ch_send(value, ch_perm(lambda y, xl: (y - dy, xl)))

    across = ch_send(mine, ch_perm(lambda y, xl: (y, 1 - xl)))
    blocks = [[(0, 0), (1, 0), (3, 0), (2, 0), (0, 1)], [(1, 1), (3, 1), (2, 1)]]
    first = [mine] + [along(mine, dy) for dy, _ in blocks[0][1:4]] + [across]
    first, weights = lax.optimization_barrier((first, weights))
    second = [along(first[-1], dy) for dy, _ in blocks[1]]
    second, out_weight = lax.optimization_barrier((second, out_weight))
    chips = [(k // XH, k % XH) for k in range(Z * XH)]
    out_ordered = by_target(out_weight, where, chips, 0)
    out_rows = jnp.concatenate([out_ordered, swap(out_ordered)], axis=1)
    groups = [
        reduce_ring_first(jnp.concatenate(first), weights),
        reduce_pair_first(jnp.concatenate(second), weights),
    ]
    groups, out_rows = lax.optimization_barrier((groups, out_rows))
    query, gate, edges = local_part(where, short_taps, decay_rates, groups, blocks)
    their_edges = swap(edges)
    gated = filtered(where, short_taps, decay_rates, residues, skip_gain[None], edges, their_edges, query, gate)

    pieces = [gated]
    for dz, dx in chips[1:]:
        pieces.append(tok_send(gated, tok_perm(lambda z, xh, c, dz=dz, dx=dx: (z - dz, xh ^ dx, c))))
    gathered = jnp.concatenate(pieces, axis=1)
    terms = []
    for k in range(BLOCKS):
        dx, dy = k // Y, k % Y
        rows = gathered[k * length : (k + 1) * length]
        term = jnp.dot(rows, out_rows, preferred_element_type=F32).astype(BF)
        if k:
            term = ch_send(term, ch_perm(lambda y, xl, dx=dx, dy=dy: (y + dy, xl ^ dx)))
        terms.append(term)
    total = add(*terms)
    cols = out_weight.shape[1]
    kept, other = total[:, :cols], swap(total[:, cols:])
    return jnp.where(core == 0, jnp.concatenate([kept, other]), jnp.concatenate([other, kept]))


def solution(mesh):
    return jax.shard_map(
        body,
        mesh=mesh,
        in_specs=(P("ch", "tok"), P("tok", "ch"), P(), P(), P(), P(), P("ch", "tok")),
        out_specs=P("ch", "tok"),
        check_vma=False,
    )
```

time: 220 us -> 194 us (0.88)
  Pallas kernels: 46.7 us -> 16.9 us
  waiting for transfers between devices: 102 us -> 79.7 us
  matrix products: 0 us -> 15.8 us
  starting transfers between devices: 56 us -> 65.9 us
  other arithmetic: 3.75 us -> 9.04 us
  local copies, waits for them, and re-layouts: 8.87 us -> 5.44 us
    pallas_call x8 -> x3, Pallas kernels: 42.5 us -> 12 us  [the longest x2 7.24 us: by_target(): pl.pallas_call(lambda *refs: reorder_kernel(targets, axis, *refs), out_sh...]
    ppermute x26 -> x23, waiting for transfers between devices: 66.7 us -> 43 us  [tok_send(): return lax.ppermute(value, 'tok', perm)]
    dot_general x0 -> x22, matrix products: none -> 15.8 us  [the longest x7 7.44 us: product(): jnp.dot(rows[:, :depth], weights[0][:, columns], preferred_element_type=F32)]
    ppermute x26 -> x23, starting transfers between devices: 39.7 us -> 45.8 us  [tok_send(): return lax.ppermute(value, 'tok', perm)]
    ppermute x14, starting transfers between devices: 16.3 us -> 20.1 us  [ch_send(): return lax.ppermute(value, 'ch', perm)]
    dynamic_slice x3 -> x0, local copies, waits for them, and re-layouts: 2.59 us -> none  [the longest x1 1.29 us: body(): weights = lax.dynamic_slice_in_dim(residues, start, LANES, 1)]
    another operation x0 -> x5, other arithmetic: none -> 2.38 us
  transfers between devices with their start and end apart: 40 -> 37, of which waited for: 18 -> 21; matrix products, arithmetic and copies ran while one was open for 4% -> 11% of each run, Pallas kernels for 19% -> 2%
where the time goes in v2:
time: 194 us; the launch traced here: 193 us
  waiting for transfers between devices  79.7 us (41%)
  starting transfers between devices  65.9 us (34%)
  Pallas kernels  16.9 us (9%)
  matrix products  15.8 us (8%)
  other arithmetic  9.04 us (5%)
  local copies, waits for them, and re-layouts  5.44 us (3%)
    ppermute x23, starting transfers between devices, tok_send(): return lax.ppermute(value, 'tok', perm)  45.8 us
    ppermute x23, waiting for transfers between devices, tok_send(): return lax.ppermute(value, 'tok', perm)  43 us
    ppermute x14, waiting for transfers between devices, ch_send(): return lax.ppermute(value, 'ch', perm)  36.7 us
    ppermute x14, starting transfers between devices, ch_send(): return lax.ppermute(value, 'ch', perm)  20.1 us
    dot_general x7, matrix products, product(): jnp.dot(rows[:, :depth], weights[0][:, columns], preferred_element_type=F32)  7.44 us
    pallas_call x2, Pallas kernels, by_target(): pl.pallas_call(lambda *refs: reorder_kernel(targets, axis, *refs), out_sh...  7.24 us
    pallas_call x1, Pallas kernels, filtered(): pl.pallas_call(filter_kernel, out_shape=jax.ShapeDtypeStruct(gate.shape,...  4.88 us
    pallas_call x1, Pallas kernels, local_part(): pl.pallas_call(lambda *refs: local_kernel(blocks, [len(terms) for terms i...  4.73 us
  transfers between devices with their start and end apart: 37, of which 21 were waited for; matrix products, arithmetic and copies ran while one was open for 11% of the time, Pallas kernels for 2%

profile of v2, /device:TPU:1, one launch (start us, length us, event | category | flops | bytes accessed | tf_op | source)
XLA Modules:
  0.0 193.1 jit_solution(4995492466712551054)
XLA Ops:
  1.0 1.5 collective-permute-start
  3.5 4.2 %by_target.2 = bf16[512,3072]{1,0:T(8,128)(2,1)} custom-call(s32[6]{0:T(128)} %stack.51.refs_0_.where_ref, bf16[512,3072]{1,0:T(8,128)(2,1)} %refs_1_.1), custom_call_target="tpu_custom_call" | custom-call | tf_op jit(solution)/shard_map/by_target/pallas_call | solution.py:88
  8.2 2.8 %collective-permute-start.1 = (bf16[128,1024]{1,0:T(8,128)(2,1)S(1)}, bf16[128,1024]{1,0:T(8,128)(2,1)S(1)}, u32[]{:S(2)}, u32[]{:S(2)}) collective-permute-start(bf16[128,1024]{1,0:T(8,128)(2,1)S(1)} %pad_maximum_fusion.4), channel_id=1, source_target_pairs={{0,6},{1,7},{2,0},{3,1},{4,2},{5,3},{6,4},{7,5},{8,14},{9,15},{10,... | collective-permute-start | bytes 786440 | tf_op jit(solution)/shard_map/ppermute | solution.py:46
  11.0 1.6 collective-permute-start.3
  12.6 1.2 collective-permute-start.4
  13.9 8.2 %collective-permute-done.1 = bf16[128,1024]{1,0:T(8,128)(2,1)S(1)} collective-permute-done((bf16[128,1024]{1,0:T(8,128)(2,1)S(1)}, bf16[128,1024]{1,0:T(8,128)(2,1)S(1)}, u32[]{:S(2)}, u32[]{:S(2)}) %collective-permute-start.1) | collective-permute-done | bytes 262176 | tf_op jit(solution)/shard_map/ppermute | solution.py:46
  22.0 3.2 %collective-permute-done.2 = bf16[128,1024]{1,0:T(8,128)(2,1)S(1)} collective-permute-done((bf16[128,1024]{1,0:T(8,128)(2,1)S(1)}, bf16[128,1024]{1,0:T(8,128)(2,1)S(1)}, u32[]{:S(2)}, u32[]{:S(2)}) %collective-permute-start.2) | collective-permute-done | bytes 262176 | tf_op jit(solution)/shard_map/ppermute | solution.py:46
  28.9 1.7 add_convert_fusion.2
  30.6 3.8 %collective-permute-start.6 = (bf16[640,768]{1,0:T(8,128)(2,1)}, bf16[640,768]{1,0:T(8,128)(2,1)}, u32[]{:S(2)}, u32[]{:S(2)}) collective-permute-start(bf16[640,768]{1,0:T(8,128)(2,1)} %add_convert_fusion.2), channel_id=1, source_target_pairs={{0,96},{8,104},{16,112},{24,120},{32,0},{40,8},{48,16},{56,24},{64... | collective-permute-start | bytes 2949128 | tf_op jit(solution)/shard_map/ppermute | solution.py:42
  34.4 1.7 add_convert_fusion.1
  36.1 1.2 fusion.1
  37.3 2.4 %collective-permute-done.13 = bf16[128,1024]{1,0:T(8,128)(2,1)S(1)} collective-permute-done((bf16[128,1024]{1,0:T(8,128)(2,1)S(1)}, bf16[128,1024]{1,0:T(8,128)(2,1)S(1)}, u32[]{:S(2)}, u32[]{:S(2)}) %collective-permute-start.13) | collective-permute-done | bytes 262176 | tf_op jit(solution)/shard_map/ppermute | solution.py:46
  42.3 2.8 %collective-permute-start.15 = (bf16[384,768]{1,0:T(8,128)(2,1)S(1)}, bf16[384,768]{1,0:T(8,128)(2,1)S(1)}, u32[]{:S(2)}, u32[]{:S(2)}) collective-permute-start(bf16[384,768]{1,0:T(8,128)(2,1)S(1)} %fusion.5), channel_id=1, source_target_pairs={{0,16},{8,24},{16,0},{24,8},{32,48},{40,56},{48,32},{56,40},{64,80... | collective-permute-start | bytes 1769480 | tf_op jit(solution)/shard_map/ppermute | solution.py:42
  45.1 1.3 fusion.4
  47.7 7.9 %collective-permute-done.15 = bf16[384,768]{1,0:T(8,128)(2,1)S(1)} collective-permute-done((bf16[384,768]{1,0:T(8,128)(2,1)S(1)}, bf16[384,768]{1,0:T(8,128)(2,1)S(1)}, u32[]{:S(2)}, u32[]{:S(2)}) %collective-permute-start.15) | collective-permute-done | bytes 589856 | tf_op jit(solution)/shard_map/ppermute | solution.py:42
  56.4 1.7 collective-permute-start.17
  58.1 1.2 add_convert_fusion
  59.3 3.0 %by_target.3 = bf16[1024,512]{1,0:T(8,128)(2,1)} custom-call(s32[6]{0:T(128)} %stack.51.refs_0_.where_ref, bf16[1024,512]{1,0:T(8,128)(2,1)} %refs_1_.2), custom_call_target="tpu_custom_call" | custom-call | tf_op jit(solution)/shard_map/by_target/pallas_call | solution.py:88
  62.3 7.9 %collective-permute-start.20 = (bf16[1024,512]{1,0:T(8,128)(2,1)}, bf16[1024,512]{1,0:T(8,128)(2,1)S(1)}, u32[]{:S(2)}, u32[]{:S(2)}) collective-permute-start(bf16[1024,512]{1,0:T(8,128)(2,1)} %by_target.3), channel_id=1, source_target_pairs={{0,8},{8,0},{16,24},{24,16},{32,40},{40,32},{48,56},{56,48},{64,72... | collective-permute-start | bytes 3145736 | tf_op jit(solution)/shard_map/ppermute | solution.py:42
  71.4 1.9 %collective-permute-start.16 = (bf16[2,192,384]{2,1,0:T(8,128)(2,1)S(1)}, bf16[2,192,384]{2,1,0:T(8,128)(2,1)S(1)}, u32[]{:S(2)}, u32[]{:S(2)}) collective-permute-start(bf16[2,192,384]{2,1,0:T(8,128)(2,1)S(1)} %pad_maximum_fusion.1), channel_id=1, source_target_pairs={{0,96},{8,104},{16,112},{24,120},{32,0},{40,8},{48,16},{56,24},{64... | collective-permute-start | bytes 884744 | tf_op jit(solution)/shard_map/ppermute | solution.py:42
  73.4 2.2 %add_convert_fusion.4 = (bf16[640,384]{1,0:T(8,128)(2,1)S(1)}, bf16[640,384]{1,0:T(8,128)(2,1)}) fusion(bf16[640,768]{1,0:T(8,128)(2,1)} %collective-permute-done.6, bf16[640,1536]{1,0:T(8,128)(2,1)S(1)} %add_convert_fusion), kind=kLoop, calls=%fused_computation.36 | loop fusion | flops 1966080 | bytes 2949120 | tf_op jit(solution)/shard_map/convert_element_type | solution.py:57
  75.6 1.7 collective-permute-start.9
  77.3 5.2 %collective-permute-done.18 = bf16[192,384]{1,0:T(8,128)(2,1)S(1)} collective-permute-done((bf16[192,384]{1,0:T(8,128)(2,1)S(1)}, bf16[192,384]{1,0:T(8,128)(2,1)S(1)}, u32[]{:S(2)}, u32[]{:S(2)}) %collective-permute-start.18) | collective-permute-done | bytes 147488 | tf_op jit(solution)/shard_map/ppermute | solution.py:42
  83.8 5.1 %collective-permute-done.9 = bf16[640,384]{1,0:T(8,128)(2,1)S(1)} collective-permute-done((bf16[640,384]{1,0:T(8,128)(2,1)S(1)}, bf16[640,384]{1,0:T(8,128)(2,1)S(1)}, u32[]{:S(2)}, u32[]{:S(2)}) %collective-permute-start.9) | collective-permute-done | bytes 491552 | tf_op jit(solution)/shard_map/ppermute | solution.py:42
  88.9 1.5 add_convert_fusion.3
  90.4 1.3 collective-permute-start.8
  91.6 2.7 %collective-permute-start.10 = (bf16[640,384]{1,0:T(8,128)(2,1)S(1)}, bf16[640,384]{1,0:T(8,128)(2,1)S(1)}, u32[]{:S(2)}, u32[]{:S(2)}) collective-permute-start(bf16[640,384]{1,0:T(8,128)(2,1)S(1)} %get-tuple-element.47), channel_id=1, source_target_pairs={{0,16},{8,24},{16,0},{24,8},{32,48},{40,56},{48,32},{56,40},{64,80... | collective-permute-start | bytes 1474568 | tf_op jit(solution)/shard_map/ppermute | solution.py:42
  96.5 2.8 %collective-permute-done.8.refs_4_ = bf16[640,384]{1,0:T(8,128)(2,1)S(1)} collective-permute-done((bf16[640,384]{1,0:T(8,128)(2,1)S(1)}, bf16[640,384]{1,0:T(8,128)(2,1)S(1)}, u32[]{:S(2)}, u32[]{:S(2)}) %collective-permute-start.8) | collective-permute-done | bytes 491552 | tf_op jit(solution)/shard_map/ppermute | solution.py:42
  99.3 1.5 collective-permute-done.10.refs_5_
  101.6 4.7 %local_part.1 = (f32[1024,128]{1,0:T(8,128)}, f32[1024,128]{1,0:T(8,128)}, f32[26,8,128]{2,1,0:T(8,128)}) custom-call(s32[6]{0:T(128)} %stack.51.refs_0_.where_ref, f32[3,3,8192]{2,1,0:T(4,128)} %taps_ref.1, f32[16,8192]{1,0:T(8,128)} %rates_ref.1, bf16[640,384]{1,0:T(8,128)(2,1)} %get-tuple-element.39.refs_3_, bf16[640,384]{1,0:T(8,128)(2,1)} %copy-done.3, ...), custom_call_target="tpu_custom_call" | custom-call | tf_op jit(solution)/shard_map/local_part/pallas_call | solution.py:298
  106.3 6.0 %collective-permute-start.21 = (f32[26,8,128]{2,1,0:T(8,128)}, f32[26,8,128]{2,1,0:T(8,128)S(1)}, u32[]{:S(2)}, u32[]{:S(2)}) collective-permute-start(f32[26,8,128]{2,1,0:T(8,128)} %get-tuple-element.43.mine_ref), channel_id=1, source_target_pairs={{0,8},{8,0},{16,24},{24,16},{32,40},{40,32},{48,56},{56,48},{64,72... | collective-permute-start | bytes 319496 | tf_op jit(solution)/shard_map/ppermute | solution.py:42
  114.2 4.9 %filtered.1 = bf16[1024,128]{1,0:T(8,128)(2,1)} custom-call(s32[6]{0:T(128)} %stack.51.refs_0_.where_ref, f32[3,3,8192]{2,1,0:T(4,128)} %taps_ref.1, f32[16,8192]{1,0:T(8,128)} %rates_ref.1, f32[16,8192]{1,0:T(8,128)} %weights_ref.1, f32[1,8192]{1,0:T(1,128)} %bitcast.43, f32[26,8,128]{2,1,0:T(8,128)} %get-tuple-element.43.mine_ref, ...), custom_call_target="tpu_custom_call" | custom-call | tf_op jit(solution)/shard_map/filtered/pallas_call | solution.py:318
  119.1 2.7 %collective-permute-start.22 = (bf16[1024,128]{1,0:T(8,128)(2,1)}, bf16[1024,128]{1,0:T(8,128)(2,1)S(1)}, u32[]{:S(2)}, u32[]{:S(2)}) collective-permute-start(bf16[1024,128]{1,0:T(8,128)(2,1)} %filtered.1), channel_id=1, source_target_pairs={{0,16},{8,24},{16,0},{24,8},{32,48},{40,56},{48,32},{56,40},{64,80... | collective-permute-start | bytes 786440 | tf_op jit(solution)/shard_map/ppermute | solution.py:42
  121.8 2.0 %collective-permute-start.23 = (bf16[1024,128]{1,0:T(8,128)(2,1)}, bf16[1024,128]{1,0:T(8,128)(2,1)S(1)}, u32[]{:S(2)}, u32[]{:S(2)}) collective-permute-start(bf16[1024,128]{1,0:T(8,128)(2,1)} %filtered.1), channel_id=1, source_target_pairs={{0,96},{8,104},{16,112},{24,120},{32,0},{40,8},{48,16},{56,24},{64... | collective-permute-start | bytes 786440 | tf_op jit(solution)/shard_map/ppermute | solution.py:42
  123.9 1.6 collective-permute-start.24
  126.6 5.4 %collective-permute-start.26 = (bf16[1024,128]{1,0:T(8,128)(2,1)}, bf16[1024,128]{1,0:T(8,128)(2,1)S(1)}, u32[]{:S(2)}, u32[]{:S(2)}) collective-permute-start(bf16[1024,128]{1,0:T(8,128)(2,1)} %filtered.1), channel_id=1, source_target_pairs={{0,80},{8,88},{16,64},{24,72},{32,112},{40,120},{48,96},{56,104},{... | collective-permute-start | bytes 786440 | tf_op jit(solution)/shard_map/ppermute | solution.py:42
  132.1 1.8 collective-permute-done.23
  135.2 7.9 %collective-permute-done.26 = bf16[1024,128]{1,0:T(8,128)(2,1)S(1)} collective-permute-done((bf16[1024,128]{1,0:T(8,128)(2,1)}, bf16[1024,128]{1,0:T(8,128)(2,1)S(1)}, u32[]{:S(2)}, u32[]{:S(2)}) %collective-permute-start.26) | collective-permute-done | bytes 262176 | tf_op jit(solution)/shard_map/ppermute | solution.py:42
  143.2 7.2 %collective-permute-done.27 = bf16[1024,128]{1,0:T(8,128)(2,1)S(1)} collective-permute-done((bf16[1024,128]{1,0:T(8,128)(2,1)}, bf16[1024,128]{1,0:T(8,128)(2,1)S(1)}, u32[]{:S(2)}, u32[]{:S(2)}) %collective-permute-start.27) | collective-permute-done | bytes 262176 | tf_op jit(solution)/shard_map/ppermute | solution.py:42
  153.4 2.1 %collective-permute-start.35 = (bf16[128,1024]{1,0:T(8,128)(2,1)S(1)}, bf16[128,1024]{1,0:T(8,128)(2,1)S(1)}, u32[]{:S(2)}, u32[]{:S(2)}) collective-permute-start(bf16[128,1024]{1,0:T(8,128)(2,1)S(1)} %convolution_convert_fusion), channel_id=1, source_target_pairs={{0,7},{1,6},{2,1},{3,0},{4,3},{5,2},{6,5},{7,4},{8,15},{9,14},{10,... | collective-permute-start | bytes 786440 | tf_op jit(solution)/shard_map/ppermute | solution.py:46
  155.5 6.2 %collective-permute-start.34 = (bf16[128,1024]{1,0:T(8,128)(2,1)S(1)}, bf16[128,1024]{1,0:T(8,128)(2,1)S(1)}, u32[]{:S(2)}, u32[]{:S(2)}) collective-permute-start(bf16[128,1024]{1,0:T(8,128)(2,1)S(1)} %convolution_convert_fusion.1), channel_id=1, source_target_pairs={{0,5},{1,4},{2,7},{3,6},{4,1},{5,0},{6,3},{7,2},{8,13},{9,12},{10,... | collective-permute-start | bytes 786440 | tf_op jit(solution)/shard_map/ppermute | solution.py:46
  162.2 3.9 %collective-permute-start.31 = (bf16[128,1024]{1,0:T(8,128)(2,1)S(1)}, bf16[128,1024]{1,0:T(8,128)(2,1)S(1)}, u32[]{:S(2)}, u32[]{:S(2)}) collective-permute-start(bf16[128,1024]{1,0:T(8,128)(2,1)S(1)} %convolution_convert_fusion.4), channel_id=1, source_target_pairs={{0,6},{1,7},{2,0},{3,1},{4,2},{5,3},{6,4},{7,5},{8,14},{9,15},{10,... | collective-permute-start | bytes 786440 | tf_op jit(solution)/shard_map/ppermute | solution.py:46
  166.1 6.1 %collective-permute-done.34 = bf16[128,1024]{1,0:T(8,128)(2,1)S(1)} collective-permute-done((bf16[128,1024]{1,0:T(8,128)(2,1)S(1)}, bf16[128,1024]{1,0:T(8,128)(2,1)S(1)}, u32[]{:S(2)}, u32[]{:S(2)}) %collective-permute-start.34) | collective-permute-done | bytes 262176 | tf_op jit(solution)/shard_map/ppermute | solution.py:46
  172.2 1.9 collective-permute-done.33
  174.0 3.2 %collective-permute-done.32 = bf16[128,1024]{1,0:T(8,128)(2,1)S(1)} collective-permute-done((bf16[128,1024]{1,0:T(8,128)(2,1)S(1)}, bf16[128,1024]{1,0:T(8,128)(2,1)S(1)}, u32[]{:S(2)}, u32[]{:S(2)}) %collective-permute-start.32) | collective-permute-done | bytes 262176 | tf_op jit(solution)/shard_map/ppermute | solution.py:46
  177.9 7.1 %collective-permute-done.30 = bf16[128,1024]{1,0:T(8,128)(2,1)S(1)} collective-permute-done((bf16[128,1024]{1,0:T(8,128)(2,1)S(1)}, bf16[128,1024]{1,0:T(8,128)(2,1)S(1)}, u32[]{:S(2)}, u32[]{:S(2)}) %collective-permute-start.30) | collective-permute-done | bytes 262176 | tf_op jit(solution)/shard_map/ppermute | solution.py:46
  185.0 4.0 %collective-permute-done.29 = bf16[128,1024]{1,0:T(8,128)(2,1)S(1)} collective-permute-done((bf16[128,1024]{1,0:T(8,128)(2,1)S(1)}, bf16[128,1024]{1,0:T(8,128)(2,1)S(1)}, u32[]{:S(2)}, u32[]{:S(2)}) %collective-permute-start.29) | collective-permute-done | bytes 262176 | tf_op jit(solution)/shard_map/ppermute | solution.py:46
  189.7 1.7 collective-permute-start.36
  (95 shorter events, 26.7 us)
Async XLA Ops:
  1.0 2.5 %collective-permute-start = (bf16[128,512]{1,0:T(8,128)(2,1)S(1)}, bf16[128,512]{1,0:T(8,128)(2,1)S(1)}, u32[]{:S(2)}, u32[]{:S(2)}) collective-permute-start(bf16[128,512]{1,0:T(8,128)(2,1)S(1)} %get-tuple-element.61), channel_id=1, source_target_pairs={{0,8},{8,0},{16,24},{24,16},{32,40},{40,32},{48,56},{56,48},{64,72... | collective-permute-start | bytes 393224 | tf_op jit(solution)/shard_map/ppermute | solution.py:42
  7.7 17.5 %collective-permute-start.5 = (bf16[512,3072]{1,0:T(8,128)(2,1)}, bf16[512,3072]{1,0:T(8,128)(2,1)S(1)}, u32[]{:S(2)}, u32[]{:S(2)}) collective-permute-start(bf16[512,3072]{1,0:T(8,128)(2,1)} %by_target.2), channel_id=1, source_target_pairs={{0,8},{8,0},{16,24},{24,16},{32,40},{40,32},{48,56},{56,48},{64,72... | collective-permute-start | bytes 9437192 | tf_op jit(solution)/shard_map/ppermute | solution.py:42
  8.2 13.8 %collective-permute-start.1 = (bf16[128,1024]{1,0:T(8,128)(2,1)S(1)}, bf16[128,1024]{1,0:T(8,128)(2,1)S(1)}, u32[]{:S(2)}, u32[]{:S(2)}) collective-permute-start(bf16[128,1024]{1,0:T(8,128)(2,1)S(1)} %pad_maximum_fusion.4), channel_id=1, source_target_pairs={{0,6},{1,7},{2,0},{3,1},{4,2},{5,3},{6,4},{7,5},{8,14},{9,15},{10,... | collective-permute-start | bytes 786440 | tf_op jit(solution)/shard_map/ppermute | solution.py:46
  11.0 14.3 %collective-permute-start.2 = (bf16[128,1024]{1,0:T(8,128)(2,1)S(1)}, bf16[128,1024]{1,0:T(8,128)(2,1)S(1)}, u32[]{:S(2)}, u32[]{:S(2)}) collective-permute-start(bf16[128,1024]{1,0:T(8,128)(2,1)S(1)} %pad_maximum_fusion.4), channel_id=1, source_target_pairs={{0,2},{1,3},{2,4},{3,5},{4,6},{5,7},{6,0},{7,1},{8,10},{9,11},{10,... | collective-permute-start | bytes 786440 | tf_op jit(solution)/shard_map/ppermute | solution.py:46
  11.0 14.3 %collective-permute-start.3 = (bf16[128,1024]{1,0:T(8,128)(2,1)S(1)}, bf16[128,1024]{1,0:T(8,128)(2,1)S(1)}, u32[]{:S(2)}, u32[]{:S(2)}) collective-permute-start(bf16[128,1024]{1,0:T(8,128)(2,1)S(1)} %pad_maximum_fusion.4), channel_id=1, source_target_pairs={{0,4},{1,5},{2,6},{3,7},{4,0},{5,1},{6,2},{7,3},{8,12},{9,13},{10,... | collective-permute-start | bytes 786440 | tf_op jit(solution)/shard_map/ppermute | solution.py:46
  12.6 12.6 %collective-permute-start.4 = (bf16[128,1024]{1,0:T(8,128)(2,1)S(1)}, bf16[128,1024]{1,0:T(8,128)(2,1)S(1)}, u32[]{:S(2)}, u32[]{:S(2)}) collective-permute-start(bf16[128,1024]{1,0:T(8,128)(2,1)S(1)} %pad_maximum_fusion.4), channel_id=1, source_target_pairs={{0,1},{1,0},{2,3},{3,2},{4,5},{5,4},{6,7},{7,6},{8,9},{9,8},{10,11... | collective-permute-start | bytes 786440 | tf_op jit(solution)/shard_map/ppermute | solution.py:46
  26.1 2.8 %copy-start = (bf16[512,3072]{1,0:T(8,128)(2,1)S(1)}, bf16[512,3072]{1,0:T(8,128)(2,1)}, u32[]{:S(2)}) copy-start(bf16[512,3072]{1,0:T(8,128)(2,1)} %by_target.2) | copy-start | bytes 9437188
  26.8 10.5 %collective-permute-start.11 = (bf16[128,1024]{1,0:T(8,128)(2,1)S(1)}, bf16[128,1024]{1,0:T(8,128)(2,1)S(1)}, u32[]{:S(2)}, u32[]{:S(2)}) collective-permute-start(bf16[128,1024]{1,0:T(8,128)(2,1)S(1)} %collective-permute-done.4), channel_id=1, source_target_pairs={{0,6},{1,7},{2,0},{3,1},{4,2},{5,3},{6,4},{7,5},{8,14},{9,15},{10,... | collective-permute-start | bytes 786440 | tf_op jit(solution)/shard_map/ppermute | solution.py:46
  27.2 10.1 %collective-permute-start.12 = (bf16[128,1024]{1,0:T(8,128)(2,1)S(1)}, bf16[128,1024]{1,0:T(8,128)(2,1)S(1)}, u32[]{:S(2)}, u32[]{:S(2)}) collective-permute-start(bf16[128,1024]{1,0:T(8,128)(2,1)S(1)} %collective-permute-done.4), channel_id=1, source_target_pairs={{0,2},{1,3},{2,4},{3,5},{4,6},{5,7},{6,0},{7,1},{8,10},{9,11},{10,... | collective-permute-start | bytes 786440 | tf_op jit(solution)/shard_map/ppermute | solution.py:46
  28.3 11.3 %collective-permute-start.13 = (bf16[128,1024]{1,0:T(8,128)(2,1)S(1)}, bf16[128,1024]{1,0:T(8,128)(2,1)S(1)}, u32[]{:S(2)}, u32[]{:S(2)}) collective-permute-start(bf16[128,1024]{1,0:T(8,128)(2,1)S(1)} %collective-permute-done.4), channel_id=1, source_target_pairs={{0,4},{1,5},{2,6},{3,7},{4,0},{5,1},{6,2},{7,3},{8,12},{9,13},{10,... | collective-permute-start | bytes 786440 | tf_op jit(solution)/shard_map/ppermute | solution.py:46
  30.6 42.7 %collective-permute-start.6 = (bf16[640,768]{1,0:T(8,128)(2,1)}, bf16[640,768]{1,0:T(8,128)(2,1)}, u32[]{:S(2)}, u32[]{:S(2)}) collective-permute-start(bf16[640,768]{1,0:T(8,128)(2,1)} %add_convert_fusion.2), channel_id=1, source_target_pairs={{0,96},{8,104},{16,112},{24,120},{32,0},{40,8},{48,16},{56,24},{64... | collective-permute-start | bytes 2949128 | tf_op jit(solution)/shard_map/ppermute | solution.py:42
  36.1 47.7 %collective-permute-start.7 = (bf16[640,768]{1,0:T(8,128)(2,1)}, bf16[640,768]{1,0:T(8,128)(2,1)}, u32[]{:S(2)}, u32[]{:S(2)}) collective-permute-start(bf16[640,768]{1,0:T(8,128)(2,1)} %add_convert_fusion.1), channel_id=1, source_target_pairs={{0,32},{8,40},{16,48},{24,56},{32,64},{40,72},{48,80},{56,88},{64,... | collective-permute-start | bytes 2949128 | tf_op jit(solution)/shard_map/ppermute | solution.py:42
  42.3 13.3 %collective-permute-start.15 = (bf16[384,768]{1,0:T(8,128)(2,1)S(1)}, bf16[384,768]{1,0:T(8,128)(2,1)S(1)}, u32[]{:S(2)}, u32[]{:S(2)}) collective-permute-start(bf16[384,768]{1,0:T(8,128)(2,1)S(1)} %fusion.5), channel_id=1, source_target_pairs={{0,16},{8,24},{16,0},{24,8},{32,48},{40,56},{48,32},{56,40},{64,80... | collective-permute-start | bytes 1769480 | tf_op jit(solution)/shard_map/ppermute | solution.py:42
  46.4 23.8 %collective-permute-start.14 = (bf16[384,768]{1,0:T(8,128)(2,1)}, bf16[384,768]{1,0:T(8,128)(2,1)}, u32[]{:S(2)}, u32[]{:S(2)}) collective-permute-start(bf16[384,768]{1,0:T(8,128)(2,1)} %fusion.4), channel_id=1, source_target_pairs={{0,16},{8,24},{16,0},{24,8},{32,48},{40,56},{48,32},{56,40},{64,80... | collective-permute-start | bytes 1769480 | tf_op jit(solution)/shard_map/ppermute | solution.py:42
  55.6 0.8 copy-start.2
  56.4 13.8 %collective-permute-start.17 = (bf16[2,192,384]{2,1,0:T(8,128)(2,1)S(1)}, bf16[2,192,384]{2,1,0:T(8,128)(2,1)}, u32[]{:S(2)}, u32[]{:S(2)}) collective-permute-start(bf16[2,192,384]{2,1,0:T(8,128)(2,1)S(1)} %pad_maximum_fusion.2), channel_id=1, source_target_pairs={{0,32},{8,40},{16,48},{24,56},{32,64},{40,72},{48,80},{56,88},{64,... | collective-permute-start | bytes 884744 | tf_op jit(solution)/shard_map/ppermute | solution.py:42
  62.3 32.0 %collective-permute-start.20 = (bf16[1024,512]{1,0:T(8,128)(2,1)}, bf16[1024,512]{1,0:T(8,128)(2,1)S(1)}, u32[]{:S(2)}, u32[]{:S(2)}) collective-permute-start(bf16[1024,512]{1,0:T(8,128)(2,1)} %by_target.3), channel_id=1, source_target_pairs={{0,8},{8,0},{16,24},{24,16},{32,40},{40,32},{48,56},{56,48},{64,72... | collective-permute-start | bytes 3145736 | tf_op jit(solution)/shard_map/ppermute | solution.py:42
  71.4 11.1 %collective-permute-start.16 = (bf16[2,192,384]{2,1,0:T(8,128)(2,1)S(1)}, bf16[2,192,384]{2,1,0:T(8,128)(2,1)S(1)}, u32[]{:S(2)}, u32[]{:S(2)}) collective-permute-start(bf16[2,192,384]{2,1,0:T(8,128)(2,1)S(1)} %pad_maximum_fusion.1), channel_id=1, source_target_pairs={{0,96},{8,104},{16,112},{24,120},{32,0},{40,8},{48,16},{56,24},{64... | collective-permute-start | bytes 884744 | tf_op jit(solution)/shard_map/ppermute | solution.py:42
  75.6 13.2 %collective-permute-start.9 = (bf16[640,384]{1,0:T(8,128)(2,1)S(1)}, bf16[640,384]{1,0:T(8,128)(2,1)S(1)}, u32[]{:S(2)}, u32[]{:S(2)}) collective-permute-start(bf16[640,384]{1,0:T(8,128)(2,1)S(1)} %get-tuple-element.49), channel_id=1, source_target_pairs={{0,96},{8,104},{16,112},{24,120},{32,0},{40,8},{48,16},{56,24},{64... | collective-permute-start | bytes 1474568 | tf_op jit(solution)/shard_map/ppermute | solution.py:42
  77.3 17.1 %copy-start.1 = (bf16[1024,512]{1,0:T(8,128)(2,1)S(1)}, bf16[1024,512]{1,0:T(8,128)(2,1)}, u32[]{:S(2)}) copy-start(bf16[1024,512]{1,0:T(8,128)(2,1)} %by_target.3) | copy-start | bytes 3145732
  77.3 5.2 %collective-permute-start.18 = (bf16[192,384]{1,0:T(8,128)(2,1)S(1)}, bf16[192,384]{1,0:T(8,128)(2,1)S(1)}, u32[]{:S(2)}, u32[]{:S(2)}) collective-permute-start(bf16[192,384]{1,0:T(8,128)(2,1)S(1)} %get-tuple-element.53), channel_id=1, source_target_pairs={{0,32},{8,40},{16,48},{24,56},{32,64},{40,72},{48,80},{56,88},{64,... | collective-permute-start | bytes 442376 | tf_op jit(solution)/shard_map/ppermute | solution.py:42
  83.7 11.0 %collective-permute-start.19 = (bf16[192,384]{1,0:T(8,128)(2,1)S(1)}, bf16[192,384]{1,0:T(8,128)(2,1)S(1)}, u32[]{:S(2)}, u32[]{:S(2)}) collective-permute-start(bf16[192,384]{1,0:T(8,128)(2,1)S(1)} %get-tuple-element.52), channel_id=1, source_target_pairs={{0,96},{8,104},{16,112},{24,120},{32,0},{40,8},{48,16},{56,24},{64... | collective-permute-start | bytes 442376 | tf_op jit(solution)/shard_map/ppermute | solution.py:42
  90.4 9.0 %collective-permute-start.8 = (bf16[640,384]{1,0:T(8,128)(2,1)S(1)}, bf16[640,384]{1,0:T(8,128)(2,1)S(1)}, u32[]{:S(2)}, u32[]{:S(2)}) collective-permute-start(bf16[640,384]{1,0:T(8,128)(2,1)S(1)} %get-tuple-element.48), channel_id=1, source_target_pairs={{0,32},{8,40},{16,48},{24,56},{32,64},{40,72},{48,80},{56,88},{64,... | collective-permute-start | bytes 1474568 | tf_op jit(solution)/shard_map/ppermute | solution.py:42
  91.6 9.2 %collective-permute-start.10 = (bf16[640,384]{1,0:T(8,128)(2,1)S(1)}, bf16[640,384]{1,0:T(8,128)(2,1)S(1)}, u32[]{:S(2)}, u32[]{:S(2)}) collective-permute-start(bf16[640,384]{1,0:T(8,128)(2,1)S(1)} %get-tuple-element.47), channel_id=1, source_target_pairs={{0,16},{8,24},{16,0},{24,8},{32,48},{40,56},{48,32},{56,40},{64,80... | collective-permute-start | bytes 1474568 | tf_op jit(solution)/shard_map/ppermute | solution.py:42
  99.3 2.3 %copy-start.3 = (bf16[640,384]{1,0:T(8,128)(2,1)}, bf16[640,384]{1,0:T(8,128)(2,1)S(1)}, u32[]{:S(2)}) copy-start(bf16[640,384]{1,0:T(8,128)(2,1)S(1)} %collective-permute-done.8.refs_4_) | copy-start | bytes 1474564
  100.8 0.8 copy-start.4
  106.3 7.2 %collective-permute-start.21 = (f32[26,8,128]{2,1,0:T(8,128)}, f32[26,8,128]{2,1,0:T(8,128)S(1)}, u32[]{:S(2)}, u32[]{:S(2)}) collective-permute-start(f32[26,8,128]{2,1,0:T(8,128)} %get-tuple-element.43.mine_ref), channel_id=1, source_target_pairs={{0,8},{8,0},{16,24},{24,16},{32,40},{40,32},{48,56},{56,48},{64,72... | collective-permute-start | bytes 319496 | tf_op jit(solution)/shard_map/ppermute | solution.py:42
  113.6 0.6 copy-start.5
  119.1 12.9 %collective-permute-start.22 = (bf16[1024,128]{1,0:T(8,128)(2,1)}, bf16[1024,128]{1,0:T(8,128)(2,1)S(1)}, u32[]{:S(2)}, u32[]{:S(2)}) collective-permute-start(bf16[1024,128]{1,0:T(8,128)(2,1)} %filtered.1), channel_id=1, source_target_pairs={{0,16},{8,24},{16,0},{24,8},{32,48},{40,56},{48,32},{56,40},{64,80... | collective-permute-start | bytes 786440 | tf_op jit(solution)/shard_map/ppermute | solution.py:42
  121.8 12.1 %collective-permute-start.23 = (bf16[1024,128]{1,0:T(8,128)(2,1)}, bf16[1024,128]{1,0:T(8,128)(2,1)S(1)}, u32[]{:S(2)}, u32[]{:S(2)}) collective-permute-start(bf16[1024,128]{1,0:T(8,128)(2,1)} %filtered.1), channel_id=1, source_target_pairs={{0,96},{8,104},{16,112},{24,120},{32,0},{40,8},{48,16},{56,24},{64... | collective-permute-start | bytes 786440 | tf_op jit(solution)/shard_map/ppermute | solution.py:42
  123.9 11.1 %collective-permute-start.24 = (bf16[1024,128]{1,0:T(8,128)(2,1)}, bf16[1024,128]{1,0:T(8,128)(2,1)S(1)}, u32[]{:S(2)}, u32[]{:S(2)}) collective-permute-start(bf16[1024,128]{1,0:T(8,128)(2,1)} %filtered.1), channel_id=1, source_target_pairs={{0,112},{8,120},{16,96},{24,104},{32,16},{40,24},{48,0},{56,8},{64... | collective-permute-start | bytes 786440 | tf_op jit(solution)/shard_map/ppermute | solution.py:42
  126.5 8.6 %collective-permute-start.25 = (bf16[1024,128]{1,0:T(8,128)(2,1)}, bf16[1024,128]{1,0:T(8,128)(2,1)S(1)}, u32[]{:S(2)}, u32[]{:S(2)}) collective-permute-start(bf16[1024,128]{1,0:T(8,128)(2,1)} %filtered.1), channel_id=1, source_target_pairs={{0,64},{8,72},{16,80},{24,88},{32,96},{40,104},{48,112},{56,120},{... | collective-permute-start | bytes 786440 | tf_op jit(solution)/shard_map/ppermute | solution.py:42
  126.6 16.5 %collective-permute-start.26 = (bf16[1024,128]{1,0:T(8,128)(2,1)}, bf16[1024,128]{1,0:T(8,128)(2,1)S(1)}, u32[]{:S(2)}, u32[]{:S(2)}) collective-permute-start(bf16[1024,128]{1,0:T(8,128)(2,1)} %filtered.1), channel_id=1, source_target_pairs={{0,80},{8,88},{16,64},{24,72},{32,112},{40,120},{48,96},{56,104},{... | collective-permute-start | bytes 786440 | tf_op jit(solution)/shard_map/ppermute | solution.py:42
  132.0 18.4 %collective-permute-start.27 = (bf16[1024,128]{1,0:T(8,128)(2,1)}, bf16[1024,128]{1,0:T(8,128)(2,1)S(1)}, u32[]{:S(2)}, u32[]{:S(2)}) collective-permute-start(bf16[1024,128]{1,0:T(8,128)(2,1)} %filtered.1), channel_id=1, source_target_pairs={{0,32},{8,40},{16,48},{24,56},{32,64},{40,72},{48,80},{56,88},{64,... | collective-permute-start | bytes 786440 | tf_op jit(solution)/shard_map/ppermute | solution.py:42
  133.9 16.6 %collective-permute-start.28 = (bf16[1024,128]{1,0:T(8,128)(2,1)}, bf16[1024,128]{1,0:T(8,128)(2,1)S(1)}, u32[]{:S(2)}, u32[]{:S(2)}) collective-permute-start(bf16[1024,128]{1,0:T(8,128)(2,1)} %filtered.1), channel_id=1, source_target_pairs={{0,48},{8,56},{16,32},{24,40},{32,80},{40,88},{48,64},{56,72},{64,... | collective-permute-start | bytes 786440 | tf_op jit(solution)/shard_map/ppermute | solution.py:42
  153.4 12.7 %collective-permute-start.35 = (bf16[128,1024]{1,0:T(8,128)(2,1)S(1)}, bf16[128,1024]{1,0:T(8,128)(2,1)S(1)}, u32[]{:S(2)}, u32[]{:S(2)}) collective-permute-start(bf16[128,1024]{1,0:T(8,128)(2,1)S(1)} %convolution_convert_fusion), channel_id=1, source_target_pairs={{0,7},{1,6},{2,1},{3,0},{4,3},{5,2},{6,5},{7,4},{8,15},{9,14},{10,... | collective-permute-start | bytes 786440 | tf_op jit(solution)/shard_map/ppermute | solution.py:46
  155.5 16.7 %collective-permute-start.34 = (bf16[128,1024]{1,0:T(8,128)(2,1)S(1)}, bf16[128,1024]{1,0:T(8,128)(2,1)S(1)}, u32[]{:S(2)}, u32[]{:S(2)}) collective-permute-start(bf16[128,1024]{1,0:T(8,128)(2,1)S(1)} %convolution_convert_fusion.1), channel_id=1, source_target_pairs={{0,5},{1,4},{2,7},{3,6},{4,1},{5,0},{6,3},{7,2},{8,13},{9,12},{10,... | collective-permute-start | bytes 786440 | tf_op jit(solution)/shard_map/ppermute | solution.py:46
  161.7 12.3 %collective-permute-start.33 = (bf16[128,1024]{1,0:T(8,128)(2,1)S(1)}, bf16[128,1024]{1,0:T(8,128)(2,1)S(1)}, u32[]{:S(2)}, u32[]{:S(2)}) collective-permute-start(bf16[128,1024]{1,0:T(8,128)(2,1)S(1)} %convolution_convert_fusion.2), channel_id=1, source_target_pairs={{0,3},{1,2},{2,5},{3,4},{4,7},{5,6},{6,1},{7,0},{8,11},{9,10},{10,... | collective-permute-start | bytes 786440 | tf_op jit(solution)/shard_map/ppermute | solution.py:46
  161.7 15.5 %collective-permute-start.32 = (bf16[128,1024]{1,0:T(8,128)(2,1)S(1)}, bf16[128,1024]{1,0:T(8,128)(2,1)S(1)}, u32[]{:S(2)}, u32[]{:S(2)}) collective-permute-start(bf16[128,1024]{1,0:T(8,128)(2,1)S(1)} %convolution_convert_fusion.3), channel_id=1, source_target_pairs={{0,1},{1,0},{2,3},{3,2},{4,5},{5,4},{6,7},{7,6},{8,9},{9,8},{10,11... | collective-permute-start | bytes 786440 | tf_op jit(solution)/shard_map/ppermute | solution.py:46
  162.2 15.7 %collective-permute-start.31 = (bf16[128,1024]{1,0:T(8,128)(2,1)S(1)}, bf16[128,1024]{1,0:T(8,128)(2,1)S(1)}, u32[]{:S(2)}, u32[]{:S(2)}) collective-permute-start(bf16[128,1024]{1,0:T(8,128)(2,1)S(1)} %convolution_convert_fusion.4), channel_id=1, source_target_pairs={{0,6},{1,7},{2,0},{3,1},{4,2},{5,3},{6,4},{7,5},{8,14},{9,15},{10,... | collective-permute-start | bytes 786440 | tf_op jit(solution)/shard_map/ppermute | solution.py:46
  166.1 18.9 %collective-permute-start.30 = (bf16[128,1024]{1,0:T(8,128)(2,1)S(1)}, bf16[128,1024]{1,0:T(8,128)(2,1)S(1)}, u32[]{:S(2)}, u32[]{:S(2)}) collective-permute-start(bf16[128,1024]{1,0:T(8,128)(2,1)S(1)} %convolution_convert_fusion.5), channel_id=1, source_target_pairs={{0,4},{1,5},{2,6},{3,7},{4,0},{5,1},{6,2},{7,3},{8,12},{9,13},{10,... | collective-permute-start | bytes 786440 | tf_op jit(solution)/shard_map/ppermute | solution.py:46
  172.2 16.8 %collective-permute-start.29 = (bf16[128,1024]{1,0:T(8,128)(2,1)S(1)}, bf16[128,1024]{1,0:T(8,128)(2,1)S(1)}, u32[]{:S(2)}, u32[]{:S(2)}) collective-permute-start(bf16[128,1024]{1,0:T(8,128)(2,1)S(1)} %convolution_convert_fusion.6), channel_id=1, source_target_pairs={{0,2},{1,3},{2,4},{3,5},{4,6},{5,7},{6,0},{7,1},{8,10},{9,11},{10,... | collective-permute-start | bytes 786440 | tf_op jit(solution)/shard_map/ppermute | solution.py:46
  189.7 2.7 %collective-permute-start.36 = (bf16[128,512]{1,0:T(8,128)(2,1)S(1)}, bf16[128,512]{1,0:T(8,128)(2,1)S(1)}, u32[]{:S(2)}, u32[]{:S(2)}) collective-permute-start(bf16[128,512]{1,0:T(8,128)(2,1)S(1)} %get-tuple-element.59), channel_id=1, source_target_pairs={{0,8},{8,0},{16,24},{24,16},{32,40},{40,32},{48,56},{56,48},{64,72... | collective-permute-start | bytes 393224 | tf_op jit(solution)/shard_map/ppermute | solution.py:42

commit v3 on v2

--- a/solution.py
+++ b/solution.py
@@ -61,48 +61,55 @@
     return pl.BlockSpec(shape, lambda *_: (0,) * len(shape))
 
 
+PLACES = [(2, 1), (1, 0), (1, 1), (3, 0), (3, 1), (2, 0), (0, 1), (0, 0)]
 TARGETS = [(2, 0), (1, 1), (2, 1), (3, 0), (1, 0), (0, 0), (0, 1), (3, 1)]
 
 
-def chip_of(where_ref, dz, dx):
-    return ((where_ref[0] + dz) & (Z - 1)) * XH + ((where_ref[1] + dx) & (XH - 1))
-
-
-def reorder_kernel(targets, axis, where_ref, in_ref, out_ref, sems):
-    size = in_ref.shape[axis] // len(targets)
+def reorder_kernel(in_ref, *refs):
+    out_refs, sems = refs[:-1], refs[-1]
+    chip = lax.axis_index("tok") >> 1
+    size = in_ref.shape[1] // len(TARGETS)
+    each = len(TARGETS) // len(out_refs)
     copies = []
-    for k, (dz, dx) in enumerate(targets):
-        source = pl.ds(pl.multiple_of(chip_of(where_ref, dz, dx) * size, size), size)
-        place = pl.ds(k * size, size)
-        if axis == 0:
-            pair = in_ref.at[source, :], out_ref.at[place, :]
-        else:
-            pair = in_ref.at[:, source], out_ref.at[:, place]
-        copies.append(pltpu.make_async_copy(*pair, sems.at[k]))
+    for k, (dz, dx) in enumerate(TARGETS):
+        target = (((chip >> 1) + dz) & (Z - 1)) * XH + ((chip + dx) & (XH - 1))
+        source = pl.ds(pl.multiple_of(target * size, size), size)
+        place = pl.ds(k % each * size, size)
+        copies.append(
+            pltpu.make_async_copy(in_ref.at[:, source], out_refs[k // each].at[:, place], sems.at[k])
+        )
         copies[-1].start()
     for copy in copies:
         copy.wait()
 
 
-def by_target(weight, where, targets, axis):
+def by_target(weight, parts):
+    shape = jax.ShapeDtypeStruct((weight.shape[0], weight.shape[1] // parts), weight.dtype)
     return pl.pallas_call(
-        lambda *refs: reorder_kernel(targets, axis, *refs),
-        out_shape=jax.ShapeDtypeStruct(weight.shape, weight.dtype),
-        in_specs=[pl.BlockSpec(memory_space=pltpu.SMEM), pl.BlockSpec(memory_space=pl.ANY)],
-        out_specs=pl.BlockSpec(memory_space=pltpu.VMEM),
-        scratch_shapes=[pltpu.SemaphoreType.DMA((len(targets),))],
+        reorder_kernel,
+        out_shape=[shape] * parts,
+        in_specs=[pl.BlockSpec(memory_space=pl.ANY)],
+        out_specs=[pl.BlockSpec(memory_space=pltpu.VMEM)] * parts,
+        scratch_shapes=[pltpu.SemaphoreType.DMA((len(TARGETS),))],
         name="by_target",
-    )(where, weight)
+    )(weight)
 
 
 def product(rows, weights, first, last):
-    depth, cols = weights[0].shape
-    width = cols // len(TARGETS)
-    columns = slice(first * width, last * width)
-    return (
-        jnp.dot(rows[:, :depth], weights[0][:, columns], preferred_element_type=F32)
-        + jnp.dot(rows[:, depth:], weights[1][:, columns], preferred_element_type=F32)
-    ).astype(BF)
+    own, other = weights
+    depth, cols = own[0].shape
+    each = len(TARGETS) // len(own)
+    width = cols // each
+    outs = []
+    for part in range(len(own)):
+        low, high = max(first - part * each, 0), min(last - part * each, each)
+        if low < high:
+            columns = slice(low * width, high * width)
+            outs.append(
+                jnp.dot(rows[:, :depth], own[part][:, columns], preferred_element_type=F32)
+                + jnp.dot(rows[:, depth:], other[part][:, columns], preferred_element_type=F32)
+            )
+    return jnp.concatenate(outs, axis=1).astype(BF)
 
 
 def split(value, count):
@@ -126,7 +133,8 @@
     far1, far2 = split(tok_send(product(rows, weights, 1, 3), X_SWAP), 2)
     far0, far3 = split(tok_send(product(rows, weights, 6, 8), X_SWAP), 2)
     near2 = product(rows, weights, 0, 1)
-    near3, near1, near0 = split(product(rows, weights, 3, 6), 3)
+    near3 = product(rows, weights, 3, 4)
+    near1, near0 = split(product(rows, weights, 4, 6), 2)
     half = rows.shape[0] // 2
     first, second = slice(0, half), slice(half, None)
 
@@ -278,12 +286,10 @@
         states,
         unroll=6,
     )
-    for g in range(XL):
-        for dy in range(Y):
-            spot = ((where_ref[3] + dy) & (Y - 1)) * XL + ((where_ref[4] + g) & (XL - 1))
-            there = pl.ds(pl.multiple_of(spot * length, length), length)
-            place = (g * Y + dy) * length
-            out_ref[place : place + length, :] = work[there, :].astype(BF)
+    for place, (dy, dx) in enumerate(PLACES):
+        spot = ((where_ref[3] + dy) & (Y - 1)) * XL + ((where_ref[4] + dx) & (XL - 1))
+        there = pl.ds(pl.multiple_of(spot * length, length), length)
+        out_ref[place * length : (place + 1) * length, :] = work[there, :].astype(BF)
 
 
 def own_lanes(shape):
@@ -342,43 +348,62 @@
     other = swap(lax.dynamic_slice_in_dim(activations, (1 - core) * length, length, 0))
     mine = jnp.concatenate([kept, other], axis=1)
     mine, proj_weight = lax.optimization_barrier((mine, proj_weight))
-    ordered = by_target(proj_weight, where, TARGETS, 1)
-    weights = (ordered, swap(ordered))
 
     def along(value, dy):
         return ch_send(value, ch_perm(lambda y, xl: (y - dy, xl)))
 
-    across = ch_send(mine, ch_perm(lambda y, xl: (y, 1 - xl)))
+    def across(value):
+        return ch_send(value, ch_perm(lambda y, xl: (y, 1 - xl)))
+
     blocks = [[(0, 0), (1, 0), (3, 0), (2, 0), (0, 1)], [(1, 1), (3, 1), (2, 1)]]
-    first = [mine] + [along(mine, dy) for dy, _ in blocks[0][1:4]] + [across]
-    first, weights = lax.optimization_barrier((first, weights))
-    second = [along(first[-1], dy) for dy, _ in blocks[1]]
-    second, out_weight = lax.optimization_barrier((second, out_weight))
-    chips = [(k // XH, k % XH) for k in range(Z * XH)]
-    out_ordered = by_target(out_weight, where, chips, 0)
-    out_rows = jnp.concatenate([out_ordered, swap(out_ordered)], axis=1)
+    first = [mine, along(mine, 1), along(mine, 3), along(mine, 2), across(mine)]
+    ordered = by_target(proj_weight, 2)
+    early, late = swap(ordered[0]), swap(ordered[1])
+    first, early = lax.optimization_barrier((first, early))
+    second = [along(first[4], 1), along(first[4], 3), across(first[3])]
+    weights = (ordered, [early, late])
     groups = [
         reduce_ring_first(jnp.concatenate(first), weights),
         reduce_pair_first(jnp.concatenate(second), weights),
     ]
-    groups, out_rows = lax.optimization_barrier((groups, out_rows))
     query, gate, edges = local_part(where, short_taps, decay_rates, groups, blocks)
+    edges, out_weight = lax.optimization_barrier((edges, out_weight))
     their_edges = swap(edges)
+    their_out = swap(out_weight)
     gated = filtered(where, short_taps, decay_rates, residues, skip_gain[None], edges, their_edges, query, gate)
 
-    pieces = [gated]
-    for dz, dx in chips[1:]:
-        pieces.append(tok_send(gated, tok_perm(lambda z, xh, c, dz=dz, dx=dx: (z - dz, xh ^ dx, c))))
-    gathered = jnp.concatenate(pieces, axis=1)
-    terms = []
-    for k in range(BLOCKS):
-        dx, dy = k // Y, k % Y
-        rows = gathered[k * length : (k + 1) * length]
-        term = jnp.dot(rows, out_rows, preferred_element_type=F32).astype(BF)
-        if k:
-            term = ch_send(term, ch_perm(lambda y, xl, dx=dx, dy=dy: (y + dy, xl ^ dx)))
-        terms.append(term)
-    total = add(*terms)
+    gated, their_out = lax.optimization_barrier((gated, their_out))
+    out_rows = jnp.concatenate([out_weight, their_out], axis=1)
+
+    pieces = {(0, 0): gated}
+    pieces[0, 1] = tok_send(gated, X_SWAP)
+    pieces[2, 0] = tok_send(gated, tok_perm(lambda z, xh, c: (z + 2, xh, c)))
+    pieces[1, 0], pieces[3, 0] = tok_send(gated, Z_DOWN), tok_send(gated, Z_UP)
+    pieces[1, 1], pieces[3, 1] = tok_send(pieces[0, 1], Z_DOWN), tok_send(pieces[0, 1], Z_UP)
+    pieces[2, 1] = tok_send(pieces[2, 0], X_SWAP)
+    gathered = jnp.zeros((gated.shape[0], Z * XH * LANES), BF)
+    for (dz, dx), piece in pieces.items():
+        chip = ((z + dz) & (Z - 1)) * XH + ((xh + dx) & (XH - 1))
+        gathered = lax.dynamic_update_slice(gathered, piece, (0, chip * LANES))
+
+    def part(first, last):
+        rows = gathered[PLACES.index(first) * length : (PLACES.index(last) + 1) * length]
+        return jnp.dot(rows, out_rows, preferred_element_type=F32)
+
+    def forward(value, dy):
+        return ch_send(value, ch_perm(lambda y, xl: (y + dy, xl)))
+
+    far = across(part((2, 1), (2, 1)).astype(BF))
+    up = forward(part((1, 0), (1, 1)).astype(BF), 1)
+    down = forward(part((3, 0), (3, 1)).astype(BF), 3)
+    opposite = forward((part((2, 0), (2, 0)) + far.astype(F32)).astype(BF), 2)
+    beside = across(
+        (part((0, 1), (0, 1)) + up[length:].astype(F32) + down[length:].astype(F32)).astype(BF)
+    )
+    total = part((0, 0), (0, 0))
+    for term in (up[:length], down[:length], opposite, beside):
+        total = total + term.astype(F32)
+    total = total.astype(BF)
     cols = out_weight.shape[1]
     kept, other = total[:, :cols], swap(total[:, cols:])
     return jnp.where(core == 0, jnp.concatenate([kept, other]), jnp.concatenate([other, kept]))

time: 194 us -> 171 us (0.88)
  starting transfers between devices: 65.9 us -> 54.7 us
  Pallas kernels: 16.9 us -> 13.2 us
  other arithmetic: 9.04 us -> 5.85 us
  matrix products: 15.8 us -> 12.8 us
    ppermute x14 -> x12, waiting for transfers between devices: 36.7 us -> 24.2 us  [ch_send(): return lax.ppermute(value, 'ch', perm)]
    ppermute x23 -> x24, waiting for transfers between devices: 43 us -> 54 us  [tok_send(): return lax.ppermute(value, 'tok', perm)]
    ppermute x23 -> x24, starting transfers between devices: 45.8 us -> 39.9 us  [tok_send(): return lax.ppermute(value, 'tok', perm)]
    ppermute x14 -> x12, starting transfers between devices: 20.1 us -> 14.7 us  [ch_send(): return lax.ppermute(value, 'ch', perm)]
    pallas_call x2 -> x1, Pallas kernels: 7.24 us -> 3.59 us  [by_target(): pl.pallas_call(reorder_kernel, out_shape=[shape] * parts, in_specs=[pl.Bl...]
    dot_general x22, matrix products: 15.8 us -> 12.8 us  [the longest x8 4.72 us: product(): jnp.dot(rows[:, :depth], own[part][:, columns], preferred_element_type=F32)]
    convert_element_type x2, other arithmetic: 3.72 us -> 1.41 us  [add(): return total.astype(BF)]
  transfers between devices with their start and end apart: 37 -> 36, of which waited for: 21 -> 19; matrix products, arithmetic and copies ran while one was open for 11% -> 11% of each run, Pallas kernels for 2% -> 3%
where the time goes in v3:
time: 171 us; the launch traced here: 170 us
  waiting for transfers between devices  78.2 us (46%)
  starting transfers between devices  54.7 us (32%)
  Pallas kernels  13.2 us (8%)
  matrix products  12.8 us (7%)
  other arithmetic  5.85 us (3%)
  local copies, waits for them, and re-layouts  5.17 us (3%)
    ppermute x24, waiting for transfers between devices, tok_send(): return lax.ppermute(value, 'tok', perm)  54 us
    ppermute x24, starting transfers between devices, tok_send(): return lax.ppermute(value, 'tok', perm)  39.9 us
    ppermute x12, waiting for transfers between devices, ch_send(): return lax.ppermute(value, 'ch', perm)  24.2 us
    ppermute x12, starting transfers between devices, ch_send(): return lax.ppermute(value, 'ch', perm)  14.7 us
    pallas_call x1, Pallas kernels, filtered(): pl.pallas_call(filter_kernel, out_shape=jax.ShapeDtypeStruct(gate.shape,...  4.88 us
    pallas_call x1, Pallas kernels, local_part(): pl.pallas_call(lambda *refs: local_kernel(blocks, [len(terms) for terms i...  4.73 us
    dot_general x8, matrix products, product(): jnp.dot(rows[:, :depth], own[part][:, columns], preferred_element_type=F32)  4.72 us
    dot_general x8, matrix products, product(): jnp.dot(rows[:, depth:], other[part][:, columns], preferred_element_type=...  4.7 us
  transfers between devices with their start and end apart: 36, of which 19 were waited for; matrix products, arithmetic and copies ran while one was open for 11% of the time, Pallas kernels for 3%

profile of v3, /device:TPU:1, one launch (start us, length us, event | category | flops | bytes accessed | tf_op | source)
XLA Modules:
  0.0 170.3 jit_solution(9034330299501641077)
XLA Ops:
  1.0 1.5 collective-permute-start
  2.5 1.0 collective-permute-done
  3.5 3.6 %by_target.1 = (bf16[512,1536]{1,0:T(8,128)(2,1)}, bf16[512,1536]{1,0:T(8,128)(2,1)}) custom-call(bf16[512,3072]{1,0:T(8,128)(2,1)} %in_ref), custom_call_target="tpu_custom_call" | custom-call | tf_op jit(solution)/shard_map/by_target/pallas_call | solution.py:88
  7.5 2.8 %collective-permute-start.1 = (bf16[128,1024]{1,0:T(8,128)(2,1)S(1)}, bf16[128,1024]{1,0:T(8,128)(2,1)S(1)}, u32[]{:S(2)}, u32[]{:S(2)}) collective-permute-start(bf16[128,1024]{1,0:T(8,128)(2,1)S(1)} %pad_maximum_fusion.3), channel_id=1, source_target_pairs={{0,6},{1,7},{2,0},{3,1},{4,2},{5,3},{6,4},{7,5},{8,14},{9,15},{10,... | collective-permute-start | bytes 786440 | tf_op jit(solution)/shard_map/ppermute | solution.py:46
  10.4 1.6 collective-permute-start.3
  12.0 1.2 collective-permute-start.4
  13.2 8.2 %collective-permute-done.1 = bf16[128,1024]{1,0:T(8,128)(2,1)S(1)} collective-permute-done((bf16[128,1024]{1,0:T(8,128)(2,1)S(1)}, bf16[128,1024]{1,0:T(8,128)(2,1)S(1)}, u32[]{:S(2)}, u32[]{:S(2)}) %collective-permute-start.1) | collective-permute-done | bytes 262176 | tf_op jit(solution)/shard_map/ppermute | solution.py:46
  21.4 1.1 collective-permute-start.6
  22.5 2.1 %collective-permute-done.2 = bf16[128,1024]{1,0:T(8,128)(2,1)S(1)} collective-permute-done((bf16[128,1024]{1,0:T(8,128)(2,1)S(1)}, bf16[128,1024]{1,0:T(8,128)(2,1)S(1)}, u32[]{:S(2)}, u32[]{:S(2)}) %collective-permute-start.2) | collective-permute-done | bytes 262176 | tf_op jit(solution)/shard_map/ppermute | solution.py:46
  24.6 1.4 collective-permute-start.12
  26.2 1.2 collective-permute-start.14
  28.9 1.7 %collective-permute-start.8 = (bf16[640,768]{1,0:T(8,128)(2,1)S(1)}, bf16[640,768]{1,0:T(8,128)(2,1)S(1)}, u32[]{:S(2)}, u32[]{:S(2)}) collective-permute-start(bf16[640,768]{1,0:T(8,128)(2,1)S(1)} %add_convert_fusion.1), channel_id=1, source_target_pairs={{0,32},{8,40},{16,48},{24,56},{32,64},{40,72},{48,80},{56,88},{64,... | collective-permute-start | bytes 2949128 | tf_op jit(solution)/shard_map/ppermute | solution.py:42
  32.7 1.2 fusion.34
  33.9 2.2 %collective-permute-start.7 = (bf16[640,768]{1,0:T(8,128)(2,1)S(1)}, bf16[640,768]{1,0:T(8,128)(2,1)S(1)}, u32[]{:S(2)}, u32[]{:S(2)}) collective-permute-start(bf16[640,768]{1,0:T(8,128)(2,1)S(1)} %add_convert_fusion.2), channel_id=1, source_target_pairs={{0,96},{8,104},{16,112},{24,120},{32,0},{40,8},{48,16},{56,24},{64... | collective-permute-start | bytes 2949128 | tf_op jit(solution)/shard_map/ppermute | solution.py:42
  36.1 1.2 add_convert_fusion
  39.2 2.5 %collective-permute-start.15 = (bf16[384,768]{1,0:T(8,128)(2,1)S(1)}, bf16[384,768]{1,0:T(8,128)(2,1)S(1)}, u32[]{:S(2)}, u32[]{:S(2)}) collective-permute-start(bf16[384,768]{1,0:T(8,128)(2,1)S(1)} %fusion.1), channel_id=1, source_target_pairs={{0,16},{8,24},{16,0},{24,8},{32,48},{40,56},{48,32},{56,40},{64,80... | collective-permute-start | bytes 1769480 | tf_op jit(solution)/shard_map/ppermute | solution.py:42
  45.1 8.1 %collective-permute-done.15 = bf16[384,768]{1,0:T(8,128)(2,1)S(1)} collective-permute-done((bf16[384,768]{1,0:T(8,128)(2,1)S(1)}, bf16[384,768]{1,0:T(8,128)(2,1)S(1)}, u32[]{:S(2)}, u32[]{:S(2)}) %collective-permute-start.15) | collective-permute-done | bytes 589856 | tf_op jit(solution)/shard_map/ppermute | solution.py:42
  53.3 12.6 %collective-permute-done.16 = bf16[384,768]{1,0:T(8,128)(2,1)S(1)} collective-permute-done((bf16[384,768]{1,0:T(8,128)(2,1)S(1)}, bf16[384,768]{1,0:T(8,128)(2,1)S(1)}, u32[]{:S(2)}, u32[]{:S(2)}) %collective-permute-start.16) | collective-permute-done | bytes 589856 | tf_op jit(solution)/shard_map/ppermute | solution.py:42
  66.0 1.3 collective-permute-start.17
  67.7 1.1 add_convert_fusion.4
  68.8 2.4 %collective-permute-start.10 = (bf16[640,384]{1,0:T(8,128)(2,1)S(1)}, bf16[640,384]{1,0:T(8,128)(2,1)S(1)}, u32[]{:S(2)}, u32[]{:S(2)}) collective-permute-start(bf16[640,384]{1,0:T(8,128)(2,1)S(1)} %get-tuple-element.41), channel_id=1, source_target_pairs={{0,96},{8,104},{16,112},{24,120},{32,0},{40,8},{48,16},{56,24},{64... | collective-permute-start | bytes 1474568 | tf_op jit(solution)/shard_map/ppermute | solution.py:42
  72.4 2.4 %collective-permute-start.20 = (bf16[192,384]{1,0:T(8,128)(2,1)}, bf16[192,384]{1,0:T(8,128)(2,1)}, u32[]{:S(2)}, u32[]{:S(2)}) collective-permute-start(bf16[192,384]{1,0:T(8,128)(2,1)} %fusion.42), channel_id=1, source_target_pairs={{0,96},{8,104},{16,112},{24,120},{32,0},{40,8},{48,16},{56,24},{64... | collective-permute-start | bytes 442376 | tf_op jit(solution)/shard_map/ppermute | solution.py:42
  75.6 6.4 %collective-permute-done.10 = bf16[640,384]{1,0:T(8,128)(2,1)S(1)} collective-permute-done((bf16[640,384]{1,0:T(8,128)(2,1)S(1)}, bf16[640,384]{1,0:T(8,128)(2,1)S(1)}, u32[]{:S(2)}, u32[]{:S(2)}) %collective-permute-start.10) | collective-permute-done | bytes 491552 | tf_op jit(solution)/shard_map/ppermute | solution.py:42
  82.3 2.8 %collective-permute-start.11 = (bf16[640,384]{1,0:T(8,128)(2,1)S(1)}, bf16[640,384]{1,0:T(8,128)(2,1)S(1)}, u32[]{:S(2)}, u32[]{:S(2)}) collective-permute-start(bf16[640,384]{1,0:T(8,128)(2,1)S(1)} %get-tuple-element.39), channel_id=1, source_target_pairs={{0,16},{8,24},{16,0},{24,8},{32,48},{40,56},{48,32},{56,40},{64,80... | collective-permute-start | bytes 1474568 | tf_op jit(solution)/shard_map/ppermute | solution.py:42
  85.8 1.2 fusion.47
  87.8 3.8 %collective-permute-done.11.refs_5_ = bf16[640,384]{1,0:T(8,128)(2,1)S(1)} collective-permute-done((bf16[640,384]{1,0:T(8,128)(2,1)S(1)}, bf16[640,384]{1,0:T(8,128)(2,1)S(1)}, u32[]{:S(2)}, u32[]{:S(2)}) %collective-permute-start.11) | collective-permute-done | bytes 491552 | tf_op jit(solution)/shard_map/ppermute | solution.py:42
  91.6 3.6 %collective-permute-done.9.refs_4_ = bf16[640,384]{1,0:T(8,128)(2,1)S(1)} collective-permute-done((bf16[640,384]{1,0:T(8,128)(2,1)S(1)}, bf16[640,384]{1,0:T(8,128)(2,1)S(1)}, u32[]{:S(2)}, u32[]{:S(2)}) %collective-permute-start.9) | collective-permute-done | bytes 491552 | tf_op jit(solution)/shard_map/ppermute | solution.py:42
  96.0 4.7 %local_part.1 = (f32[1024,128]{1,0:T(8,128)}, f32[1024,128]{1,0:T(8,128)}, f32[26,8,128]{2,1,0:T(8,128)}) custom-call(s32[6]{0:T(128)} %stack.51.refs_0_.where_ref, f32[3,3,8192]{2,1,0:T(4,128)} %taps_ref.1, f32[16,8192]{1,0:T(8,128)} %rates_ref.1, bf16[640,384]{1,0:T(8,128)(2,1)} %get-tuple-element.42.refs_3_, bf16[640,384]{1,0:T(8,128)(2,1)} %copy-done.5, ...), custom_call_target="tpu_custom_call" | custom-call | tf_op jit(solution)/shard_map/local_part/pallas_call | solution.py:304
  100.7 6.0 %collective-permute-start.22 = (bf16[1024,512]{1,0:T(8,128)(2,1)S(1)}, bf16[1024,512]{1,0:T(8,128)(2,1)S(1)}, u32[]{:S(2)}, u32[]{:S(2)}) collective-permute-start(bf16[1024,512]{1,0:T(8,128)(2,1)S(1)} %copy-done.3), channel_id=1, source_target_pairs={{0,8},{8,0},{16,24},{24,16},{32,40},{40,32},{48,56},{56,48},{64,72... | collective-permute-start | bytes 3145736 | tf_op jit(solution)/shard_map/ppermute | solution.py:42
  106.8 2.4 %collective-permute-done.21.theirs_ref = f32[26,8,128]{2,1,0:T(8,128)S(1)} collective-permute-done((f32[26,8,128]{2,1,0:T(8,128)}, f32[26,8,128]{2,1,0:T(8,128)S(1)}, u32[]{:S(2)}, u32[]{:S(2)}) %collective-permute-start.21) | collective-permute-done | bytes 106528 | tf_op jit(solution)/shard_map/ppermute | solution.py:42
  109.8 4.9 %filtered.1 = bf16[1024,128]{1,0:T(8,128)(2,1)} custom-call(s32[6]{0:T(128)} %stack.51.refs_0_.where_ref, f32[3,3,8192]{2,1,0:T(4,128)} %taps_ref.1, f32[16,8192]{1,0:T(8,128)} %rates_ref.1, f32[16,8192]{1,0:T(8,128)} %weights_ref.1, f32[1,8192]{1,0:T(1,128)} %bitcast.43, f32[26,8,128]{2,1,0:T(8,128)} %get-tuple-element.33.mine_ref, ...), custom_call_target="tpu_custom_call" | custom-call | tf_op jit(solution)/shard_map/filtered/pallas_call | solution.py:324
  114.7 1.5 collective-permute-start.23
  116.6 1.6 collective-permute-start.25
  119.3 5.0 %collective-permute-done.23 = bf16[1024,128]{1,0:T(8,128)(2,1)S(1)} collective-permute-done((bf16[1024,128]{1,0:T(8,128)(2,1)}, bf16[1024,128]{1,0:T(8,128)(2,1)S(1)}, u32[]{:S(2)}, u32[]{:S(2)}) %collective-permute-start.23) | collective-permute-done | bytes 262176 | tf_op jit(solution)/shard_map/ppermute | solution.py:42
  124.3 1.7 %collective-permute-start.27 = (bf16[1024,128]{1,0:T(8,128)(2,1)S(1)}, bf16[1024,128]{1,0:T(8,128)(2,1)S(1)}, u32[]{:S(2)}, u32[]{:S(2)}) collective-permute-start(bf16[1024,128]{1,0:T(8,128)(2,1)S(1)} %collective-permute-done.23), channel_id=1, source_target_pairs={{0,96},{8,104},{16,112},{24,120},{32,0},{40,8},{48,16},{56,24},{64... | collective-permute-start | bytes 786440 | tf_op jit(solution)/shard_map/ppermute | solution.py:42
  126.0 1.4 collective-permute-start.29
  127.6 2.8 %collective-permute-done.25 = bf16[1024,128]{1,0:T(8,128)(2,1)S(1)} collective-permute-done((bf16[1024,128]{1,0:T(8,128)(2,1)S(1)}, bf16[1024,128]{1,0:T(8,128)(2,1)S(1)}, u32[]{:S(2)}, u32[]{:S(2)}) %collective-permute-start.25) | collective-permute-done | bytes 262176 | tf_op jit(solution)/shard_map/ppermute | solution.py:42
  130.5 1.3 collective-permute-done.26
  131.9 4.1 %collective-permute-done.27 = bf16[1024,128]{1,0:T(8,128)(2,1)S(1)} collective-permute-done((bf16[1024,128]{1,0:T(8,128)(2,1)S(1)}, bf16[1024,128]{1,0:T(8,128)(2,1)S(1)}, u32[]{:S(2)}, u32[]{:S(2)}) %collective-permute-start.27) | collective-permute-done | bytes 262176 | tf_op jit(solution)/shard_map/ppermute | solution.py:42
  136.1 1.3 collective-permute-done.28
  140.5 2.7 %collective-permute-start.31 = (bf16[256,1024]{1,0:T(8,128)(2,1)S(1)}, bf16[256,1024]{1,0:T(8,128)(2,1)S(1)}, u32[]{:S(2)}, u32[]{:S(2)}) collective-permute-start(bf16[256,1024]{1,0:T(8,128)(2,1)S(1)} %convolution_convert_fusion), channel_id=1, source_target_pairs={{0,6},{1,7},{2,0},{3,1},{4,2},{5,3},{6,4},{7,5},{8,14},{9,15},{10,... | collective-permute-start | bytes 1572872 | tf_op jit(solution)/shard_map/ppermute | solution.py:46
  143.2 3.0 %collective-permute-done.32 = bf16[128,1024]{1,0:T(8,128)(2,1)S(1)} collective-permute-done((bf16[128,1024]{1,0:T(8,128)(2,1)S(1)}, bf16[128,1024]{1,0:T(8,128)(2,1)S(1)}, u32[]{:S(2)}, u32[]{:S(2)}) %collective-permute-start.32) | collective-permute-done | bytes 262176 | tf_op jit(solution)/shard_map/ppermute | solution.py:46
  146.7 1.3 collective-permute-start.33
  148.0 6.4 %collective-permute-done.30 = bf16[256,1024]{1,0:T(8,128)(2,1)S(1)} collective-permute-done((bf16[256,1024]{1,0:T(8,128)(2,1)S(1)}, bf16[256,1024]{1,0:T(8,128)(2,1)S(1)}, u32[]{:S(2)}, u32[]{:S(2)}) %collective-permute-start.30) | collective-permute-done | bytes 524320 | tf_op jit(solution)/shard_map/ppermute | solution.py:46
  154.9 1.4 collective-permute-start.34
  156.2 4.4 %collective-permute-done.33 = bf16[128,1024]{1,0:T(8,128)(2,1)S(1)} collective-permute-done((bf16[128,1024]{1,0:T(8,128)(2,1)S(1)}, bf16[128,1024]{1,0:T(8,128)(2,1)S(1)}, u32[]{:S(2)}, u32[]{:S(2)}) %collective-permute-start.33) | collective-permute-done | bytes 262176 | tf_op jit(solution)/shard_map/ppermute | solution.py:46
  161.3 7.3 %collective-permute-start.35 = (bf16[128,512]{1,0:T(8,128)(2,1)S(1)}, bf16[128,512]{1,0:T(8,128)(2,1)S(1)}, u32[]{:S(2)}, u32[]{:S(2)}) collective-permute-start(bf16[128,512]{1,0:T(8,128)(2,1)S(1)} %get-tuple-element.49), channel_id=1, source_target_pairs={{0,8},{8,0},{16,24},{24,16},{32,40},{40,32},{48,56},{56,48},{64,72... | collective-permute-start | bytes 393224 | tf_op jit(solution)/shard_map/ppermute | solution.py:42
  168.6 1.0 collective-permute-done.35
  (99 shorter events, 23.5 us)
Async XLA Ops:
  1.0 2.5 %collective-permute-start = (bf16[128,512]{1,0:T(8,128)(2,1)S(1)}, bf16[128,512]{1,0:T(8,128)(2,1)S(1)}, u32[]{:S(2)}, u32[]{:S(2)}) collective-permute-start(bf16[128,512]{1,0:T(8,128)(2,1)S(1)} %get-tuple-element.51), channel_id=1, source_target_pairs={{0,8},{8,0},{16,24},{24,16},{32,40},{40,32},{48,56},{56,48},{64,72... | collective-permute-start | bytes 393224 | tf_op jit(solution)/shard_map/ppermute | solution.py:42
  7.1 20.4 %copy-start.1 = (bf16[512,1536]{1,0:T(8,128)(2,1)S(1)}, bf16[512,1536]{1,0:T(8,128)(2,1)}, u32[]{:S(2)}) copy-start(bf16[512,1536]{1,0:T(8,128)(2,1)} %get-tuple-element.24) | copy-start | bytes 4718596
  7.1 17.5 %collective-permute-start.5 = (bf16[512,1536]{1,0:T(8,128)(2,1)}, bf16[512,1536]{1,0:T(8,128)(2,1)S(1)}, u32[]{:S(2)}, u32[]{:S(2)}) collective-permute-start(bf16[512,1536]{1,0:T(8,128)(2,1)} %get-tuple-element.24), channel_id=1, source_target_pairs={{0,8},{8,0},{16,24},{24,16},{32,40},{40,32},{48,56},{56,48},{64,72... | collective-permute-start | bytes 4718600 | tf_op jit(solution)/shard_map/ppermute | solution.py:42
  7.5 13.8 %collective-permute-start.1 = (bf16[128,1024]{1,0:T(8,128)(2,1)S(1)}, bf16[128,1024]{1,0:T(8,128)(2,1)S(1)}, u32[]{:S(2)}, u32[]{:S(2)}) collective-permute-start(bf16[128,1024]{1,0:T(8,128)(2,1)S(1)} %pad_maximum_fusion.3), channel_id=1, source_target_pairs={{0,6},{1,7},{2,0},{3,1},{4,2},{5,3},{6,4},{7,5},{8,14},{9,15},{10,... | collective-permute-start | bytes 786440 | tf_op jit(solution)/shard_map/ppermute | solution.py:46
  10.4 14.3 %collective-permute-start.2 = (bf16[128,1024]{1,0:T(8,128)(2,1)S(1)}, bf16[128,1024]{1,0:T(8,128)(2,1)S(1)}, u32[]{:S(2)}, u32[]{:S(2)}) collective-permute-start(bf16[128,1024]{1,0:T(8,128)(2,1)S(1)} %pad_maximum_fusion.3), channel_id=1, source_target_pairs={{0,2},{1,3},{2,4},{3,5},{4,6},{5,7},{6,0},{7,1},{8,10},{9,11},{10,... | collective-permute-start | bytes 786440 | tf_op jit(solution)/shard_map/ppermute | solution.py:46
  10.4 14.3 %collective-permute-start.3 = (bf16[128,1024]{1,0:T(8,128)(2,1)S(1)}, bf16[128,1024]{1,0:T(8,128)(2,1)S(1)}, u32[]{:S(2)}, u32[]{:S(2)}) collective-permute-start(bf16[128,1024]{1,0:T(8,128)(2,1)S(1)} %pad_maximum_fusion.3), channel_id=1, source_target_pairs={{0,4},{1,5},{2,6},{3,7},{4,0},{5,1},{6,2},{7,3},{8,12},{9,13},{10,... | collective-permute-start | bytes 786440 | tf_op jit(solution)/shard_map/ppermute | solution.py:46
  12.0 12.6 %collective-permute-start.4 = (bf16[128,1024]{1,0:T(8,128)(2,1)S(1)}, bf16[128,1024]{1,0:T(8,128)(2,1)S(1)}, u32[]{:S(2)}, u32[]{:S(2)}) collective-permute-start(bf16[128,1024]{1,0:T(8,128)(2,1)S(1)} %pad_maximum_fusion.3), channel_id=1, source_target_pairs={{0,1},{1,0},{2,3},{3,2},{4,5},{5,4},{6,7},{7,6},{8,9},{9,8},{10,11... | collective-permute-start | bytes 786440 | tf_op jit(solution)/shard_map/ppermute | solution.py:46
  21.4 12.5 %collective-permute-start.6 = (bf16[512,1536]{1,0:T(8,128)(2,1)}, bf16[512,1536]{1,0:T(8,128)(2,1)S(1)}, u32[]{:S(2)}, u32[]{:S(2)}) collective-permute-start(bf16[512,1536]{1,0:T(8,128)(2,1)} %get-tuple-element.30), channel_id=1, source_target_pairs={{0,8},{8,0},{16,24},{24,16},{32,40},{40,32},{48,56},{56,48},{64,72... | collective-permute-start | bytes 4718600 | tf_op jit(solution)/shard_map/ppermute | solution.py:42
  24.6 12.7 %collective-permute-start.12 = (bf16[128,1024]{1,0:T(8,128)(2,1)S(1)}, bf16[128,1024]{1,0:T(8,128)(2,1)S(1)}, u32[]{:S(2)}, u32[]{:S(2)}) collective-permute-start(bf16[128,1024]{1,0:T(8,128)(2,1)S(1)} %collective-permute-done.4), channel_id=1, source_target_pairs={{0,6},{1,7},{2,0},{3,1},{4,2},{5,3},{6,4},{7,5},{8,14},{9,15},{10,... | collective-permute-start | bytes 786440 | tf_op jit(solution)/shard_map/ppermute | solution.py:46
  26.0 11.3 %collective-permute-start.13 = (bf16[128,1024]{1,0:T(8,128)(2,1)S(1)}, bf16[128,1024]{1,0:T(8,128)(2,1)S(1)}, u32[]{:S(2)}, u32[]{:S(2)}) collective-permute-start(bf16[128,1024]{1,0:T(8,128)(2,1)S(1)} %collective-permute-done.4), channel_id=1, source_target_pairs={{0,2},{1,3},{2,4},{3,5},{4,6},{5,7},{6,0},{7,1},{8,10},{9,11},{10,... | collective-permute-start | bytes 786440 | tf_op jit(solution)/shard_map/ppermute | solution.py:46
  26.2 11.2 %collective-permute-start.14 = (bf16[128,1024]{1,0:T(8,128)(2,1)S(1)}, bf16[128,1024]{1,0:T(8,128)(2,1)S(1)}, u32[]{:S(2)}, u32[]{:S(2)}) collective-permute-start(bf16[128,1024]{1,0:T(8,128)(2,1)S(1)} %collective-permute-done.3), channel_id=1, source_target_pairs={{0,1},{1,0},{2,3},{3,2},{4,5},{5,4},{6,7},{7,6},{8,9},{9,8},{10,11... | collective-permute-start | bytes 786440 | tf_op jit(solution)/shard_map/ppermute | solution.py:46
  28.9 46.7 %collective-permute-start.8 = (bf16[640,768]{1,0:T(8,128)(2,1)S(1)}, bf16[640,768]{1,0:T(8,128)(2,1)S(1)}, u32[]{:S(2)}, u32[]{:S(2)}) collective-permute-start(bf16[640,768]{1,0:T(8,128)(2,1)S(1)} %add_convert_fusion.1), channel_id=1, source_target_pairs={{0,32},{8,40},{16,48},{24,56},{32,64},{40,72},{48,80},{56,88},{64,... | collective-permute-start | bytes 2949128 | tf_op jit(solution)/shard_map/ppermute | solution.py:42
  31.3 1.4 copy-start
  33.9 33.8 %collective-permute-start.7 = (bf16[640,768]{1,0:T(8,128)(2,1)S(1)}, bf16[640,768]{1,0:T(8,128)(2,1)S(1)}, u32[]{:S(2)}, u32[]{:S(2)}) collective-permute-start(bf16[640,768]{1,0:T(8,128)(2,1)S(1)} %add_convert_fusion.2), channel_id=1, source_target_pairs={{0,96},{8,104},{16,112},{24,120},{32,0},{40,8},{48,16},{56,24},{64... | collective-permute-start | bytes 2949128 | tf_op jit(solution)/shard_map/ppermute | solution.py:42
  39.2 14.0 %collective-permute-start.15 = (bf16[384,768]{1,0:T(8,128)(2,1)S(1)}, bf16[384,768]{1,0:T(8,128)(2,1)S(1)}, u32[]{:S(2)}, u32[]{:S(2)}) collective-permute-start(bf16[384,768]{1,0:T(8,128)(2,1)S(1)} %fusion.1), channel_id=1, source_target_pairs={{0,16},{8,24},{16,0},{24,8},{32,48},{40,56},{48,32},{56,40},{64,80... | collective-permute-start | bytes 1769480 | tf_op jit(solution)/shard_map/ppermute | solution.py:42
  43.6 22.3 %collective-permute-start.16 = (bf16[384,768]{1,0:T(8,128)(2,1)S(1)}, bf16[384,768]{1,0:T(8,128)(2,1)S(1)}, u32[]{:S(2)}, u32[]{:S(2)}) collective-permute-start(bf16[384,768]{1,0:T(8,128)(2,1)S(1)} %fusion.2), channel_id=1, source_target_pairs={{0,16},{8,24},{16,0},{24,8},{32,48},{40,56},{48,32},{56,40},{64,80... | collective-permute-start | bytes 1769480 | tf_op jit(solution)/shard_map/ppermute | solution.py:42
  66.0 5.6 %collective-permute-start.17 = (bf16[2,192,384]{2,1,0:T(8,128)(2,1)S(1)}, bf16[2,192,384]{2,1,0:T(8,128)(2,1)S(1)}, u32[]{:S(2)}, u32[]{:S(2)}) collective-permute-start(bf16[2,192,384]{2,1,0:T(8,128)(2,1)S(1)} %pad_maximum_fusion), channel_id=1, source_target_pairs={{0,96},{8,104},{16,112},{24,120},{32,0},{40,8},{48,16},{56,24},{64... | collective-permute-start | bytes 884744 | tf_op jit(solution)/shard_map/ppermute | solution.py:42
  67.3 7.5 %collective-permute-start.18 = (bf16[2,192,384]{2,1,0:T(8,128)(2,1)S(1)}, bf16[2,192,384]{2,1,0:T(8,128)(2,1)S(1)}, u32[]{:S(2)}, u32[]{:S(2)}) collective-permute-start(bf16[2,192,384]{2,1,0:T(8,128)(2,1)S(1)} %pad_maximum_fusion.1), channel_id=1, source_target_pairs={{0,32},{8,40},{16,48},{24,56},{32,64},{40,72},{48,80},{56,88},{64,... | collective-permute-start | bytes 884744 | tf_op jit(solution)/shard_map/ppermute | solution.py:42
  68.8 13.2 %collective-permute-start.10 = (bf16[640,384]{1,0:T(8,128)(2,1)S(1)}, bf16[640,384]{1,0:T(8,128)(2,1)S(1)}, u32[]{:S(2)}, u32[]{:S(2)}) collective-permute-start(bf16[640,384]{1,0:T(8,128)(2,1)S(1)} %get-tuple-element.41), channel_id=1, source_target_pairs={{0,96},{8,104},{16,112},{24,120},{32,0},{40,8},{48,16},{56,24},{64... | collective-permute-start | bytes 1474568 | tf_op jit(solution)/shard_map/ppermute | solution.py:42
  72.4 13.4 %collective-permute-start.20 = (bf16[192,384]{1,0:T(8,128)(2,1)}, bf16[192,384]{1,0:T(8,128)(2,1)}, u32[]{:S(2)}, u32[]{:S(2)}) collective-permute-start(bf16[192,384]{1,0:T(8,128)(2,1)} %fusion.42), channel_id=1, source_target_pairs={{0,96},{8,104},{16,112},{24,120},{32,0},{40,8},{48,16},{56,24},{64... | collective-permute-start | bytes 442376 | tf_op jit(solution)/shard_map/ppermute | solution.py:42
  74.8 7.5 %copy-start.6 = (bf16[2,192,384]{2,1,0:T(8,128)(2,1)}, bf16[2,192,384]{2,1,0:T(8,128)(2,1)S(1)}, u32[]{:S(2)}) copy-start(bf16[2,192,384]{2,1,0:T(8,128)(2,1)S(1)} %collective-permute-done.18) | copy-start | bytes 884740
  75.6 10.2 %collective-permute-start.19 = (bf16[192,384]{1,0:T(8,128)(2,1)}, bf16[192,384]{1,0:T(8,128)(2,1)}, u32[]{:S(2)}, u32[]{:S(2)}) collective-permute-start(bf16[192,384]{1,0:T(8,128)(2,1)} %fusion.45), channel_id=1, source_target_pairs={{0,32},{8,40},{16,48},{24,56},{32,64},{40,72},{48,80},{56,88},{64,... | collective-permute-start | bytes 442376 | tf_op jit(solution)/shard_map/ppermute | solution.py:42
  82.3 9.3 %collective-permute-start.11 = (bf16[640,384]{1,0:T(8,128)(2,1)S(1)}, bf16[640,384]{1,0:T(8,128)(2,1)S(1)}, u32[]{:S(2)}, u32[]{:S(2)}) collective-permute-start(bf16[640,384]{1,0:T(8,128)(2,1)S(1)} %get-tuple-element.39), channel_id=1, source_target_pairs={{0,16},{8,24},{16,0},{24,8},{32,48},{40,56},{48,32},{56,40},{64,80... | collective-permute-start | bytes 1474568 | tf_op jit(solution)/shard_map/ppermute | solution.py:42
  85.1 10.0 %collective-permute-start.9 = (bf16[640,384]{1,0:T(8,128)(2,1)S(1)}, bf16[640,384]{1,0:T(8,128)(2,1)S(1)}, u32[]{:S(2)}, u32[]{:S(2)}) collective-permute-start(bf16[640,384]{1,0:T(8,128)(2,1)S(1)} %get-tuple-element.40), channel_id=1, source_target_pairs={{0,32},{8,40},{16,48},{24,56},{32,64},{40,72},{48,80},{56,88},{64,... | collective-permute-start | bytes 1474568 | tf_op jit(solution)/shard_map/ppermute | solution.py:42
  87.0 13.7 %copy-start.3 = (bf16[1024,512]{1,0:T(8,128)(2,1)S(1)}, bf16[1024,512]{1,0:T(8,128)(2,1)}, u32[]{:S(2)}) copy-start(bf16[1024,512]{1,0:T(8,128)(2,1)} %param.13) | copy-start | bytes 3145732
  91.6 3.6 %copy-start.4 = (bf16[640,384]{1,0:T(8,128)(2,1)}, bf16[640,384]{1,0:T(8,128)(2,1)S(1)}, u32[]{:S(2)}) copy-start(bf16[640,384]{1,0:T(8,128)(2,1)S(1)} %collective-permute-done.11.refs_5_) | copy-start | bytes 1474564
  95.2 0.8 copy-start.5
  100.7 14.0 %collective-permute-start.22 = (bf16[1024,512]{1,0:T(8,128)(2,1)S(1)}, bf16[1024,512]{1,0:T(8,128)(2,1)S(1)}, u32[]{:S(2)}, u32[]{:S(2)}) collective-permute-start(bf16[1024,512]{1,0:T(8,128)(2,1)S(1)} %copy-done.3), channel_id=1, source_target_pairs={{0,8},{8,0},{16,24},{24,16},{32,40},{40,32},{48,56},{56,48},{64,72... | collective-permute-start | bytes 3145736 | tf_op jit(solution)/shard_map/ppermute | solution.py:42
  106.7 2.5 %collective-permute-start.21 = (f32[26,8,128]{2,1,0:T(8,128)}, f32[26,8,128]{2,1,0:T(8,128)S(1)}, u32[]{:S(2)}, u32[]{:S(2)}) collective-permute-start(f32[26,8,128]{2,1,0:T(8,128)} %get-tuple-element.33.mine_ref), channel_id=1, source_target_pairs={{0,8},{8,0},{16,24},{24,16},{32,40},{40,32},{48,56},{56,48},{64,72... | collective-permute-start | bytes 319496 | tf_op jit(solution)/shard_map/ppermute | solution.py:42
  109.2 0.7 copy-start.7
  114.7 1.9 %copy-start.2 = (bf16[1024,128]{1,0:T(8,128)(2,1)S(1)}, bf16[1024,128]{1,0:T(8,128)(2,1)}, u32[]{:S(2)}) copy-start(bf16[1024,128]{1,0:T(8,128)(2,1)} %filtered.1) | copy-start | bytes 786436
  114.7 9.6 %collective-permute-start.23 = (bf16[1024,128]{1,0:T(8,128)(2,1)}, bf16[1024,128]{1,0:T(8,128)(2,1)S(1)}, u32[]{:S(2)}, u32[]{:S(2)}) collective-permute-start(bf16[1024,128]{1,0:T(8,128)(2,1)} %filtered.1), channel_id=1, source_target_pairs={{0,16},{8,24},{16,0},{24,8},{32,48},{40,56},{48,32},{56,40},{64,80... | collective-permute-start | bytes 786440 | tf_op jit(solution)/shard_map/ppermute | solution.py:42
  116.2 9.8 %collective-permute-start.24 = (bf16[1024,128]{1,0:T(8,128)(2,1)}, bf16[1024,128]{1,0:T(8,128)(2,1)S(1)}, u32[]{:S(2)}, u32[]{:S(2)}) collective-permute-start(bf16[1024,128]{1,0:T(8,128)(2,1)} %filtered.1), channel_id=1, source_target_pairs={{0,64},{8,72},{16,80},{24,88},{32,96},{40,104},{48,112},{56,120},{... | collective-permute-start | bytes 786440 | tf_op jit(solution)/shard_map/ppermute | solution.py:42
  116.6 13.8 %collective-permute-start.25 = (bf16[1024,128]{1,0:T(8,128)(2,1)S(1)}, bf16[1024,128]{1,0:T(8,128)(2,1)S(1)}, u32[]{:S(2)}, u32[]{:S(2)}) collective-permute-start(bf16[1024,128]{1,0:T(8,128)(2,1)S(1)} %copy-done.2), channel_id=1, source_target_pairs={{0,96},{8,104},{16,112},{24,120},{32,0},{40,8},{48,16},{56,24},{64... | collective-permute-start | bytes 786440 | tf_op jit(solution)/shard_map/ppermute | solution.py:42
  118.2 13.6 %collective-permute-start.26 = (bf16[1024,128]{1,0:T(8,128)(2,1)S(1)}, bf16[1024,128]{1,0:T(8,128)(2,1)S(1)}, u32[]{:S(2)}, u32[]{:S(2)}) collective-permute-start(bf16[1024,128]{1,0:T(8,128)(2,1)S(1)} %copy-done.2), channel_id=1, source_target_pairs={{0,32},{8,40},{16,48},{24,56},{32,64},{40,72},{48,80},{56,88},{64,... | collective-permute-start | bytes 786440 | tf_op jit(solution)/shard_map/ppermute | solution.py:42
  124.3 11.7 %collective-permute-start.27 = (bf16[1024,128]{1,0:T(8,128)(2,1)S(1)}, bf16[1024,128]{1,0:T(8,128)(2,1)S(1)}, u32[]{:S(2)}, u32[]{:S(2)}) collective-permute-start(bf16[1024,128]{1,0:T(8,128)(2,1)S(1)} %collective-permute-done.23), channel_id=1, source_target_pairs={{0,96},{8,104},{16,112},{24,120},{32,0},{40,8},{48,16},{56,24},{64... | collective-permute-start | bytes 786440 | tf_op jit(solution)/shard_map/ppermute | solution.py:42
  126.0 11.4 %collective-permute-start.28 = (bf16[1024,128]{1,0:T(8,128)(2,1)S(1)}, bf16[1024,128]{1,0:T(8,128)(2,1)S(1)}, u32[]{:S(2)}, u32[]{:S(2)}) collective-permute-start(bf16[1024,128]{1,0:T(8,128)(2,1)S(1)} %collective-permute-done.23), channel_id=1, source_target_pairs={{0,32},{8,40},{16,48},{24,56},{32,64},{40,72},{48,80},{56,88},{64,... | collective-permute-start | bytes 786440 | tf_op jit(solution)/shard_map/ppermute | solution.py:42
  126.0 11.4 %collective-permute-start.29 = (bf16[1024,128]{1,0:T(8,128)(2,1)S(1)}, bf16[1024,128]{1,0:T(8,128)(2,1)S(1)}, u32[]{:S(2)}, u32[]{:S(2)}) collective-permute-start(bf16[1024,128]{1,0:T(8,128)(2,1)S(1)} %collective-permute-done.24), channel_id=1, source_target_pairs={{0,16},{8,24},{16,0},{24,8},{32,48},{40,56},{48,32},{56,40},{64,80... | collective-permute-start | bytes 786440 | tf_op jit(solution)/shard_map/ppermute | solution.py:42
  138.8 7.5 %collective-permute-start.32 = (bf16[128,1024]{1,0:T(8,128)(2,1)S(1)}, bf16[128,1024]{1,0:T(8,128)(2,1)S(1)}, u32[]{:S(2)}, u32[]{:S(2)}) collective-permute-start(bf16[128,1024]{1,0:T(8,128)(2,1)S(1)} %convolution_convert_fusion.2), channel_id=1, source_target_pairs={{0,1},{1,0},{2,3},{3,2},{4,5},{5,4},{6,7},{7,6},{8,9},{9,8},{10,11... | collective-permute-start | bytes 786440 | tf_op jit(solution)/shard_map/ppermute | solution.py:46
  140.4 14.0 %collective-permute-start.30 = (bf16[256,1024]{1,0:T(8,128)(2,1)S(1)}, bf16[256,1024]{1,0:T(8,128)(2,1)S(1)}, u32[]{:S(2)}, u32[]{:S(2)}) collective-permute-start(bf16[256,1024]{1,0:T(8,128)(2,1)S(1)} %convolution_convert_fusion.1), channel_id=1, source_target_pairs={{0,2},{1,3},{2,4},{3,5},{4,6},{5,7},{6,0},{7,1},{8,10},{9,11},{10,... | collective-permute-start | bytes 1572872 | tf_op jit(solution)/shard_map/ppermute | solution.py:46
  140.5 13.9 %collective-permute-start.31 = (bf16[256,1024]{1,0:T(8,128)(2,1)S(1)}, bf16[256,1024]{1,0:T(8,128)(2,1)S(1)}, u32[]{:S(2)}, u32[]{:S(2)}) collective-permute-start(bf16[256,1024]{1,0:T(8,128)(2,1)S(1)} %convolution_convert_fusion), channel_id=1, source_target_pairs={{0,6},{1,7},{2,0},{3,1},{4,2},{5,3},{6,4},{7,5},{8,14},{9,15},{10,... | collective-permute-start | bytes 1572872 | tf_op jit(solution)/shard_map/ppermute | solution.py:46
  146.7 13.9 %collective-permute-start.33 = (bf16[128,1024]{1,0:T(8,128)(2,1)S(1)}, bf16[128,1024]{1,0:T(8,128)(2,1)S(1)}, u32[]{:S(2)}, u32[]{:S(2)}) collective-permute-start(bf16[128,1024]{1,0:T(8,128)(2,1)S(1)} %fusion.11), channel_id=1, source_target_pairs={{0,4},{1,5},{2,6},{3,7},{4,0},{5,1},{6,2},{7,3},{8,12},{9,13},{10,... | collective-permute-start | bytes 786440 | tf_op jit(solution)/shard_map/ppermute | solution.py:46
  154.9 5.7 %collective-permute-start.34 = (bf16[128,1024]{1,0:T(8,128)(2,1)S(1)}, bf16[128,1024]{1,0:T(8,128)(2,1)S(1)}, u32[]{:S(2)}, u32[]{:S(2)}) collective-permute-start(bf16[128,1024]{1,0:T(8,128)(2,1)S(1)} %fusion.10), channel_id=1, source_target_pairs={{0,1},{1,0},{2,3},{3,2},{4,5},{5,4},{6,7},{7,6},{8,9},{9,8},{10,11... | collective-permute-start | bytes 786440 | tf_op jit(solution)/shard_map/ppermute | solution.py:46
  161.3 8.3 %collective-permute-start.35 = (bf16[128,512]{1,0:T(8,128)(2,1)S(1)}, bf16[128,512]{1,0:T(8,128)(2,1)S(1)}, u32[]{:S(2)}, u32[]{:S(2)}) collective-permute-start(bf16[128,512]{1,0:T(8,128)(2,1)S(1)} %get-tuple-element.49), channel_id=1, source_target_pairs={{0,8},{8,0},{16,24},{24,16},{32,40},{40,32},{48,56},{56,48},{64,72... | collective-permute-start | bytes 393224 | tf_op jit(solution)/shard_map/ppermute | solution.py:42

commit v4 on v3

--- a/solution.py
+++ b/solution.py
@@ -65,32 +65,33 @@
 TARGETS = [(2, 0), (1, 1), (2, 1), (3, 0), (1, 0), (0, 0), (0, 1), (3, 1)]
 
 
-def reorder_kernel(in_ref, *refs):
+def reorder_kernel(parts, in_ref, *refs):
     out_refs, sems = refs[:-1], refs[-1]
     chip = lax.axis_index("tok") >> 1
     size = in_ref.shape[1] // len(TARGETS)
-    each = len(TARGETS) // len(out_refs)
     copies = []
-    for k, (dz, dx) in enumerate(TARGETS):
-        target = (((chip >> 1) + dz) & (Z - 1)) * XH + ((chip + dx) & (XH - 1))
-        source = pl.ds(pl.multiple_of(target * size, size), size)
-        place = pl.ds(k % each * size, size)
-        copies.append(
-            pltpu.make_async_copy(in_ref.at[:, source], out_refs[k // each].at[:, place], sems.at[k])
-        )
-        copies[-1].start()
+    for targets, out_ref in zip(parts, out_refs):
+        for k, (dz, dx) in enumerate(targets):
+            target = (((chip >> 1) + dz) & (Z - 1)) * XH + ((chip + dx) & (XH - 1))
+            source = pl.ds(pl.multiple_of(target * size, size), size)
+            place = pl.ds(k * size, size)
+            sem = sems.at[len(copies)]
+            copies.append(pltpu.make_async_copy(in_ref.at[:, source], out_ref.at[:, place], sem))
+            copies[-1].start()
     for copy in copies:
         copy.wait()
 
 
-def by_target(weight, parts):
-    shape = jax.ShapeDtypeStruct((weight.shape[0], weight.shape[1] // parts), weight.dtype)
+def by_target(weight, *parts):
+    width = weight.shape[1] // len(TARGETS)
     return pl.pallas_call(
-        reorder_kernel,
-        out_shape=[shape] * parts,
+        lambda *refs: reorder_kernel(parts, *refs),
+        out_shape=[
+            jax.ShapeDtypeStruct((weight.shape[0], width * len(targets)), weight.dtype) for targets in parts
+        ],
         in_specs=[pl.BlockSpec(memory_space=pl.ANY)],
-        out_specs=[pl.BlockSpec(memory_space=pltpu.VMEM)] * parts,
-        scratch_shapes=[pltpu.SemaphoreType.DMA((len(TARGETS),))],
+        out_specs=[pl.BlockSpec(memory_space=pltpu.VMEM)] * len(parts),
+        scratch_shapes=[pltpu.SemaphoreType.DMA((sum(len(targets) for targets in parts),))],
         name="by_target",
     )(weight)
 
@@ -98,7 +99,7 @@
 def product(rows, weights, first, last):
     own, other = weights
     depth, cols = own[0].shape
-    each = len(TARGETS) // len(own)
+    each = len(TARGETS) // 2
     width = cols // each
     outs = []
     for part in range(len(own)):
@@ -117,25 +118,27 @@
     return [value[:, k * width : (k + 1) * width] for k in range(count)]
 
 
-def reduce_ring_first(rows, weights):
-    up = tok_send(product(rows, weights, 0, 2), Z_UP)
-    down = tok_send(product(rows, weights, 2, 4), Z_DOWN)
+def reduce_groups(rows, leaving, late_rows, weights):
+    up, down = tok_send(leaving[0], Z_UP), tok_send(leaving[1], Z_DOWN)
+    rows, late_rows = lax.optimization_barrier((rows, late_rows))
     near_up, near, far, far_down = split(product(rows, weights, 4, 8), 4)
+
+    far1, far2 = split(tok_send(product(late_rows, weights, 1, 3), X_SWAP), 2)
+    far0, far3 = split(tok_send(product(late_rows, weights, 6, 8), X_SWAP), 2)
+    near2 = product(late_rows, weights, 0, 1)
+    near3 = product(late_rows, weights, 3, 4)
+    near1, near0 = split(product(late_rows, weights, 4, 6), 2)
     near_in, far_in = split(up, 2)
     far_more, near_more = split(down, 2)
+    far_down = tok_send(add(far_down, far_more), Z_DOWN)
     near_up = tok_send(add(near_up, near_in), Z_UP)
-    far_down = tok_send(add(far_down, far_more), Z_DOWN)
-    across = tok_send(add(far, far_in, far_down), X_SWAP)
-    return [add(near, near_more), near_up, across]
-
-
-def reduce_pair_first(rows, weights):
-    far1, far2 = split(tok_send(product(rows, weights, 1, 3), X_SWAP), 2)
-    far0, far3 = split(tok_send(product(rows, weights, 6, 8), X_SWAP), 2)
-    near2 = product(rows, weights, 0, 1)
-    near3 = product(rows, weights, 3, 4)
-    near1, near0 = split(product(rows, weights, 4, 6), 2)
-    half = rows.shape[0] // 2
+    near_up, far_down, near0, near1, near2, near3 = lax.optimization_barrier(
+        (near_up, far_down, near0, near1, near2, near3)
+    )
+    crossed = tok_send(add(far, far_in, far_down), X_SWAP)
+    terms = [add(near, near_more), near_up, crossed]
+
+    half = late_rows.shape[0] // 2
     first, second = slice(0, half), slice(half, None)
 
     def both(near, far, side):
@@ -145,7 +148,7 @@
     down = tok_send(jnp.stack([both(near2, far2, second), both(near3, far3, first)]).astype(BF), Z_DOWN)
     from_below = tok_send((both(near1, far1, first) + up[0].astype(F32)).astype(BF), Z_UP)
     from_above = tok_send((both(near3, far3, second) + down[0].astype(F32)).astype(BF), Z_DOWN)
-    return [
+    late_terms = [
         jnp.concatenate(
             [
                 both(near0, far0, first) + down[1].astype(F32) + from_below.astype(F32),
@@ -153,6 +156,7 @@
             ]
         ).astype(BF)
     ]
+    return [terms, late_terms]
 
 
 def features(block):
@@ -345,9 +349,10 @@
     length = activations.shape[0] // CORES
 
     kept = lax.dynamic_slice_in_dim(activations, core * length, length, 0)
-    other = swap(lax.dynamic_slice_in_dim(activations, (1 - core) * length, length, 0))
+    other = lax.dynamic_slice_in_dim(activations, (1 - core) * length, length, 0)
+    other, proj_weight = lax.optimization_barrier((other, proj_weight))
+    other = swap(other)
     mine = jnp.concatenate([kept, other], axis=1)
-    mine, proj_weight = lax.optimization_barrier((mine, proj_weight))
 
     def along(value, dy):
         return ch_send(value, ch_perm(lambda y, xl: (y - dy, xl)))
@@ -357,15 +362,16 @@
 
     blocks = [[(0, 0), (1, 0), (3, 0), (2, 0), (0, 1)], [(1, 1), (3, 1), (2, 1)]]
     first = [mine, along(mine, 1), along(mine, 3), along(mine, 2), across(mine)]
-    ordered = by_target(proj_weight, 2)
-    early, late = swap(ordered[0]), swap(ordered[1])
-    first, early = lax.optimization_barrier((first, early))
+    half = len(TARGETS) // 2
+    early, late = by_target(proj_weight, TARGETS[:half], TARGETS[half:])
+    early, late = (early, swap(early)), (late, swap(late))
+    first[4], first[1], first[2], early = lax.optimization_barrier((first[4], first[1], first[2], early))
     second = [along(first[4], 1), along(first[4], 3), across(first[3])]
-    weights = (ordered, [early, late])
-    groups = [
-        reduce_ring_first(jnp.concatenate(first), weights),
-        reduce_pair_first(jnp.concatenate(second), weights),
-    ]
+    weights = list(zip(early, late))
+    rows = jnp.concatenate(first)
+    leaving = product(rows, weights, 0, 2), product(rows, weights, 2, 4)
+    groups = reduce_groups(rows, leaving, jnp.concatenate(second), weights)
+    groups, out_weight = lax.optimization_barrier((groups, out_weight))
     query, gate, edges = local_part(where, short_taps, decay_rates, groups, blocks)
     edges, out_weight = lax.optimization_barrier((edges, out_weight))
     their_edges = swap(edges)
@@ -394,14 +400,12 @@
         return ch_send(value, ch_perm(lambda y, xl: (y + dy, xl)))
 
     far = across(part((2, 1), (2, 1)).astype(BF))
-    up = forward(part((1, 0), (1, 1)).astype(BF), 1)
-    down = forward(part((3, 0), (3, 1)).astype(BF), 3)
+    up, down = [forward(part((dy, 1), (dy, 1)).astype(BF), dy) for dy in (1, 3)]
+    near_up, near_down = [forward(part((dy, 0), (dy, 0)).astype(BF), dy) for dy in (1, 3)]
     opposite = forward((part((2, 0), (2, 0)) + far.astype(F32)).astype(BF), 2)
-    beside = across(
-        (part((0, 1), (0, 1)) + up[length:].astype(F32) + down[length:].astype(F32)).astype(BF)
-    )
+    beside = across((part((0, 1), (0, 1)) + up.astype(F32) + down.astype(F32)).astype(BF))
     total = part((0, 0), (0, 0))
-    for term in (up[:length], down[:length], opposite, beside):
+    for term in (near_up, near_down, opposite, beside):
         total = total + term.astype(F32)
     total = total.astype(BF)
     cols = out_weight.shape[1]

time: 171 us -> 164 us (0.959)
  waiting for transfers between devices: 78.2 us -> 67.6 us
  starting transfers between devices: 54.7 us -> 60.9 us
  other arithmetic: 5.85 us -> 3.53 us
    ppermute x24, waiting for transfers between devices: 54 us -> 46.6 us  [tok_send(): return lax.ppermute(value, 'tok', perm)]
    ppermute x24, starting transfers between devices: 39.9 us -> 44.5 us  [tok_send(): return lax.ppermute(value, 'tok', perm)]
    ppermute x12 -> x14, waiting for transfers between devices: 24.2 us -> 21 us  [ch_send(): return lax.ppermute(value, 'ch', perm)]
    ppermute x12 -> x14, starting transfers between devices: 14.7 us -> 16.5 us  [ch_send(): return lax.ppermute(value, 'ch', perm)]
    dot_general x6 -> x8, matrix products: 3.39 us -> 3.76 us  [part(): return jnp.dot(rows, out_rows, preferred_element_type=F32)]
  transfers between devices with their start and end apart: 36 -> 38, of which waited for: 19 -> 21; matrix products, arithmetic and copies ran while one was open for 11% -> 9% of each run, Pallas kernels for 3% -> 3%
where the time goes in v4:
time: 164 us
  waiting for transfers between devices  67.6 us (41%)
  starting transfers between devices  60.9 us (37%)
  Pallas kernels  13.2 us (8%)
  matrix products  13.1 us (8%)
  local copies, waits for them, and re-layouts  5.19 us (3%)
  other arithmetic  3.53 us (2%)
    ppermute x24, waiting for transfers between devices, tok_send(): return lax.ppermute(value, 'tok', perm)  46.6 us
    ppermute x24, starting transfers between devices, tok_send(): return lax.ppermute(value, 'tok', perm)  44.5 us
    ppermute x14, waiting for transfers between devices, ch_send(): return lax.ppermute(value, 'ch', perm)  21 us
    ppermute x14, starting transfers between devices, ch_send(): return lax.ppermute(value, 'ch', perm)  16.5 us
    pallas_call x1, Pallas kernels, filtered(): pl.pallas_call(filter_kernel, out_shape=jax.ShapeDtypeStruct(gate.shape,...  4.88 us
    pallas_call x1, Pallas kernels, local_part(): pl.pallas_call(lambda *refs: local_kernel(blocks, [len(terms) for terms i...  4.72 us
    dot_general x8, matrix products, product(): jnp.dot(rows[:, depth:], other[part][:, columns], preferred_element_type=...  4.69 us
    dot_general x8, matrix products, product(): jnp.dot(rows[:, :depth], own[part][:, columns], preferred_element_type=F32)  4.67 us
  transfers between devices with their start and end apart: 38, of which 21 were waited for; matrix products, arithmetic and copies ran while one was open for 9% of the time, Pallas kernels for 3%

profile of v4, /device:TPU:1, one launch (start us, length us, event | category | flops | bytes accessed | tf_op | source)
XLA Modules:
  0.0 164.1 jit_solution(10793695786354444422)
XLA Ops:
  1.0 3.6 %by_target.1 = (bf16[512,1536]{1,0:T(8,128)(2,1)}, bf16[512,1536]{1,0:T(8,128)(2,1)}) custom-call(bf16[512,3072]{1,0:T(8,128)(2,1)} %refs_0_), custom_call_target="tpu_custom_call" | custom-call | tf_op jit(solution)/shard_map/by_target/pallas_call | solution.py:87
  4.6 1.5 collective-permute-start.4
  6.2 3.0 %collective-permute-done = bf16[128,512]{1,0:T(8,128)(2,1)S(1)} collective-permute-done((bf16[128,512]{1,0:T(8,128)(2,1)S(1)}, bf16[128,512]{1,0:T(8,128)(2,1)S(1)}, u32[]{:S(2)}, u32[]{:S(2)}) %collective-permute-start) | collective-permute-done | bytes 131104 | tf_op jit(solution)/shard_map/ppermute | solution.py:42
  9.2 1.4 collective-permute-start.3
  10.7 2.6 %collective-permute-start.5 = (bf16[128,1024]{1,0:T(8,128)(2,1)S(1)}, bf16[128,1024]{1,0:T(8,128)(2,1)S(1)}, u32[]{:S(2)}, u32[]{:S(2)}) collective-permute-start(bf16[128,1024]{1,0:T(8,128)(2,1)S(1)} %get-tuple-element.76), channel_id=1, source_target_pairs={{0,4},{1,5},{2,6},{3,7},{4,0},{5,1},{6,2},{7,3},{8,12},{9,13},{10,... | collective-permute-start | bytes 786440 | tf_op jit(solution)/shard_map/ppermute | solution.py:46
  13.3 1.1 collective-permute-start.2
  14.4 1.2 collective-permute-start.1
  15.6 3.0 %collective-permute-done.3 = bf16[128,1024]{1,0:T(8,128)(2,1)S(1)} collective-permute-done((bf16[128,1024]{1,0:T(8,128)(2,1)S(1)}, bf16[128,1024]{1,0:T(8,128)(2,1)S(1)}, u32[]{:S(2)}, u32[]{:S(2)}) %collective-permute-start.3) | collective-permute-done | bytes 262176 | tf_op jit(solution)/shard_map/ppermute | solution.py:46
  19.4 5.8 %collective-permute-done.5 = bf16[128,1024]{1,0:T(8,128)(2,1)S(1)} collective-permute-done((bf16[128,1024]{1,0:T(8,128)(2,1)S(1)}, bf16[128,1024]{1,0:T(8,128)(2,1)S(1)}, u32[]{:S(2)}, u32[]{:S(2)}) %collective-permute-start.5) | collective-permute-done | bytes 262176 | tf_op jit(solution)/shard_map/ppermute | solution.py:46
  25.2 1.2 collective-permute-start.8
  26.5 2.7 %collective-permute-start.6 = (bf16[128,1024]{1,0:T(8,128)(2,1)S(1)}, bf16[128,1024]{1,0:T(8,128)(2,1)S(1)}, u32[]{:S(2)}, u32[]{:S(2)}) collective-permute-start(bf16[128,1024]{1,0:T(8,128)(2,1)S(1)} %collective-permute-done.1), channel_id=1, source_target_pairs={{0,6},{1,7},{2,0},{3,1},{4,2},{5,3},{6,4},{7,5},{8,14},{9,15},{10,... | collective-permute-start | bytes 786440 | tf_op jit(solution)/shard_map/ppermute | solution.py:46
  32.1 3.8 %collective-permute-start.10 = (bf16[640,768]{1,0:T(8,128)(2,1)S(1)}, bf16[640,768]{1,0:T(8,128)(2,1)S(1)}, u32[]{:S(2)}, u32[]{:S(2)}) collective-permute-start(bf16[640,768]{1,0:T(8,128)(2,1)S(1)} %add_convert_fusion.2), channel_id=1, source_target_pairs={{0,96},{8,104},{16,112},{24,120},{32,0},{40,8},{48,16},{56,24},{64... | collective-permute-start | bytes 2949128 | tf_op jit(solution)/shard_map/ppermute | solution.py:42
  37.7 2.5 %collective-permute-start.16 = (bf16[384,768]{1,0:T(8,128)(2,1)S(1)}, bf16[384,768]{1,0:T(8,128)(2,1)S(1)}, u32[]{:S(2)}, u32[]{:S(2)}) collective-permute-start(bf16[384,768]{1,0:T(8,128)(2,1)S(1)} %fusion.2), channel_id=1, source_target_pairs={{0,16},{8,24},{16,0},{24,8},{32,48},{40,56},{48,32},{56,40},{64,80... | collective-permute-start | bytes 1769480 | tf_op jit(solution)/shard_map/ppermute | solution.py:42
  44.1 1.2 fusion.28
  45.3 1.2 add_convert_fusion
  46.5 8.7 %collective-permute-done.10 = bf16[640,768]{1,0:T(8,128)(2,1)S(1)} collective-permute-done((bf16[640,768]{1,0:T(8,128)(2,1)S(1)}, bf16[640,768]{1,0:T(8,128)(2,1)S(1)}, u32[]{:S(2)}, u32[]{:S(2)}) %collective-permute-start.10) | collective-permute-done | bytes 983072 | tf_op jit(solution)/shard_map/ppermute | solution.py:42
  55.1 3.9 %collective-permute-done.11 = bf16[640,768]{1,0:T(8,128)(2,1)S(1)} collective-permute-done((bf16[640,768]{1,0:T(8,128)(2,1)S(1)}, bf16[640,768]{1,0:T(8,128)(2,1)S(1)}, u32[]{:S(2)}, u32[]{:S(2)}) %collective-permute-start.11) | collective-permute-done | bytes 983072 | tf_op jit(solution)/shard_map/ppermute | solution.py:42
  59.0 1.2 add_convert_fusion.4
  60.3 1.5 collective-permute-start.12
  62.2 7.8 %collective-permute-done.13 = bf16[640,384]{1,0:T(8,128)(2,1)S(1)} collective-permute-done((bf16[640,384]{1,0:T(8,128)(2,1)S(1)}, bf16[640,384]{1,0:T(8,128)(2,1)S(1)}, u32[]{:S(2)}, u32[]{:S(2)}) %collective-permute-start.13) | collective-permute-done | bytes 491552 | tf_op jit(solution)/shard_map/ppermute | solution.py:42
  70.0 1.2 collective-permute-done.12.refs_4_
  71.8 1.2 collective-permute-start.18
  73.1 4.0 %collective-permute-done.17 = bf16[2,192,384]{2,1,0:T(8,128)(2,1)S(1)} collective-permute-done((bf16[2,192,384]{2,1,0:T(8,128)(2,1)S(1)}, bf16[2,192,384]{2,1,0:T(8,128)(2,1)S(1)}, u32[]{:S(2)}, u32[]{:S(2)}) %collective-permute-start.17) | collective-permute-done | bytes 294944 | tf_op jit(solution)/shard_map/ppermute | solution.py:42
  77.1 1.6 collective-permute-start.20
  79.3 2.5 %collective-permute-start.14 = (bf16[640,384]{1,0:T(8,128)(2,1)S(1)}, bf16[640,384]{1,0:T(8,128)(2,1)S(1)}, u32[]{:S(2)}, u32[]{:S(2)}) collective-permute-start(bf16[640,384]{1,0:T(8,128)(2,1)S(1)} %add_convert_fusion.3), channel_id=1, source_target_pairs={{0,16},{8,24},{16,0},{24,8},{32,48},{40,56},{48,32},{56,40},{64,80... | collective-permute-start | bytes 1474568 | tf_op jit(solution)/shard_map/ppermute | solution.py:42
  83.1 1.5 collective-permute-done.19
  85.5 3.0 %collective-permute-done.14.refs_5_ = bf16[640,384]{1,0:T(8,128)(2,1)S(1)} collective-permute-done((bf16[640,384]{1,0:T(8,128)(2,1)S(1)}, bf16[640,384]{1,0:T(8,128)(2,1)S(1)}, u32[]{:S(2)}, u32[]{:S(2)}) %collective-permute-start.14) | collective-permute-done | bytes 491552 | tf_op jit(solution)/shard_map/ppermute | solution.py:42
  89.3 4.7 %local_part.1 = (f32[1024,128]{1,0:T(8,128)}, f32[1024,128]{1,0:T(8,128)}, f32[26,8,128]{2,1,0:T(8,128)}) custom-call(s32[6]{0:T(128)} %stack.51.refs_0_.where_ref, f32[3,3,8192]{2,1,0:T(4,128)} %taps_ref.1, f32[16,8192]{1,0:T(8,128)} %rates_ref.1, bf16[640,384]{1,0:T(8,128)(2,1)} %get-tuple-element.51.refs_3_, bf16[640,384]{1,0:T(8,128)(2,1)} %copy-done.4, ...), custom_call_target="tpu_custom_call" | custom-call | tf_op jit(solution)/shard_map/local_part/pallas_call | solution.py:308
  94.1 8.1 %collective-permute-start.22 = (bf16[1024,512]{1,0:T(8,128)(2,1)S(1)}, bf16[1024,512]{1,0:T(8,128)(2,1)S(1)}, u32[]{:S(2)}, u32[]{:S(2)}) collective-permute-start(bf16[1024,512]{1,0:T(8,128)(2,1)S(1)} %copy-done.3), channel_id=1, source_target_pairs={{0,8},{8,0},{16,24},{24,16},{32,40},{40,32},{48,56},{56,48},{64,72... | collective-permute-start | bytes 3145736 | tf_op jit(solution)/shard_map/ppermute | solution.py:42
  102.2 2.4 %collective-permute-done.21.theirs_ref = f32[26,8,128]{2,1,0:T(8,128)S(1)} collective-permute-done((f32[26,8,128]{2,1,0:T(8,128)}, f32[26,8,128]{2,1,0:T(8,128)S(1)}, u32[]{:S(2)}, u32[]{:S(2)}) %collective-permute-start.21) | collective-permute-done | bytes 106528 | tf_op jit(solution)/shard_map/ppermute | solution.py:42
  105.3 4.9 %filtered.1 = bf16[1024,128]{1,0:T(8,128)(2,1)} custom-call(s32[6]{0:T(128)} %stack.51.refs_0_.where_ref, f32[3,3,8192]{2,1,0:T(4,128)} %taps_ref.1, f32[16,8192]{1,0:T(8,128)} %rates_ref.1, f32[16,8192]{1,0:T(8,128)} %weights_ref.1, f32[1,8192]{1,0:T(1,128)} %bitcast.45, f32[26,8,128]{2,1,0:T(8,128)} %get-tuple-element.57.mine_ref, ...), custom_call_target="tpu_custom_call" | custom-call | tf_op jit(solution)/shard_map/filtered/pallas_call | solution.py:328
  110.6 2.4 %collective-permute-start.23 = (bf16[1024,128]{1,0:T(8,128)(2,1)}, bf16[1024,128]{1,0:T(8,128)(2,1)S(1)}, u32[]{:S(2)}, u32[]{:S(2)}) collective-permute-start(bf16[1024,128]{1,0:T(8,128)(2,1)} %filtered.1), channel_id=1, source_target_pairs={{0,16},{8,24},{16,0},{24,8},{32,48},{40,56},{48,32},{56,40},{64,80... | collective-permute-start | bytes 786440 | tf_op jit(solution)/shard_map/ppermute | solution.py:42
  113.2 1.7 %collective-permute-start.26 = (bf16[1024,128]{1,0:T(8,128)(2,1)S(1)}, bf16[1024,128]{1,0:T(8,128)(2,1)S(1)}, u32[]{:S(2)}, u32[]{:S(2)}) collective-permute-start(bf16[1024,128]{1,0:T(8,128)(2,1)S(1)} %copy-done.2), channel_id=1, source_target_pairs={{0,32},{8,40},{16,48},{24,56},{32,64},{40,72},{48,80},{56,88},{64,... | collective-permute-start | bytes 786440 | tf_op jit(solution)/shard_map/ppermute | solution.py:42
  114.8 1.1 collective-permute-start.25
  116.4 3.4 %collective-permute-done.23 = bf16[1024,128]{1,0:T(8,128)(2,1)S(1)} collective-permute-done((bf16[1024,128]{1,0:T(8,128)(2,1)}, bf16[1024,128]{1,0:T(8,128)(2,1)S(1)}, u32[]{:S(2)}, u32[]{:S(2)}) %collective-permute-start.23) | collective-permute-done | bytes 262176 | tf_op jit(solution)/shard_map/ppermute | solution.py:42
  119.8 1.6 collective-permute-start.28
  121.3 1.1 collective-permute-start.27
  122.4 2.4 %collective-permute-start.29 = (bf16[1024,128]{1,0:T(8,128)(2,1)S(1)}, bf16[1024,128]{1,0:T(8,128)(2,1)S(1)}, u32[]{:S(2)}, u32[]{:S(2)}) collective-permute-start(bf16[1024,128]{1,0:T(8,128)(2,1)S(1)} %collective-permute-done.24), channel_id=1, source_target_pairs={{0,16},{8,24},{16,0},{24,8},{32,48},{40,56},{48,32},{56,40},{64,80... | collective-permute-start | bytes 786440 | tf_op jit(solution)/shard_map/ppermute | solution.py:42
  125.9 3.3 %collective-permute-done.27 = bf16[1024,128]{1,0:T(8,128)(2,1)S(1)} collective-permute-done((bf16[1024,128]{1,0:T(8,128)(2,1)S(1)}, bf16[1024,128]{1,0:T(8,128)(2,1)S(1)}, u32[]{:S(2)}, u32[]{:S(2)}) %collective-permute-start.27) | collective-permute-done | bytes 262176 | tf_op jit(solution)/shard_map/ppermute | solution.py:42
  129.3 2.2 %collective-permute-done.28 = bf16[1024,128]{1,0:T(8,128)(2,1)S(1)} collective-permute-done((bf16[1024,128]{1,0:T(8,128)(2,1)S(1)}, bf16[1024,128]{1,0:T(8,128)(2,1)S(1)}, u32[]{:S(2)}, u32[]{:S(2)}) %collective-permute-start.28) | collective-permute-done | bytes 262176 | tf_op jit(solution)/shard_map/ppermute | solution.py:42
  133.6 2.7 %collective-permute-start.31 = (bf16[128,1024]{1,0:T(8,128)(2,1)S(1)}, bf16[128,1024]{1,0:T(8,128)(2,1)S(1)}, u32[]{:S(2)}, u32[]{:S(2)}) collective-permute-start(bf16[128,1024]{1,0:T(8,128)(2,1)S(1)} %convolution_convert_fusion.3), channel_id=1, source_target_pairs={{0,6},{1,7},{2,0},{3,1},{4,2},{5,3},{6,4},{7,5},{8,14},{9,15},{10,... | collective-permute-start | bytes 786440 | tf_op jit(solution)/shard_map/ppermute | solution.py:46
  137.0 2.7 %collective-permute-start.35 = (bf16[128,1024]{1,0:T(8,128)(2,1)S(1)}, bf16[128,1024]{1,0:T(8,128)(2,1)S(1)}, u32[]{:S(2)}, u32[]{:S(2)}) collective-permute-start(bf16[128,1024]{1,0:T(8,128)(2,1)S(1)} %convolution_convert_fusion), channel_id=1, source_target_pairs={{0,6},{1,7},{2,0},{3,1},{4,2},{5,3},{6,4},{7,5},{8,14},{9,15},{10,... | collective-permute-start | bytes 786440 | tf_op jit(solution)/shard_map/ppermute | solution.py:46
  139.7 2.7 %collective-permute-done.32 = bf16[128,1024]{1,0:T(8,128)(2,1)S(1)} collective-permute-done((bf16[128,1024]{1,0:T(8,128)(2,1)S(1)}, bf16[128,1024]{1,0:T(8,128)(2,1)S(1)}, u32[]{:S(2)}, u32[]{:S(2)}) %collective-permute-start.32) | collective-permute-done | bytes 262176 | tf_op jit(solution)/shard_map/ppermute | solution.py:46
  142.9 4.2 %collective-permute-done.34 = bf16[128,1024]{1,0:T(8,128)(2,1)S(1)} collective-permute-done((bf16[128,1024]{1,0:T(8,128)(2,1)S(1)}, bf16[128,1024]{1,0:T(8,128)(2,1)S(1)}, u32[]{:S(2)}, u32[]{:S(2)}) %collective-permute-start.34) | collective-permute-done | bytes 262176 | tf_op jit(solution)/shard_map/ppermute | solution.py:46
  147.9 2.3 %collective-permute-done.33 = bf16[128,1024]{1,0:T(8,128)(2,1)S(1)} collective-permute-done((bf16[128,1024]{1,0:T(8,128)(2,1)S(1)}, bf16[128,1024]{1,0:T(8,128)(2,1)S(1)}, u32[]{:S(2)}, u32[]{:S(2)}) %collective-permute-start.33) | collective-permute-done | bytes 262176 | tf_op jit(solution)/shard_map/ppermute | solution.py:46
  150.3 2.9 %collective-permute-done.36 = bf16[128,1024]{1,0:T(8,128)(2,1)S(1)} collective-permute-done((bf16[128,1024]{1,0:T(8,128)(2,1)S(1)}, bf16[128,1024]{1,0:T(8,128)(2,1)S(1)}, u32[]{:S(2)}, u32[]{:S(2)}) %collective-permute-start.36) | collective-permute-done | bytes 262176 | tf_op jit(solution)/shard_map/ppermute | solution.py:46
  153.8 8.6 %collective-permute-start.37 = (bf16[128,512]{1,0:T(8,128)(2,1)S(1)}, bf16[128,512]{1,0:T(8,128)(2,1)S(1)}, u32[]{:S(2)}, u32[]{:S(2)}) collective-permute-start(bf16[128,512]{1,0:T(8,128)(2,1)S(1)} %get-tuple-element.74), channel_id=1, source_target_pairs={{0,8},{8,0},{16,24},{24,16},{32,40},{40,32},{48,56},{56,48},{64,72... | collective-permute-start | bytes 393224 | tf_op jit(solution)/shard_map/ppermute | solution.py:42
  162.4 1.0 collective-permute-done.37
  (101 shorter events, 23.3 us)
Async XLA Ops:
  4.6 21.9 %collective-permute-start.4 = (bf16[512,1536]{1,0:T(8,128)(2,1)}, bf16[512,1536]{1,0:T(8,128)(2,1)S(1)}, u32[]{:S(2)}, u32[]{:S(2)}) collective-permute-start(bf16[512,1536]{1,0:T(8,128)(2,1)} %get-tuple-element.42), channel_id=1, source_target_pairs={{0,8},{8,0},{16,24},{24,16},{32,40},{40,32},{48,56},{56,48},{64,72... | collective-permute-start | bytes 4718600 | tf_op jit(solution)/shard_map/ppermute | solution.py:42
  6.1 3.1 %collective-permute-start = (bf16[128,512]{1,0:T(8,128)(2,1)S(1)}, bf16[128,512]{1,0:T(8,128)(2,1)S(1)}, u32[]{:S(2)}, u32[]{:S(2)}) collective-permute-start(bf16[128,512]{1,0:T(8,128)(2,1)S(1)} %get-tuple-element.34), channel_id=1, source_target_pairs={{0,8},{8,0},{16,24},{24,16},{32,40},{40,32},{48,56},{56,48},{64,72... | collective-permute-start | bytes 393224 | tf_op jit(solution)/shard_map/ppermute | solution.py:42
  9.2 9.4 %collective-permute-start.3 = (bf16[128,1024]{1,0:T(8,128)(2,1)S(1)}, bf16[128,1024]{1,0:T(8,128)(2,1)S(1)}, u32[]{:S(2)}, u32[]{:S(2)}) collective-permute-start(bf16[128,1024]{1,0:T(8,128)(2,1)S(1)} %get-tuple-element.76), channel_id=1, source_target_pairs={{0,2},{1,3},{2,4},{3,5},{4,6},{5,7},{6,0},{7,1},{8,10},{9,11},{10,... | collective-permute-start | bytes 786440 | tf_op jit(solution)/shard_map/ppermute | solution.py:46
  10.7 14.5 %collective-permute-start.5 = (bf16[128,1024]{1,0:T(8,128)(2,1)S(1)}, bf16[128,1024]{1,0:T(8,128)(2,1)S(1)}, u32[]{:S(2)}, u32[]{:S(2)}) collective-permute-start(bf16[128,1024]{1,0:T(8,128)(2,1)S(1)} %get-tuple-element.76), channel_id=1, source_target_pairs={{0,4},{1,5},{2,6},{3,7},{4,0},{5,1},{6,2},{7,3},{8,12},{9,13},{10,... | collective-permute-start | bytes 786440 | tf_op jit(solution)/shard_map/ppermute | solution.py:46
  13.3 13.1 %collective-permute-start.2 = (bf16[128,1024]{1,0:T(8,128)(2,1)S(1)}, bf16[128,1024]{1,0:T(8,128)(2,1)S(1)}, u32[]{:S(2)}, u32[]{:S(2)}) collective-permute-start(bf16[128,1024]{1,0:T(8,128)(2,1)S(1)} %get-tuple-element.76), channel_id=1, source_target_pairs={{0,6},{1,7},{2,0},{3,1},{4,2},{5,3},{6,4},{7,5},{8,14},{9,15},{10,... | collective-permute-start | bytes 786440 | tf_op jit(solution)/shard_map/ppermute | solution.py:46
  14.4 12.1 %collective-permute-start.1 = (bf16[128,1024]{1,0:T(8,128)(2,1)S(1)}, bf16[128,1024]{1,0:T(8,128)(2,1)S(1)}, u32[]{:S(2)}, u32[]{:S(2)}) collective-permute-start(bf16[128,1024]{1,0:T(8,128)(2,1)S(1)} %get-tuple-element.76), channel_id=1, source_target_pairs={{0,1},{1,0},{2,3},{3,2},{4,5},{5,4},{6,7},{7,6},{8,9},{9,8},{10,11... | collective-permute-start | bytes 786440 | tf_op jit(solution)/shard_map/ppermute | solution.py:46
  18.6 23.3 %collective-permute-start.9 = (bf16[512,1536]{1,0:T(8,128)(2,1)}, bf16[512,1536]{1,0:T(8,128)(2,1)S(1)}, u32[]{:S(2)}, u32[]{:S(2)}) collective-permute-start(bf16[512,1536]{1,0:T(8,128)(2,1)} %get-tuple-element.41), channel_id=1, source_target_pairs={{0,8},{8,0},{16,24},{24,16},{32,40},{40,32},{48,56},{56,48},{64,72... | collective-permute-start | bytes 4718600 | tf_op jit(solution)/shard_map/ppermute | solution.py:42
  25.2 11.3 %collective-permute-start.8 = (bf16[128,1024]{1,0:T(8,128)(2,1)S(1)}, bf16[128,1024]{1,0:T(8,128)(2,1)S(1)}, u32[]{:S(2)}, u32[]{:S(2)}) collective-permute-start(bf16[128,1024]{1,0:T(8,128)(2,1)S(1)} %collective-permute-done.5), channel_id=1, source_target_pairs={{0,1},{1,0},{2,3},{3,2},{4,5},{5,4},{6,7},{7,6},{8,9},{9,8},{10,11... | collective-permute-start | bytes 786440 | tf_op jit(solution)/shard_map/ppermute | solution.py:46
  26.4 10.2 %collective-permute-start.7 = (bf16[128,1024]{1,0:T(8,128)(2,1)S(1)}, bf16[128,1024]{1,0:T(8,128)(2,1)S(1)}, u32[]{:S(2)}, u32[]{:S(2)}) collective-permute-start(bf16[128,1024]{1,0:T(8,128)(2,1)S(1)} %collective-permute-done.1), channel_id=1, source_target_pairs={{0,2},{1,3},{2,4},{3,5},{4,6},{5,7},{6,0},{7,1},{8,10},{9,11},{10,... | collective-permute-start | bytes 786440 | tf_op jit(solution)/shard_map/ppermute | solution.py:46
  26.5 10.1 %collective-permute-start.6 = (bf16[128,1024]{1,0:T(8,128)(2,1)S(1)}, bf16[128,1024]{1,0:T(8,128)(2,1)S(1)}, u32[]{:S(2)}, u32[]{:S(2)}) collective-permute-start(bf16[128,1024]{1,0:T(8,128)(2,1)S(1)} %collective-permute-done.1), channel_id=1, source_target_pairs={{0,6},{1,7},{2,0},{3,1},{4,2},{5,3},{6,4},{7,5},{8,14},{9,15},{10,... | collective-permute-start | bytes 786440 | tf_op jit(solution)/shard_map/ppermute | solution.py:46
  30.0 1.4 copy-start.1
  32.1 23.1 %collective-permute-start.10 = (bf16[640,768]{1,0:T(8,128)(2,1)S(1)}, bf16[640,768]{1,0:T(8,128)(2,1)S(1)}, u32[]{:S(2)}, u32[]{:S(2)}) collective-permute-start(bf16[640,768]{1,0:T(8,128)(2,1)S(1)} %add_convert_fusion.2), channel_id=1, source_target_pairs={{0,96},{8,104},{16,112},{24,120},{32,0},{40,8},{48,16},{56,24},{64... | collective-permute-start | bytes 2949128 | tf_op jit(solution)/shard_map/ppermute | solution.py:42
  36.6 22.5 %collective-permute-start.11 = (bf16[640,768]{1,0:T(8,128)(2,1)S(1)}, bf16[640,768]{1,0:T(8,128)(2,1)S(1)}, u32[]{:S(2)}, u32[]{:S(2)}) collective-permute-start(bf16[640,768]{1,0:T(8,128)(2,1)S(1)} %add_convert_fusion.1), channel_id=1, source_target_pairs={{0,32},{8,40},{16,48},{24,56},{32,64},{40,72},{48,80},{56,88},{64,... | collective-permute-start | bytes 2949128 | tf_op jit(solution)/shard_map/ppermute | solution.py:42
  37.7 3.3 %copy-start = (bf16[512,1536]{1,0:T(8,128)(2,1)S(1)}, bf16[512,1536]{1,0:T(8,128)(2,1)}, u32[]{:S(2)}) copy-start(bf16[512,1536]{1,0:T(8,128)(2,1)} %get-tuple-element.41) | copy-start | bytes 4718596
  37.7 33.5 %collective-permute-start.16 = (bf16[384,768]{1,0:T(8,128)(2,1)S(1)}, bf16[384,768]{1,0:T(8,128)(2,1)S(1)}, u32[]{:S(2)}, u32[]{:S(2)}) collective-permute-start(bf16[384,768]{1,0:T(8,128)(2,1)S(1)} %fusion.2), channel_id=1, source_target_pairs={{0,16},{8,24},{16,0},{24,8},{32,48},{40,56},{48,32},{56,40},{64,80... | collective-permute-start | bytes 1769480 | tf_op jit(solution)/shard_map/ppermute | solution.py:42
  42.4 28.8 %collective-permute-start.15 = (bf16[384,768]{1,0:T(8,128)(2,1)S(1)}, bf16[384,768]{1,0:T(8,128)(2,1)S(1)}, u32[]{:S(2)}, u32[]{:S(2)}) collective-permute-start(bf16[384,768]{1,0:T(8,128)(2,1)S(1)} %fusion.1), channel_id=1, source_target_pairs={{0,16},{8,24},{16,0},{24,8},{32,48},{40,56},{48,32},{56,40},{64,80... | collective-permute-start | bytes 1769480 | tf_op jit(solution)/shard_map/ppermute | solution.py:42
  60.3 9.7 %collective-permute-start.13 = (bf16[640,384]{1,0:T(8,128)(2,1)S(1)}, bf16[640,384]{1,0:T(8,128)(2,1)S(1)}, u32[]{:S(2)}, u32[]{:S(2)}) collective-permute-start(bf16[640,384]{1,0:T(8,128)(2,1)S(1)} %get-tuple-element.63), channel_id=1, source_target_pairs={{0,96},{8,104},{16,112},{24,120},{32,0},{40,8},{48,16},{56,24},{64... | collective-permute-start | bytes 1474568 | tf_op jit(solution)/shard_map/ppermute | solution.py:42
  60.3 10.9 %collective-permute-start.12 = (bf16[640,384]{1,0:T(8,128)(2,1)S(1)}, bf16[640,384]{1,0:T(8,128)(2,1)S(1)}, u32[]{:S(2)}, u32[]{:S(2)}) collective-permute-start(bf16[640,384]{1,0:T(8,128)(2,1)S(1)} %get-tuple-element.65), channel_id=1, source_target_pairs={{0,32},{8,40},{16,48},{24,56},{32,64},{40,72},{48,80},{56,88},{64,... | collective-permute-start | bytes 1474568 | tf_op jit(solution)/shard_map/ppermute | solution.py:42
  71.2 7.6 %copy-start.4 = (bf16[640,384]{1,0:T(8,128)(2,1)}, bf16[640,384]{1,0:T(8,128)(2,1)S(1)}, u32[]{:S(2)}) copy-start(bf16[640,384]{1,0:T(8,128)(2,1)S(1)} %collective-permute-done.12.refs_4_) | copy-start | bytes 1474564
  71.4 5.6 %collective-permute-start.17 = (bf16[2,192,384]{2,1,0:T(8,128)(2,1)S(1)}, bf16[2,192,384]{2,1,0:T(8,128)(2,1)S(1)}, u32[]{:S(2)}, u32[]{:S(2)}) collective-permute-start(bf16[2,192,384]{2,1,0:T(8,128)(2,1)S(1)} %pad_maximum_fusion.1), channel_id=1, source_target_pairs={{0,96},{8,104},{16,112},{24,120},{32,0},{40,8},{48,16},{56,24},{64... | collective-permute-start | bytes 884744 | tf_op jit(solution)/shard_map/ppermute | solution.py:42
  71.8 6.9 %collective-permute-start.18 = (bf16[2,192,384]{2,1,0:T(8,128)(2,1)S(1)}, bf16[2,192,384]{2,1,0:T(8,128)(2,1)S(1)}, u32[]{:S(2)}, u32[]{:S(2)}) collective-permute-start(bf16[2,192,384]{2,1,0:T(8,128)(2,1)S(1)} %pad_maximum_fusion.2), channel_id=1, source_target_pairs={{0,32},{8,40},{16,48},{24,56},{32,64},{40,72},{48,80},{56,88},{64,... | collective-permute-start | bytes 884744 | tf_op jit(solution)/shard_map/ppermute | solution.py:42
  77.1 6.0 %collective-permute-start.20 = (bf16[192,384]{1,0:T(8,128)(2,1)S(1)}, bf16[192,384]{1,0:T(8,128)(2,1)S(1)}, u32[]{:S(2)}, u32[]{:S(2)}) collective-permute-start(bf16[192,384]{1,0:T(8,128)(2,1)S(1)} %fusion.40), channel_id=1, source_target_pairs={{0,96},{8,104},{16,112},{24,120},{32,0},{40,8},{48,16},{56,24},{64... | collective-permute-start | bytes 442376 | tf_op jit(solution)/shard_map/ppermute | solution.py:42
  78.8 5.8 %collective-permute-start.19 = (bf16[192,384]{1,0:T(8,128)(2,1)S(1)}, bf16[192,384]{1,0:T(8,128)(2,1)S(1)}, u32[]{:S(2)}, u32[]{:S(2)}) collective-permute-start(bf16[192,384]{1,0:T(8,128)(2,1)S(1)} %fusion.43), channel_id=1, source_target_pairs={{0,32},{8,40},{16,48},{24,56},{32,64},{40,72},{48,80},{56,88},{64,... | collective-permute-start | bytes 442376 | tf_op jit(solution)/shard_map/ppermute | solution.py:42
  79.3 9.3 %collective-permute-start.14 = (bf16[640,384]{1,0:T(8,128)(2,1)S(1)}, bf16[640,384]{1,0:T(8,128)(2,1)S(1)}, u32[]{:S(2)}, u32[]{:S(2)}) collective-permute-start(bf16[640,384]{1,0:T(8,128)(2,1)S(1)} %add_convert_fusion.3), channel_id=1, source_target_pairs={{0,16},{8,24},{16,0},{24,8},{32,48},{40,56},{48,32},{56,40},{64,80... | collective-permute-start | bytes 1474568 | tf_op jit(solution)/shard_map/ppermute | solution.py:42
  84.8 9.3 %copy-start.3 = (bf16[1024,512]{1,0:T(8,128)(2,1)S(1)}, bf16[1024,512]{1,0:T(8,128)(2,1)}, u32[]{:S(2)}) copy-start(bf16[1024,512]{1,0:T(8,128)(2,1)} %param.13) | copy-start | bytes 3145732
  88.5 0.8 copy-start.5
  94.1 16.2 %collective-permute-start.22 = (bf16[1024,512]{1,0:T(8,128)(2,1)S(1)}, bf16[1024,512]{1,0:T(8,128)(2,1)S(1)}, u32[]{:S(2)}, u32[]{:S(2)}) collective-permute-start(bf16[1024,512]{1,0:T(8,128)(2,1)S(1)} %copy-done.3), channel_id=1, source_target_pairs={{0,8},{8,0},{16,24},{24,16},{32,40},{40,32},{48,56},{56,48},{64,72... | collective-permute-start | bytes 3145736 | tf_op jit(solution)/shard_map/ppermute | solution.py:42
  102.2 2.5 %collective-permute-start.21 = (f32[26,8,128]{2,1,0:T(8,128)}, f32[26,8,128]{2,1,0:T(8,128)S(1)}, u32[]{:S(2)}, u32[]{:S(2)}) collective-permute-start(f32[26,8,128]{2,1,0:T(8,128)} %get-tuple-element.57.mine_ref), channel_id=1, source_target_pairs={{0,8},{8,0},{16,24},{24,16},{32,40},{40,32},{48,56},{56,48},{64,72... | collective-permute-start | bytes 319496 | tf_op jit(solution)/shard_map/ppermute | solution.py:42
  104.7 0.6 copy-start.6
  110.2 3.0 %copy-start.2 = (bf16[1024,128]{1,0:T(8,128)(2,1)S(1)}, bf16[1024,128]{1,0:T(8,128)(2,1)}, u32[]{:S(2)}) copy-start(bf16[1024,128]{1,0:T(8,128)(2,1)} %filtered.1) | copy-start | bytes 786436
  110.2 12.2 %collective-permute-start.24 = (bf16[1024,128]{1,0:T(8,128)(2,1)}, bf16[1024,128]{1,0:T(8,128)(2,1)S(1)}, u32[]{:S(2)}, u32[]{:S(2)}) collective-permute-start(bf16[1024,128]{1,0:T(8,128)(2,1)} %filtered.1), channel_id=1, source_target_pairs={{0,64},{8,72},{16,80},{24,88},{32,96},{40,104},{48,112},{56,120},{... | collective-permute-start | bytes 786440 | tf_op jit(solution)/shard_map/ppermute | solution.py:42
  110.6 9.2 %collective-permute-start.23 = (bf16[1024,128]{1,0:T(8,128)(2,1)}, bf16[1024,128]{1,0:T(8,128)(2,1)S(1)}, u32[]{:S(2)}, u32[]{:S(2)}) collective-permute-start(bf16[1024,128]{1,0:T(8,128)(2,1)} %filtered.1), channel_id=1, source_target_pairs={{0,16},{8,24},{16,0},{24,8},{32,48},{40,56},{48,32},{56,40},{64,80... | collective-permute-start | bytes 786440 | tf_op jit(solution)/shard_map/ppermute | solution.py:42
  113.2 12.7 %collective-permute-start.26 = (bf16[1024,128]{1,0:T(8,128)(2,1)S(1)}, bf16[1024,128]{1,0:T(8,128)(2,1)S(1)}, u32[]{:S(2)}, u32[]{:S(2)}) collective-permute-start(bf16[1024,128]{1,0:T(8,128)(2,1)S(1)} %copy-done.2), channel_id=1, source_target_pairs={{0,32},{8,40},{16,48},{24,56},{32,64},{40,72},{48,80},{56,88},{64,... | collective-permute-start | bytes 786440 | tf_op jit(solution)/shard_map/ppermute | solution.py:42
  114.8 10.2 %collective-permute-start.25 = (bf16[1024,128]{1,0:T(8,128)(2,1)S(1)}, bf16[1024,128]{1,0:T(8,128)(2,1)S(1)}, u32[]{:S(2)}, u32[]{:S(2)}) collective-permute-start(bf16[1024,128]{1,0:T(8,128)(2,1)S(1)} %copy-done.2), channel_id=1, source_target_pairs={{0,96},{8,104},{16,112},{24,120},{32,0},{40,8},{48,16},{56,24},{64... | collective-permute-start | bytes 786440 | tf_op jit(solution)/shard_map/ppermute | solution.py:42
  119.8 11.7 %collective-permute-start.28 = (bf16[1024,128]{1,0:T(8,128)(2,1)S(1)}, bf16[1024,128]{1,0:T(8,128)(2,1)S(1)}, u32[]{:S(2)}, u32[]{:S(2)}) collective-permute-start(bf16[1024,128]{1,0:T(8,128)(2,1)S(1)} %collective-permute-done.23), channel_id=1, source_target_pairs={{0,32},{8,40},{16,48},{24,56},{32,64},{40,72},{48,80},{56,88},{64,... | collective-permute-start | bytes 786440 | tf_op jit(solution)/shard_map/ppermute | solution.py:42
  121.3 7.9 %collective-permute-start.27 = (bf16[1024,128]{1,0:T(8,128)(2,1)S(1)}, bf16[1024,128]{1,0:T(8,128)(2,1)S(1)}, u32[]{:S(2)}, u32[]{:S(2)}) collective-permute-start(bf16[1024,128]{1,0:T(8,128)(2,1)S(1)} %collective-permute-done.23), channel_id=1, source_target_pairs={{0,96},{8,104},{16,112},{24,120},{32,0},{40,8},{48,16},{56,24},{64... | collective-permute-start | bytes 786440 | tf_op jit(solution)/shard_map/ppermute | solution.py:42
  122.4 9.1 %collective-permute-start.29 = (bf16[1024,128]{1,0:T(8,128)(2,1)S(1)}, bf16[1024,128]{1,0:T(8,128)(2,1)S(1)}, u32[]{:S(2)}, u32[]{:S(2)}) collective-permute-start(bf16[1024,128]{1,0:T(8,128)(2,1)S(1)} %collective-permute-done.24), channel_id=1, source_target_pairs={{0,16},{8,24},{16,0},{24,8},{32,48},{40,56},{48,32},{56,40},{64,80... | collective-permute-start | bytes 786440 | tf_op jit(solution)/shard_map/ppermute | solution.py:42
  133.5 14.4 %collective-permute-start.30 = (bf16[128,1024]{1,0:T(8,128)(2,1)S(1)}, bf16[128,1024]{1,0:T(8,128)(2,1)S(1)}, u32[]{:S(2)}, u32[]{:S(2)}) collective-permute-start(bf16[128,1024]{1,0:T(8,128)(2,1)S(1)} %convolution_convert_fusion.4), channel_id=1, source_target_pairs={{0,2},{1,3},{2,4},{3,5},{4,6},{5,7},{6,0},{7,1},{8,10},{9,11},{10,... | collective-permute-start | bytes 786440 | tf_op jit(solution)/shard_map/ppermute | solution.py:46
  133.6 14.4 %collective-permute-start.31 = (bf16[128,1024]{1,0:T(8,128)(2,1)S(1)}, bf16[128,1024]{1,0:T(8,128)(2,1)S(1)}, u32[]{:S(2)}, u32[]{:S(2)}) collective-permute-start(bf16[128,1024]{1,0:T(8,128)(2,1)S(1)} %convolution_convert_fusion.3), channel_id=1, source_target_pairs={{0,6},{1,7},{2,0},{3,1},{4,2},{5,3},{6,4},{7,5},{8,14},{9,15},{10,... | collective-permute-start | bytes 786440 | tf_op jit(solution)/shard_map/ppermute | solution.py:46
  136.2 6.2 %collective-permute-start.32 = (bf16[128,1024]{1,0:T(8,128)(2,1)S(1)}, bf16[128,1024]{1,0:T(8,128)(2,1)S(1)}, u32[]{:S(2)}, u32[]{:S(2)}) collective-permute-start(bf16[128,1024]{1,0:T(8,128)(2,1)S(1)} %convolution_convert_fusion.2), channel_id=1, source_target_pairs={{0,1},{1,0},{2,3},{3,2},{4,5},{5,4},{6,7},{7,6},{8,9},{9,8},{10,11... | collective-permute-start | bytes 786440 | tf_op jit(solution)/shard_map/ppermute | solution.py:46
  136.5 10.6 %collective-permute-start.34 = (bf16[128,1024]{1,0:T(8,128)(2,1)S(1)}, bf16[128,1024]{1,0:T(8,128)(2,1)S(1)}, u32[]{:S(2)}, u32[]{:S(2)}) collective-permute-start(bf16[128,1024]{1,0:T(8,128)(2,1)S(1)} %convolution_convert_fusion.1), channel_id=1, source_target_pairs={{0,2},{1,3},{2,4},{3,5},{4,6},{5,7},{6,0},{7,1},{8,10},{9,11},{10,... | collective-permute-start | bytes 786440 | tf_op jit(solution)/shard_map/ppermute | solution.py:46
  137.0 10.2 %collective-permute-start.35 = (bf16[128,1024]{1,0:T(8,128)(2,1)S(1)}, bf16[128,1024]{1,0:T(8,128)(2,1)S(1)}, u32[]{:S(2)}, u32[]{:S(2)}) collective-permute-start(bf16[128,1024]{1,0:T(8,128)(2,1)S(1)} %convolution_convert_fusion), channel_id=1, source_target_pairs={{0,6},{1,7},{2,0},{3,1},{4,2},{5,3},{6,4},{7,5},{8,14},{9,15},{10,... | collective-permute-start | bytes 786440 | tf_op jit(solution)/shard_map/ppermute | solution.py:46
  142.8 7.4 %collective-permute-start.33 = (bf16[128,1024]{1,0:T(8,128)(2,1)S(1)}, bf16[128,1024]{1,0:T(8,128)(2,1)S(1)}, u32[]{:S(2)}, u32[]{:S(2)}) collective-permute-start(bf16[128,1024]{1,0:T(8,128)(2,1)S(1)} %fusion.11), channel_id=1, source_target_pairs={{0,4},{1,5},{2,6},{3,7},{4,0},{5,1},{6,2},{7,3},{8,12},{9,13},{10,... | collective-permute-start | bytes 786440 | tf_op jit(solution)/shard_map/ppermute | solution.py:46
  147.6 5.6 %collective-permute-start.36 = (bf16[128,1024]{1,0:T(8,128)(2,1)S(1)}, bf16[128,1024]{1,0:T(8,128)(2,1)S(1)}, u32[]{:S(2)}, u32[]{:S(2)}) collective-permute-start(bf16[128,1024]{1,0:T(8,128)(2,1)S(1)} %fusion.10), channel_id=1, source_target_pairs={{0,1},{1,0},{2,3},{3,2},{4,5},{5,4},{6,7},{7,6},{8,9},{9,8},{10,11... | collective-permute-start | bytes 786440 | tf_op jit(solution)/shard_map/ppermute | solution.py:46
  153.8 9.5 %collective-permute-start.37 = (bf16[128,512]{1,0:T(8,128)(2,1)S(1)}, bf16[128,512]{1,0:T(8,128)(2,1)S(1)}, u32[]{:S(2)}, u32[]{:S(2)}) collective-permute-start(bf16[128,512]{1,0:T(8,128)(2,1)S(1)} %get-tuple-element.74), channel_id=1, source_target_pairs={{0,8},{8,0},{16,24},{24,16},{32,40},{40,32},{48,56},{56,48},{64,72... | collective-permute-start | bytes 393224 | tf_op jit(solution)/shard_map/ppermute | solution.py:42

commit v5 on v4

--- a/solution.py
+++ b/solution.py
@@ -349,10 +349,9 @@
     length = activations.shape[0] // CORES
 
     kept = lax.dynamic_slice_in_dim(activations, core * length, length, 0)
-    other = lax.dynamic_slice_in_dim(activations, (1 - core) * length, length, 0)
-    other, proj_weight = lax.optimization_barrier((other, proj_weight))
-    other = swap(other)
+    other = swap(lax.dynamic_slice_in_dim(activations, (1 - core) * length, length, 0))
     mine = jnp.concatenate([kept, other], axis=1)
+    mine, proj_weight = lax.optimization_barrier((mine, proj_weight))
 
     def along(value, dy):
         return ch_send(value, ch_perm(lambda y, xl: (y - dy, xl)))
@@ -401,7 +400,8 @@
 
     far = across(part((2, 1), (2, 1)).astype(BF))
     up, down = [forward(part((dy, 1), (dy, 1)).astype(BF), dy) for dy in (1, 3)]
-    near_up, near_down = [forward(part((dy, 0), (dy, 0)).astype(BF), dy) for dy in (1, 3)]
+    far, *near = lax.optimization_barrier((far, part((1, 0), (1, 0)).astype(BF), part((3, 0), (3, 0)).astype(BF)))
+    near_up, near_down = forward(near[0], 1), forward(near[1], 3)
     opposite = forward((part((2, 0), (2, 0)) + far.astype(F32)).astype(BF), 2)
     beside = across((part((0, 1), (0, 1)) + up.astype(F32) + down.astype(F32)).astype(BF))
     total = part((0, 0), (0, 0))

time: 164 us -> 157 us (0.957)
  starting transfers between devices: 60.9 us -> 55 us
    ppermute x24, starting transfers between devices: 44.5 us -> 37.1 us  [tok_send(): return lax.ppermute(value, 'tok', perm)]
  transfers between devices with their start and end apart: 38 -> 38, of which waited for: 21 -> 20; matrix products, arithmetic and copies ran while one was open for 9% -> 10% of each run, Pallas kernels for 3% -> 3%
where the time goes in v5:
time: 157 us
  waiting for transfers between devices  66.4 us (42%)
  starting transfers between devices  55 us (35%)
  Pallas kernels  13.2 us (8%)
  matrix products  13.1 us (8%)
  local copies, waits for them, and re-layouts  5.13 us (3%)
  other arithmetic  3.49 us (2%)
    ppermute x24, waiting for transfers between devices, tok_send(): return lax.ppermute(value, 'tok', perm)  45.3 us
    ppermute x24, starting transfers between devices, tok_send(): return lax.ppermute(value, 'tok', perm)  37.1 us
    ppermute x14, waiting for transfers between devices, ch_send(): return lax.ppermute(value, 'ch', perm)  21 us
    ppermute x14, starting transfers between devices, ch_send(): return lax.ppermute(value, 'ch', perm)  17.9 us
    pallas_call x1, Pallas kernels, filtered(): pl.pallas_call(filter_kernel, out_shape=jax.ShapeDtypeStruct(gate.shape,...  4.88 us
    pallas_call x1, Pallas kernels, local_part(): pl.pallas_call(lambda *refs: local_kernel(blocks, [len(terms) for terms i...  4.72 us
    dot_general x8, matrix products, product(): jnp.dot(rows[:, depth:], other[part][:, columns], preferred_element_type=...  4.68 us
    dot_general x8, matrix products, product(): jnp.dot(rows[:, :depth], own[part][:, columns], preferred_element_type=F32)  4.67 us
  transfers between devices with their start and end apart: 38, of which 20 were waited for; matrix products, arithmetic and copies ran while one was open for 10% of the time, Pallas kernels for 3%

profile of v5, /device:TPU:1, one launch (start us, length us, event | category | flops | bytes accessed | tf_op | source)
XLA Modules:
  0.0 156.8 jit_solution(15082473501938179196)
XLA Ops:
  0.0 1.0 constant_dynamic-slice_fusion.1
  1.0 1.5 collective-permute-start
  2.5 1.0 collective-permute-done
  3.5 3.6 %by_target.1 = (bf16[512,1536]{1,0:T(8,128)(2,1)}, bf16[512,1536]{1,0:T(8,128)(2,1)}) custom-call(bf16[512,3072]{1,0:T(8,128)(2,1)} %refs_0_), custom_call_target="tpu_custom_call" | custom-call | tf_op jit(solution)/shard_map/by_target/pallas_call | solution.py:87
  7.5 3.0 %collective-permute-start.5 = (bf16[128,1024]{1,0:T(8,128)(2,1)S(1)}, bf16[128,1024]{1,0:T(8,128)(2,1)S(1)}, u32[]{:S(2)}, u32[]{:S(2)}) collective-permute-start(bf16[128,1024]{1,0:T(8,128)(2,1)S(1)} %pad_maximum_fusion.4), channel_id=1, source_target_pairs={{0,4},{1,5},{2,6},{3,7},{4,0},{5,1},{6,2},{7,3},{8,12},{9,13},{10,... | collective-permute-start | bytes 786440 | tf_op jit(solution)/shard_map/ppermute | solution.py:46
  10.9 2.3 %collective-permute-start.2 = (bf16[128,1024]{1,0:T(8,128)(2,1)S(1)}, bf16[128,1024]{1,0:T(8,128)(2,1)S(1)}, u32[]{:S(2)}, u32[]{:S(2)}) collective-permute-start(bf16[128,1024]{1,0:T(8,128)(2,1)S(1)} %pad_maximum_fusion.4), channel_id=1, source_target_pairs={{0,6},{1,7},{2,0},{3,1},{4,2},{5,3},{6,4},{7,5},{8,14},{9,15},{10,... | collective-permute-start | bytes 786440 | tf_op jit(solution)/shard_map/ppermute | solution.py:46
  13.2 1.2 collective-permute-start.1
  14.5 2.5 %collective-permute-done.5 = bf16[128,1024]{1,0:T(8,128)(2,1)S(1)} collective-permute-done((bf16[128,1024]{1,0:T(8,128)(2,1)S(1)}, bf16[128,1024]{1,0:T(8,128)(2,1)S(1)}, u32[]{:S(2)}, u32[]{:S(2)}) %collective-permute-start.5) | collective-permute-done | bytes 262176 | tf_op jit(solution)/shard_map/ppermute | solution.py:46
  16.9 1.5 collective-permute-start.9
  18.4 4.6 %collective-permute-done.3 = bf16[128,1024]{1,0:T(8,128)(2,1)S(1)} collective-permute-done((bf16[128,1024]{1,0:T(8,128)(2,1)S(1)}, bf16[128,1024]{1,0:T(8,128)(2,1)S(1)}, u32[]{:S(2)}, u32[]{:S(2)}) %collective-permute-start.3) | collective-permute-done | bytes 262176 | tf_op jit(solution)/shard_map/ppermute | solution.py:46
  22.9 1.3 collective-permute-start.8
  24.2 1.0 collective-permute-start.7
  25.3 1.7 %collective-permute-start.6 = (bf16[128,1024]{1,0:T(8,128)(2,1)S(1)}, bf16[128,1024]{1,0:T(8,128)(2,1)S(1)}, u32[]{:S(2)}, u32[]{:S(2)}) collective-permute-start(bf16[128,1024]{1,0:T(8,128)(2,1)S(1)} %collective-permute-done.1), channel_id=1, source_target_pairs={{0,6},{1,7},{2,0},{3,1},{4,2},{5,3},{6,4},{7,5},{8,14},{9,15},{10,... | collective-permute-start | bytes 786440 | tf_op jit(solution)/shard_map/ppermute | solution.py:46
  29.8 3.8 %collective-permute-start.10 = (bf16[640,768]{1,0:T(8,128)(2,1)S(1)}, bf16[640,768]{1,0:T(8,128)(2,1)S(1)}, u32[]{:S(2)}, u32[]{:S(2)}) collective-permute-start(bf16[640,768]{1,0:T(8,128)(2,1)S(1)} %add_convert_fusion.2), channel_id=1, source_target_pairs={{0,96},{8,104},{16,112},{24,120},{32,0},{40,8},{48,16},{56,24},{64... | collective-permute-start | bytes 2949128 | tf_op jit(solution)/shard_map/ppermute | solution.py:42
  35.5 2.5 %collective-permute-start.16 = (bf16[384,768]{1,0:T(8,128)(2,1)S(1)}, bf16[384,768]{1,0:T(8,128)(2,1)S(1)}, u32[]{:S(2)}, u32[]{:S(2)}) collective-permute-start(bf16[384,768]{1,0:T(8,128)(2,1)S(1)} %fusion.2), channel_id=1, source_target_pairs={{0,16},{8,24},{16,0},{24,8},{32,48},{40,56},{48,32},{56,40},{64,80... | collective-permute-start | bytes 1769480 | tf_op jit(solution)/shard_map/ppermute | solution.py:42
  41.9 1.2 fusion.28
  43.1 1.2 add_convert_fusion
  44.3 9.1 %collective-permute-done.10 = bf16[640,768]{1,0:T(8,128)(2,1)S(1)} collective-permute-done((bf16[640,768]{1,0:T(8,128)(2,1)S(1)}, bf16[640,768]{1,0:T(8,128)(2,1)S(1)}, u32[]{:S(2)}, u32[]{:S(2)}) %collective-permute-start.10) | collective-permute-done | bytes 983072 | tf_op jit(solution)/shard_map/ppermute | solution.py:42
  53.4 3.9 %collective-permute-done.11 = bf16[640,768]{1,0:T(8,128)(2,1)S(1)} collective-permute-done((bf16[640,768]{1,0:T(8,128)(2,1)S(1)}, bf16[640,768]{1,0:T(8,128)(2,1)S(1)}, u32[]{:S(2)}, u32[]{:S(2)}) %collective-permute-start.11) | collective-permute-done | bytes 983072 | tf_op jit(solution)/shard_map/ppermute | solution.py:42
  57.3 1.2 add_convert_fusion.4
  58.5 1.5 collective-permute-start.12
  60.4 8.3 %collective-permute-done.13 = bf16[640,384]{1,0:T(8,128)(2,1)S(1)} collective-permute-done((bf16[640,384]{1,0:T(8,128)(2,1)S(1)}, bf16[640,384]{1,0:T(8,128)(2,1)S(1)}, u32[]{:S(2)}, u32[]{:S(2)}) %collective-permute-start.13) | collective-permute-done | bytes 491552 | tf_op jit(solution)/shard_map/ppermute | solution.py:42
  68.7 1.2 collective-permute-done.12.refs_4_
  70.5 1.2 collective-permute-start.18
  71.8 4.0 %collective-permute-done.17 = bf16[2,192,384]{2,1,0:T(8,128)(2,1)S(1)} collective-permute-done((bf16[2,192,384]{2,1,0:T(8,128)(2,1)S(1)}, bf16[2,192,384]{2,1,0:T(8,128)(2,1)S(1)}, u32[]{:S(2)}, u32[]{:S(2)}) %collective-permute-start.17) | collective-permute-done | bytes 294944 | tf_op jit(solution)/shard_map/ppermute | solution.py:42
  75.8 1.6 collective-permute-start.20
  78.0 2.5 %collective-permute-start.14 = (bf16[640,384]{1,0:T(8,128)(2,1)S(1)}, bf16[640,384]{1,0:T(8,128)(2,1)S(1)}, u32[]{:S(2)}, u32[]{:S(2)}) collective-permute-start(bf16[640,384]{1,0:T(8,128)(2,1)S(1)} %add_convert_fusion.3), channel_id=1, source_target_pairs={{0,16},{8,24},{16,0},{24,8},{32,48},{40,56},{48,32},{56,40},{64,80... | collective-permute-start | bytes 1474568 | tf_op jit(solution)/shard_map/ppermute | solution.py:42
  81.5 1.3 collective-permute-done.19
  83.8 3.5 %collective-permute-done.14.refs_5_ = bf16[640,384]{1,0:T(8,128)(2,1)S(1)} collective-permute-done((bf16[640,384]{1,0:T(8,128)(2,1)S(1)}, bf16[640,384]{1,0:T(8,128)(2,1)S(1)}, u32[]{:S(2)}, u32[]{:S(2)}) %collective-permute-start.14) | collective-permute-done | bytes 491552 | tf_op jit(solution)/shard_map/ppermute | solution.py:42
  88.0 4.7 %local_part.1 = (f32[1024,128]{1,0:T(8,128)}, f32[1024,128]{1,0:T(8,128)}, f32[26,8,128]{2,1,0:T(8,128)}) custom-call(s32[6]{0:T(128)} %stack.51.refs_0_.where_ref, f32[3,3,8192]{2,1,0:T(4,128)} %taps_ref.1, f32[16,8192]{1,0:T(8,128)} %rates_ref.1, bf16[640,384]{1,0:T(8,128)(2,1)} %get-tuple-element.54.refs_3_, bf16[640,384]{1,0:T(8,128)(2,1)} %copy-done.4, ...), custom_call_target="tpu_custom_call" | custom-call | tf_op jit(solution)/shard_map/local_part/pallas_call | solution.py:308
  92.8 7.3 %collective-permute-start.22 = (bf16[1024,512]{1,0:T(8,128)(2,1)S(1)}, bf16[1024,512]{1,0:T(8,128)(2,1)S(1)}, u32[]{:S(2)}, u32[]{:S(2)}) collective-permute-start(bf16[1024,512]{1,0:T(8,128)(2,1)S(1)} %copy-done.3), channel_id=1, source_target_pairs={{0,8},{8,0},{16,24},{24,16},{32,40},{40,32},{48,56},{56,48},{64,72... | collective-permute-start | bytes 3145736 | tf_op jit(solution)/shard_map/ppermute | solution.py:42
  100.2 2.4 %collective-permute-done.21.theirs_ref = f32[26,8,128]{2,1,0:T(8,128)S(1)} collective-permute-done((f32[26,8,128]{2,1,0:T(8,128)}, f32[26,8,128]{2,1,0:T(8,128)S(1)}, u32[]{:S(2)}, u32[]{:S(2)}) %collective-permute-start.21) | collective-permute-done | bytes 106528 | tf_op jit(solution)/shard_map/ppermute | solution.py:42
  103.2 4.9 %filtered.1 = bf16[1024,128]{1,0:T(8,128)(2,1)} custom-call(s32[6]{0:T(128)} %stack.51.refs_0_.where_ref, f32[3,3,8192]{2,1,0:T(4,128)} %taps_ref.1, f32[16,8192]{1,0:T(8,128)} %rates_ref.1, f32[16,8192]{1,0:T(8,128)} %weights_ref.1, f32[1,8192]{1,0:T(1,128)} %bitcast.45, f32[26,8,128]{2,1,0:T(8,128)} %get-tuple-element.60.mine_ref, ...), custom_call_target="tpu_custom_call" | custom-call | tf_op jit(solution)/shard_map/filtered/pallas_call | solution.py:328
  108.8 2.4 %collective-permute-start.23 = (bf16[1024,128]{1,0:T(8,128)(2,1)}, bf16[1024,128]{1,0:T(8,128)(2,1)S(1)}, u32[]{:S(2)}, u32[]{:S(2)}) collective-permute-start(bf16[1024,128]{1,0:T(8,128)(2,1)} %filtered.1), channel_id=1, source_target_pairs={{0,16},{8,24},{16,0},{24,8},{32,48},{40,56},{48,32},{56,40},{64,80... | collective-permute-start | bytes 786440 | tf_op jit(solution)/shard_map/ppermute | solution.py:42
  111.4 1.2 collective-permute-start.26
  112.6 1.5 collective-permute-start.25
  114.6 3.3 %collective-permute-done.23 = bf16[1024,128]{1,0:T(8,128)(2,1)S(1)} collective-permute-done((bf16[1024,128]{1,0:T(8,128)(2,1)}, bf16[1024,128]{1,0:T(8,128)(2,1)S(1)}, u32[]{:S(2)}, u32[]{:S(2)}) %collective-permute-start.23) | collective-permute-done | bytes 262176 | tf_op jit(solution)/shard_map/ppermute | solution.py:42
  118.0 1.1 collective-permute-start.28
  119.1 1.5 collective-permute-start.27
  120.6 2.4 %collective-permute-start.29 = (bf16[1024,128]{1,0:T(8,128)(2,1)S(1)}, bf16[1024,128]{1,0:T(8,128)(2,1)S(1)}, u32[]{:S(2)}, u32[]{:S(2)}) collective-permute-start(bf16[1024,128]{1,0:T(8,128)(2,1)S(1)} %collective-permute-done.24), channel_id=1, source_target_pairs={{0,16},{8,24},{16,0},{24,8},{32,48},{40,56},{48,32},{56,40},{64,80... | collective-permute-start | bytes 786440 | tf_op jit(solution)/shard_map/ppermute | solution.py:42
  123.9 3.1 %collective-permute-done.27 = bf16[1024,128]{1,0:T(8,128)(2,1)S(1)} collective-permute-done((bf16[1024,128]{1,0:T(8,128)(2,1)S(1)}, bf16[1024,128]{1,0:T(8,128)(2,1)S(1)}, u32[]{:S(2)}, u32[]{:S(2)}) %collective-permute-start.27) | collective-permute-done | bytes 262176 | tf_op jit(solution)/shard_map/ppermute | solution.py:42
  127.1 2.3 %collective-permute-done.28 = bf16[1024,128]{1,0:T(8,128)(2,1)S(1)} collective-permute-done((bf16[1024,128]{1,0:T(8,128)(2,1)S(1)}, bf16[1024,128]{1,0:T(8,128)(2,1)S(1)}, u32[]{:S(2)}, u32[]{:S(2)}) %collective-permute-start.28) | collective-permute-done | bytes 262176 | tf_op jit(solution)/shard_map/ppermute | solution.py:42
  131.7 2.7 %collective-permute-start.35 = (bf16[128,1024]{1,0:T(8,128)(2,1)S(1)}, bf16[128,1024]{1,0:T(8,128)(2,1)S(1)}, u32[]{:S(2)}, u32[]{:S(2)}) collective-permute-start(bf16[128,1024]{1,0:T(8,128)(2,1)S(1)} %convolution_convert_fusion), channel_id=1, source_target_pairs={{0,6},{1,7},{2,0},{3,1},{4,2},{5,3},{6,4},{7,5},{8,14},{9,15},{10,... | collective-permute-start | bytes 786440 | tf_op jit(solution)/shard_map/ppermute | solution.py:46
  134.9 3.0 %collective-permute-done.30 = bf16[128,1024]{1,0:T(8,128)(2,1)S(1)} collective-permute-done((bf16[128,1024]{1,0:T(8,128)(2,1)S(1)}, bf16[128,1024]{1,0:T(8,128)(2,1)S(1)}, u32[]{:S(2)}, u32[]{:S(2)}) %collective-permute-start.30) | collective-permute-done | bytes 262176 | tf_op jit(solution)/shard_map/ppermute | solution.py:46
  139.3 2.4 %collective-permute-start.32 = (bf16[128,1024]{1,0:T(8,128)(2,1)S(1)}, bf16[128,1024]{1,0:T(8,128)(2,1)S(1)}, u32[]{:S(2)}, u32[]{:S(2)}) collective-permute-start(bf16[128,1024]{1,0:T(8,128)(2,1)S(1)} %convolution_convert_fusion.2), channel_id=1, source_target_pairs={{0,6},{1,7},{2,0},{3,1},{4,2},{5,3},{6,4},{7,5},{8,14},{9,15},{10,... | collective-permute-start | bytes 786440 | tf_op jit(solution)/shard_map/ppermute | solution.py:46
  142.8 2.7 %collective-permute-done.33 = bf16[128,1024]{1,0:T(8,128)(2,1)S(1)} collective-permute-done((bf16[128,1024]{1,0:T(8,128)(2,1)S(1)}, bf16[128,1024]{1,0:T(8,128)(2,1)S(1)}, u32[]{:S(2)}, u32[]{:S(2)}) %collective-permute-start.33) | collective-permute-done | bytes 262176 | tf_op jit(solution)/shard_map/ppermute | solution.py:46
  145.5 8.3 %collective-permute-done.31 = bf16[128,1024]{1,0:T(8,128)(2,1)S(1)} collective-permute-done((bf16[128,1024]{1,0:T(8,128)(2,1)S(1)}, bf16[128,1024]{1,0:T(8,128)(2,1)S(1)}, u32[]{:S(2)}, u32[]{:S(2)}) %collective-permute-start.31) | collective-permute-done | bytes 262176 | tf_op jit(solution)/shard_map/ppermute | solution.py:46
  155.0 1.0 collective-permute-done.37
  (102 shorter events, 23.7 us)
Async XLA Ops:
  1.0 2.5 %collective-permute-start = (bf16[128,512]{1,0:T(8,128)(2,1)S(1)}, bf16[128,512]{1,0:T(8,128)(2,1)S(1)}, u32[]{:S(2)}, u32[]{:S(2)}) collective-permute-start(bf16[128,512]{1,0:T(8,128)(2,1)S(1)} %get-tuple-element.82), channel_id=1, source_target_pairs={{0,8},{8,0},{16,24},{24,16},{32,40},{40,32},{48,56},{56,48},{64,72... | collective-permute-start | bytes 393224 | tf_op jit(solution)/shard_map/ppermute | solution.py:42
  7.1 17.1 %collective-permute-start.4 = (bf16[512,1536]{1,0:T(8,128)(2,1)}, bf16[512,1536]{1,0:T(8,128)(2,1)S(1)}, u32[]{:S(2)}, u32[]{:S(2)}) collective-permute-start(bf16[512,1536]{1,0:T(8,128)(2,1)} %get-tuple-element.45), channel_id=1, source_target_pairs={{0,8},{8,0},{16,24},{24,16},{32,40},{40,32},{48,56},{56,48},{64,72... | collective-permute-start | bytes 4718600 | tf_op jit(solution)/shard_map/ppermute | solution.py:42
  7.5 9.4 %collective-permute-start.5 = (bf16[128,1024]{1,0:T(8,128)(2,1)S(1)}, bf16[128,1024]{1,0:T(8,128)(2,1)S(1)}, u32[]{:S(2)}, u32[]{:S(2)}) collective-permute-start(bf16[128,1024]{1,0:T(8,128)(2,1)S(1)} %pad_maximum_fusion.4), channel_id=1, source_target_pairs={{0,4},{1,5},{2,6},{3,7},{4,0},{5,1},{6,2},{7,3},{8,12},{9,13},{10,... | collective-permute-start | bytes 786440 | tf_op jit(solution)/shard_map/ppermute | solution.py:46
  10.5 12.4 %collective-permute-start.3 = (bf16[128,1024]{1,0:T(8,128)(2,1)S(1)}, bf16[128,1024]{1,0:T(8,128)(2,1)S(1)}, u32[]{:S(2)}, u32[]{:S(2)}) collective-permute-start(bf16[128,1024]{1,0:T(8,128)(2,1)S(1)} %pad_maximum_fusion.4), channel_id=1, source_target_pairs={{0,2},{1,3},{2,4},{3,5},{4,6},{5,7},{6,0},{7,1},{8,10},{9,11},{10,... | collective-permute-start | bytes 786440 | tf_op jit(solution)/shard_map/ppermute | solution.py:46
  10.9 13.3 %collective-permute-start.2 = (bf16[128,1024]{1,0:T(8,128)(2,1)S(1)}, bf16[128,1024]{1,0:T(8,128)(2,1)S(1)}, u32[]{:S(2)}, u32[]{:S(2)}) collective-permute-start(bf16[128,1024]{1,0:T(8,128)(2,1)S(1)} %pad_maximum_fusion.4), channel_id=1, source_target_pairs={{0,6},{1,7},{2,0},{3,1},{4,2},{5,3},{6,4},{7,5},{8,14},{9,15},{10,... | collective-permute-start | bytes 786440 | tf_op jit(solution)/shard_map/ppermute | solution.py:46
  13.2 11.0 %collective-permute-start.1 = (bf16[128,1024]{1,0:T(8,128)(2,1)S(1)}, bf16[128,1024]{1,0:T(8,128)(2,1)S(1)}, u32[]{:S(2)}, u32[]{:S(2)}) collective-permute-start(bf16[128,1024]{1,0:T(8,128)(2,1)S(1)} %pad_maximum_fusion.4), channel_id=1, source_target_pairs={{0,1},{1,0},{2,3},{3,2},{4,5},{5,4},{6,7},{7,6},{8,9},{9,8},{10,11... | collective-permute-start | bytes 786440 | tf_op jit(solution)/shard_map/ppermute | solution.py:46
  16.9 22.8 %collective-permute-start.9 = (bf16[512,1536]{1,0:T(8,128)(2,1)}, bf16[512,1536]{1,0:T(8,128)(2,1)S(1)}, u32[]{:S(2)}, u32[]{:S(2)}) collective-permute-start(bf16[512,1536]{1,0:T(8,128)(2,1)} %get-tuple-element.44), channel_id=1, source_target_pairs={{0,8},{8,0},{16,24},{24,16},{32,40},{40,32},{48,56},{56,48},{64,72... | collective-permute-start | bytes 4718600 | tf_op jit(solution)/shard_map/ppermute | solution.py:42
  22.9 11.4 %collective-permute-start.8 = (bf16[128,1024]{1,0:T(8,128)(2,1)S(1)}, bf16[128,1024]{1,0:T(8,128)(2,1)S(1)}, u32[]{:S(2)}, u32[]{:S(2)}) collective-permute-start(bf16[128,1024]{1,0:T(8,128)(2,1)S(1)} %collective-permute-done.5), channel_id=1, source_target_pairs={{0,1},{1,0},{2,3},{3,2},{4,5},{5,4},{6,7},{7,6},{8,9},{9,8},{10,11... | collective-permute-start | bytes 786440 | tf_op jit(solution)/shard_map/ppermute | solution.py:46
  24.2 10.2 %collective-permute-start.7 = (bf16[128,1024]{1,0:T(8,128)(2,1)S(1)}, bf16[128,1024]{1,0:T(8,128)(2,1)S(1)}, u32[]{:S(2)}, u32[]{:S(2)}) collective-permute-start(bf16[128,1024]{1,0:T(8,128)(2,1)S(1)} %collective-permute-done.1), channel_id=1, source_target_pairs={{0,2},{1,3},{2,4},{3,5},{4,6},{5,7},{6,0},{7,1},{8,10},{9,11},{10,... | collective-permute-start | bytes 786440 | tf_op jit(solution)/shard_map/ppermute | solution.py:46
  25.3 9.2 %collective-permute-start.6 = (bf16[128,1024]{1,0:T(8,128)(2,1)S(1)}, bf16[128,1024]{1,0:T(8,128)(2,1)S(1)}, u32[]{:S(2)}, u32[]{:S(2)}) collective-permute-start(bf16[128,1024]{1,0:T(8,128)(2,1)S(1)} %collective-permute-done.1), channel_id=1, source_target_pairs={{0,6},{1,7},{2,0},{3,1},{4,2},{5,3},{6,4},{7,5},{8,14},{9,15},{10,... | collective-permute-start | bytes 786440 | tf_op jit(solution)/shard_map/ppermute | solution.py:46
  27.7 1.4 copy-start.1
  29.8 23.6 %collective-permute-start.10 = (bf16[640,768]{1,0:T(8,128)(2,1)S(1)}, bf16[640,768]{1,0:T(8,128)(2,1)S(1)}, u32[]{:S(2)}, u32[]{:S(2)}) collective-permute-start(bf16[640,768]{1,0:T(8,128)(2,1)S(1)} %add_convert_fusion.2), channel_id=1, source_target_pairs={{0,96},{8,104},{16,112},{24,120},{32,0},{40,8},{48,16},{56,24},{64... | collective-permute-start | bytes 2949128 | tf_op jit(solution)/shard_map/ppermute | solution.py:42
  34.4 22.9 %collective-permute-start.11 = (bf16[640,768]{1,0:T(8,128)(2,1)S(1)}, bf16[640,768]{1,0:T(8,128)(2,1)S(1)}, u32[]{:S(2)}, u32[]{:S(2)}) collective-permute-start(bf16[640,768]{1,0:T(8,128)(2,1)S(1)} %add_convert_fusion.1), channel_id=1, source_target_pairs={{0,32},{8,40},{16,48},{24,56},{32,64},{40,72},{48,80},{56,88},{64,... | collective-permute-start | bytes 2949128 | tf_op jit(solution)/shard_map/ppermute | solution.py:42
  35.5 3.3 %copy-start = (bf16[512,1536]{1,0:T(8,128)(2,1)S(1)}, bf16[512,1536]{1,0:T(8,128)(2,1)}, u32[]{:S(2)}) copy-start(bf16[512,1536]{1,0:T(8,128)(2,1)} %get-tuple-element.44) | copy-start | bytes 4718596
  35.5 34.5 %collective-permute-start.16 = (bf16[384,768]{1,0:T(8,128)(2,1)S(1)}, bf16[384,768]{1,0:T(8,128)(2,1)S(1)}, u32[]{:S(2)}, u32[]{:S(2)}) collective-permute-start(bf16[384,768]{1,0:T(8,128)(2,1)S(1)} %fusion.2), channel_id=1, source_target_pairs={{0,16},{8,24},{16,0},{24,8},{32,48},{40,56},{48,32},{56,40},{64,80... | collective-permute-start | bytes 1769480 | tf_op jit(solution)/shard_map/ppermute | solution.py:42
  40.2 29.7 %collective-permute-start.15 = (bf16[384,768]{1,0:T(8,128)(2,1)S(1)}, bf16[384,768]{1,0:T(8,128)(2,1)S(1)}, u32[]{:S(2)}, u32[]{:S(2)}) collective-permute-start(bf16[384,768]{1,0:T(8,128)(2,1)S(1)} %fusion.1), channel_id=1, source_target_pairs={{0,16},{8,24},{16,0},{24,8},{32,48},{40,56},{48,32},{56,40},{64,80... | collective-permute-start | bytes 1769480 | tf_op jit(solution)/shard_map/ppermute | solution.py:42
  58.5 10.2 %collective-permute-start.13 = (bf16[640,384]{1,0:T(8,128)(2,1)S(1)}, bf16[640,384]{1,0:T(8,128)(2,1)S(1)}, u32[]{:S(2)}, u32[]{:S(2)}) collective-permute-start(bf16[640,384]{1,0:T(8,128)(2,1)S(1)} %get-tuple-element.69), channel_id=1, source_target_pairs={{0,96},{8,104},{16,112},{24,120},{32,0},{40,8},{48,16},{56,24},{64... | collective-permute-start | bytes 1474568 | tf_op jit(solution)/shard_map/ppermute | solution.py:42
  58.5 11.4 %collective-permute-start.12 = (bf16[640,384]{1,0:T(8,128)(2,1)S(1)}, bf16[640,384]{1,0:T(8,128)(2,1)S(1)}, u32[]{:S(2)}, u32[]{:S(2)}) collective-permute-start(bf16[640,384]{1,0:T(8,128)(2,1)S(1)} %get-tuple-element.71), channel_id=1, source_target_pairs={{0,32},{8,40},{16,48},{24,56},{32,64},{40,72},{48,80},{56,88},{64,... | collective-permute-start | bytes 1474568 | tf_op jit(solution)/shard_map/ppermute | solution.py:42
  69.9 7.6 %copy-start.4 = (bf16[640,384]{1,0:T(8,128)(2,1)}, bf16[640,384]{1,0:T(8,128)(2,1)S(1)}, u32[]{:S(2)}) copy-start(bf16[640,384]{1,0:T(8,128)(2,1)S(1)} %collective-permute-done.12.refs_4_) | copy-start | bytes 1474564
  70.1 5.6 %collective-permute-start.17 = (bf16[2,192,384]{2,1,0:T(8,128)(2,1)S(1)}, bf16[2,192,384]{2,1,0:T(8,128)(2,1)S(1)}, u32[]{:S(2)}, u32[]{:S(2)}) collective-permute-start(bf16[2,192,384]{2,1,0:T(8,128)(2,1)S(1)} %pad_maximum_fusion.1), channel_id=1, source_target_pairs={{0,96},{8,104},{16,112},{24,120},{32,0},{40,8},{48,16},{56,24},{64... | collective-permute-start | bytes 884744 | tf_op jit(solution)/shard_map/ppermute | solution.py:42
  70.5 6.9 %collective-permute-start.18 = (bf16[2,192,384]{2,1,0:T(8,128)(2,1)S(1)}, bf16[2,192,384]{2,1,0:T(8,128)(2,1)S(1)}, u32[]{:S(2)}, u32[]{:S(2)}) collective-permute-start(bf16[2,192,384]{2,1,0:T(8,128)(2,1)S(1)} %pad_maximum_fusion.2), channel_id=1, source_target_pairs={{0,32},{8,40},{16,48},{24,56},{32,64},{40,72},{48,80},{56,88},{64,... | collective-permute-start | bytes 884744 | tf_op jit(solution)/shard_map/ppermute | solution.py:42
  75.8 5.7 %collective-permute-start.20 = (bf16[192,384]{1,0:T(8,128)(2,1)S(1)}, bf16[192,384]{1,0:T(8,128)(2,1)S(1)}, u32[]{:S(2)}, u32[]{:S(2)}) collective-permute-start(bf16[192,384]{1,0:T(8,128)(2,1)S(1)} %fusion.40), channel_id=1, source_target_pairs={{0,96},{8,104},{16,112},{24,120},{32,0},{40,8},{48,16},{56,24},{64... | collective-permute-start | bytes 442376 | tf_op jit(solution)/shard_map/ppermute | solution.py:42
  77.5 5.4 %collective-permute-start.19 = (bf16[192,384]{1,0:T(8,128)(2,1)S(1)}, bf16[192,384]{1,0:T(8,128)(2,1)S(1)}, u32[]{:S(2)}, u32[]{:S(2)}) collective-permute-start(bf16[192,384]{1,0:T(8,128)(2,1)S(1)} %fusion.43), channel_id=1, source_target_pairs={{0,32},{8,40},{16,48},{24,56},{32,64},{40,72},{48,80},{56,88},{64,... | collective-permute-start | bytes 442376 | tf_op jit(solution)/shard_map/ppermute | solution.py:42
  78.0 9.3 %collective-permute-start.14 = (bf16[640,384]{1,0:T(8,128)(2,1)S(1)}, bf16[640,384]{1,0:T(8,128)(2,1)S(1)}, u32[]{:S(2)}, u32[]{:S(2)}) collective-permute-start(bf16[640,384]{1,0:T(8,128)(2,1)S(1)} %add_convert_fusion.3), channel_id=1, source_target_pairs={{0,16},{8,24},{16,0},{24,8},{32,48},{40,56},{48,32},{56,40},{64,80... | collective-permute-start | bytes 1474568 | tf_op jit(solution)/shard_map/ppermute | solution.py:42
  83.0 9.7 %copy-start.3 = (bf16[1024,512]{1,0:T(8,128)(2,1)S(1)}, bf16[1024,512]{1,0:T(8,128)(2,1)}, u32[]{:S(2)}) copy-start(bf16[1024,512]{1,0:T(8,128)(2,1)} %param.13) | copy-start | bytes 3145732
  87.2 0.8 copy-start.5
  92.8 15.4 %collective-permute-start.22 = (bf16[1024,512]{1,0:T(8,128)(2,1)S(1)}, bf16[1024,512]{1,0:T(8,128)(2,1)S(1)}, u32[]{:S(2)}, u32[]{:S(2)}) collective-permute-start(bf16[1024,512]{1,0:T(8,128)(2,1)S(1)} %copy-done.3), channel_id=1, source_target_pairs={{0,8},{8,0},{16,24},{24,16},{32,40},{40,32},{48,56},{56,48},{64,72... | collective-permute-start | bytes 3145736 | tf_op jit(solution)/shard_map/ppermute | solution.py:42
  100.1 2.5 %collective-permute-start.21 = (f32[26,8,128]{2,1,0:T(8,128)}, f32[26,8,128]{2,1,0:T(8,128)S(1)}, u32[]{:S(2)}, u32[]{:S(2)}) collective-permute-start(f32[26,8,128]{2,1,0:T(8,128)} %get-tuple-element.60.mine_ref), channel_id=1, source_target_pairs={{0,8},{8,0},{16,24},{24,16},{32,40},{40,32},{48,56},{56,48},{64,72... | collective-permute-start | bytes 319496 | tf_op jit(solution)/shard_map/ppermute | solution.py:42
  102.6 0.6 copy-start.6
  108.1 3.2 %copy-start.2 = (bf16[1024,128]{1,0:T(8,128)(2,1)S(1)}, bf16[1024,128]{1,0:T(8,128)(2,1)}, u32[]{:S(2)}) copy-start(bf16[1024,128]{1,0:T(8,128)(2,1)} %filtered.1) | copy-start | bytes 786436
  108.1 12.5 %collective-permute-start.24 = (bf16[1024,128]{1,0:T(8,128)(2,1)}, bf16[1024,128]{1,0:T(8,128)(2,1)S(1)}, u32[]{:S(2)}, u32[]{:S(2)}) collective-permute-start(bf16[1024,128]{1,0:T(8,128)(2,1)} %filtered.1), channel_id=1, source_target_pairs={{0,64},{8,72},{16,80},{24,88},{32,96},{40,104},{48,112},{56,120},{... | collective-permute-start | bytes 786440 | tf_op jit(solution)/shard_map/ppermute | solution.py:42
  108.8 9.2 %collective-permute-start.23 = (bf16[1024,128]{1,0:T(8,128)(2,1)}, bf16[1024,128]{1,0:T(8,128)(2,1)S(1)}, u32[]{:S(2)}, u32[]{:S(2)}) collective-permute-start(bf16[1024,128]{1,0:T(8,128)(2,1)} %filtered.1), channel_id=1, source_target_pairs={{0,16},{8,24},{16,0},{24,8},{32,48},{40,56},{48,32},{56,40},{64,80... | collective-permute-start | bytes 786440 | tf_op jit(solution)/shard_map/ppermute | solution.py:42
  111.4 12.4 %collective-permute-start.26 = (bf16[1024,128]{1,0:T(8,128)(2,1)S(1)}, bf16[1024,128]{1,0:T(8,128)(2,1)S(1)}, u32[]{:S(2)}, u32[]{:S(2)}) collective-permute-start(bf16[1024,128]{1,0:T(8,128)(2,1)S(1)} %copy-done.2), channel_id=1, source_target_pairs={{0,32},{8,40},{16,48},{24,56},{32,64},{40,72},{48,80},{56,88},{64,... | collective-permute-start | bytes 786440 | tf_op jit(solution)/shard_map/ppermute | solution.py:42
  112.6 10.7 %collective-permute-start.25 = (bf16[1024,128]{1,0:T(8,128)(2,1)S(1)}, bf16[1024,128]{1,0:T(8,128)(2,1)S(1)}, u32[]{:S(2)}, u32[]{:S(2)}) collective-permute-start(bf16[1024,128]{1,0:T(8,128)(2,1)S(1)} %copy-done.2), channel_id=1, source_target_pairs={{0,96},{8,104},{16,112},{24,120},{32,0},{40,8},{48,16},{56,24},{64... | collective-permute-start | bytes 786440 | tf_op jit(solution)/shard_map/ppermute | solution.py:42
  118.0 11.4 %collective-permute-start.28 = (bf16[1024,128]{1,0:T(8,128)(2,1)S(1)}, bf16[1024,128]{1,0:T(8,128)(2,1)S(1)}, u32[]{:S(2)}, u32[]{:S(2)}) collective-permute-start(bf16[1024,128]{1,0:T(8,128)(2,1)S(1)} %collective-permute-done.23), channel_id=1, source_target_pairs={{0,32},{8,40},{16,48},{24,56},{32,64},{40,72},{48,80},{56,88},{64,... | collective-permute-start | bytes 786440 | tf_op jit(solution)/shard_map/ppermute | solution.py:42
  119.1 7.9 %collective-permute-start.27 = (bf16[1024,128]{1,0:T(8,128)(2,1)S(1)}, bf16[1024,128]{1,0:T(8,128)(2,1)S(1)}, u32[]{:S(2)}, u32[]{:S(2)}) collective-permute-start(bf16[1024,128]{1,0:T(8,128)(2,1)S(1)} %collective-permute-done.23), channel_id=1, source_target_pairs={{0,96},{8,104},{16,112},{24,120},{32,0},{40,8},{48,16},{56,24},{64... | collective-permute-start | bytes 786440 | tf_op jit(solution)/shard_map/ppermute | solution.py:42
  120.6 8.8 %collective-permute-start.29 = (bf16[1024,128]{1,0:T(8,128)(2,1)S(1)}, bf16[1024,128]{1,0:T(8,128)(2,1)S(1)}, u32[]{:S(2)}, u32[]{:S(2)}) collective-permute-start(bf16[1024,128]{1,0:T(8,128)(2,1)S(1)} %collective-permute-done.24), channel_id=1, source_target_pairs={{0,16},{8,24},{16,0},{24,8},{32,48},{40,56},{48,32},{56,40},{64,80... | collective-permute-start | bytes 786440 | tf_op jit(solution)/shard_map/ppermute | solution.py:42
  131.4 6.5 %collective-permute-start.30 = (bf16[128,1024]{1,0:T(8,128)(2,1)S(1)}, bf16[128,1024]{1,0:T(8,128)(2,1)S(1)}, u32[]{:S(2)}, u32[]{:S(2)}) collective-permute-start(bf16[128,1024]{1,0:T(8,128)(2,1)S(1)} %convolution_convert_fusion.4), channel_id=1, source_target_pairs={{0,1},{1,0},{2,3},{3,2},{4,5},{5,4},{6,7},{7,6},{8,9},{9,8},{10,11... | collective-permute-start | bytes 786440 | tf_op jit(solution)/shard_map/ppermute | solution.py:46
  131.7 9.9 %collective-permute-start.34 = (bf16[128,1024]{1,0:T(8,128)(2,1)S(1)}, bf16[128,1024]{1,0:T(8,128)(2,1)S(1)}, u32[]{:S(2)}, u32[]{:S(2)}) collective-permute-start(bf16[128,1024]{1,0:T(8,128)(2,1)S(1)} %convolution_convert_fusion.1), channel_id=1, source_target_pairs={{0,2},{1,3},{2,4},{3,5},{4,6},{5,7},{6,0},{7,1},{8,10},{9,11},{10,... | collective-permute-start | bytes 786440 | tf_op jit(solution)/shard_map/ppermute | solution.py:46
  131.7 9.9 %collective-permute-start.35 = (bf16[128,1024]{1,0:T(8,128)(2,1)S(1)}, bf16[128,1024]{1,0:T(8,128)(2,1)S(1)}, u32[]{:S(2)}, u32[]{:S(2)}) collective-permute-start(bf16[128,1024]{1,0:T(8,128)(2,1)S(1)} %convolution_convert_fusion), channel_id=1, source_target_pairs={{0,6},{1,7},{2,0},{3,1},{4,2},{5,3},{6,4},{7,5},{8,14},{9,15},{10,... | collective-permute-start | bytes 786440 | tf_op jit(solution)/shard_map/ppermute | solution.py:46
  138.4 7.2 %collective-permute-start.33 = (bf16[128,1024]{1,0:T(8,128)(2,1)S(1)}, bf16[128,1024]{1,0:T(8,128)(2,1)S(1)}, u32[]{:S(2)}, u32[]{:S(2)}) collective-permute-start(bf16[128,1024]{1,0:T(8,128)(2,1)S(1)} %fusion.11), channel_id=1, source_target_pairs={{0,4},{1,5},{2,6},{3,7},{4,0},{5,1},{6,2},{7,3},{8,12},{9,13},{10,... | collective-permute-start | bytes 786440 | tf_op jit(solution)/shard_map/ppermute | solution.py:46
  139.0 14.8 %collective-permute-start.31 = (bf16[128,1024]{1,0:T(8,128)(2,1)S(1)}, bf16[128,1024]{1,0:T(8,128)(2,1)S(1)}, u32[]{:S(2)}, u32[]{:S(2)}) collective-permute-start(bf16[128,1024]{1,0:T(8,128)(2,1)S(1)} %convolution_convert_fusion.3), channel_id=1, source_target_pairs={{0,2},{1,3},{2,4},{3,5},{4,6},{5,7},{6,0},{7,1},{8,10},{9,11},{10,... | collective-permute-start | bytes 786440 | tf_op jit(solution)/shard_map/ppermute | solution.py:46
  139.3 14.5 %collective-permute-start.32 = (bf16[128,1024]{1,0:T(8,128)(2,1)S(1)}, bf16[128,1024]{1,0:T(8,128)(2,1)S(1)}, u32[]{:S(2)}, u32[]{:S(2)}) collective-permute-start(bf16[128,1024]{1,0:T(8,128)(2,1)S(1)} %convolution_convert_fusion.2), channel_id=1, source_target_pairs={{0,6},{1,7},{2,0},{3,1},{4,2},{5,3},{6,4},{7,5},{8,14},{9,15},{10,... | collective-permute-start | bytes 786440 | tf_op jit(solution)/shard_map/ppermute | solution.py:46
  142.1 11.7 %collective-permute-start.36 = (bf16[128,1024]{1,0:T(8,128)(2,1)S(1)}, bf16[128,1024]{1,0:T(8,128)(2,1)S(1)}, u32[]{:S(2)}, u32[]{:S(2)}) collective-permute-start(bf16[128,1024]{1,0:T(8,128)(2,1)S(1)} %fusion.10), channel_id=1, source_target_pairs={{0,1},{1,0},{2,3},{3,2},{4,5},{5,4},{6,7},{7,6},{8,9},{9,8},{10,11... | collective-permute-start | bytes 786440 | tf_op jit(solution)/shard_map/ppermute | solution.py:46
  154.4 1.6 %collective-permute-start.37 = (bf16[128,512]{1,0:T(8,128)(2,1)S(1)}, bf16[128,512]{1,0:T(8,128)(2,1)S(1)}, u32[]{:S(2)}, u32[]{:S(2)}) collective-permute-start(bf16[128,512]{1,0:T(8,128)(2,1)S(1)} %get-tuple-element.80), channel_id=1, source_target_pairs={{0,8},{8,0},{16,24},{24,16},{32,40},{40,32},{48,56},{56,48},{64,72... | collective-permute-start | bytes 393224 | tf_op jit(solution)/shard_map/ppermute | solution.py:42

commit v6 on v5

--- a/solution.py
+++ b/solution.py
@@ -180,8 +180,8 @@
     term_refs = [refs[start : start + count] for start, count in zip(starts, counts)]
     query_ref, gate_ref, edge_ref = refs[flat : flat + 3]
     raw_refs = refs[flat + 3 : flat + 6]
-    key_ref, value_ref = refs[flat + 6 :]
-    length = gate_ref.shape[0] // BLOCKS
+    key_ref, value_ref, query_work, gate_work = refs[flat + 6 :]
+    length = gate_ref.shape[0]
     order = rates_ref.shape[0]
     rows = lax.broadcasted_iota(jnp.int32, (length, LANES), 0)
     for refs_here, group in zip(term_refs, groups):
@@ -200,20 +200,22 @@
                     moved = jnp.where(rows >= back, pltpu.roll(raw, back, 0), 0.0)
                     total = total + taps_ref[f, back : back + 1, :] * moved
                 mixed.append(total)
-            query_ref[there, :] = mixed[0]
+            query_work[spot] = mixed[0]
             key_ref[there, :] = mixed[1]
             value_ref[there, :] = mixed[2]
-            gate_ref[there, :] = mixed[1] * mixed[2]
+            gate_work[spot] = mixed[1] * mixed[2]
+    gate_ref[...] = jnp.transpose(gate_work[...], (1, 0, 2))
+    query_ref[...] = jnp.transpose(query_work[...], (1, 0, 2))
     decay = [
         jnp.broadcast_to(jnp.exp(-rates_ref[n : n + 1, :]), (BLOCKS, LANES)) for n in range(order)
     ]
 
     def step(r, states):
-        gate = every(gate_ref, r, length)
+        gate = gate_ref[r]
         return tuple(decay[n] * states[n] + gate for n in range(order))
 
     states = lax.fori_loop(
-        2, length, step, tuple(jnp.zeros((BLOCKS, LANES), F32) for _ in range(order)), unroll=6
+        2, length, step, tuple(jnp.zeros((BLOCKS, LANES), F32) for _ in range(order)), unroll=14
     )
     for n in range(order):
         edge_ref[n] = states[n]
@@ -228,8 +230,8 @@
             at += 1
 
 
-def filter_kernel(where_ref, taps_ref, rates_ref, weights_ref, skip_ref, mine_ref, theirs_ref, query_ref, gate_ref, out_ref, work):
-    length = gate_ref.shape[0] // BLOCKS
+def filter_kernel(where_ref, taps_ref, rates_ref, weights_ref, skip_ref, mine_ref, theirs_ref, query_ref, gate_ref, out_ref, work, turned):
+    length = gate_ref.shape[0]
     order = rates_ref.shape[0]
     core = where_ref[2]
     first = core == 0
@@ -278,22 +280,22 @@
         terms = [weights[n] * states[n] for n in range(order)] + [skip * gate]
         while len(terms) > 1:
             terms = [a + b for a, b in zip(terms[::2], terms[1::2])] + terms[len(terms) // 2 * 2 :]
-        work[pl.ds(r, BLOCKS, stride=length), :] = query * terms[0]
+        work[r] = query * terms[0]
         return states
 
-    states = advance(0, tuple(states), gate0, every(query_ref, 0, length) + query0)
-    states = advance(1, states, gate1, every(query_ref, 1, length) + query1)
+    states = advance(0, tuple(states), gate0, query_ref[0] + query0)
+    states = advance(1, states, gate1, query_ref[1] + query1)
     lax.fori_loop(
         2,
         length,
-        lambda r, states: advance(r, states, every(gate_ref, r, length), every(query_ref, r, length)),
+        lambda r, states: advance(r, states, gate_ref[r], query_ref[r]),
         states,
-        unroll=6,
+        unroll=14,
     )
+    turned[...] = jnp.transpose(work[...], (1, 0, 2))
     for place, (dy, dx) in enumerate(PLACES):
         spot = ((where_ref[3] + dy) & (Y - 1)) * XL + ((where_ref[4] + dx) & (XL - 1))
-        there = pl.ds(pl.multiple_of(spot * length, length), length)
-        out_ref[place * length : (place + 1) * length, :] = work[there, :].astype(BF)
+        out_ref[place * length : (place + 1) * length, :] = turned[spot].astype(BF)
 
 
 def own_lanes(shape):
@@ -304,7 +306,7 @@
     tokens = sum(len(group) for group in blocks) * blocks_length(groups[0][0], blocks[0])
     flat = [term for terms in groups for term in terms]
     edges = (rates.shape[0] + 10, BLOCKS, LANES)
-    tall = jax.ShapeDtypeStruct((tokens, LANES), F32)
+    tall = jax.ShapeDtypeStruct((tokens // BLOCKS, BLOCKS, LANES), F32)
     return pl.pallas_call(
         lambda *refs: local_kernel(blocks, [len(terms) for terms in groups], *refs),
         out_shape=(tall, tall, jax.ShapeDtypeStruct(edges, F32)),
@@ -314,7 +316,8 @@
             in_specs=[own_lanes(taps.shape[:-1] + (LANES,)), own_lanes(rates.shape[:-1] + (LANES,))]
             + [whole(term.shape) for term in flat],
             out_specs=[whole(tall.shape), whole(tall.shape), whole(edges)],
-            scratch_shapes=[pltpu.VMEM((tokens, LANES), F32)] * 5,
+            scratch_shapes=[pltpu.VMEM((tokens, LANES), F32)] * 5
+            + [pltpu.VMEM((BLOCKS, tokens // BLOCKS, LANES), F32)] * 2,
         ),
         name="local_part",
     )(where, taps, rates, *flat)
@@ -327,14 +330,14 @@
 def filtered(where, taps, rates, weights, skip, mine, theirs, query, gate):
     return pl.pallas_call(
         filter_kernel,
-        out_shape=jax.ShapeDtypeStruct(gate.shape, BF),
+        out_shape=jax.ShapeDtypeStruct((gate.shape[0] * BLOCKS, LANES), BF),
         grid_spec=pltpu.PrefetchScalarGridSpec(
             num_scalar_prefetch=1,
             grid=(1,),
             in_specs=[own_lanes(array.shape[:-1] + (LANES,)) for array in (taps, rates, weights, skip)]
             + [whole(array.shape) for array in (mine, theirs, query, gate)],
-            out_specs=whole(gate.shape),
-            scratch_shapes=[pltpu.VMEM(gate.shape, F32)],
+            out_specs=whole((gate.shape[0] * BLOCKS, LANES)),
+            scratch_shapes=[pltpu.VMEM(gate.shape, F32), pltpu.VMEM((BLOCKS, gate.shape[0], LANES), F32)],
         ),
         name="filtered",
     )(where, taps, rates, weights, skip, mine, theirs, query, gate)

time: 157 us -> 156 us (level)
  no operation moved by 1% of the time
where the time goes in v6:
time: 156 us
  waiting for transfers between devices  66.3 us (42%)
  starting transfers between devices  55 us (35%)
  matrix products  13.1 us (8%)
  Pallas kernels  12.3 us (8%)
  local copies, waits for them, and re-layouts  5.13 us (3%)
  other arithmetic  3.49 us (2%)
    ppermute x24, waiting for transfers between devices, tok_send(): return lax.ppermute(value, 'tok', perm)  45.3 us
    ppermute x24, starting transfers between devices, tok_send(): return lax.ppermute(value, 'tok', perm)  37.1 us
    ppermute x14, waiting for transfers between devices, ch_send(): return lax.ppermute(value, 'ch', perm)  21 us
    ppermute x14, starting transfers between devices, ch_send(): return lax.ppermute(value, 'ch', perm)  17.9 us
    dot_general x8, matrix products, product(): jnp.dot(rows[:, depth:], other[part][:, columns], preferred_element_type=...  4.68 us
    dot_general x8, matrix products, product(): jnp.dot(rows[:, :depth], own[part][:, columns], preferred_element_type=F32)  4.67 us
    pallas_call x1, Pallas kernels, local_part(): pl.pallas_call(lambda *refs: local_kernel(blocks, [len(terms) for terms i...  4.56 us
    pallas_call x1, Pallas kernels, filtered(): pl.pallas_call(filter_kernel, out_shape=jax.ShapeDtypeStruct((gate.shape[...  4.19 us
  transfers between devices with their start and end apart: 38, of which 20 were waited for; matrix products, arithmetic and copies ran while one was open for 10% of the time, Pallas kernels for 3%

profile of v6, /device:TPU:1, one launch (start us, length us, event | category | flops | bytes accessed | tf_op | source)
XLA Modules:
  0.0 155.9 jit_solution(9341374019745226606)
XLA Ops:
  0.0 1.0 constant_dynamic-slice_fusion.1
  1.0 1.5 collective-permute-start
  2.5 1.0 collective-permute-done
  3.5 3.6 %by_target.1 = (bf16[512,1536]{1,0:T(8,128)(2,1)}, bf16[512,1536]{1,0:T(8,128)(2,1)}) custom-call(bf16[512,3072]{1,0:T(8,128)(2,1)} %refs_0_), custom_call_target="tpu_custom_call" | custom-call | tf_op jit(solution)/shard_map/by_target/pallas_call | solution.py:87
  7.5 3.0 %collective-permute-start.5 = (bf16[128,1024]{1,0:T(8,128)(2,1)S(1)}, bf16[128,1024]{1,0:T(8,128)(2,1)S(1)}, u32[]{:S(2)}, u32[]{:S(2)}) collective-permute-start(bf16[128,1024]{1,0:T(8,128)(2,1)S(1)} %pad_maximum_fusion.4), channel_id=1, source_target_pairs={{0,4},{1,5},{2,6},{3,7},{4,0},{5,1},{6,2},{7,3},{8,12},{9,13},{10,... | collective-permute-start | bytes 786440 | tf_op jit(solution)/shard_map/ppermute | solution.py:46
  10.9 2.3 %collective-permute-start.2 = (bf16[128,1024]{1,0:T(8,128)(2,1)S(1)}, bf16[128,1024]{1,0:T(8,128)(2,1)S(1)}, u32[]{:S(2)}, u32[]{:S(2)}) collective-permute-start(bf16[128,1024]{1,0:T(8,128)(2,1)S(1)} %pad_maximum_fusion.4), channel_id=1, source_target_pairs={{0,6},{1,7},{2,0},{3,1},{4,2},{5,3},{6,4},{7,5},{8,14},{9,15},{10,... | collective-permute-start | bytes 786440 | tf_op jit(solution)/shard_map/ppermute | solution.py:46
  13.2 1.2 collective-permute-start.1
  14.5 2.5 %collective-permute-done.5 = bf16[128,1024]{1,0:T(8,128)(2,1)S(1)} collective-permute-done((bf16[128,1024]{1,0:T(8,128)(2,1)S(1)}, bf16[128,1024]{1,0:T(8,128)(2,1)S(1)}, u32[]{:S(2)}, u32[]{:S(2)}) %collective-permute-start.5) | collective-permute-done | bytes 262176 | tf_op jit(solution)/shard_map/ppermute | solution.py:46
  16.9 1.5 collective-permute-start.9
  18.4 4.6 %collective-permute-done.3 = bf16[128,1024]{1,0:T(8,128)(2,1)S(1)} collective-permute-done((bf16[128,1024]{1,0:T(8,128)(2,1)S(1)}, bf16[128,1024]{1,0:T(8,128)(2,1)S(1)}, u32[]{:S(2)}, u32[]{:S(2)}) %collective-permute-start.3) | collective-permute-done | bytes 262176 | tf_op jit(solution)/shard_map/ppermute | solution.py:46
  22.9 1.3 collective-permute-start.8
  24.2 1.0 collective-permute-start.7
  25.3 1.7 %collective-permute-start.6 = (bf16[128,1024]{1,0:T(8,128)(2,1)S(1)}, bf16[128,1024]{1,0:T(8,128)(2,1)S(1)}, u32[]{:S(2)}, u32[]{:S(2)}) collective-permute-start(bf16[128,1024]{1,0:T(8,128)(2,1)S(1)} %collective-permute-done.1), channel_id=1, source_target_pairs={{0,6},{1,7},{2,0},{3,1},{4,2},{5,3},{6,4},{7,5},{8,14},{9,15},{10,... | collective-permute-start | bytes 786440 | tf_op jit(solution)/shard_map/ppermute | solution.py:46
  29.8 3.8 %collective-permute-start.10 = (bf16[640,768]{1,0:T(8,128)(2,1)S(1)}, bf16[640,768]{1,0:T(8,128)(2,1)S(1)}, u32[]{:S(2)}, u32[]{:S(2)}) collective-permute-start(bf16[640,768]{1,0:T(8,128)(2,1)S(1)} %add_convert_fusion.2), channel_id=1, source_target_pairs={{0,96},{8,104},{16,112},{24,120},{32,0},{40,8},{48,16},{56,24},{64... | collective-permute-start | bytes 2949128 | tf_op jit(solution)/shard_map/ppermute | solution.py:42
  35.5 2.5 %collective-permute-start.16 = (bf16[384,768]{1,0:T(8,128)(2,1)S(1)}, bf16[384,768]{1,0:T(8,128)(2,1)S(1)}, u32[]{:S(2)}, u32[]{:S(2)}) collective-permute-start(bf16[384,768]{1,0:T(8,128)(2,1)S(1)} %fusion.2), channel_id=1, source_target_pairs={{0,16},{8,24},{16,0},{24,8},{32,48},{40,56},{48,32},{56,40},{64,80... | collective-permute-start | bytes 1769480 | tf_op jit(solution)/shard_map/ppermute | solution.py:42
  41.9 1.2 fusion.28
  43.1 1.2 add_convert_fusion
  44.3 9.1 %collective-permute-done.10 = bf16[640,768]{1,0:T(8,128)(2,1)S(1)} collective-permute-done((bf16[640,768]{1,0:T(8,128)(2,1)S(1)}, bf16[640,768]{1,0:T(8,128)(2,1)S(1)}, u32[]{:S(2)}, u32[]{:S(2)}) %collective-permute-start.10) | collective-permute-done | bytes 983072 | tf_op jit(solution)/shard_map/ppermute | solution.py:42
  53.4 3.9 %collective-permute-done.11 = bf16[640,768]{1,0:T(8,128)(2,1)S(1)} collective-permute-done((bf16[640,768]{1,0:T(8,128)(2,1)S(1)}, bf16[640,768]{1,0:T(8,128)(2,1)S(1)}, u32[]{:S(2)}, u32[]{:S(2)}) %collective-permute-start.11) | collective-permute-done | bytes 983072 | tf_op jit(solution)/shard_map/ppermute | solution.py:42
  57.3 1.2 add_convert_fusion.4
  58.5 1.5 collective-permute-start.12
  60.4 8.3 %collective-permute-done.13 = bf16[640,384]{1,0:T(8,128)(2,1)S(1)} collective-permute-done((bf16[640,384]{1,0:T(8,128)(2,1)S(1)}, bf16[640,384]{1,0:T(8,128)(2,1)S(1)}, u32[]{:S(2)}, u32[]{:S(2)}) %collective-permute-start.13) | collective-permute-done | bytes 491552 | tf_op jit(solution)/shard_map/ppermute | solution.py:42
  68.7 1.2 collective-permute-done.12.refs_4_
  70.5 1.2 collective-permute-start.18
  71.8 4.0 %collective-permute-done.17 = bf16[2,192,384]{2,1,0:T(8,128)(2,1)S(1)} collective-permute-done((bf16[2,192,384]{2,1,0:T(8,128)(2,1)S(1)}, bf16[2,192,384]{2,1,0:T(8,128)(2,1)S(1)}, u32[]{:S(2)}, u32[]{:S(2)}) %collective-permute-start.17) | collective-permute-done | bytes 294944 | tf_op jit(solution)/shard_map/ppermute | solution.py:42
  75.8 1.6 %collective-permute-start.20 = (bf16[192,384]{1,0:T(8,128)(2,1)S(1)}, bf16[192,384]{1,0:T(8,128)(2,1)S(1)}, u32[]{:S(2)}, u32[]{:S(2)}) collective-permute-start(bf16[192,384]{1,0:T(8,128)(2,1)S(1)} %fusion.40), channel_id=1, source_target_pairs={{0,96},{8,104},{16,112},{24,120},{32,0},{40,8},{48,16},{56,24},{64... | collective-permute-start | bytes 442376 | tf_op jit(solution)/shard_map/ppermute | solution.py:42
  78.0 2.5 %collective-permute-start.14 = (bf16[640,384]{1,0:T(8,128)(2,1)S(1)}, bf16[640,384]{1,0:T(8,128)(2,1)S(1)}, u32[]{:S(2)}, u32[]{:S(2)}) collective-permute-start(bf16[640,384]{1,0:T(8,128)(2,1)S(1)} %add_convert_fusion.3), channel_id=1, source_target_pairs={{0,16},{8,24},{16,0},{24,8},{32,48},{40,56},{48,32},{56,40},{64,80... | collective-permute-start | bytes 1474568 | tf_op jit(solution)/shard_map/ppermute | solution.py:42
  81.5 1.3 collective-permute-done.19
  83.8 3.5 %collective-permute-done.14.refs_5_ = bf16[640,384]{1,0:T(8,128)(2,1)S(1)} collective-permute-done((bf16[640,384]{1,0:T(8,128)(2,1)S(1)}, bf16[640,384]{1,0:T(8,128)(2,1)S(1)}, u32[]{:S(2)}, u32[]{:S(2)}) %collective-permute-start.14) | collective-permute-done | bytes 491552 | tf_op jit(solution)/shard_map/ppermute | solution.py:42
  88.0 4.6 %local_part.1 = (f32[128,8,128]{2,1,0:T(8,128)}, f32[128,8,128]{2,1,0:T(8,128)}, f32[26,8,128]{2,1,0:T(8,128)}) custom-call(s32[6]{0:T(128)} %stack.51.refs_0_.where_ref, f32[3,3,8192]{2,1,0:T(4,128)} %taps_ref.1, f32[16,8192]{1,0:T(8,128)} %rates_ref.1, bf16[640,384]{1,0:T(8,128)(2,1)} %get-tuple-element.54.refs_3_, bf16[640,384]{1,0:T(8,128)(2,1)} %copy-done.4, ...), custom_call_target="tpu_custom_call" | custom-call | tf_op jit(solution)/shard_map/local_part/pallas_call | solution.py:310
  92.6 7.3 %collective-permute-start.22 = (bf16[1024,512]{1,0:T(8,128)(2,1)S(1)}, bf16[1024,512]{1,0:T(8,128)(2,1)S(1)}, u32[]{:S(2)}, u32[]{:S(2)}) collective-permute-start(bf16[1024,512]{1,0:T(8,128)(2,1)S(1)} %copy-done.3), channel_id=1, source_target_pairs={{0,8},{8,0},{16,24},{24,16},{32,40},{40,32},{48,56},{56,48},{64,72... | collective-permute-start | bytes 3145736 | tf_op jit(solution)/shard_map/ppermute | solution.py:42
  100.0 2.4 %collective-permute-done.21.theirs_ref = f32[26,8,128]{2,1,0:T(8,128)S(1)} collective-permute-done((f32[26,8,128]{2,1,0:T(8,128)}, f32[26,8,128]{2,1,0:T(8,128)S(1)}, u32[]{:S(2)}, u32[]{:S(2)}) %collective-permute-start.21) | collective-permute-done | bytes 106528 | tf_op jit(solution)/shard_map/ppermute | solution.py:42
  103.1 4.2 %filtered.1 = bf16[1024,128]{1,0:T(8,128)(2,1)} custom-call(s32[6]{0:T(128)} %stack.51.refs_0_.where_ref, f32[3,3,8192]{2,1,0:T(4,128)} %taps_ref.1, f32[16,8192]{1,0:T(8,128)} %rates_ref.1, f32[16,8192]{1,0:T(8,128)} %weights_ref.1, f32[1,8192]{1,0:T(1,128)} %bitcast.45, f32[26,8,128]{2,1,0:T(8,128)} %get-tuple-element.60.mine_ref, ...), custom_call_target="tpu_custom_call" | custom-call | tf_op jit(solution)/shard_map/filtered/pallas_call | solution.py:331
  108.0 2.4 %collective-permute-start.23 = (bf16[1024,128]{1,0:T(8,128)(2,1)}, bf16[1024,128]{1,0:T(8,128)(2,1)S(1)}, u32[]{:S(2)}, u32[]{:S(2)}) collective-permute-start(bf16[1024,128]{1,0:T(8,128)(2,1)} %filtered.1), channel_id=1, source_target_pairs={{0,16},{8,24},{16,0},{24,8},{32,48},{40,56},{48,32},{56,40},{64,80... | collective-permute-start | bytes 786440 | tf_op jit(solution)/shard_map/ppermute | solution.py:42
  110.5 1.2 collective-permute-start.26
  111.7 1.5 collective-permute-start.25
  113.8 3.3 %collective-permute-done.23 = bf16[1024,128]{1,0:T(8,128)(2,1)S(1)} collective-permute-done((bf16[1024,128]{1,0:T(8,128)(2,1)}, bf16[1024,128]{1,0:T(8,128)(2,1)S(1)}, u32[]{:S(2)}, u32[]{:S(2)}) %collective-permute-start.23) | collective-permute-done | bytes 262176 | tf_op jit(solution)/shard_map/ppermute | solution.py:42
  117.1 1.1 collective-permute-start.28
  118.3 1.5 collective-permute-start.27
  119.8 2.4 %collective-permute-start.29 = (bf16[1024,128]{1,0:T(8,128)(2,1)S(1)}, bf16[1024,128]{1,0:T(8,128)(2,1)S(1)}, u32[]{:S(2)}, u32[]{:S(2)}) collective-permute-start(bf16[1024,128]{1,0:T(8,128)(2,1)S(1)} %collective-permute-done.24), channel_id=1, source_target_pairs={{0,16},{8,24},{16,0},{24,8},{32,48},{40,56},{48,32},{56,40},{64,80... | collective-permute-start | bytes 786440 | tf_op jit(solution)/shard_map/ppermute | solution.py:42
  123.0 3.1 %collective-permute-done.27 = bf16[1024,128]{1,0:T(8,128)(2,1)S(1)} collective-permute-done((bf16[1024,128]{1,0:T(8,128)(2,1)S(1)}, bf16[1024,128]{1,0:T(8,128)(2,1)S(1)}, u32[]{:S(2)}, u32[]{:S(2)}) %collective-permute-start.27) | collective-permute-done | bytes 262176 | tf_op jit(solution)/shard_map/ppermute | solution.py:42
  126.2 2.3 %collective-permute-done.28 = bf16[1024,128]{1,0:T(8,128)(2,1)S(1)} collective-permute-done((bf16[1024,128]{1,0:T(8,128)(2,1)S(1)}, bf16[1024,128]{1,0:T(8,128)(2,1)S(1)}, u32[]{:S(2)}, u32[]{:S(2)}) %collective-permute-start.28) | collective-permute-done | bytes 262176 | tf_op jit(solution)/shard_map/ppermute | solution.py:42
  130.9 2.7 %collective-permute-start.35 = (bf16[128,1024]{1,0:T(8,128)(2,1)S(1)}, bf16[128,1024]{1,0:T(8,128)(2,1)S(1)}, u32[]{:S(2)}, u32[]{:S(2)}) collective-permute-start(bf16[128,1024]{1,0:T(8,128)(2,1)S(1)} %convolution_convert_fusion), channel_id=1, source_target_pairs={{0,6},{1,7},{2,0},{3,1},{4,2},{5,3},{6,4},{7,5},{8,14},{9,15},{10,... | collective-permute-start | bytes 786440 | tf_op jit(solution)/shard_map/ppermute | solution.py:46
  134.0 3.0 %collective-permute-done.30 = bf16[128,1024]{1,0:T(8,128)(2,1)S(1)} collective-permute-done((bf16[128,1024]{1,0:T(8,128)(2,1)S(1)}, bf16[128,1024]{1,0:T(8,128)(2,1)S(1)}, u32[]{:S(2)}, u32[]{:S(2)}) %collective-permute-start.30) | collective-permute-done | bytes 262176 | tf_op jit(solution)/shard_map/ppermute | solution.py:46
  138.4 2.4 %collective-permute-start.32 = (bf16[128,1024]{1,0:T(8,128)(2,1)S(1)}, bf16[128,1024]{1,0:T(8,128)(2,1)S(1)}, u32[]{:S(2)}, u32[]{:S(2)}) collective-permute-start(bf16[128,1024]{1,0:T(8,128)(2,1)S(1)} %convolution_convert_fusion.2), channel_id=1, source_target_pairs={{0,6},{1,7},{2,0},{3,1},{4,2},{5,3},{6,4},{7,5},{8,14},{9,15},{10,... | collective-permute-start | bytes 786440 | tf_op jit(solution)/shard_map/ppermute | solution.py:46
  142.0 2.7 %collective-permute-done.33 = bf16[128,1024]{1,0:T(8,128)(2,1)S(1)} collective-permute-done((bf16[128,1024]{1,0:T(8,128)(2,1)S(1)}, bf16[128,1024]{1,0:T(8,128)(2,1)S(1)}, u32[]{:S(2)}, u32[]{:S(2)}) %collective-permute-start.33) | collective-permute-done | bytes 262176 | tf_op jit(solution)/shard_map/ppermute | solution.py:46
  144.7 8.3 %collective-permute-done.31 = bf16[128,1024]{1,0:T(8,128)(2,1)S(1)} collective-permute-done((bf16[128,1024]{1,0:T(8,128)(2,1)S(1)}, bf16[128,1024]{1,0:T(8,128)(2,1)S(1)}, u32[]{:S(2)}, u32[]{:S(2)}) %collective-permute-start.31) | collective-permute-done | bytes 262176 | tf_op jit(solution)/shard_map/ppermute | solution.py:46
  154.2 1.0 collective-permute-done.37
  (102 shorter events, 23.7 us)
Async XLA Ops:
  1.0 2.5 %collective-permute-start = (bf16[128,512]{1,0:T(8,128)(2,1)S(1)}, bf16[128,512]{1,0:T(8,128)(2,1)S(1)}, u32[]{:S(2)}, u32[]{:S(2)}) collective-permute-start(bf16[128,512]{1,0:T(8,128)(2,1)S(1)} %get-tuple-element.82), channel_id=1, source_target_pairs={{0,8},{8,0},{16,24},{24,16},{32,40},{40,32},{48,56},{56,48},{64,72... | collective-permute-start | bytes 393224 | tf_op jit(solution)/shard_map/ppermute | solution.py:42
  7.1 17.1 %collective-permute-start.4 = (bf16[512,1536]{1,0:T(8,128)(2,1)}, bf16[512,1536]{1,0:T(8,128)(2,1)S(1)}, u32[]{:S(2)}, u32[]{:S(2)}) collective-permute-start(bf16[512,1536]{1,0:T(8,128)(2,1)} %get-tuple-element.45), channel_id=1, source_target_pairs={{0,8},{8,0},{16,24},{24,16},{32,40},{40,32},{48,56},{56,48},{64,72... | collective-permute-start | bytes 4718600 | tf_op jit(solution)/shard_map/ppermute | solution.py:42
  7.5 9.4 %collective-permute-start.5 = (bf16[128,1024]{1,0:T(8,128)(2,1)S(1)}, bf16[128,1024]{1,0:T(8,128)(2,1)S(1)}, u32[]{:S(2)}, u32[]{:S(2)}) collective-permute-start(bf16[128,1024]{1,0:T(8,128)(2,1)S(1)} %pad_maximum_fusion.4), channel_id=1, source_target_pairs={{0,4},{1,5},{2,6},{3,7},{4,0},{5,1},{6,2},{7,3},{8,12},{9,13},{10,... | collective-permute-start | bytes 786440 | tf_op jit(solution)/shard_map/ppermute | solution.py:46
  10.5 12.4 %collective-permute-start.3 = (bf16[128,1024]{1,0:T(8,128)(2,1)S(1)}, bf16[128,1024]{1,0:T(8,128)(2,1)S(1)}, u32[]{:S(2)}, u32[]{:S(2)}) collective-permute-start(bf16[128,1024]{1,0:T(8,128)(2,1)S(1)} %pad_maximum_fusion.4), channel_id=1, source_target_pairs={{0,2},{1,3},{2,4},{3,5},{4,6},{5,7},{6,0},{7,1},{8,10},{9,11},{10,... | collective-permute-start | bytes 786440 | tf_op jit(solution)/shard_map/ppermute | solution.py:46
  10.9 13.3 %collective-permute-start.2 = (bf16[128,1024]{1,0:T(8,128)(2,1)S(1)}, bf16[128,1024]{1,0:T(8,128)(2,1)S(1)}, u32[]{:S(2)}, u32[]{:S(2)}) collective-permute-start(bf16[128,1024]{1,0:T(8,128)(2,1)S(1)} %pad_maximum_fusion.4), channel_id=1, source_target_pairs={{0,6},{1,7},{2,0},{3,1},{4,2},{5,3},{6,4},{7,5},{8,14},{9,15},{10,... | collective-permute-start | bytes 786440 | tf_op jit(solution)/shard_map/ppermute | solution.py:46
  13.2 11.0 %collective-permute-start.1 = (bf16[128,1024]{1,0:T(8,128)(2,1)S(1)}, bf16[128,1024]{1,0:T(8,128)(2,1)S(1)}, u32[]{:S(2)}, u32[]{:S(2)}) collective-permute-start(bf16[128,1024]{1,0:T(8,128)(2,1)S(1)} %pad_maximum_fusion.4), channel_id=1, source_target_pairs={{0,1},{1,0},{2,3},{3,2},{4,5},{5,4},{6,7},{7,6},{8,9},{9,8},{10,11... | collective-permute-start | bytes 786440 | tf_op jit(solution)/shard_map/ppermute | solution.py:46
  16.9 22.8 %collective-permute-start.9 = (bf16[512,1536]{1,0:T(8,128)(2,1)}, bf16[512,1536]{1,0:T(8,128)(2,1)S(1)}, u32[]{:S(2)}, u32[]{:S(2)}) collective-permute-start(bf16[512,1536]{1,0:T(8,128)(2,1)} %get-tuple-element.44), channel_id=1, source_target_pairs={{0,8},{8,0},{16,24},{24,16},{32,40},{40,32},{48,56},{56,48},{64,72... | collective-permute-start | bytes 4718600 | tf_op jit(solution)/shard_map/ppermute | solution.py:42
  22.9 11.4 %collective-permute-start.8 = (bf16[128,1024]{1,0:T(8,128)(2,1)S(1)}, bf16[128,1024]{1,0:T(8,128)(2,1)S(1)}, u32[]{:S(2)}, u32[]{:S(2)}) collective-permute-start(bf16[128,1024]{1,0:T(8,128)(2,1)S(1)} %collective-permute-done.5), channel_id=1, source_target_pairs={{0,1},{1,0},{2,3},{3,2},{4,5},{5,4},{6,7},{7,6},{8,9},{9,8},{10,11... | collective-permute-start | bytes 786440 | tf_op jit(solution)/shard_map/ppermute | solution.py:46
  24.2 10.2 %collective-permute-start.7 = (bf16[128,1024]{1,0:T(8,128)(2,1)S(1)}, bf16[128,1024]{1,0:T(8,128)(2,1)S(1)}, u32[]{:S(2)}, u32[]{:S(2)}) collective-permute-start(bf16[128,1024]{1,0:T(8,128)(2,1)S(1)} %collective-permute-done.1), channel_id=1, source_target_pairs={{0,2},{1,3},{2,4},{3,5},{4,6},{5,7},{6,0},{7,1},{8,10},{9,11},{10,... | collective-permute-start | bytes 786440 | tf_op jit(solution)/shard_map/ppermute | solution.py:46
  25.3 9.2 %collective-permute-start.6 = (bf16[128,1024]{1,0:T(8,128)(2,1)S(1)}, bf16[128,1024]{1,0:T(8,128)(2,1)S(1)}, u32[]{:S(2)}, u32[]{:S(2)}) collective-permute-start(bf16[128,1024]{1,0:T(8,128)(2,1)S(1)} %collective-permute-done.1), channel_id=1, source_target_pairs={{0,6},{1,7},{2,0},{3,1},{4,2},{5,3},{6,4},{7,5},{8,14},{9,15},{10,... | collective-permute-start | bytes 786440 | tf_op jit(solution)/shard_map/ppermute | solution.py:46
  27.7 1.4 copy-start.1
  29.8 23.6 %collective-permute-start.10 = (bf16[640,768]{1,0:T(8,128)(2,1)S(1)}, bf16[640,768]{1,0:T(8,128)(2,1)S(1)}, u32[]{:S(2)}, u32[]{:S(2)}) collective-permute-start(bf16[640,768]{1,0:T(8,128)(2,1)S(1)} %add_convert_fusion.2), channel_id=1, source_target_pairs={{0,96},{8,104},{16,112},{24,120},{32,0},{40,8},{48,16},{56,24},{64... | collective-permute-start | bytes 2949128 | tf_op jit(solution)/shard_map/ppermute | solution.py:42
  34.4 22.9 %collective-permute-start.11 = (bf16[640,768]{1,0:T(8,128)(2,1)S(1)}, bf16[640,768]{1,0:T(8,128)(2,1)S(1)}, u32[]{:S(2)}, u32[]{:S(2)}) collective-permute-start(bf16[640,768]{1,0:T(8,128)(2,1)S(1)} %add_convert_fusion.1), channel_id=1, source_target_pairs={{0,32},{8,40},{16,48},{24,56},{32,64},{40,72},{48,80},{56,88},{64,... | collective-permute-start | bytes 2949128 | tf_op jit(solution)/shard_map/ppermute | solution.py:42
  35.5 3.3 %copy-start = (bf16[512,1536]{1,0:T(8,128)(2,1)S(1)}, bf16[512,1536]{1,0:T(8,128)(2,1)}, u32[]{:S(2)}) copy-start(bf16[512,1536]{1,0:T(8,128)(2,1)} %get-tuple-element.44) | copy-start | bytes 4718596
  35.5 34.5 %collective-permute-start.16 = (bf16[384,768]{1,0:T(8,128)(2,1)S(1)}, bf16[384,768]{1,0:T(8,128)(2,1)S(1)}, u32[]{:S(2)}, u32[]{:S(2)}) collective-permute-start(bf16[384,768]{1,0:T(8,128)(2,1)S(1)} %fusion.2), channel_id=1, source_target_pairs={{0,16},{8,24},{16,0},{24,8},{32,48},{40,56},{48,32},{56,40},{64,80... | collective-permute-start | bytes 1769480 | tf_op jit(solution)/shard_map/ppermute | solution.py:42
  40.2 29.7 %collective-permute-start.15 = (bf16[384,768]{1,0:T(8,128)(2,1)S(1)}, bf16[384,768]{1,0:T(8,128)(2,1)S(1)}, u32[]{:S(2)}, u32[]{:S(2)}) collective-permute-start(bf16[384,768]{1,0:T(8,128)(2,1)S(1)} %fusion.1), channel_id=1, source_target_pairs={{0,16},{8,24},{16,0},{24,8},{32,48},{40,56},{48,32},{56,40},{64,80... | collective-permute-start | bytes 1769480 | tf_op jit(solution)/shard_map/ppermute | solution.py:42
  58.5 10.2 %collective-permute-start.13 = (bf16[640,384]{1,0:T(8,128)(2,1)S(1)}, bf16[640,384]{1,0:T(8,128)(2,1)S(1)}, u32[]{:S(2)}, u32[]{:S(2)}) collective-permute-start(bf16[640,384]{1,0:T(8,128)(2,1)S(1)} %get-tuple-element.69), channel_id=1, source_target_pairs={{0,96},{8,104},{16,112},{24,120},{32,0},{40,8},{48,16},{56,24},{64... | collective-permute-start | bytes 1474568 | tf_op jit(solution)/shard_map/ppermute | solution.py:42
  58.5 11.4 %collective-permute-start.12 = (bf16[640,384]{1,0:T(8,128)(2,1)S(1)}, bf16[640,384]{1,0:T(8,128)(2,1)S(1)}, u32[]{:S(2)}, u32[]{:S(2)}) collective-permute-start(bf16[640,384]{1,0:T(8,128)(2,1)S(1)} %get-tuple-element.71), channel_id=1, source_target_pairs={{0,32},{8,40},{16,48},{24,56},{32,64},{40,72},{48,80},{56,88},{64,... | collective-permute-start | bytes 1474568 | tf_op jit(solution)/shard_map/ppermute | solution.py:42
  69.9 7.6 %copy-start.4 = (bf16[640,384]{1,0:T(8,128)(2,1)}, bf16[640,384]{1,0:T(8,128)(2,1)S(1)}, u32[]{:S(2)}) copy-start(bf16[640,384]{1,0:T(8,128)(2,1)S(1)} %collective-permute-done.12.refs_4_) | copy-start | bytes 1474564
  70.1 5.6 %collective-permute-start.17 = (bf16[2,192,384]{2,1,0:T(8,128)(2,1)S(1)}, bf16[2,192,384]{2,1,0:T(8,128)(2,1)S(1)}, u32[]{:S(2)}, u32[]{:S(2)}) collective-permute-start(bf16[2,192,384]{2,1,0:T(8,128)(2,1)S(1)} %pad_maximum_fusion.1), channel_id=1, source_target_pairs={{0,96},{8,104},{16,112},{24,120},{32,0},{40,8},{48,16},{56,24},{64... | collective-permute-start | bytes 884744 | tf_op jit(solution)/shard_map/ppermute | solution.py:42
  70.5 6.9 %collective-permute-start.18 = (bf16[2,192,384]{2,1,0:T(8,128)(2,1)S(1)}, bf16[2,192,384]{2,1,0:T(8,128)(2,1)S(1)}, u32[]{:S(2)}, u32[]{:S(2)}) collective-permute-start(bf16[2,192,384]{2,1,0:T(8,128)(2,1)S(1)} %pad_maximum_fusion.2), channel_id=1, source_target_pairs={{0,32},{8,40},{16,48},{24,56},{32,64},{40,72},{48,80},{56,88},{64,... | collective-permute-start | bytes 884744 | tf_op jit(solution)/shard_map/ppermute | solution.py:42
  75.8 5.7 %collective-permute-start.20 = (bf16[192,384]{1,0:T(8,128)(2,1)S(1)}, bf16[192,384]{1,0:T(8,128)(2,1)S(1)}, u32[]{:S(2)}, u32[]{:S(2)}) collective-permute-start(bf16[192,384]{1,0:T(8,128)(2,1)S(1)} %fusion.40), channel_id=1, source_target_pairs={{0,96},{8,104},{16,112},{24,120},{32,0},{40,8},{48,16},{56,24},{64... | collective-permute-start | bytes 442376 | tf_op jit(solution)/shard_map/ppermute | solution.py:42
  77.5 5.4 %collective-permute-start.19 = (bf16[192,384]{1,0:T(8,128)(2,1)S(1)}, bf16[192,384]{1,0:T(8,128)(2,1)S(1)}, u32[]{:S(2)}, u32[]{:S(2)}) collective-permute-start(bf16[192,384]{1,0:T(8,128)(2,1)S(1)} %fusion.43), channel_id=1, source_target_pairs={{0,32},{8,40},{16,48},{24,56},{32,64},{40,72},{48,80},{56,88},{64,... | collective-permute-start | bytes 442376 | tf_op jit(solution)/shard_map/ppermute | solution.py:42
  78.0 9.3 %collective-permute-start.14 = (bf16[640,384]{1,0:T(8,128)(2,1)S(1)}, bf16[640,384]{1,0:T(8,128)(2,1)S(1)}, u32[]{:S(2)}, u32[]{:S(2)}) collective-permute-start(bf16[640,384]{1,0:T(8,128)(2,1)S(1)} %add_convert_fusion.3), channel_id=1, source_target_pairs={{0,16},{8,24},{16,0},{24,8},{32,48},{40,56},{48,32},{56,40},{64,80... | collective-permute-start | bytes 1474568 | tf_op jit(solution)/shard_map/ppermute | solution.py:42
  83.0 9.6 %copy-start.3 = (bf16[1024,512]{1,0:T(8,128)(2,1)S(1)}, bf16[1024,512]{1,0:T(8,128)(2,1)}, u32[]{:S(2)}) copy-start(bf16[1024,512]{1,0:T(8,128)(2,1)} %param.13) | copy-start | bytes 3145732
  87.2 0.8 copy-start.5
  92.6 14.7 %collective-permute-start.22 = (bf16[1024,512]{1,0:T(8,128)(2,1)S(1)}, bf16[1024,512]{1,0:T(8,128)(2,1)S(1)}, u32[]{:S(2)}, u32[]{:S(2)}) collective-permute-start(bf16[1024,512]{1,0:T(8,128)(2,1)S(1)} %copy-done.3), channel_id=1, source_target_pairs={{0,8},{8,0},{16,24},{24,16},{32,40},{40,32},{48,56},{56,48},{64,72... | collective-permute-start | bytes 3145736 | tf_op jit(solution)/shard_map/ppermute | solution.py:42
  99.9 2.5 %collective-permute-start.21 = (f32[26,8,128]{2,1,0:T(8,128)}, f32[26,8,128]{2,1,0:T(8,128)S(1)}, u32[]{:S(2)}, u32[]{:S(2)}) collective-permute-start(f32[26,8,128]{2,1,0:T(8,128)} %get-tuple-element.60.mine_ref), channel_id=1, source_target_pairs={{0,8},{8,0},{16,24},{24,16},{32,40},{40,32},{48,56},{56,48},{64,72... | collective-permute-start | bytes 319496 | tf_op jit(solution)/shard_map/ppermute | solution.py:42
  102.4 0.6 copy-start.6
  107.3 3.2 %copy-start.2 = (bf16[1024,128]{1,0:T(8,128)(2,1)S(1)}, bf16[1024,128]{1,0:T(8,128)(2,1)}, u32[]{:S(2)}) copy-start(bf16[1024,128]{1,0:T(8,128)(2,1)} %filtered.1) | copy-start | bytes 786436
  107.3 12.5 %collective-permute-start.24 = (bf16[1024,128]{1,0:T(8,128)(2,1)}, bf16[1024,128]{1,0:T(8,128)(2,1)S(1)}, u32[]{:S(2)}, u32[]{:S(2)}) collective-permute-start(bf16[1024,128]{1,0:T(8,128)(2,1)} %filtered.1), channel_id=1, source_target_pairs={{0,64},{8,72},{16,80},{24,88},{32,96},{40,104},{48,112},{56,120},{... | collective-permute-start | bytes 786440 | tf_op jit(solution)/shard_map/ppermute | solution.py:42
  108.0 9.2 %collective-permute-start.23 = (bf16[1024,128]{1,0:T(8,128)(2,1)}, bf16[1024,128]{1,0:T(8,128)(2,1)S(1)}, u32[]{:S(2)}, u32[]{:S(2)}) collective-permute-start(bf16[1024,128]{1,0:T(8,128)(2,1)} %filtered.1), channel_id=1, source_target_pairs={{0,16},{8,24},{16,0},{24,8},{32,48},{40,56},{48,32},{56,40},{64,80... | collective-permute-start | bytes 786440 | tf_op jit(solution)/shard_map/ppermute | solution.py:42
  110.5 12.4 %collective-permute-start.26 = (bf16[1024,128]{1,0:T(8,128)(2,1)S(1)}, bf16[1024,128]{1,0:T(8,128)(2,1)S(1)}, u32[]{:S(2)}, u32[]{:S(2)}) collective-permute-start(bf16[1024,128]{1,0:T(8,128)(2,1)S(1)} %copy-done.2), channel_id=1, source_target_pairs={{0,32},{8,40},{16,48},{24,56},{32,64},{40,72},{48,80},{56,88},{64,... | collective-permute-start | bytes 786440 | tf_op jit(solution)/shard_map/ppermute | solution.py:42
  111.7 10.7 %collective-permute-start.25 = (bf16[1024,128]{1,0:T(8,128)(2,1)S(1)}, bf16[1024,128]{1,0:T(8,128)(2,1)S(1)}, u32[]{:S(2)}, u32[]{:S(2)}) collective-permute-start(bf16[1024,128]{1,0:T(8,128)(2,1)S(1)} %copy-done.2), channel_id=1, source_target_pairs={{0,96},{8,104},{16,112},{24,120},{32,0},{40,8},{48,16},{56,24},{64... | collective-permute-start | bytes 786440 | tf_op jit(solution)/shard_map/ppermute | solution.py:42
  117.1 11.4 %collective-permute-start.28 = (bf16[1024,128]{1,0:T(8,128)(2,1)S(1)}, bf16[1024,128]{1,0:T(8,128)(2,1)S(1)}, u32[]{:S(2)}, u32[]{:S(2)}) collective-permute-start(bf16[1024,128]{1,0:T(8,128)(2,1)S(1)} %collective-permute-done.23), channel_id=1, source_target_pairs={{0,32},{8,40},{16,48},{24,56},{32,64},{40,72},{48,80},{56,88},{64,... | collective-permute-start | bytes 786440 | tf_op jit(solution)/shard_map/ppermute | solution.py:42
  118.3 7.9 %collective-permute-start.27 = (bf16[1024,128]{1,0:T(8,128)(2,1)S(1)}, bf16[1024,128]{1,0:T(8,128)(2,1)S(1)}, u32[]{:S(2)}, u32[]{:S(2)}) collective-permute-start(bf16[1024,128]{1,0:T(8,128)(2,1)S(1)} %collective-permute-done.23), channel_id=1, source_target_pairs={{0,96},{8,104},{16,112},{24,120},{32,0},{40,8},{48,16},{56,24},{64... | collective-permute-start | bytes 786440 | tf_op jit(solution)/shard_map/ppermute | solution.py:42
  119.8 8.8 %collective-permute-start.29 = (bf16[1024,128]{1,0:T(8,128)(2,1)S(1)}, bf16[1024,128]{1,0:T(8,128)(2,1)S(1)}, u32[]{:S(2)}, u32[]{:S(2)}) collective-permute-start(bf16[1024,128]{1,0:T(8,128)(2,1)S(1)} %collective-permute-done.24), channel_id=1, source_target_pairs={{0,16},{8,24},{16,0},{24,8},{32,48},{40,56},{48,32},{56,40},{64,80... | collective-permute-start | bytes 786440 | tf_op jit(solution)/shard_map/ppermute | solution.py:42
  130.6 6.5 %collective-permute-start.30 = (bf16[128,1024]{1,0:T(8,128)(2,1)S(1)}, bf16[128,1024]{1,0:T(8,128)(2,1)S(1)}, u32[]{:S(2)}, u32[]{:S(2)}) collective-permute-start(bf16[128,1024]{1,0:T(8,128)(2,1)S(1)} %convolution_convert_fusion.4), channel_id=1, source_target_pairs={{0,1},{1,0},{2,3},{3,2},{4,5},{5,4},{6,7},{7,6},{8,9},{9,8},{10,11... | collective-permute-start | bytes 786440 | tf_op jit(solution)/shard_map/ppermute | solution.py:46
  130.9 9.9 %collective-permute-start.34 = (bf16[128,1024]{1,0:T(8,128)(2,1)S(1)}, bf16[128,1024]{1,0:T(8,128)(2,1)S(1)}, u32[]{:S(2)}, u32[]{:S(2)}) collective-permute-start(bf16[128,1024]{1,0:T(8,128)(2,1)S(1)} %convolution_convert_fusion.1), channel_id=1, source_target_pairs={{0,2},{1,3},{2,4},{3,5},{4,6},{5,7},{6,0},{7,1},{8,10},{9,11},{10,... | collective-permute-start | bytes 786440 | tf_op jit(solution)/shard_map/ppermute | solution.py:46
  130.9 9.9 %collective-permute-start.35 = (bf16[128,1024]{1,0:T(8,128)(2,1)S(1)}, bf16[128,1024]{1,0:T(8,128)(2,1)S(1)}, u32[]{:S(2)}, u32[]{:S(2)}) collective-permute-start(bf16[128,1024]{1,0:T(8,128)(2,1)S(1)} %convolution_convert_fusion), channel_id=1, source_target_pairs={{0,6},{1,7},{2,0},{3,1},{4,2},{5,3},{6,4},{7,5},{8,14},{9,15},{10,... | collective-permute-start | bytes 786440 | tf_op jit(solution)/shard_map/ppermute | solution.py:46
  137.5 7.2 %collective-permute-start.33 = (bf16[128,1024]{1,0:T(8,128)(2,1)S(1)}, bf16[128,1024]{1,0:T(8,128)(2,1)S(1)}, u32[]{:S(2)}, u32[]{:S(2)}) collective-permute-start(bf16[128,1024]{1,0:T(8,128)(2,1)S(1)} %fusion.11), channel_id=1, source_target_pairs={{0,4},{1,5},{2,6},{3,7},{4,0},{5,1},{6,2},{7,3},{8,12},{9,13},{10,... | collective-permute-start | bytes 786440 | tf_op jit(solution)/shard_map/ppermute | solution.py:46
  138.1 14.8 %collective-permute-start.31 = (bf16[128,1024]{1,0:T(8,128)(2,1)S(1)}, bf16[128,1024]{1,0:T(8,128)(2,1)S(1)}, u32[]{:S(2)}, u32[]{:S(2)}) collective-permute-start(bf16[128,1024]{1,0:T(8,128)(2,1)S(1)} %convolution_convert_fusion.3), channel_id=1, source_target_pairs={{0,2},{1,3},{2,4},{3,5},{4,6},{5,7},{6,0},{7,1},{8,10},{9,11},{10,... | collective-permute-start | bytes 786440 | tf_op jit(solution)/shard_map/ppermute | solution.py:46
  138.4 14.5 %collective-permute-start.32 = (bf16[128,1024]{1,0:T(8,128)(2,1)S(1)}, bf16[128,1024]{1,0:T(8,128)(2,1)S(1)}, u32[]{:S(2)}, u32[]{:S(2)}) collective-permute-start(bf16[128,1024]{1,0:T(8,128)(2,1)S(1)} %convolution_convert_fusion.2), channel_id=1, source_target_pairs={{0,6},{1,7},{2,0},{3,1},{4,2},{5,3},{6,4},{7,5},{8,14},{9,15},{10,... | collective-permute-start | bytes 786440 | tf_op jit(solution)/shard_map/ppermute | solution.py:46
  141.3 11.7 %collective-permute-start.36 = (bf16[128,1024]{1,0:T(8,128)(2,1)S(1)}, bf16[128,1024]{1,0:T(8,128)(2,1)S(1)}, u32[]{:S(2)}, u32[]{:S(2)}) collective-permute-start(bf16[128,1024]{1,0:T(8,128)(2,1)S(1)} %fusion.10), channel_id=1, source_target_pairs={{0,1},{1,0},{2,3},{3,2},{4,5},{5,4},{6,7},{7,6},{8,9},{9,8},{10,11... | collective-permute-start | bytes 786440 | tf_op jit(solution)/shard_map/ppermute | solution.py:46
  153.6 1.6 %collective-permute-start.37 = (bf16[128,512]{1,0:T(8,128)(2,1)S(1)}, bf16[128,512]{1,0:T(8,128)(2,1)S(1)}, u32[]{:S(2)}, u32[]{:S(2)}) collective-permute-start(bf16[128,512]{1,0:T(8,128)(2,1)S(1)} %get-tuple-element.80), channel_id=1, source_target_pairs={{0,8},{8,0},{16,24},{24,16},{32,40},{40,32},{48,56},{56,48},{64,72... | collective-permute-start | bytes 393224 | tf_op jit(solution)/shard_map/ppermute | solution.py:42

commit v7 on v6

--- a/solution.py
+++ b/solution.py
@@ -149,12 +149,8 @@
     from_below = tok_send((both(near1, far1, first) + up[0].astype(F32)).astype(BF), Z_UP)
     from_above = tok_send((both(near3, far3, second) + down[0].astype(F32)).astype(BF), Z_DOWN)
     late_terms = [
-        jnp.concatenate(
-            [
-                both(near0, far0, first) + down[1].astype(F32) + from_below.astype(F32),
-                both(near0, far0, second) + up[1].astype(F32) + from_above.astype(F32),
-            ]
-        ).astype(BF)
+        (both(near0, far0, first) + down[1].astype(F32) + from_below.astype(F32)).astype(BF),
+        (both(near0, far0, second) + up[1].astype(F32) + from_above.astype(F32)).astype(BF),
     ]
     return [terms, late_terms]
 
@@ -187,9 +183,10 @@
     for refs_here, group in zip(term_refs, groups):
         for place, (dy, dx) in enumerate(group):
             here = slice(place * length, (place + 1) * length)
-            block = refs_here[0][here, :].astype(F32)
-            for ref in refs_here[1:]:
-                block = block + ref[here, :].astype(F32)
+            if refs_here[0].shape[0] < len(group) * length:
+                block = jnp.concatenate([ref[...] for ref in refs_here])[here].astype(F32)
+            else:
+                block = sum(ref[here, :].astype(F32) for ref in refs_here)
             spot = ((where_ref[3] + dy) & (Y - 1)) * XL + ((where_ref[4] + dx) & (XL - 1))
             there = pl.ds(pl.multiple_of(spot * length, length), length)
             mixed = []

time: 156 us -> 154 us (0.987)
  waiting for transfers between devices: 66.3 us -> 57.1 us
  starting transfers between devices: 55 us -> 59.7 us
  other arithmetic: 3.49 us -> 5.76 us
    ppermute x24, waiting for transfers between devices: 45.3 us -> 38.1 us  [tok_send(): return lax.ppermute(value, 'tok', perm)]
    ppermute x24, starting transfers between devices: 37.1 us -> 41.8 us  [tok_send(): return lax.ppermute(value, 'tok', perm)]
    ppermute x14, waiting for transfers between devices: 21 us -> 19 us  [ch_send(): return lax.ppermute(value, 'ch', perm)]
    convert_element_type x0 -> x1, other arithmetic: none -> 1.84 us  [reduce_groups(): (both(near0, far0, second) + up[1].astype(F32) + from_above.astype(F32))....]
  transfers between devices with their start and end apart: 38 -> 38, of which waited for: 20 -> 17; matrix products, arithmetic and copies ran while one was open for 10% -> 11% of each run, Pallas kernels for 3% -> 3%
where the time goes in v7:
time: 154 us
  starting transfers between devices  59.7 us (39%)
  waiting for transfers between devices  57.1 us (37%)
  matrix products  13.1 us (9%)
  Pallas kernels  12.4 us (8%)
  other arithmetic  5.76 us (4%)
  local copies, waits for them, and re-layouts  5.13 us (3%)
    ppermute x24, starting transfers between devices, tok_send(): return lax.ppermute(value, 'tok', perm)  41.8 us
    ppermute x24, waiting for transfers between devices, tok_send(): return lax.ppermute(value, 'tok', perm)  38.1 us
    ppermute x14, waiting for transfers between devices, ch_send(): return lax.ppermute(value, 'ch', perm)  19 us
    ppermute x14, starting transfers between devices, ch_send(): return lax.ppermute(value, 'ch', perm)  17.9 us
    dot_general x8, matrix products, product(): jnp.dot(rows[:, :depth], own[part][:, columns], preferred_element_type=F32)  4.69 us
    dot_general x8, matrix products, product(): jnp.dot(rows[:, depth:], other[part][:, columns], preferred_element_type=...  4.68 us
    pallas_call x1, Pallas kernels, local_part(): pl.pallas_call(lambda *refs: local_kernel(blocks, [len(terms) for terms i...  4.59 us
    pallas_call x1, Pallas kernels, filtered(): pl.pallas_call(filter_kernel, out_shape=jax.ShapeDtypeStruct((gate.shape[...  4.19 us
  transfers between devices with their start and end apart: 38, of which 17 were waited for; matrix products, arithmetic and copies ran while one was open for 11% of the time, Pallas kernels for 3%

profile of v7, /device:TPU:1, one launch (start us, length us, event | category | flops | bytes accessed | tf_op | source)
XLA Modules:
  0.0 153.7 jit_solution(13996280053464669735)
XLA Ops:
  1.0 1.5 collective-permute-start
  2.5 1.0 collective-permute-done
  3.5 3.6 %by_target.1 = (bf16[512,1536]{1,0:T(8,128)(2,1)}, bf16[512,1536]{1,0:T(8,128)(2,1)}) custom-call(bf16[512,3072]{1,0:T(8,128)(2,1)} %refs_0_), custom_call_target="tpu_custom_call" | custom-call | tf_op jit(solution)/shard_map/by_target/pallas_call | solution.py:87
  7.5 3.0 %collective-permute-start.5 = (bf16[128,1024]{1,0:T(8,128)(2,1)S(1)}, bf16[128,1024]{1,0:T(8,128)(2,1)S(1)}, u32[]{:S(2)}, u32[]{:S(2)}) collective-permute-start(bf16[128,1024]{1,0:T(8,128)(2,1)S(1)} %pad_maximum_fusion.3), channel_id=1, source_target_pairs={{0,4},{1,5},{2,6},{3,7},{4,0},{5,1},{6,2},{7,3},{8,12},{9,13},{10,... | collective-permute-start | bytes 786440 | tf_op jit(solution)/shard_map/ppermute | solution.py:46
  10.9 2.3 %collective-permute-start.2 = (bf16[128,1024]{1,0:T(8,128)(2,1)S(1)}, bf16[128,1024]{1,0:T(8,128)(2,1)S(1)}, u32[]{:S(2)}, u32[]{:S(2)}) collective-permute-start(bf16[128,1024]{1,0:T(8,128)(2,1)S(1)} %pad_maximum_fusion.3), channel_id=1, source_target_pairs={{0,6},{1,7},{2,0},{3,1},{4,2},{5,3},{6,4},{7,5},{8,14},{9,15},{10,... | collective-permute-start | bytes 786440 | tf_op jit(solution)/shard_map/ppermute | solution.py:46
  13.2 1.2 collective-permute-start.1
  14.5 2.5 %collective-permute-done.5 = bf16[128,1024]{1,0:T(8,128)(2,1)S(1)} collective-permute-done((bf16[128,1024]{1,0:T(8,128)(2,1)S(1)}, bf16[128,1024]{1,0:T(8,128)(2,1)S(1)}, u32[]{:S(2)}, u32[]{:S(2)}) %collective-permute-start.5) | collective-permute-done | bytes 262176 | tf_op jit(solution)/shard_map/ppermute | solution.py:46
  16.9 1.5 collective-permute-start.9
  18.4 4.6 %collective-permute-done.3 = bf16[128,1024]{1,0:T(8,128)(2,1)S(1)} collective-permute-done((bf16[128,1024]{1,0:T(8,128)(2,1)S(1)}, bf16[128,1024]{1,0:T(8,128)(2,1)S(1)}, u32[]{:S(2)}, u32[]{:S(2)}) %collective-permute-start.3) | collective-permute-done | bytes 262176 | tf_op jit(solution)/shard_map/ppermute | solution.py:46
  22.9 1.3 collective-permute-start.8
  24.2 1.0 collective-permute-start.7
  25.3 1.7 %collective-permute-start.6 = (bf16[128,1024]{1,0:T(8,128)(2,1)S(1)}, bf16[128,1024]{1,0:T(8,128)(2,1)S(1)}, u32[]{:S(2)}, u32[]{:S(2)}) collective-permute-start(bf16[128,1024]{1,0:T(8,128)(2,1)S(1)} %collective-permute-done.1), channel_id=1, source_target_pairs={{0,6},{1,7},{2,0},{3,1},{4,2},{5,3},{6,4},{7,5},{8,14},{9,15},{10,... | collective-permute-start | bytes 786440 | tf_op jit(solution)/shard_map/ppermute | solution.py:46
  29.8 3.8 %collective-permute-start.10 = (bf16[640,768]{1,0:T(8,128)(2,1)S(1)}, bf16[640,768]{1,0:T(8,128)(2,1)S(1)}, u32[]{:S(2)}, u32[]{:S(2)}) collective-permute-start(bf16[640,768]{1,0:T(8,128)(2,1)S(1)} %add_convert_fusion.2), channel_id=1, source_target_pairs={{0,96},{8,104},{16,112},{24,120},{32,0},{40,8},{48,16},{56,24},{64... | collective-permute-start | bytes 2949128 | tf_op jit(solution)/shard_map/ppermute | solution.py:42
  35.5 2.5 %collective-permute-start.16 = (bf16[384,768]{1,0:T(8,128)(2,1)S(1)}, bf16[384,768]{1,0:T(8,128)(2,1)S(1)}, u32[]{:S(2)}, u32[]{:S(2)}) collective-permute-start(bf16[384,768]{1,0:T(8,128)(2,1)S(1)} %fusion.2), channel_id=1, source_target_pairs={{0,16},{8,24},{16,0},{24,8},{32,48},{40,56},{48,32},{56,40},{64,80... | collective-permute-start | bytes 1769480 | tf_op jit(solution)/shard_map/ppermute | solution.py:42
  41.9 1.2 fusion.28
  43.1 1.2 add_convert_fusion
  44.3 9.1 %collective-permute-done.10 = bf16[640,768]{1,0:T(8,128)(2,1)S(1)} collective-permute-done((bf16[640,768]{1,0:T(8,128)(2,1)S(1)}, bf16[640,768]{1,0:T(8,128)(2,1)S(1)}, u32[]{:S(2)}, u32[]{:S(2)}) %collective-permute-start.10) | collective-permute-done | bytes 983072 | tf_op jit(solution)/shard_map/ppermute | solution.py:42
  53.4 3.9 %collective-permute-done.11 = bf16[640,768]{1,0:T(8,128)(2,1)S(1)} collective-permute-done((bf16[640,768]{1,0:T(8,128)(2,1)S(1)}, bf16[640,768]{1,0:T(8,128)(2,1)S(1)}, u32[]{:S(2)}, u32[]{:S(2)}) %collective-permute-start.11) | collective-permute-done | bytes 983072 | tf_op jit(solution)/shard_map/ppermute | solution.py:42
  57.3 1.2 add_convert_fusion.4
  58.5 1.5 collective-permute-start.12
  60.4 8.3 %collective-permute-done.13 = bf16[640,384]{1,0:T(8,128)(2,1)S(1)} collective-permute-done((bf16[640,384]{1,0:T(8,128)(2,1)S(1)}, bf16[640,384]{1,0:T(8,128)(2,1)S(1)}, u32[]{:S(2)}, u32[]{:S(2)}) %collective-permute-start.13) | collective-permute-done | bytes 491552 | tf_op jit(solution)/shard_map/ppermute | solution.py:42
  68.7 1.2 collective-permute-done.12.refs_4_
  70.3 2.7 %collective-permute-start.17 = (bf16[2,192,384]{2,1,0:T(8,128)(2,1)S(1)}, bf16[2,192,384]{2,1,0:T(8,128)(2,1)S(1)}, u32[]{:S(2)}, u32[]{:S(2)}) collective-permute-start(bf16[2,192,384]{2,1,0:T(8,128)(2,1)S(1)} %pad_maximum_fusion.1), channel_id=1, source_target_pairs={{0,96},{8,104},{16,112},{24,120},{32,0},{40,8},{48,16},{56,24},{64... | collective-permute-start | bytes 884744 | tf_op jit(solution)/shard_map/ppermute | solution.py:42
  73.2 2.5 %collective-permute-start.14 = (bf16[640,384]{1,0:T(8,128)(2,1)S(1)}, bf16[640,384]{1,0:T(8,128)(2,1)S(1)}, u32[]{:S(2)}, u32[]{:S(2)}) collective-permute-start(bf16[640,384]{1,0:T(8,128)(2,1)S(1)} %add_convert_fusion.3), channel_id=1, source_target_pairs={{0,16},{8,24},{16,0},{24,8},{32,48},{40,56},{48,32},{56,40},{64,80... | collective-permute-start | bytes 1474568 | tf_op jit(solution)/shard_map/ppermute | solution.py:42
  75.7 1.2 collective-permute-done.18
  78.4 2.7 %collective-permute-start.20 = (bf16[192,384]{1,0:T(8,128)(2,1)}, bf16[192,384]{1,0:T(8,128)(2,1)}, u32[]{:S(2)}, u32[]{:S(2)}) collective-permute-start(bf16[192,384]{1,0:T(8,128)(2,1)} %fusion.40), channel_id=1, source_target_pairs={{0,96},{8,104},{16,112},{24,120},{32,0},{40,8},{48,16},{56,24},{64... | collective-permute-start | bytes 442376 | tf_op jit(solution)/shard_map/ppermute | solution.py:42
  81.7 1.7 %collective-permute-done.19 = bf16[192,384]{1,0:T(8,128)(2,1)} collective-permute-done((bf16[192,384]{1,0:T(8,128)(2,1)}, bf16[192,384]{1,0:T(8,128)(2,1)}, u32[]{:S(2)}, u32[]{:S(2)}) %collective-permute-start.19) | collective-permute-done | bytes 147488 | tf_op jit(solution)/shard_map/ppermute | solution.py:42
  83.5 1.8 %fusion.42 = (bf16[192,384]{1,0:T(8,128)(2,1)}, bf16[192,384]{1,0:T(8,128)(2,1)}) fusion(bf16[192,384]{1,0:T(8,128)(2,1)} %collective-permute-done.20, bf16[2,192,384]{2,1,0:T(8,128)(2,1)S(1)} %collective-permute-done.18, bf16[384,768]{1,0:T(8,128)(2,1)S(1)} %collective-permute-done.15, bf16[384,384]{1,0:T(8,128)(2,1)S(1)} %get-tuple-element.51, ...), kind=kLoop, calls=%fused_computation.67 | loop fusion | flops 1179648 | bytes 1474560 | tf_op jit(solution)/shard_map/convert_element_type | solution.py:153
  86.1 4.6 %local_part.1 = (f32[128,8,128]{2,1,0:T(8,128)}, f32[128,8,128]{2,1,0:T(8,128)}, f32[26,8,128]{2,1,0:T(8,128)}) custom-call(s32[6]{0:T(128)} %stack.51.refs_0_.where_ref, f32[3,3,8192]{2,1,0:T(4,128)} %taps_ref.1, f32[16,8192]{1,0:T(8,128)} %rates_ref.1, bf16[640,384]{1,0:T(8,128)(2,1)} %get-tuple-element.55.refs_3_, bf16[640,384]{1,0:T(8,128)(2,1)} %copy-done.4, ...), custom_call_target="tpu_custom_call" | custom-call | tf_op jit(solution)/shard_map/local_part/pallas_call | solution.py:307
  90.7 5.7 %collective-permute-start.22 = (bf16[1024,512]{1,0:T(8,128)(2,1)S(1)}, bf16[1024,512]{1,0:T(8,128)(2,1)S(1)}, u32[]{:S(2)}, u32[]{:S(2)}) collective-permute-start(bf16[1024,512]{1,0:T(8,128)(2,1)S(1)} %copy-done.3), channel_id=1, source_target_pairs={{0,8},{8,0},{16,24},{24,16},{32,40},{40,32},{48,56},{56,48},{64,72... | collective-permute-start | bytes 3145736 | tf_op jit(solution)/shard_map/ppermute | solution.py:42
  96.5 2.4 %collective-permute-done.21.theirs_ref = f32[26,8,128]{2,1,0:T(8,128)S(1)} collective-permute-done((f32[26,8,128]{2,1,0:T(8,128)}, f32[26,8,128]{2,1,0:T(8,128)S(1)}, u32[]{:S(2)}, u32[]{:S(2)}) %collective-permute-start.21) | collective-permute-done | bytes 106528 | tf_op jit(solution)/shard_map/ppermute | solution.py:42
  99.6 4.2 %filtered.1 = bf16[1024,128]{1,0:T(8,128)(2,1)} custom-call(s32[6]{0:T(128)} %stack.51.refs_0_.where_ref, f32[3,3,8192]{2,1,0:T(4,128)} %taps_ref.1, f32[16,8192]{1,0:T(8,128)} %rates_ref.1, f32[16,8192]{1,0:T(8,128)} %weights_ref.1, f32[1,8192]{1,0:T(1,128)} %bitcast.45, f32[26,8,128]{2,1,0:T(8,128)} %get-tuple-element.62.mine_ref, ...), custom_call_target="tpu_custom_call" | custom-call | tf_op jit(solution)/shard_map/filtered/pallas_call | solution.py:328
  103.8 1.7 %collective-permute-start.24 = (bf16[1024,128]{1,0:T(8,128)(2,1)}, bf16[1024,128]{1,0:T(8,128)(2,1)S(1)}, u32[]{:S(2)}, u32[]{:S(2)}) collective-permute-start(bf16[1024,128]{1,0:T(8,128)(2,1)} %filtered.1), channel_id=1, source_target_pairs={{0,64},{8,72},{16,80},{24,88},{32,96},{40,104},{48,112},{56,120},{... | collective-permute-start | bytes 786440 | tf_op jit(solution)/shard_map/ppermute | solution.py:42
  105.5 2.4 %collective-permute-start.23 = (bf16[1024,128]{1,0:T(8,128)(2,1)}, bf16[1024,128]{1,0:T(8,128)(2,1)S(1)}, u32[]{:S(2)}, u32[]{:S(2)}) collective-permute-start(bf16[1024,128]{1,0:T(8,128)(2,1)} %filtered.1), channel_id=1, source_target_pairs={{0,16},{8,24},{16,0},{24,8},{32,48},{40,56},{48,32},{56,40},{64,80... | collective-permute-start | bytes 786440 | tf_op jit(solution)/shard_map/ppermute | solution.py:42
  108.1 2.4 %collective-permute-start.26 = (bf16[1024,128]{1,0:T(8,128)(2,1)S(1)}, bf16[1024,128]{1,0:T(8,128)(2,1)S(1)}, u32[]{:S(2)}, u32[]{:S(2)}) collective-permute-start(bf16[1024,128]{1,0:T(8,128)(2,1)S(1)} %copy-done.2), channel_id=1, source_target_pairs={{0,32},{8,40},{16,48},{24,56},{32,64},{40,72},{48,80},{56,88},{64,... | collective-permute-start | bytes 786440 | tf_op jit(solution)/shard_map/ppermute | solution.py:42
  111.3 3.3 %collective-permute-done.23 = bf16[1024,128]{1,0:T(8,128)(2,1)S(1)} collective-permute-done((bf16[1024,128]{1,0:T(8,128)(2,1)}, bf16[1024,128]{1,0:T(8,128)(2,1)S(1)}, u32[]{:S(2)}, u32[]{:S(2)}) %collective-permute-start.23) | collective-permute-done | bytes 262176 | tf_op jit(solution)/shard_map/ppermute | solution.py:42
  114.7 2.3 %collective-permute-start.28 = (bf16[1024,128]{1,0:T(8,128)(2,1)S(1)}, bf16[1024,128]{1,0:T(8,128)(2,1)S(1)}, u32[]{:S(2)}, u32[]{:S(2)}) collective-permute-start(bf16[1024,128]{1,0:T(8,128)(2,1)S(1)} %collective-permute-done.23), channel_id=1, source_target_pairs={{0,32},{8,40},{16,48},{24,56},{32,64},{40,72},{48,80},{56,88},{64,... | collective-permute-start | bytes 786440 | tf_op jit(solution)/shard_map/ppermute | solution.py:42
  117.3 2.4 %collective-permute-start.29 = (bf16[1024,128]{1,0:T(8,128)(2,1)S(1)}, bf16[1024,128]{1,0:T(8,128)(2,1)S(1)}, u32[]{:S(2)}, u32[]{:S(2)}) collective-permute-start(bf16[1024,128]{1,0:T(8,128)(2,1)S(1)} %collective-permute-done.24), channel_id=1, source_target_pairs={{0,16},{8,24},{16,0},{24,8},{32,48},{40,56},{48,32},{56,40},{64,80... | collective-permute-start | bytes 786440 | tf_op jit(solution)/shard_map/ppermute | solution.py:42
  120.2 4.8 %collective-permute-done.27 = bf16[1024,128]{1,0:T(8,128)(2,1)S(1)} collective-permute-done((bf16[1024,128]{1,0:T(8,128)(2,1)S(1)}, bf16[1024,128]{1,0:T(8,128)(2,1)S(1)}, u32[]{:S(2)}, u32[]{:S(2)}) %collective-permute-start.27) | collective-permute-done | bytes 262176 | tf_op jit(solution)/shard_map/ppermute | solution.py:42
  127.4 2.7 %collective-permute-start.35 = (bf16[128,1024]{1,0:T(8,128)(2,1)S(1)}, bf16[128,1024]{1,0:T(8,128)(2,1)S(1)}, u32[]{:S(2)}, u32[]{:S(2)}) collective-permute-start(bf16[128,1024]{1,0:T(8,128)(2,1)S(1)} %convolution_convert_fusion), channel_id=1, source_target_pairs={{0,6},{1,7},{2,0},{3,1},{4,2},{5,3},{6,4},{7,5},{8,14},{9,15},{10,... | collective-permute-start | bytes 786440 | tf_op jit(solution)/shard_map/ppermute | solution.py:46
  130.6 1.8 %collective-permute-done.30 = bf16[128,1024]{1,0:T(8,128)(2,1)S(1)} collective-permute-done((bf16[128,1024]{1,0:T(8,128)(2,1)S(1)}, bf16[128,1024]{1,0:T(8,128)(2,1)S(1)}, u32[]{:S(2)}, u32[]{:S(2)}) %collective-permute-start.30) | collective-permute-done | bytes 262176 | tf_op jit(solution)/shard_map/ppermute | solution.py:46
  133.0 1.0 collective-permute-start.31
  134.0 1.7 %collective-permute-start.32 = (bf16[128,1024]{1,0:T(8,128)(2,1)S(1)}, bf16[128,1024]{1,0:T(8,128)(2,1)S(1)}, u32[]{:S(2)}, u32[]{:S(2)}) collective-permute-start(bf16[128,1024]{1,0:T(8,128)(2,1)S(1)} %convolution_convert_fusion.2), channel_id=1, source_target_pairs={{0,6},{1,7},{2,0},{3,1},{4,2},{5,3},{6,4},{7,5},{8,14},{9,15},{10,... | collective-permute-start | bytes 786440 | tf_op jit(solution)/shard_map/ppermute | solution.py:46
  136.2 1.1 collective-permute-start.36
  137.3 2.5 %collective-permute-done.33 = bf16[128,1024]{1,0:T(8,128)(2,1)S(1)} collective-permute-done((bf16[128,1024]{1,0:T(8,128)(2,1)S(1)}, bf16[128,1024]{1,0:T(8,128)(2,1)S(1)}, u32[]{:S(2)}, u32[]{:S(2)}) %collective-permute-start.33) | collective-permute-done | bytes 262176 | tf_op jit(solution)/shard_map/ppermute | solution.py:46
  139.9 7.6 %collective-permute-done.31 = bf16[128,1024]{1,0:T(8,128)(2,1)S(1)} collective-permute-done((bf16[128,1024]{1,0:T(8,128)(2,1)S(1)}, bf16[128,1024]{1,0:T(8,128)(2,1)S(1)}, u32[]{:S(2)}, u32[]{:S(2)}) %collective-permute-start.31) | collective-permute-done | bytes 262176 | tf_op jit(solution)/shard_map/ppermute | solution.py:46
  148.1 3.9 %collective-permute-start.37 = (bf16[128,512]{1,0:T(8,128)(2,1)S(1)}, bf16[128,512]{1,0:T(8,128)(2,1)S(1)}, u32[]{:S(2)}, u32[]{:S(2)}) collective-permute-start(bf16[128,512]{1,0:T(8,128)(2,1)S(1)} %get-tuple-element.82), channel_id=1, source_target_pairs={{0,8},{8,0},{16,24},{24,16},{32,40},{40,32},{48,56},{56,48},{64,72... | collective-permute-start | bytes 393224 | tf_op jit(solution)/shard_map/ppermute | solution.py:42
  151.9 1.0 collective-permute-done.37
  (101 shorter events, 21.8 us)
Async XLA Ops:
  1.0 2.5 %collective-permute-start = (bf16[128,512]{1,0:T(8,128)(2,1)S(1)}, bf16[128,512]{1,0:T(8,128)(2,1)S(1)}, u32[]{:S(2)}, u32[]{:S(2)}) collective-permute-start(bf16[128,512]{1,0:T(8,128)(2,1)S(1)} %get-tuple-element.84), channel_id=1, source_target_pairs={{0,8},{8,0},{16,24},{24,16},{32,40},{40,32},{48,56},{56,48},{64,72... | collective-permute-start | bytes 393224 | tf_op jit(solution)/shard_map/ppermute | solution.py:42
  7.1 17.1 %collective-permute-start.4 = (bf16[512,1536]{1,0:T(8,128)(2,1)}, bf16[512,1536]{1,0:T(8,128)(2,1)S(1)}, u32[]{:S(2)}, u32[]{:S(2)}) collective-permute-start(bf16[512,1536]{1,0:T(8,128)(2,1)} %get-tuple-element.46), channel_id=1, source_target_pairs={{0,8},{8,0},{16,24},{24,16},{32,40},{40,32},{48,56},{56,48},{64,72... | collective-permute-start | bytes 4718600 | tf_op jit(solution)/shard_map/ppermute | solution.py:42
  7.5 9.4 %collective-permute-start.5 = (bf16[128,1024]{1,0:T(8,128)(2,1)S(1)}, bf16[128,1024]{1,0:T(8,128)(2,1)S(1)}, u32[]{:S(2)}, u32[]{:S(2)}) collective-permute-start(bf16[128,1024]{1,0:T(8,128)(2,1)S(1)} %pad_maximum_fusion.3), channel_id=1, source_target_pairs={{0,4},{1,5},{2,6},{3,7},{4,0},{5,1},{6,2},{7,3},{8,12},{9,13},{10,... | collective-permute-start | bytes 786440 | tf_op jit(solution)/shard_map/ppermute | solution.py:46
  10.5 12.4 %collective-permute-start.3 = (bf16[128,1024]{1,0:T(8,128)(2,1)S(1)}, bf16[128,1024]{1,0:T(8,128)(2,1)S(1)}, u32[]{:S(2)}, u32[]{:S(2)}) collective-permute-start(bf16[128,1024]{1,0:T(8,128)(2,1)S(1)} %pad_maximum_fusion.3), channel_id=1, source_target_pairs={{0,2},{1,3},{2,4},{3,5},{4,6},{5,7},{6,0},{7,1},{8,10},{9,11},{10,... | collective-permute-start | bytes 786440 | tf_op jit(solution)/shard_map/ppermute | solution.py:46
  10.9 13.3 %collective-permute-start.2 = (bf16[128,1024]{1,0:T(8,128)(2,1)S(1)}, bf16[128,1024]{1,0:T(8,128)(2,1)S(1)}, u32[]{:S(2)}, u32[]{:S(2)}) collective-permute-start(bf16[128,1024]{1,0:T(8,128)(2,1)S(1)} %pad_maximum_fusion.3), channel_id=1, source_target_pairs={{0,6},{1,7},{2,0},{3,1},{4,2},{5,3},{6,4},{7,5},{8,14},{9,15},{10,... | collective-permute-start | bytes 786440 | tf_op jit(solution)/shard_map/ppermute | solution.py:46
  13.2 11.0 %collective-permute-start.1 = (bf16[128,1024]{1,0:T(8,128)(2,1)S(1)}, bf16[128,1024]{1,0:T(8,128)(2,1)S(1)}, u32[]{:S(2)}, u32[]{:S(2)}) collective-permute-start(bf16[128,1024]{1,0:T(8,128)(2,1)S(1)} %pad_maximum_fusion.3), channel_id=1, source_target_pairs={{0,1},{1,0},{2,3},{3,2},{4,5},{5,4},{6,7},{7,6},{8,9},{9,8},{10,11... | collective-permute-start | bytes 786440 | tf_op jit(solution)/shard_map/ppermute | solution.py:46
  16.9 22.8 %collective-permute-start.9 = (bf16[512,1536]{1,0:T(8,128)(2,1)}, bf16[512,1536]{1,0:T(8,128)(2,1)S(1)}, u32[]{:S(2)}, u32[]{:S(2)}) collective-permute-start(bf16[512,1536]{1,0:T(8,128)(2,1)} %get-tuple-element.45), channel_id=1, source_target_pairs={{0,8},{8,0},{16,24},{24,16},{32,40},{40,32},{48,56},{56,48},{64,72... | collective-permute-start | bytes 4718600 | tf_op jit(solution)/shard_map/ppermute | solution.py:42
  22.9 11.4 %collective-permute-start.8 = (bf16[128,1024]{1,0:T(8,128)(2,1)S(1)}, bf16[128,1024]{1,0:T(8,128)(2,1)S(1)}, u32[]{:S(2)}, u32[]{:S(2)}) collective-permute-start(bf16[128,1024]{1,0:T(8,128)(2,1)S(1)} %collective-permute-done.5), channel_id=1, source_target_pairs={{0,1},{1,0},{2,3},{3,2},{4,5},{5,4},{6,7},{7,6},{8,9},{9,8},{10,11... | collective-permute-start | bytes 786440 | tf_op jit(solution)/shard_map/ppermute | solution.py:46
  24.2 10.2 %collective-permute-start.7 = (bf16[128,1024]{1,0:T(8,128)(2,1)S(1)}, bf16[128,1024]{1,0:T(8,128)(2,1)S(1)}, u32[]{:S(2)}, u32[]{:S(2)}) collective-permute-start(bf16[128,1024]{1,0:T(8,128)(2,1)S(1)} %collective-permute-done.1), channel_id=1, source_target_pairs={{0,2},{1,3},{2,4},{3,5},{4,6},{5,7},{6,0},{7,1},{8,10},{9,11},{10,... | collective-permute-start | bytes 786440 | tf_op jit(solution)/shard_map/ppermute | solution.py:46
  25.3 9.2 %collective-permute-start.6 = (bf16[128,1024]{1,0:T(8,128)(2,1)S(1)}, bf16[128,1024]{1,0:T(8,128)(2,1)S(1)}, u32[]{:S(2)}, u32[]{:S(2)}) collective-permute-start(bf16[128,1024]{1,0:T(8,128)(2,1)S(1)} %collective-permute-done.1), channel_id=1, source_target_pairs={{0,6},{1,7},{2,0},{3,1},{4,2},{5,3},{6,4},{7,5},{8,14},{9,15},{10,... | collective-permute-start | bytes 786440 | tf_op jit(solution)/shard_map/ppermute | solution.py:46
  27.7 1.4 copy-start.1
  29.8 23.6 %collective-permute-start.10 = (bf16[640,768]{1,0:T(8,128)(2,1)S(1)}, bf16[640,768]{1,0:T(8,128)(2,1)S(1)}, u32[]{:S(2)}, u32[]{:S(2)}) collective-permute-start(bf16[640,768]{1,0:T(8,128)(2,1)S(1)} %add_convert_fusion.2), channel_id=1, source_target_pairs={{0,96},{8,104},{16,112},{24,120},{32,0},{40,8},{48,16},{56,24},{64... | collective-permute-start | bytes 2949128 | tf_op jit(solution)/shard_map/ppermute | solution.py:42
  34.4 22.9 %collective-permute-start.11 = (bf16[640,768]{1,0:T(8,128)(2,1)S(1)}, bf16[640,768]{1,0:T(8,128)(2,1)S(1)}, u32[]{:S(2)}, u32[]{:S(2)}) collective-permute-start(bf16[640,768]{1,0:T(8,128)(2,1)S(1)} %add_convert_fusion.1), channel_id=1, source_target_pairs={{0,32},{8,40},{16,48},{24,56},{32,64},{40,72},{48,80},{56,88},{64,... | collective-permute-start | bytes 2949128 | tf_op jit(solution)/shard_map/ppermute | solution.py:42
  35.5 3.3 %copy-start = (bf16[512,1536]{1,0:T(8,128)(2,1)S(1)}, bf16[512,1536]{1,0:T(8,128)(2,1)}, u32[]{:S(2)}) copy-start(bf16[512,1536]{1,0:T(8,128)(2,1)} %get-tuple-element.45) | copy-start | bytes 4718596
  35.5 34.4 %collective-permute-start.16 = (bf16[384,768]{1,0:T(8,128)(2,1)S(1)}, bf16[384,768]{1,0:T(8,128)(2,1)S(1)}, u32[]{:S(2)}, u32[]{:S(2)}) collective-permute-start(bf16[384,768]{1,0:T(8,128)(2,1)S(1)} %fusion.2), channel_id=1, source_target_pairs={{0,16},{8,24},{16,0},{24,8},{32,48},{40,56},{48,32},{56,40},{64,80... | collective-permute-start | bytes 1769480 | tf_op jit(solution)/shard_map/ppermute | solution.py:42
  40.2 30.0 %collective-permute-start.15 = (bf16[384,768]{1,0:T(8,128)(2,1)S(1)}, bf16[384,768]{1,0:T(8,128)(2,1)S(1)}, u32[]{:S(2)}, u32[]{:S(2)}) collective-permute-start(bf16[384,768]{1,0:T(8,128)(2,1)S(1)} %fusion.1), channel_id=1, source_target_pairs={{0,16},{8,24},{16,0},{24,8},{32,48},{40,56},{48,32},{56,40},{64,80... | collective-permute-start | bytes 1769480 | tf_op jit(solution)/shard_map/ppermute | solution.py:42
  58.5 10.2 %collective-permute-start.13 = (bf16[640,384]{1,0:T(8,128)(2,1)S(1)}, bf16[640,384]{1,0:T(8,128)(2,1)S(1)}, u32[]{:S(2)}, u32[]{:S(2)}) collective-permute-start(bf16[640,384]{1,0:T(8,128)(2,1)S(1)} %get-tuple-element.71), channel_id=1, source_target_pairs={{0,96},{8,104},{16,112},{24,120},{32,0},{40,8},{48,16},{56,24},{64... | collective-permute-start | bytes 1474568 | tf_op jit(solution)/shard_map/ppermute | solution.py:42
  58.5 11.4 %collective-permute-start.12 = (bf16[640,384]{1,0:T(8,128)(2,1)S(1)}, bf16[640,384]{1,0:T(8,128)(2,1)S(1)}, u32[]{:S(2)}, u32[]{:S(2)}) collective-permute-start(bf16[640,384]{1,0:T(8,128)(2,1)S(1)} %get-tuple-element.73), channel_id=1, source_target_pairs={{0,32},{8,40},{16,48},{24,56},{32,64},{40,72},{48,80},{56,88},{64,... | collective-permute-start | bytes 1474568 | tf_op jit(solution)/shard_map/ppermute | solution.py:42
  69.9 3.3 %copy-start.4 = (bf16[640,384]{1,0:T(8,128)(2,1)}, bf16[640,384]{1,0:T(8,128)(2,1)S(1)}, u32[]{:S(2)}) copy-start(bf16[640,384]{1,0:T(8,128)(2,1)S(1)} %collective-permute-done.12.refs_4_) | copy-start | bytes 1474564
  70.1 6.9 %collective-permute-start.18 = (bf16[2,192,384]{2,1,0:T(8,128)(2,1)S(1)}, bf16[2,192,384]{2,1,0:T(8,128)(2,1)S(1)}, u32[]{:S(2)}, u32[]{:S(2)}) collective-permute-start(bf16[2,192,384]{2,1,0:T(8,128)(2,1)S(1)} %pad_maximum_fusion.2), channel_id=1, source_target_pairs={{0,32},{8,40},{16,48},{24,56},{32,64},{40,72},{48,80},{56,88},{64,... | collective-permute-start | bytes 884744 | tf_op jit(solution)/shard_map/ppermute | solution.py:42
  70.3 7.4 %collective-permute-start.17 = (bf16[2,192,384]{2,1,0:T(8,128)(2,1)S(1)}, bf16[2,192,384]{2,1,0:T(8,128)(2,1)S(1)}, u32[]{:S(2)}, u32[]{:S(2)}) collective-permute-start(bf16[2,192,384]{2,1,0:T(8,128)(2,1)S(1)} %pad_maximum_fusion.1), channel_id=1, source_target_pairs={{0,96},{8,104},{16,112},{24,120},{32,0},{40,8},{48,16},{56,24},{64... | collective-permute-start | bytes 884744 | tf_op jit(solution)/shard_map/ppermute | solution.py:42
  73.2 12.1 %collective-permute-start.14 = (bf16[640,384]{1,0:T(8,128)(2,1)S(1)}, bf16[640,384]{1,0:T(8,128)(2,1)S(1)}, u32[]{:S(2)}, u32[]{:S(2)}) collective-permute-start(bf16[640,384]{1,0:T(8,128)(2,1)S(1)} %add_convert_fusion.3), channel_id=1, source_target_pairs={{0,16},{8,24},{16,0},{24,8},{32,48},{40,56},{48,32},{56,40},{64,80... | collective-permute-start | bytes 1474568 | tf_op jit(solution)/shard_map/ppermute | solution.py:42
  77.7 5.7 %collective-permute-start.19 = (bf16[192,384]{1,0:T(8,128)(2,1)}, bf16[192,384]{1,0:T(8,128)(2,1)}, u32[]{:S(2)}, u32[]{:S(2)}) collective-permute-start(bf16[192,384]{1,0:T(8,128)(2,1)} %fusion.43), channel_id=1, source_target_pairs={{0,32},{8,40},{16,48},{24,56},{32,64},{40,72},{48,80},{56,88},{64,... | collective-permute-start | bytes 442376 | tf_op jit(solution)/shard_map/ppermute | solution.py:42
  78.4 5.1 %collective-permute-start.20 = (bf16[192,384]{1,0:T(8,128)(2,1)}, bf16[192,384]{1,0:T(8,128)(2,1)}, u32[]{:S(2)}, u32[]{:S(2)}) collective-permute-start(bf16[192,384]{1,0:T(8,128)(2,1)} %fusion.40), channel_id=1, source_target_pairs={{0,96},{8,104},{16,112},{24,120},{32,0},{40,8},{48,16},{56,24},{64... | collective-permute-start | bytes 442376 | tf_op jit(solution)/shard_map/ppermute | solution.py:42
  81.7 9.0 %copy-start.3 = (bf16[1024,512]{1,0:T(8,128)(2,1)S(1)}, bf16[1024,512]{1,0:T(8,128)(2,1)}, u32[]{:S(2)}) copy-start(bf16[1024,512]{1,0:T(8,128)(2,1)} %param.13) | copy-start | bytes 3145732
  85.3 0.8 copy-start.5
  90.7 13.1 %collective-permute-start.22 = (bf16[1024,512]{1,0:T(8,128)(2,1)S(1)}, bf16[1024,512]{1,0:T(8,128)(2,1)S(1)}, u32[]{:S(2)}, u32[]{:S(2)}) collective-permute-start(bf16[1024,512]{1,0:T(8,128)(2,1)S(1)} %copy-done.3), channel_id=1, source_target_pairs={{0,8},{8,0},{16,24},{24,16},{32,40},{40,32},{48,56},{56,48},{64,72... | collective-permute-start | bytes 3145736 | tf_op jit(solution)/shard_map/ppermute | solution.py:42
  96.4 2.5 %collective-permute-start.21 = (f32[26,8,128]{2,1,0:T(8,128)}, f32[26,8,128]{2,1,0:T(8,128)S(1)}, u32[]{:S(2)}, u32[]{:S(2)}) collective-permute-start(f32[26,8,128]{2,1,0:T(8,128)} %get-tuple-element.62.mine_ref), channel_id=1, source_target_pairs={{0,8},{8,0},{16,24},{24,16},{32,40},{40,32},{48,56},{56,48},{64,72... | collective-permute-start | bytes 319496 | tf_op jit(solution)/shard_map/ppermute | solution.py:42
  99.0 0.6 copy-start.6
  103.8 4.3 %copy-start.2 = (bf16[1024,128]{1,0:T(8,128)(2,1)S(1)}, bf16[1024,128]{1,0:T(8,128)(2,1)}, u32[]{:S(2)}) copy-start(bf16[1024,128]{1,0:T(8,128)(2,1)} %filtered.1) | copy-start | bytes 786436
  103.8 13.5 %collective-permute-start.24 = (bf16[1024,128]{1,0:T(8,128)(2,1)}, bf16[1024,128]{1,0:T(8,128)(2,1)S(1)}, u32[]{:S(2)}, u32[]{:S(2)}) collective-permute-start(bf16[1024,128]{1,0:T(8,128)(2,1)} %filtered.1), channel_id=1, source_target_pairs={{0,64},{8,72},{16,80},{24,88},{32,96},{40,104},{48,112},{56,120},{... | collective-permute-start | bytes 786440 | tf_op jit(solution)/shard_map/ppermute | solution.py:42
  105.5 9.2 %collective-permute-start.23 = (bf16[1024,128]{1,0:T(8,128)(2,1)}, bf16[1024,128]{1,0:T(8,128)(2,1)S(1)}, u32[]{:S(2)}, u32[]{:S(2)}) collective-permute-start(bf16[1024,128]{1,0:T(8,128)(2,1)} %filtered.1), channel_id=1, source_target_pairs={{0,16},{8,24},{16,0},{24,8},{32,48},{40,56},{48,32},{56,40},{64,80... | collective-permute-start | bytes 786440 | tf_op jit(solution)/shard_map/ppermute | solution.py:42
  108.1 12.0 %collective-permute-start.26 = (bf16[1024,128]{1,0:T(8,128)(2,1)S(1)}, bf16[1024,128]{1,0:T(8,128)(2,1)S(1)}, u32[]{:S(2)}, u32[]{:S(2)}) collective-permute-start(bf16[1024,128]{1,0:T(8,128)(2,1)S(1)} %copy-done.2), channel_id=1, source_target_pairs={{0,32},{8,40},{16,48},{24,56},{32,64},{40,72},{48,80},{56,88},{64,... | collective-permute-start | bytes 786440 | tf_op jit(solution)/shard_map/ppermute | solution.py:42
  110.5 9.5 %collective-permute-start.25 = (bf16[1024,128]{1,0:T(8,128)(2,1)S(1)}, bf16[1024,128]{1,0:T(8,128)(2,1)S(1)}, u32[]{:S(2)}, u32[]{:S(2)}) collective-permute-start(bf16[1024,128]{1,0:T(8,128)(2,1)S(1)} %copy-done.2), channel_id=1, source_target_pairs={{0,96},{8,104},{16,112},{24,120},{32,0},{40,8},{48,16},{56,24},{64... | collective-permute-start | bytes 786440 | tf_op jit(solution)/shard_map/ppermute | solution.py:42
  114.7 10.4 %collective-permute-start.28 = (bf16[1024,128]{1,0:T(8,128)(2,1)S(1)}, bf16[1024,128]{1,0:T(8,128)(2,1)S(1)}, u32[]{:S(2)}, u32[]{:S(2)}) collective-permute-start(bf16[1024,128]{1,0:T(8,128)(2,1)S(1)} %collective-permute-done.23), channel_id=1, source_target_pairs={{0,32},{8,40},{16,48},{24,56},{32,64},{40,72},{48,80},{56,88},{64,... | collective-permute-start | bytes 786440 | tf_op jit(solution)/shard_map/ppermute | solution.py:42
  117.0 8.0 %collective-permute-start.27 = (bf16[1024,128]{1,0:T(8,128)(2,1)S(1)}, bf16[1024,128]{1,0:T(8,128)(2,1)S(1)}, u32[]{:S(2)}, u32[]{:S(2)}) collective-permute-start(bf16[1024,128]{1,0:T(8,128)(2,1)S(1)} %collective-permute-done.23), channel_id=1, source_target_pairs={{0,96},{8,104},{16,112},{24,120},{32,0},{40,8},{48,16},{56,24},{64... | collective-permute-start | bytes 786440 | tf_op jit(solution)/shard_map/ppermute | solution.py:42
  117.3 7.8 %collective-permute-start.29 = (bf16[1024,128]{1,0:T(8,128)(2,1)S(1)}, bf16[1024,128]{1,0:T(8,128)(2,1)S(1)}, u32[]{:S(2)}, u32[]{:S(2)}) collective-permute-start(bf16[1024,128]{1,0:T(8,128)(2,1)S(1)} %collective-permute-done.24), channel_id=1, source_target_pairs={{0,16},{8,24},{16,0},{24,8},{32,48},{40,56},{48,32},{56,40},{64,80... | collective-permute-start | bytes 786440 | tf_op jit(solution)/shard_map/ppermute | solution.py:42
  127.1 5.3 %collective-permute-start.30 = (bf16[128,1024]{1,0:T(8,128)(2,1)S(1)}, bf16[128,1024]{1,0:T(8,128)(2,1)S(1)}, u32[]{:S(2)}, u32[]{:S(2)}) collective-permute-start(bf16[128,1024]{1,0:T(8,128)(2,1)S(1)} %convolution_convert_fusion.4), channel_id=1, source_target_pairs={{0,1},{1,0},{2,3},{3,2},{4,5},{5,4},{6,7},{7,6},{8,9},{9,8},{10,11... | collective-permute-start | bytes 786440 | tf_op jit(solution)/shard_map/ppermute | solution.py:46
  127.4 8.3 %collective-permute-start.34 = (bf16[128,1024]{1,0:T(8,128)(2,1)S(1)}, bf16[128,1024]{1,0:T(8,128)(2,1)S(1)}, u32[]{:S(2)}, u32[]{:S(2)}) collective-permute-start(bf16[128,1024]{1,0:T(8,128)(2,1)S(1)} %convolution_convert_fusion.1), channel_id=1, source_target_pairs={{0,2},{1,3},{2,4},{3,5},{4,6},{5,7},{6,0},{7,1},{8,10},{9,11},{10,... | collective-permute-start | bytes 786440 | tf_op jit(solution)/shard_map/ppermute | solution.py:46
  127.4 8.3 %collective-permute-start.35 = (bf16[128,1024]{1,0:T(8,128)(2,1)S(1)}, bf16[128,1024]{1,0:T(8,128)(2,1)S(1)}, u32[]{:S(2)}, u32[]{:S(2)}) collective-permute-start(bf16[128,1024]{1,0:T(8,128)(2,1)S(1)} %convolution_convert_fusion), channel_id=1, source_target_pairs={{0,6},{1,7},{2,0},{3,1},{4,2},{5,3},{6,4},{7,5},{8,14},{9,15},{10,... | collective-permute-start | bytes 786440 | tf_op jit(solution)/shard_map/ppermute | solution.py:46
  132.9 7.0 %collective-permute-start.33 = (bf16[128,1024]{1,0:T(8,128)(2,1)S(1)}, bf16[128,1024]{1,0:T(8,128)(2,1)S(1)}, u32[]{:S(2)}, u32[]{:S(2)}) collective-permute-start(bf16[128,1024]{1,0:T(8,128)(2,1)S(1)} %fusion.11), channel_id=1, source_target_pairs={{0,4},{1,5},{2,6},{3,7},{4,0},{5,1},{6,2},{7,3},{8,12},{9,13},{10,... | collective-permute-start | bytes 786440 | tf_op jit(solution)/shard_map/ppermute | solution.py:46
  133.0 14.5 %collective-permute-start.31 = (bf16[128,1024]{1,0:T(8,128)(2,1)S(1)}, bf16[128,1024]{1,0:T(8,128)(2,1)S(1)}, u32[]{:S(2)}, u32[]{:S(2)}) collective-permute-start(bf16[128,1024]{1,0:T(8,128)(2,1)S(1)} %convolution_convert_fusion.3), channel_id=1, source_target_pairs={{0,2},{1,3},{2,4},{3,5},{4,6},{5,7},{6,0},{7,1},{8,10},{9,11},{10,... | collective-permute-start | bytes 786440 | tf_op jit(solution)/shard_map/ppermute | solution.py:46
  134.0 13.5 %collective-permute-start.32 = (bf16[128,1024]{1,0:T(8,128)(2,1)S(1)}, bf16[128,1024]{1,0:T(8,128)(2,1)S(1)}, u32[]{:S(2)}, u32[]{:S(2)}) collective-permute-start(bf16[128,1024]{1,0:T(8,128)(2,1)S(1)} %convolution_convert_fusion.2), channel_id=1, source_target_pairs={{0,6},{1,7},{2,0},{3,1},{4,2},{5,3},{6,4},{7,5},{8,14},{9,15},{10,... | collective-permute-start | bytes 786440 | tf_op jit(solution)/shard_map/ppermute | solution.py:46
  136.2 11.3 %collective-permute-start.36 = (bf16[128,1024]{1,0:T(8,128)(2,1)S(1)}, bf16[128,1024]{1,0:T(8,128)(2,1)S(1)}, u32[]{:S(2)}, u32[]{:S(2)}) collective-permute-start(bf16[128,1024]{1,0:T(8,128)(2,1)S(1)} %fusion.10), channel_id=1, source_target_pairs={{0,1},{1,0},{2,3},{3,2},{4,5},{5,4},{6,7},{7,6},{8,9},{9,8},{10,11... | collective-permute-start | bytes 786440 | tf_op jit(solution)/shard_map/ppermute | solution.py:46
  148.1 4.8 %collective-permute-start.37 = (bf16[128,512]{1,0:T(8,128)(2,1)S(1)}, bf16[128,512]{1,0:T(8,128)(2,1)S(1)}, u32[]{:S(2)}, u32[]{:S(2)}) collective-permute-start(bf16[128,512]{1,0:T(8,128)(2,1)S(1)} %get-tuple-element.82), channel_id=1, source_target_pairs={{0,8},{8,0},{16,24},{24,16},{32,40},{40,32},{48,56},{56,48},{64,72... | collective-permute-start | bytes 393224 | tf_op jit(solution)/shard_map/ppermute | solution.py:42
